TPU v7x, 256 devices: a whole 4x4x8 slice. The times are simulated.
256 devices in a mesh: dp: 32 (over y, z_hi, core), factor: 8 (over z_lo, x).
Axes of the slice: x: 4, y: 4, z: 8 (z_hi: 4, z_lo: 2; z = z_hi * 2 + z_lo), core: 2. Of those that a mesh axis runs over, the one named last changes fastest.
Arguments:
- grad_out: bfloat16 [32, 128, 14336], P('dp', None, 'factor'), may hold values from -6 to 6
- act_in: bfloat16 [32, 128, 4096], P('dp', None, 'factor'), may hold values from -6 to 6
- basis_out: bfloat16 [14336, 14336], P('factor', 'dp'), may hold values from -0.046875 to 0.046875
- basis_in: bfloat16 [4096, 4096], P('factor', 'dp'), may hold values from -0.09375 to 0.09375
- eigen_vals: bfloat16 [14336, 4096], P('dp'), may hold values from 0.25 to 4
- query_out: bfloat16 [16, 8, 14336], P(None, None, 'factor'), may hold values from -0.01171875 to 0.01171875
- query_in: bfloat16 [16, 8, 4096], P(None, None, 'factor'), may hold values from -0.01171875 to 0.01171875
Outputs:
- scores: float32 [32, 16], P('factor')
All inputs are finite; a program needn't handle non-finite values.
Results may differ from a plain program's by a relative error of at most 0.023.
Values may be sent and summed in bfloat16 or wider, within the bound.
No kernel may reach another device: no remote copies, remote signals or barrier semaphores. Data moves between devices by JAX's collectives and lax.ppermute only.
A program may use at most 128 MiB of HBM per device.

v0:
```python
import jax
import jax.numpy as jnp
from jax import lax
from jax.experimental import pallas as pl
from jax.experimental.pallas import tpu as pltpu
from jax.sharding import Mesh, PartitionSpec as P


AXES = ("y", "zh", "c", "zl", "x")
SIZES = (4, 4, 2, 2, 4)
BF = jnp.bfloat16
F32 = jnp.float32


def shift(value, axis, by):
    n = SIZES[AXES.index(axis)]
    return lax.ppermute(value, axis, [(i, (i + by) % n) for i in range(n)])


def gather(value, axis):
    return jnp.stack([value] + [shift(value, axis, -by) for by in (1, 2, 3)])


def exchange(value, axes):
    return lax.all_to_all(value, axes, 0, 0, tiled=True)


def spread(value, axes, n):
    return exchange(jnp.broadcast_to(value[None], (n,) + value.shape), axes)


def dot(a, b):
    return jnp.dot(a, b, preferred_element_type=F32)


def dot_t(a, b):
    return lax.dot_general(a, b, (((1,), (1,)), ((), ())), preferred_element_type=F32)


def rotate_in_kernel(at_ref, act, w, out):
    y = lax.rem(at_ref[0] + pl.program_id(0), 4)
    for z in range(4):
        zh = lax.rem(at_ref[1] + z, 4)
        out[lax.rem(zh, 2), y, zh // 2] = dot(act[0, z], w[...]).astype(BF)


def rotate_in(at, act, w):
    tokens, unit = act.shape[2:]
    n = w.shape[1]
    spec = pltpu.PrefetchScalarGridSpec(
        num_scalar_prefetch=1,
        grid=(4,),
        in_specs=[
            pl.BlockSpec((1, 4, tokens, unit), lambda y, _: (y, 0, 0, 0)),
            pl.BlockSpec((unit, n), lambda y, _: (0, 0)),
        ],
        out_specs=pl.BlockSpec((2, 4, 2, tokens, n), lambda y, _: (0, 0, 0, 0, 0)),
    )
    return pl.pallas_call(
        rotate_in_kernel,
        grid_spec=spec,
        out_shape=jax.ShapeDtypeStruct((2, 4, 2, tokens, n), BF),
        cost_estimate=pl.CostEstimate(
            flops=2 * 16 * tokens * unit * n, bytes_accessed=2 * 16 * tokens * (unit + n), transcendentals=0
        ),
        name="rotate_in",
    )(at, act, w)


def score_kernel(at_ref, grad, act, eig0, eig1, value, query, out, flipped, total):
    step = pl.program_id(0)
    n = eig0.shape[0]
    width = act.shape[4]

    @pl.when(step == 0)
    def _():
        for s in range(2):
            flipped[s] = grad[s].T
        total[...] = jnp.zeros_like(total)

    def body(e, _):
        zh = lax.rem(at_ref[1] + e, 4)
        cols = pl.ds(pl.multiple_of(zh * width, width), width)
        held = value[:, cols]
        for k, eig in enumerate((eig0, eig1)):
            here = slice(k * n, (k + 1) * n)
            inverse = 1.0 / eig[:, cols].astype(F32)
            for s in range(2):
                which = at_ref[2] if s == 0 else 1 - at_ref[2]
                contracted = dot(flipped[s, here, :], act[0, e, which])
                total[s, here, :] += dot_t((contracted * inverse).astype(BF), held)
        return 0

    lax.fori_loop(0, 4, body, 0)

    @pl.when(step == pl.num_programs(0) - 1)
    def _():
        for s in range(2):
            out[s : s + 1, :] = (total[s] * query[...]).sum(0, keepdims=True)


def score(at, grad, act, eig0, eig1, value, query):
    _, tokens, both = grad.shape
    n = eig0.shape[0]
    width = act.shape[4]
    cols = 4 * width
    rows = value.shape[0]
    spec = pltpu.PrefetchScalarGridSpec(
        num_scalar_prefetch=1,
        grid=(4,),
        in_specs=[
            pl.BlockSpec((2, tokens, both), lambda j, at: (0, 0, 0)),
            pl.BlockSpec((1, 4, 2, tokens, width), lambda j, at: (j, 0, 0, 0, 0)),
            pl.BlockSpec((n, cols), lambda j, at: (0, lax.rem(at[0] + j, 4))),
            pl.BlockSpec((n, cols), lambda j, at: (0, lax.rem(at[0] + j, 4))),
            pl.BlockSpec((rows, cols), lambda j, at: (0, lax.rem(at[0] + j, 4))),
            pl.BlockSpec((both, rows), lambda j, at: (0, 0)),
        ],
        out_specs=pl.BlockSpec((8, rows), lambda j, at: (0, 0)),
        scratch_shapes=[pltpu.VMEM((2, both, tokens), BF), pltpu.VMEM((2, both, rows), F32)],
    )
    return pl.pallas_call(
        score_kernel,
        grid_spec=spec,
        out_shape=jax.ShapeDtypeStruct((8, rows), F32),
        cost_estimate=pl.CostEstimate(
            flops=2 * 2 * both * 4 * cols * (tokens + rows),
            bytes_accessed=2 * both * 4 * cols,
            transcendentals=0,
        ),
        name="score",
    )(at, grad, act, eig0, eig1, value, query)


def shards(grad_out, act_in, basis_out, basis_in, eigen_vals, query_out, query_in):
    yi, zi, ci, li = (lax.axis_index(a) for a in ("y", "zh", "c", "zl"))
    tokens, unit = grad_out.shape[1:]
    queries, rank = query_out.shape[:2]
    rows = queries * rank
    half_rows = rows // 2
    width = basis_out.shape[1]
    first = ci == 0

    same = li == zi % 2
    low = jnp.where(same, zi, (zi + 3) % 4) // 2
    at = jnp.stack([yi, zi, low]).astype(jnp.int32)

    out_t = basis_out.T
    out_both = jnp.concatenate([out_t, shift(out_t, "c", 1)], 0)
    in_other = shift(basis_in, "c", 1)
    in_both = jnp.where(
        first, jnp.concatenate([basis_in, in_other], 1), jnp.concatenate([in_other, basis_in], 1)
    )
    eigen_other = shift(eigen_vals, "c", 1)

    act = gather(gather(act_in[0], "zh"), "y")
    part = rotate_in(at, act, in_both)
    both = part.shape[-1]
    act_sum = exchange(part.reshape(8, 2, tokens, both), ("zl", "x"))
    act_sum = act_sum.reshape(8, 2, tokens, both).astype(F32).sum(0).astype(BF)
    act_rot = gather(gather(act_sum, "zh"), "y")

    mine = lax.dynamic_slice_in_dim(query_out.reshape(rows, unit), ci * half_rows, half_rows, 0)
    mine_in = lax.dynamic_slice_in_dim(query_in.reshape(rows, -1), ci * half_rows, half_rows, 0)
    query = jnp.concatenate([dot_t(mine, out_both), dot(mine_in, in_both)], 1).astype(BF)
    some = half_rows // 8
    query = exchange(query.reshape(8, some, -1), ("zl", "x")).reshape(8, some, -1)
    query = query.astype(F32).sum(0).astype(BF)
    value = spread(query[:, 2 * width :], ("y", "zh"), 16).reshape(16, some, both)
    value = value.transpose(1, 0, 2).reshape(some, 16 * both)
    query = spread(jnp.concatenate([query[:, : 2 * width], value], 1), ("zl", "x"), 8)
    query = query.reshape(half_rows, -1)
    swapped = jnp.concatenate(
        [query[:, width : 2 * width], query[:, :width], query[:, 2 * width :]], 1
    )
    query = jnp.concatenate([query, shift(swapped, "c", 1)], 0)
    query_rot = query[:, : 2 * width].astype(F32).T
    value_rot = query[:, 2 * width :]

    grad = grad_out[0]
    plus, far, minus = (shift(grad, "zh", -by) for by in (1, 2, 3))
    blocks = []
    for some_blocks in ((grad,), (plus, minus), (far,)):
        some_blocks = jnp.stack(some_blocks)
        found = lax.all_gather(some_blocks, "y", axis=0, tiled=True)
        product = dot_t(found.reshape(-1, unit), out_both).astype(BF)
        product = exchange(product.reshape(-1, tokens, 2 * width), "x")
        product = product.reshape(4, -1, tokens, 2 * width).astype(F32).sum(0)
        blocks.extend(product[b] for b in range(product.shape[0]))
    own, plus, minus, far = blocks
    slots = []
    for k, (a, b) in enumerate(((own, minus), (plus, far))):
        mine_first = same if k == 0 else ~same
        keep = jnp.where(mine_first, a, b)
        give = jnp.where(mine_first, b, a).astype(BF)
        if k == 0:
            give, keep = lax.optimization_barrier((give, keep))
        got = shift(give, "zl", 1)
        slots.append((keep.astype(BF).astype(F32) + got.astype(F32)).astype(BF))

    result = score(at, jnp.stack(slots), act_rot, eigen_vals, eigen_other, value_rot, query_rot)[:2]
    result = result.reshape(2, queries, rank).sum(-1)
    result = jnp.where(low == 0, result, result[::-1])
    turned = jnp.concatenate([result[:, queries // 2 :], result[:, : queries // 2]], 1)
    result = jnp.where(first, result, turned)
    result = spread(result, ("y", "zh"), 16).reshape(16, 2, queries).sum(0)
    result = spread(result, ("c", "zl", "x"), 16).reshape(2, 2, 4, 2, queries)
    result = result.transpose(2, 3, 1, 0, 4).reshape(8, 4, queries)
    return lax.dynamic_index_in_dim(result, li * 4 + lax.axis_index("x"), 0, False)


def solution(mesh):
    fine = Mesh(mesh.devices.reshape(SIZES), AXES)
    dp, factor = ("y", "zh", "c"), ("zl", "x")
    in_specs = (
        P(dp, None, factor),
        P(dp, None, factor),
        P(factor, dp),
        P(factor, dp),
        P(dp, None),
        P(None, None, factor),
        P(None, None, factor),
    )

    return jax.shard_map(
        shards, mesh=fine, in_specs=in_specs, out_specs=P(factor, None), check_vma=False
    )
```

profile of v0, /device:TPU:2, one launch (start us, length us, event | category | flops | bytes accessed | tf_op | source)
XLA Modules:
  0.0 309.1 jit_solution(4850414106299892178)
XLA Ops:
  7.3 7.3 %collective-permute-start.4 = (bf16[128,1792]{1,0:T(8,128)(2,1)}, bf16[128,1792]{1,0:T(8,128)(2,1)S(1)}, u32[]{:S(2)}, u32[]{:S(2)}) collective-permute-start(bf16[128,1792]{1,0:T(8,128)(2,1)} %bitcast.92), channel_id=1, source_target_pairs={{0,32},{16,48},{32,0},{48,16},{1,33},{17,49},{33,1},{49,17},{2,34}... | collective-permute-start | bytes 1376264 | tf_op jit(solution)/shard_map/ppermute | solution.py:17
  14.6 13.0 %collective-permute-done.4 = bf16[128,1792]{1,0:T(8,128)(2,1)S(1)} collective-permute-done((bf16[128,1792]{1,0:T(8,128)(2,1)}, bf16[128,1792]{1,0:T(8,128)(2,1)S(1)}, u32[]{:S(2)}, u32[]{:S(2)}) %collective-permute-start.4) | collective-permute-done | bytes 458784 | tf_op jit(solution)/shard_map/ppermute | solution.py:17
  28.4 12.3 %collective-permute-start = (bf16[128,1792]{1,0:T(8,128)(2,1)}, bf16[128,1792]{1,0:T(8,128)(2,1)S(1)}, u32[]{:S(2)}, u32[]{:S(2)}) collective-permute-start(bf16[128,1792]{1,0:T(8,128)(2,1)} %bitcast.93), channel_id=1, source_target_pairs={{0,48},{16,0},{32,16},{48,32},{1,49},{17,1},{33,17},{49,33},{2,50}... | collective-permute-start | bytes 1376264 | tf_op jit(solution)/shard_map/ppermute | solution.py:17
  40.7 17.9 %collective-permute-done = bf16[128,1792]{1,0:T(8,128)(2,1)S(1)} collective-permute-done((bf16[128,1792]{1,0:T(8,128)(2,1)}, bf16[128,1792]{1,0:T(8,128)(2,1)S(1)}, u32[]{:S(2)}, u32[]{:S(2)}) %collective-permute-start) | collective-permute-done | bytes 458784 | tf_op jit(solution)/shard_map/ppermute | solution.py:17
  58.6 5.5 %collective-permute-done.1 = bf16[128,1792]{1,0:T(8,128)(2,1)S(1)} collective-permute-done((bf16[128,1792]{1,0:T(8,128)(2,1)}, bf16[128,1792]{1,0:T(8,128)(2,1)S(1)}, u32[]{:S(2)}, u32[]{:S(2)}) %collective-permute-start.1) | collective-permute-done | bytes 458784 | tf_op jit(solution)/shard_map/ppermute | solution.py:17
  65.2 2.7 collective-permute-start.7
  68.2 2.9 collective-permute-done.6
  71.1 6.3 %collective-permute-done.7 = bf16[128,512]{1,0:T(8,128)(2,1)S(1)} collective-permute-done((bf16[128,512]{1,0:T(8,128)(2,1)S(1)}, bf16[128,512]{1,0:T(8,128)(2,1)S(1)}, u32[]{:S(2)}, u32[]{:S(2)}) %collective-permute-start.7) | collective-permute-done | bytes 131104 | tf_op jit(solution)/shard_map/ppermute | solution.py:17
  77.4 2.5 collective-permute-done.8
  79.9 3.1 collective-permute-start.9
  86.8 3.0 fusion
  90.5 7.0 %all-to-all-start.4 = ((bf16[8,8,1152]{2,1,0:T(8,128)(2,1)}), bf16[8,8,1152]{2,1,0:T(8,128)(2,1)S(1)}, u32[]{:S(2)}, u32[]{:S(2)}) async-start(bf16[8,8,1152]{2,1,0:T(8,128)(2,1)} %pad_maximum_fusion.8), calls=%async_computation.4 | async-start | bytes 294912 | tf_op jit(solution)/shard_map/all_to_all | solution.py:25
  98.1 4.5 %all-to-all-done.4 = bf16[8,8,1152]{2,1,0:T(8,128)(2,1)S(1)} async-done(((bf16[8,8,1152]{2,1,0:T(8,128)(2,1)}), bf16[8,8,1152]{2,1,0:T(8,128)(2,1)S(1)}, u32[]{:S(2)}, u32[]{:S(2)}) %all-to-all-start.4) | async-done | bytes 147488 | tf_op jit(solution)/shard_map/all_to_all | solution.py:25
  103.3 3.9 %all-to-all-start.5 = ((bf16[16,8,256]{2,1,0:T(8,128)(2,1)}), bf16[16,8,256]{2,1,0:T(8,128)(2,1)S(1)}, u32[]{:S(2)}, u32[]{:S(2)}) async-start(bf16[16,8,256]{2,1,0:T(8,128)(2,1)} %broadcast_in_dim.8), calls=%async_computation.5 | async-start | bytes 131072 | tf_op jit(solution)/shard_map/all_to_all | solution.py:25
  107.2 10.2 %collective-permute-done.11 = bf16[4,128,512]{2,1,0:T(8,128)(2,1)S(1)} collective-permute-done((bf16[4,128,512]{2,1,0:T(8,128)(2,1)S(1)}, bf16[4,128,512]{2,1,0:T(8,128)(2,1)S(1)}, u32[]{:S(2)}, u32[]{:S(2)}) %collective-permute-start.11) | collective-permute-done | bytes 524320 | tf_op jit(solution)/shard_map/ppermute | solution.py:17
  117.4 1.6 pad_maximum_fusion.1.act
  119.0 4.8 %rotate_in.1 = bf16[2,4,2,128,256]{4,3,2,1,0:T(8,128)(2,1)} custom-call(s32[3]{0:T(128)} %pad_add_fusion.at_ref, bf16[4,4,128,512]{3,2,1,0:T(8,128)(2,1)} %pad_maximum_fusion.1.act, bf16[512,256]{1,0:T(8,128)(2,1)} %copy-done.1), custom_call_target="tpu_custom_call" | custom-call | flops 536870912 | bytes 3145728 | tf_op jit(solution)/shard_map/rotate_in/pallas_call | solution.py:59
  123.9 4.9 %all-to-all-start.3 = ((bf16[8,2,128,256]{3,2,1,0:T(8,128)(2,1)}), bf16[8,2,128,256]{3,2,1,0:T(8,128)(2,1)S(1)}, u32[]{:S(2)}, u32[]{:S(2)}) async-start(bf16[8,2,128,256]{3,2,1,0:T(8,128)(2,1)} %bitcast.82), calls=%async_computation.3 | async-start | bytes 2097152 | tf_op jit(solution)/shard_map/all_to_all | solution.py:25
  128.8 13.7 %all-to-all-done.3 = bf16[8,2,128,256]{3,2,1,0:T(8,128)(2,1)S(1)} async-done(((bf16[8,2,128,256]{3,2,1,0:T(8,128)(2,1)}), bf16[8,2,128,256]{3,2,1,0:T(8,128)(2,1)S(1)}, u32[]{:S(2)}, u32[]{:S(2)}) %all-to-all-start.3) | async-done | bytes 1048608 | tf_op jit(solution)/shard_map/all_to_all | solution.py:25
  143.4 4.8 %all-to-all-start.6 = ((bf16[8,8,4992]{2,1,0:T(8,128)(2,1)}), bf16[8,8,4992]{2,1,0:T(8,128)(2,1)S(1)}, u32[]{:S(2)}, u32[]{:S(2)}) async-start(bf16[8,8,4992]{2,1,0:T(8,128)(2,1)} %broadcast_in_dim.9), calls=%async_computation.6 | async-start | bytes 1277952 | tf_op jit(solution)/shard_map/all_to_all | solution.py:25
  148.2 5.5 %convolution_convert_fusion.2 = bf16[896,512]{0,1:T(8,128)(2,1)} fusion(bf16[512,1792]{1,0:T(8,128)(2,1)} %bitcast.109, bf16[448,1792]{1,0:T(8,128)(2,1)} %collective-permute-done.2, bf16[448,1792]{1,0:T(8,128)(2,1)} %bitcast.112), kind=kOutput, calls=%fused_computation.8 | convolution fusion | flops 1651048448 | bytes 5963776 | tf_op jit(solution)/shard_map/dot_general | solution.py:37
  153.7 3.9 %all-to-all-done.6 = bf16[8,8,4992]{2,1,0:T(8,128)(2,1)S(1)} async-done(((bf16[8,8,4992]{2,1,0:T(8,128)(2,1)}), bf16[8,8,4992]{2,1,0:T(8,128)(2,1)S(1)}, u32[]{:S(2)}, u32[]{:S(2)}) %all-to-all-start.6) | async-done | bytes 639008 | tf_op jit(solution)/shard_map/all_to_all | solution.py:25
  157.6 4.7 %all-to-all-start.1 = ((bf16[4,128,896]{2,1,0:T(8,128)(2,1)}), bf16[4,128,896]{2,1,0:T(8,128)(2,1)S(1)}, u32[]{:S(2)}, u32[]{:S(2)}) async-start(bf16[4,128,896]{2,1,0:T(8,128)(2,1)} %bitcast.84), calls=%async_computation.1 | async-start | bytes 1835008 | tf_op jit(solution)/shard_map/all_to_all | solution.py:25
  162.3 5.5 %convolution_convert_fusion.1 = bf16[896,512]{0,1:T(8,128)(2,1)} fusion(bf16[512,1792]{1,0:T(8,128)(2,1)} %all-gather.9.cloned.1.call-done, bf16[448,1792]{1,0:T(8,128)(2,1)} %collective-permute-done.2, bf16[448,1792]{1,0:T(8,128)(2,1)} %bitcast.113), kind=kOutput, calls=%fused_computation.7 | convolution fusion | flops 1651048448 | bytes 5963776 | tf_op jit(solution)/shard_map/dot_general | solution.py:37
  167.8 5.7 %all-to-all-done.1 = bf16[4,128,896]{2,1,0:T(8,128)(2,1)S(1)} async-done(((bf16[4,128,896]{2,1,0:T(8,128)(2,1)}), bf16[4,128,896]{2,1,0:T(8,128)(2,1)S(1)}, u32[]{:S(2)}, u32[]{:S(2)}) %all-to-all-start.1) | async-done | bytes 917536 | tf_op jit(solution)/shard_map/all_to_all | solution.py:25
  173.5 5.6 %all-to-all-start.2 = ((bf16[4,128,896]{2,1,0:T(8,128)(2,1)}), bf16[4,128,896]{2,1,0:T(8,128)(2,1)}, u32[]{:S(2)}, u32[]{:S(2)}) async-start(bf16[4,128,896]{2,1,0:T(8,128)(2,1)} %bitcast.85), calls=%async_computation.2 | async-start | bytes 1835008 | tf_op jit(solution)/shard_map/all_to_all | solution.py:25
  179.2 8.3 %convolution_convert_fusion = bf16[1024,896]{1,0:T(8,128)(2,1)} fusion(bf16[1024,1792]{1,0:T(8,128)(2,1)} %bitcast.108, bf16[448,1792]{1,0:T(8,128)(2,1)} %collective-permute-done.2, bf16[448,1792]{1,0:T(8,128)(2,1)} %bitcast.114), kind=kOutput, calls=%fused_computation.6 | convolution fusion | flops 3295674368 | bytes 8716288 | tf_op jit(solution)/shard_map/dot_general | solution.py:37
  187.4 1.9 all-to-all-done.2
  189.3 5.8 %all-to-all-start = ((bf16[8,128,896]{2,1,0:T(8,128)(2,1)}), bf16[8,128,896]{2,1,0:T(8,128)(2,1)}, u32[]{:S(2)}, u32[]{:S(2)}) async-start(bf16[8,128,896]{2,1,0:T(8,128)(2,1)} %bitcast.83), calls=%async_computation | async-start | bytes 3670016 | tf_op jit(solution)/shard_map/all_to_all | solution.py:25
  196.1 2.2 collective-permute-start.15
  198.3 11.4 %collective-permute-done.13 = bf16[2,128,256]{2,1,0:T(8,128)(2,1)S(1)} collective-permute-done((bf16[2,128,256]{2,1,0:T(8,128)(2,1)S(1)}, bf16[2,128,256]{2,1,0:T(8,128)(2,1)S(1)}, u32[]{:S(2)}, u32[]{:S(2)}) %collective-permute-start.13) | collective-permute-done | bytes 131104 | tf_op jit(solution)/shard_map/ppermute | solution.py:17
  211.5 1.8 collective-permute-start.18
  215.6 7.2 %collective-permute-done.16 = bf16[4,2,128,256]{3,2,1,0:T(8,128)(2,1)} collective-permute-done((bf16[4,2,128,256]{3,2,1,0:T(8,128)(2,1)}, bf16[4,2,128,256]{3,2,1,0:T(8,128)(2,1)}, u32[]{:S(2)}, u32[]{:S(2)}) %collective-permute-start.16) | collective-permute-done | bytes 524320 | tf_op jit(solution)/shard_map/ppermute | solution.py:17
  222.8 1.6 collective-permute-done.17
  224.4 5.5 %collective-permute-done.18 = bf16[4,2,128,256]{3,2,1,0:T(8,128)(2,1)} collective-permute-done((bf16[4,2,128,256]{3,2,1,0:T(8,128)(2,1)}, bf16[4,2,128,256]{3,2,1,0:T(8,128)(2,1)}, u32[]{:S(2)}, u32[]{:S(2)}) %collective-permute-start.18) | collective-permute-done | bytes 524320 | tf_op jit(solution)/shard_map/ppermute | solution.py:17
  229.9 3.1 %pad_maximum_fusion.2.act = bf16[4,4,2,128,256]{4,3,2,1,0:T(8,128)(2,1)} fusion(bf16[1,4,2,128,256]{4,3,2,1,0:T(8,128)(2,1)} %bitcast.35, bf16[1,4,2,128,256]{4,3,2,1,0:T(8,128)(2,1)} %bitcast.34, bf16[1,4,2,128,256]{4,3,2,1,0:T(8,128)(2,1)} %bitcast.33, bf16[1,4,2,128,256]{4,3,2,1,0:T(8,128)(2,1)} %get-tuple-element.13), kind=kLoop, calls=%fused_computation.3 | loop fusion | flops 3145728 | bytes 4194304 | tf_op jit(solution)/shard_map/stack | solution.py:21
  233.8 2.0 copy.31
  235.8 2.1 convert_reduce_fusion.1
  238.0 1.8 convert_reduce_fusion
  239.8 1.9 fusion.3
  241.7 7.7 %collective-permute-start.3 = (bf16[128,896]{1,0:T(8,128)(2,1)}, bf16[128,896]{1,0:T(8,128)(2,1)}, u32[]{:S(2)}, u32[]{:S(2)}) collective-permute-start(bf16[128,896]{1,0:T(8,128)(2,1)} %get-tuple-element.8), channel_id=1, source_target_pairs={{0,4},{4,0},{1,5},{5,1},{2,6},{6,2},{3,7},{7,3},{8,12},{12,8},{9,1... | collective-permute-start | bytes 688136 | tf_op jit(solution)/shard_map/ppermute | solution.py:17
  249.4 1.6 fusion.2
  250.9 2.3 copy.32.value
  256.5 5.0 %collective-permute-done.5 = bf16[128,896]{1,0:T(8,128)(2,1)S(1)} collective-permute-done((bf16[128,896]{1,0:T(8,128)(2,1)S(1)}, bf16[128,896]{1,0:T(8,128)(2,1)S(1)}, u32[]{:S(2)}, u32[]{:S(2)}) %collective-permute-start.5) | collective-permute-done | bytes 229408 | tf_op jit(solution)/shard_map/ppermute | solution.py:17
  262.4 15.8 %score.1 = f32[8,128]{1,0:T(8,128)} custom-call(s32[3]{0:T(128)} %pad_add_fusion.at_ref, bf16[2,128,896]{2,1,0:T(8,128)(2,1)} %pad_maximum_fusion.6.grad, bf16[4,4,2,128,256]{4,3,2,1,0:T(8,128)(2,1)} %pad_maximum_fusion.2.act, bf16[448,4096]{1,0:T(8,128)(2,1)} %eig0.1, bf16[448,4096]{1,0:T(8,128)(2,1)} %collective-permute-done.19.eig1, ...), custom_call_target="tpu_custom_call" | custom-call | flops 3758096384 | bytes 7340032 | tf_op jit(solution)/shard_map/score/pallas_call | solution.py:122
  279.2 12.5 %all_to_all.45 = f32[16,2,16]{2,1,0:T(2,128)S(1)} all-to-all(f32[16,2,16]{2,1,0:T(2,128)S(1)} %broadcast_in_dim.10), channel_id=1, replica_groups=mesh['y'=4,'zh'=4,'c'=2,'zl'=2,'x'=4] {'y','zh'}, dimensions={0} | all-to-all | bytes 4096 | tf_op jit(solution)/shard_map/all_to_all | solution.py:25
  292.4 4.9 %all-to-all-start.8 = ((f32[16,2,16]{2,1,0:T(2,128)}), f32[16,2,16]{2,1,0:T(2,128)S(1)}, u32[]{:S(2)}, u32[]{:S(2)}) async-start(f32[16,2,16]{2,1,0:T(2,128)} %broadcast_in_dim.11), calls=%async_computation.8 | async-start | bytes 32768 | tf_op jit(solution)/shard_map/all_to_all | solution.py:25
  297.3 4.7 %all-to-all-done.8 = f32[16,2,16]{2,1,0:T(2,128)S(1)} async-done(((f32[16,2,16]{2,1,0:T(2,128)}), f32[16,2,16]{2,1,0:T(2,128)S(1)}, u32[]{:S(2)}, u32[]{:S(2)}) %all-to-all-start.8) | async-done | bytes 2080 | tf_op jit(solution)/shard_map/all_to_all | solution.py:25
  (88 shorter events, 22.0 us)
Async XLA Ops:
  6.5 80.2 %copy-start = (bf16[16,8,1792]{2,1,0:T(8,128)(2,1)S(1)}, bf16[16,8,1792]{2,1,0:T(8,128)(2,1)}, u32[]{:S(2)}) copy-start(bf16[16,8,1792]{2,1,0:T(8,128)(2,1)} %param.12) | copy-start | bytes 1376260
  6.5 58.6 %copy-start.7 = (bf16[1,128,512]{2,1,0:T(8,128)(2,1)S(1)}, bf16[1,128,512]{2,1,0:T(8,128)(2,1)}, u32[]{:S(2)}) copy-start(bf16[1,128,512]{2,1,0:T(8,128)(2,1)} %param.8) | copy-start | bytes 393220
  6.5 61.6 %copy-start.8 = (bf16[512,128]{1,0:T(8,128)(2,1)S(1)}, bf16[512,128]{1,0:T(8,128)(2,1)}, u32[]{:S(2)}) copy-start(bf16[512,128]{1,0:T(8,128)(2,1)} %param.10) | copy-start | bytes 393220
  6.5 141.6 %all-gather.7.cloned.1.call-start = ((), (), s32[]{:S(2)}) async-start(), calls=%async_computation.10 | async-start | bytes 2293760 | tf_op jit(solution)/shard_map/all_gather | solution.py:185
  7.3 155.1 %all-gather.9.cloned.1.call-start = ((), (), s32[]{:S(2)}) async-start(), calls=%async_computation.11 | async-start | bytes 2293760 | tf_op jit(solution)/shard_map/all_gather | solution.py:185
  7.3 20.3 %collective-permute-start.4 = (bf16[128,1792]{1,0:T(8,128)(2,1)}, bf16[128,1792]{1,0:T(8,128)(2,1)S(1)}, u32[]{:S(2)}, u32[]{:S(2)}) collective-permute-start(bf16[128,1792]{1,0:T(8,128)(2,1)} %bitcast.92), channel_id=1, source_target_pairs={{0,32},{16,48},{32,0},{48,16},{1,33},{17,49},{33,1},{49,17},{2,34}... | collective-permute-start | bytes 1376264 | tf_op jit(solution)/shard_map/ppermute | solution.py:17
  27.6 0.8 copy-start.5
  28.4 150.8 %all-gather.5.cloned.1.call-start = ((), (), s32[]{:S(2)}) async-start(), calls=%async_computation.9 | async-start | bytes 4587520 | tf_op jit(solution)/shard_map/all_gather | solution.py:185
  28.4 30.2 %collective-permute-start = (bf16[128,1792]{1,0:T(8,128)(2,1)}, bf16[128,1792]{1,0:T(8,128)(2,1)S(1)}, u32[]{:S(2)}, u32[]{:S(2)}) collective-permute-start(bf16[128,1792]{1,0:T(8,128)(2,1)} %bitcast.93), channel_id=1, source_target_pairs={{0,48},{16,0},{32,16},{48,32},{1,49},{17,1},{33,17},{49,33},{2,50}... | collective-permute-start | bytes 1376264 | tf_op jit(solution)/shard_map/ppermute | solution.py:17
  40.7 23.4 %collective-permute-start.1 = (bf16[128,1792]{1,0:T(8,128)(2,1)}, bf16[128,1792]{1,0:T(8,128)(2,1)S(1)}, u32[]{:S(2)}, u32[]{:S(2)}) collective-permute-start(bf16[128,1792]{1,0:T(8,128)(2,1)} %bitcast.94), channel_id=1, source_target_pairs={{0,16},{16,32},{32,48},{48,0},{1,17},{17,33},{33,49},{49,1},{2,18}... | collective-permute-start | bytes 1376264 | tf_op jit(solution)/shard_map/ppermute | solution.py:17
  40.7 46.0 %collective-permute-start.2 = (bf16[448,1792]{1,0:T(8,128)(2,1)}, bf16[448,1792]{1,0:T(8,128)(2,1)}, u32[]{:S(2)}, u32[]{:S(2)}) collective-permute-start(bf16[448,1792]{1,0:T(8,128)(2,1)} %bitcast.110), channel_id=1, source_target_pairs={{0,8},{8,0},{1,9},{9,1},{2,10},{10,2},{3,11},{11,3},{4,12},{12,4},... | collective-permute-start | bytes 4816904 | tf_op jit(solution)/shard_map/ppermute | solution.py:17
  65.1 6.0 %collective-permute-start.6 = (bf16[128,512]{1,0:T(8,128)(2,1)S(1)}, bf16[128,512]{1,0:T(8,128)(2,1)S(1)}, u32[]{:S(2)}, u32[]{:S(2)}) collective-permute-start(bf16[128,512]{1,0:T(8,128)(2,1)S(1)} %bitcast.96), channel_id=1, source_target_pairs={{0,48},{16,0},{32,16},{48,32},{1,49},{17,1},{33,17},{49,33},{2,50}... | collective-permute-start | bytes 393224 | tf_op jit(solution)/shard_map/ppermute | solution.py:17
  65.2 12.1 %collective-permute-start.7 = (bf16[128,512]{1,0:T(8,128)(2,1)S(1)}, bf16[128,512]{1,0:T(8,128)(2,1)S(1)}, u32[]{:S(2)}, u32[]{:S(2)}) collective-permute-start(bf16[128,512]{1,0:T(8,128)(2,1)S(1)} %bitcast.97), channel_id=1, source_target_pairs={{0,32},{16,48},{32,0},{48,16},{1,33},{17,49},{33,1},{49,17},{2,34}... | collective-permute-start | bytes 393224 | tf_op jit(solution)/shard_map/ppermute | solution.py:17
  68.0 11.8 %collective-permute-start.8 = (bf16[128,512]{1,0:T(8,128)(2,1)S(1)}, bf16[128,512]{1,0:T(8,128)(2,1)S(1)}, u32[]{:S(2)}, u32[]{:S(2)}) collective-permute-start(bf16[128,512]{1,0:T(8,128)(2,1)S(1)} %bitcast.98), channel_id=1, source_target_pairs={{0,16},{16,32},{32,48},{48,0},{1,17},{17,33},{33,49},{49,1},{2,18}... | collective-permute-start | bytes 393224 | tf_op jit(solution)/shard_map/ppermute | solution.py:17
  68.2 16.5 %collective-permute-start.12 = (bf16[512,128]{1,0:T(8,128)(2,1)S(1)}, bf16[512,128]{1,0:T(8,128)(2,1)}, u32[]{:S(2)}, u32[]{:S(2)}) collective-permute-start(bf16[512,128]{1,0:T(8,128)(2,1)S(1)} %copy-done.8), channel_id=1, source_target_pairs={{0,8},{8,0},{1,9},{9,1},{2,10},{10,2},{3,11},{11,3},{4,12},{12,4},... | collective-permute-start | bytes 393224 | tf_op jit(solution)/shard_map/ppermute | solution.py:17
  79.9 27.3 %collective-permute-start.9 = (bf16[4,128,512]{2,1,0:T(8,128)(2,1)S(1)}, bf16[4,128,512]{2,1,0:T(8,128)(2,1)S(1)}, u32[]{:S(2)}, u32[]{:S(2)}) collective-permute-start(bf16[4,128,512]{2,1,0:T(8,128)(2,1)S(1)} %get-tuple-element.16), channel_id=1, source_target_pairs={{0,192},{64,0},{128,64},{192,128},{1,193},{65,1},{129,65},{193,129... | collective-permute-start | bytes 1572872 | tf_op jit(solution)/shard_map/ppermute | solution.py:17
  83.0 24.2 %collective-permute-start.10 = (bf16[4,128,512]{2,1,0:T(8,128)(2,1)S(1)}, bf16[4,128,512]{2,1,0:T(8,128)(2,1)S(1)}, u32[]{:S(2)}, u32[]{:S(2)}) collective-permute-start(bf16[4,128,512]{2,1,0:T(8,128)(2,1)S(1)} %get-tuple-element.16), channel_id=1, source_target_pairs={{0,128},{64,192},{128,0},{192,64},{1,129},{65,193},{129,1},{193,65... | collective-permute-start | bytes 1572872 | tf_op jit(solution)/shard_map/ppermute | solution.py:17
  83.6 33.8 %collective-permute-start.11 = (bf16[4,128,512]{2,1,0:T(8,128)(2,1)S(1)}, bf16[4,128,512]{2,1,0:T(8,128)(2,1)S(1)}, u32[]{:S(2)}, u32[]{:S(2)}) collective-permute-start(bf16[4,128,512]{2,1,0:T(8,128)(2,1)S(1)} %get-tuple-element.16), channel_id=1, source_target_pairs={{0,64},{64,128},{128,192},{192,0},{1,65},{65,129},{129,193},{193,1... | collective-permute-start | bytes 1572872 | tf_op jit(solution)/shard_map/ppermute | solution.py:17
  85.7 4.1 %copy-start.1 = (bf16[512,256]{1,0:T(8,128)(2,1)}, bf16[512,256]{1,0:T(8,128)(2,1)S(1)}, u32[]{:S(2)}) copy-start(bf16[512,256]{1,0:T(8,128)(2,1)S(1)} %maximum_select_fusion.w) | copy-start | bytes 786436
  90.5 12.1 %all-to-all-start.4 = ((bf16[8,8,1152]{2,1,0:T(8,128)(2,1)}), bf16[8,8,1152]{2,1,0:T(8,128)(2,1)S(1)}, u32[]{:S(2)}, u32[]{:S(2)}) async-start(bf16[8,8,1152]{2,1,0:T(8,128)(2,1)} %pad_maximum_fusion.8), calls=%async_computation.4 | async-start | bytes 294912 | tf_op jit(solution)/shard_map/all_to_all | solution.py:25
  103.3 20.6 %all-to-all-start.5 = ((bf16[16,8,256]{2,1,0:T(8,128)(2,1)}), bf16[16,8,256]{2,1,0:T(8,128)(2,1)S(1)}, u32[]{:S(2)}, u32[]{:S(2)}) async-start(bf16[16,8,256]{2,1,0:T(8,128)(2,1)} %broadcast_in_dim.8), calls=%async_computation.5 | async-start | bytes 131072 | tf_op jit(solution)/shard_map/all_to_all | solution.py:25
  123.9 18.5 %all-to-all-start.3 = ((bf16[8,2,128,256]{3,2,1,0:T(8,128)(2,1)}), bf16[8,2,128,256]{3,2,1,0:T(8,128)(2,1)S(1)}, u32[]{:S(2)}, u32[]{:S(2)}) async-start(bf16[8,2,128,256]{3,2,1,0:T(8,128)(2,1)} %bitcast.82), calls=%async_computation.3 | async-start | bytes 2097152 | tf_op jit(solution)/shard_map/all_to_all | solution.py:25
  143.4 14.2 %all-to-all-start.6 = ((bf16[8,8,4992]{2,1,0:T(8,128)(2,1)}), bf16[8,8,4992]{2,1,0:T(8,128)(2,1)S(1)}, u32[]{:S(2)}, u32[]{:S(2)}) async-start(bf16[8,8,4992]{2,1,0:T(8,128)(2,1)} %broadcast_in_dim.9), calls=%async_computation.6 | async-start | bytes 1277952 | tf_op jit(solution)/shard_map/all_to_all | solution.py:25
  157.6 15.9 %all-to-all-start.1 = ((bf16[4,128,896]{2,1,0:T(8,128)(2,1)}), bf16[4,128,896]{2,1,0:T(8,128)(2,1)S(1)}, u32[]{:S(2)}, u32[]{:S(2)}) async-start(bf16[4,128,896]{2,1,0:T(8,128)(2,1)} %bitcast.84), calls=%async_computation.1 | async-start | bytes 1835008 | tf_op jit(solution)/shard_map/all_to_all | solution.py:25
  162.3 100.1 %collective-permute-start.19 = (bf16[448,4096]{1,0:T(8,128)(2,1)}, bf16[448,4096]{1,0:T(8,128)(2,1)}, u32[]{:S(2)}, u32[]{:S(2)}) collective-permute-start(bf16[448,4096]{1,0:T(8,128)(2,1)} %eig0.1), channel_id=1, source_target_pairs={{0,8},{8,0},{1,9},{9,1},{2,10},{10,2},{3,11},{11,3},{4,12},{12,4},... | collective-permute-start | bytes 11010056 | tf_op jit(solution)/shard_map/ppermute | solution.py:17
  173.5 15.8 %all-to-all-start.2 = ((bf16[4,128,896]{2,1,0:T(8,128)(2,1)}), bf16[4,128,896]{2,1,0:T(8,128)(2,1)}, u32[]{:S(2)}, u32[]{:S(2)}) async-start(bf16[4,128,896]{2,1,0:T(8,128)(2,1)} %bitcast.85), calls=%async_computation.2 | async-start | bytes 1835008 | tf_op jit(solution)/shard_map/all_to_all | solution.py:25
  189.3 48.6 %all-to-all-start = ((bf16[8,128,896]{2,1,0:T(8,128)(2,1)}), bf16[8,128,896]{2,1,0:T(8,128)(2,1)}, u32[]{:S(2)}, u32[]{:S(2)}) async-start(bf16[8,128,896]{2,1,0:T(8,128)(2,1)} %bitcast.83), calls=%async_computation | async-start | bytes 3670016 | tf_op jit(solution)/shard_map/all_to_all | solution.py:25
  195.3 14.4 %collective-permute-start.13 = (bf16[2,128,256]{2,1,0:T(8,128)(2,1)S(1)}, bf16[2,128,256]{2,1,0:T(8,128)(2,1)S(1)}, u32[]{:S(2)}, u32[]{:S(2)}) collective-permute-start(bf16[2,128,256]{2,1,0:T(8,128)(2,1)S(1)} %reduce_sum.72), channel_id=1, source_target_pairs={{0,48},{16,0},{32,16},{48,32},{1,49},{17,1},{33,17},{49,33},{2,50}... | collective-permute-start | bytes 393224 | tf_op jit(solution)/shard_map/ppermute | solution.py:17
  195.4 14.3 %collective-permute-start.14 = (bf16[2,128,256]{2,1,0:T(8,128)(2,1)S(1)}, bf16[2,128,256]{2,1,0:T(8,128)(2,1)S(1)}, u32[]{:S(2)}, u32[]{:S(2)}) collective-permute-start(bf16[2,128,256]{2,1,0:T(8,128)(2,1)S(1)} %reduce_sum.72), channel_id=1, source_target_pairs={{0,32},{16,48},{32,0},{48,16},{1,33},{17,49},{33,1},{49,17},{2,34}... | collective-permute-start | bytes 393224 | tf_op jit(solution)/shard_map/ppermute | solution.py:17
  196.1 14.1 %collective-permute-start.15 = (bf16[2,128,256]{2,1,0:T(8,128)(2,1)S(1)}, bf16[2,128,256]{2,1,0:T(8,128)(2,1)S(1)}, u32[]{:S(2)}, u32[]{:S(2)}) collective-permute-start(bf16[2,128,256]{2,1,0:T(8,128)(2,1)S(1)} %reduce_sum.72), channel_id=1, source_target_pairs={{0,16},{16,32},{32,48},{48,0},{1,17},{17,33},{33,49},{49,1},{2,18}... | collective-permute-start | bytes 393224 | tf_op jit(solution)/shard_map/ppermute | solution.py:17
  211.2 11.5 %collective-permute-start.16 = (bf16[4,2,128,256]{3,2,1,0:T(8,128)(2,1)}, bf16[4,2,128,256]{3,2,1,0:T(8,128)(2,1)}, u32[]{:S(2)}, u32[]{:S(2)}) collective-permute-start(bf16[4,2,128,256]{3,2,1,0:T(8,128)(2,1)} %get-tuple-element.14), channel_id=1, source_target_pairs={{0,192},{64,0},{128,64},{192,128},{1,193},{65,1},{129,65},{193,129... | collective-permute-start | bytes 1572872 | tf_op jit(solution)/shard_map/ppermute | solution.py:17
  211.2 13.2 %collective-permute-start.17 = (bf16[4,2,128,256]{3,2,1,0:T(8,128)(2,1)}, bf16[4,2,128,256]{3,2,1,0:T(8,128)(2,1)}, u32[]{:S(2)}, u32[]{:S(2)}) collective-permute-start(bf16[4,2,128,256]{3,2,1,0:T(8,128)(2,1)} %get-tuple-element.14), channel_id=1, source_target_pairs={{0,128},{64,192},{128,0},{192,64},{1,129},{65,193},{129,1},{193,65... | collective-permute-start | bytes 1572872 | tf_op jit(solution)/shard_map/ppermute | solution.py:17
  211.5 18.4 %collective-permute-start.18 = (bf16[4,2,128,256]{3,2,1,0:T(8,128)(2,1)}, bf16[4,2,128,256]{3,2,1,0:T(8,128)(2,1)}, u32[]{:S(2)}, u32[]{:S(2)}) collective-permute-start(bf16[4,2,128,256]{3,2,1,0:T(8,128)(2,1)} %get-tuple-element.14), channel_id=1, source_target_pairs={{0,64},{64,128},{128,192},{192,0},{1,65},{65,129},{129,193},{193,1... | collective-permute-start | bytes 1572872 | tf_op jit(solution)/shard_map/ppermute | solution.py:17
  214.5 19.4 %collective-permute-start.20 = (bf16[64,4992]{1,0:T(8,128)(2,1)}, bf16[64,4992]{1,0:T(8,128)(2,1)}, u32[]{:S(2)}, u32[]{:S(2)}) collective-permute-start(bf16[64,4992]{1,0:T(8,128)(2,1)} %concatenate.37), channel_id=1, source_target_pairs={{0,8},{8,0},{1,9},{9,1},{2,10},{10,2},{3,11},{11,3},{4,12},{12,4},... | collective-permute-start | bytes 1916936 | tf_op jit(solution)/shard_map/ppermute | solution.py:17
  238.0 1.8 copy-start.2
  241.7 13.8 %collective-permute-start.3 = (bf16[128,896]{1,0:T(8,128)(2,1)}, bf16[128,896]{1,0:T(8,128)(2,1)}, u32[]{:S(2)}, u32[]{:S(2)}) collective-permute-start(bf16[128,896]{1,0:T(8,128)(2,1)} %get-tuple-element.8), channel_id=1, source_target_pairs={{0,4},{4,0},{1,5},{5,1},{2,6},{6,2},{3,7},{7,3},{8,12},{12,8},{9,1... | collective-permute-start | bytes 688136 | tf_op jit(solution)/shard_map/ppermute | solution.py:17
  253.3 0.9 copy-start.6
  253.3 2.2 copy-start.4
  253.3 8.2 %copy-start.3 = (bf16[128,896]{1,0:T(8,128)(2,1)S(1)}, bf16[128,896]{1,0:T(8,128)(2,1)}, u32[]{:S(2)}) copy-start(bf16[128,896]{1,0:T(8,128)(2,1)} %convert_reduce_fusion.1) | copy-start | bytes 688132
  254.2 7.2 %collective-permute-start.5 = (bf16[128,896]{1,0:T(8,128)(2,1)S(1)}, bf16[128,896]{1,0:T(8,128)(2,1)S(1)}, u32[]{:S(2)}, u32[]{:S(2)}) collective-permute-start(bf16[128,896]{1,0:T(8,128)(2,1)S(1)} %copy-done.6), channel_id=1, source_target_pairs={{0,4},{4,0},{1,5},{5,1},{2,6},{6,2},{3,7},{7,3},{8,12},{12,8},{9,1... | collective-permute-start | bytes 688136 | tf_op jit(solution)/shard_map/ppermute | solution.py:17
  292.4 9.6 %all-to-all-start.8 = ((f32[16,2,16]{2,1,0:T(2,128)}), f32[16,2,16]{2,1,0:T(2,128)S(1)}, u32[]{:S(2)}, u32[]{:S(2)}) async-start(f32[16,2,16]{2,1,0:T(2,128)} %broadcast_in_dim.11), calls=%async_computation.8 | async-start | bytes 32768 | tf_op jit(solution)/shard_map/all_to_all | solution.py:25
Sparse Core Ops, SparseCore 0:
  9.1 34.1 all-gather.6
  45.1 31.1 all-gather.8
  78.1 60.4 all-gather.4
where the time goes:
time: 312 us; the launch traced here: 309 us
  waiting for transfers between devices  126 us (40%)
  starting transfers between devices  81.8 us (26%)
  matrix products  23.3 us (7%)
  other arithmetic  20.6 us (7%)
  Pallas kernels  20.6 us (7%)
  between operations  13.3 us (4%)
  blocking collectives  12.5 us (4%)
  local copies, waits for them, and re-layouts  11.1 us (4%)
    ppermute x21, waiting for transfers between devices, shift(): return lax.ppermute(value, axis, [(i, (i + by) % n) for i in range(n)])  90.7 us
    all_to_all x8, starting transfers between devices, exchange(): return lax.all_to_all(value, axes, 0, 0, tiled=True)  41.7 us
    ppermute x21, starting transfers between devices, shift(): return lax.ppermute(value, axis, [(i, (i + by) % n) for i in range(n)])  40 us
    all_to_all x8, waiting for transfers between devices, exchange(): return lax.all_to_all(value, axes, 0, 0, tiled=True)  34.4 us
    dot_general x4, matrix products, dot_t(): lax.dot_general(a, b, (((1,), (1,)), ((), ())), preferred_element_type=F32)  22.2 us
    pallas_call x1, Pallas kernels, score(): pl.pallas_call(score_kernel, grid_spec=spec, out_shape=jax.ShapeDtypeStru...  15.8 us
    all_to_all x1, blocking collectives, exchange(): return lax.all_to_all(value, axes, 0, 0, tiled=True)  12.5 us
  transfers between devices with their start and end apart: 32, of which 20 were waited for; matrix products, arithmetic and copies ran while one was open for 17% of the time, Pallas kernels for 2%

commit v1 on v0

--- a/solution.py
+++ b/solution.py
@@ -18,7 +18,17 @@
 
 
 def gather(value, axis):
-    return jnp.stack([value] + [shift(value, axis, -by) for by in (1, 2, 3)])
+    return [value] + [shift(value, axis, -by) for by in (1, 2, 3)]
+
+
+def from_owner(value, by):
+    pairs = [(2 * h + h % 2, 2 * ((h - by) % 4) + h % 2) for h in range(4)]
+    return lax.ppermute(value, ("zh", "zl"), pairs)
+
+
+def to_owner(value):
+    pairs = [(2 * h + 1 - h % 2, 2 * h + h % 2) for h in range(4)]
+    return lax.ppermute(value, ("zh", "zl"), pairs)
 
 
 def exchange(value, axes):
@@ -37,40 +47,38 @@
     return lax.dot_general(a, b, (((1,), (1,)), ((), ())), preferred_element_type=F32)
 
 
-def rotate_in_kernel(at_ref, act, w, out):
-    y = lax.rem(at_ref[0] + pl.program_id(0), 4)
-    for z in range(4):
-        zh = lax.rem(at_ref[1] + z, 4)
-        out[lax.rem(zh, 2), y, zh // 2] = dot(act[0, z], w[...]).astype(BF)
-
-
-def rotate_in(at, act, w):
-    tokens, unit = act.shape[2:]
-    n = w.shape[1]
-    spec = pltpu.PrefetchScalarGridSpec(
-        num_scalar_prefetch=1,
-        grid=(4,),
-        in_specs=[
-            pl.BlockSpec((1, 4, tokens, unit), lambda y, _: (y, 0, 0, 0)),
-            pl.BlockSpec((unit, n), lambda y, _: (0, 0)),
-        ],
-        out_specs=pl.BlockSpec((2, 4, 2, tokens, n), lambda y, _: (0, 0, 0, 0, 0)),
-    )
+def rotate_in_kernel(at_ref, a0, a1, a2, a3, w0, w1, w2, w3, out, act):
+    tokens = a0.shape[0]
+    n = w0.shape[1]
+    for d, a in enumerate((a0, a1, a2, a3)):
+        y = lax.rem(at_ref[0] + d, 4)
+        act[pl.ds(pl.multiple_of(y * tokens, tokens), tokens), :] = a[...]
+    for d, w in enumerate((w0, w1, w2, w3)):
+        zh = lax.rem(at_ref[1] + d, 4)
+        out[:, pl.ds(pl.multiple_of(zh * n, n), n)] = dot(act[...], w[...]).astype(BF)
+
+
+def rotate_in(at, acts, bases):
+    tokens, unit = acts[0].shape
+    n = bases[0].shape[1]
+    vmem = pl.BlockSpec(memory_space=pltpu.VMEM)
     return pl.pallas_call(
         rotate_in_kernel,
-        grid_spec=spec,
-        out_shape=jax.ShapeDtypeStruct((2, 4, 2, tokens, n), BF),
+        in_specs=[pl.BlockSpec(memory_space=pltpu.SMEM)] + [vmem] * 8,
+        out_specs=vmem,
+        out_shape=jax.ShapeDtypeStruct((4 * tokens, 4 * n), BF),
+        scratch_shapes=[pltpu.VMEM((4 * tokens, unit), BF)],
         cost_estimate=pl.CostEstimate(
             flops=2 * 16 * tokens * unit * n, bytes_accessed=2 * 16 * tokens * (unit + n), transcendentals=0
         ),
         name="rotate_in",
-    )(at, act, w)
+    )(at, *acts, *bases)
 
 
 def score_kernel(at_ref, grad, act, eig0, eig1, value, query, out, flipped, total):
     step = pl.program_id(0)
     n = eig0.shape[0]
-    width = act.shape[4]
+    width = act.shape[3] // 4
 
     @pl.when(step == 0)
     def _():
@@ -79,15 +87,13 @@
         total[...] = jnp.zeros_like(total)
 
     def body(e, _):
-        zh = lax.rem(at_ref[1] + e, 4)
-        cols = pl.ds(pl.multiple_of(zh * width, width), width)
+        cols = pl.ds(pl.multiple_of(e * width, width), width)
         held = value[:, cols]
         for k, eig in enumerate((eig0, eig1)):
             here = slice(k * n, (k + 1) * n)
             inverse = 1.0 / eig[:, cols].astype(F32)
             for s in range(2):
-                which = at_ref[2] if s == 0 else 1 - at_ref[2]
-                contracted = dot(flipped[s, here, :], act[0, e, which])
+                contracted = dot(flipped[s, here, :], act[0, s, :, cols])
                 total[s, here, :] += dot_t((contracted * inverse).astype(BF), held)
         return 0
 
@@ -102,15 +108,14 @@
 def score(at, grad, act, eig0, eig1, value, query):
     _, tokens, both = grad.shape
     n = eig0.shape[0]
-    width = act.shape[4]
-    cols = 4 * width
+    cols = act.shape[3]
     rows = value.shape[0]
     spec = pltpu.PrefetchScalarGridSpec(
         num_scalar_prefetch=1,
         grid=(4,),
         in_specs=[
             pl.BlockSpec((2, tokens, both), lambda j, at: (0, 0, 0)),
-            pl.BlockSpec((1, 4, 2, tokens, width), lambda j, at: (j, 0, 0, 0, 0)),
+            pl.BlockSpec((1, 2, tokens, cols), lambda j, at: (j, 0, 0, 0)),
             pl.BlockSpec((n, cols), lambda j, at: (0, lax.rem(at[0] + j, 4))),
             pl.BlockSpec((n, cols), lambda j, at: (0, lax.rem(at[0] + j, 4))),
             pl.BlockSpec((rows, cols), lambda j, at: (0, lax.rem(at[0] + j, 4))),
@@ -143,22 +148,24 @@
 
     same = li == zi % 2
     low = jnp.where(same, zi, (zi + 3) % 4) // 2
-    at = jnp.stack([yi, zi, low]).astype(jnp.int32)
+    at = jnp.stack([yi, zi]).astype(jnp.int32)
 
     out_t = basis_out.T
     out_both = jnp.concatenate([out_t, shift(out_t, "c", 1)], 0)
+    out_both = lax.optimization_barrier(out_both)
     in_other = shift(basis_in, "c", 1)
     in_both = jnp.where(
         first, jnp.concatenate([basis_in, in_other], 1), jnp.concatenate([in_other, basis_in], 1)
     )
+    both = in_both.shape[1]
     eigen_other = shift(eigen_vals, "c", 1)
 
-    act = gather(gather(act_in[0], "zh"), "y")
-    part = rotate_in(at, act, in_both)
-    both = part.shape[-1]
-    act_sum = exchange(part.reshape(8, 2, tokens, both), ("zl", "x"))
-    act_sum = act_sum.reshape(8, 2, tokens, both).astype(F32).sum(0).astype(BF)
-    act_rot = gather(gather(act_sum, "zh"), "y")
+    part = rotate_in(at, gather(act_in[0], "y"), gather(in_both, "zh"))
+    part = exchange(part.reshape(4, tokens, 4 * both), "x").astype(F32).sum(0).astype(BF)
+    part = (part.astype(F32) + to_owner(part).astype(F32)).astype(BF)
+    plus, far, minus = (from_owner(part, by) for by in (1, 2, 3))
+    act_rot = jnp.stack([jnp.where(same, part, minus), jnp.where(same, far, plus)])
+    act_rot = jnp.stack(gather(act_rot, "y"))
 
     mine = lax.dynamic_slice_in_dim(query_out.reshape(rows, unit), ci * half_rows, half_rows, 0)
     mine_in = lax.dynamic_slice_in_dim(query_in.reshape(rows, -1), ci * half_rows, half_rows, 0)
@@ -188,17 +195,12 @@
         product = product.reshape(4, -1, tokens, 2 * width).astype(F32).sum(0)
         blocks.extend(product[b] for b in range(product.shape[0]))
     own, plus, minus, far = blocks
-    slots = []
-    for k, (a, b) in enumerate(((own, minus), (plus, far))):
-        mine_first = same if k == 0 else ~same
-        keep = jnp.where(mine_first, a, b)
-        give = jnp.where(mine_first, b, a).astype(BF)
-        if k == 0:
-            give, keep = lax.optimization_barrier((give, keep))
-        got = shift(give, "zl", 1)
-        slots.append((keep.astype(BF).astype(F32) + got.astype(F32)).astype(BF))
-
-    result = score(at, jnp.stack(slots), act_rot, eigen_vals, eigen_other, value_rot, query_rot)[:2]
+    keep = jnp.stack([jnp.where(same, own, minus), jnp.where(same, far, plus)])
+    give = jnp.stack([jnp.where(same, minus, own), jnp.where(same, plus, far)])
+    got = shift(give.astype(BF), "zl", 1)
+    slots = (keep.astype(BF).astype(F32) + got.astype(F32)).astype(BF)
+
+    result = score(at, slots, act_rot, eigen_vals, eigen_other, value_rot, query_rot)[:2]
     result = result.reshape(2, queries, rank).sum(-1)
     result = jnp.where(low == 0, result, result[::-1])
     turned = jnp.concatenate([result[:, queries // 2 :], result[:, : queries // 2]], 1)

time: 312 us -> 305 us (0.978)
  waiting for transfers between devices: 126 us -> 96.7 us
  starting transfers between devices: 81.8 us -> 95.5 us
  blocking collectives: 12.5 us -> 20.8 us
    ppermute x21 -> x17, waiting for transfers between devices: 90.7 us -> 63.3 us  [shift(): return lax.ppermute(value, axis, [(i, (i + by) % n) for i in range(n)])]
    all_to_all x8, waiting for transfers between devices: 34.4 us -> 19.7 us  [exchange(): return lax.all_to_all(value, axes, 0, 0, tiled=True)]
    ppermute x0 -> x4, waiting for transfers between devices: none -> 13 us  [the longest x1 11.6 us: to_owner(): return lax.ppermute(value, ('zh', 'zl'), pairs)]
    all_to_all x8, starting transfers between devices: 41.7 us -> 51.5 us  [exchange(): return lax.all_to_all(value, axes, 0, 0, tiled=True)]
    ppermute x0 -> x4, starting transfers between devices: none -> 8.29 us  [the longest x3 7 us: from_owner(): return lax.ppermute(value, ('zh', 'zl'), pairs)]
    all_to_all x1, blocking collectives: 12.5 us -> 20.8 us  [exchange(): return lax.all_to_all(value, axes, 0, 0, tiled=True)]
    ppermute x21 -> x17, starting transfers between devices: 40 us -> 35.7 us  [shift(): return lax.ppermute(value, axis, [(i, (i + by) % n) for i in range(n)])]
    another operation x8 -> x7, other arithmetic: 8.39 us -> 8.78 us  [the longest x2 4.78 us: shards(): act_rot = jnp.stack(gather(act_rot, 'y'))]
  transfers between devices with their start and end apart: 32 -> 32, of which waited for: 20 -> 15; matrix products, arithmetic and copies ran while one was open for 17% -> 17% of each run, Pallas kernels for 2% -> 1%
where the time goes in v1:
time: 305 us; the launch traced here: 301 us
  waiting for transfers between devices  96.7 us (32%)
  starting transfers between devices  95.5 us (31%)
  other arithmetic  21.9 us (7%)
  blocking collectives  20.8 us (7%)
  matrix products  20.6 us (7%)
  Pallas kernels  19 us (6%)
  local copies, waits for them, and re-layouts  13.5 us (4%)
  between operations  13.4 us (4%)
    ppermute x17, waiting for transfers between devices, shift(): return lax.ppermute(value, axis, [(i, (i + by) % n) for i in range(n)])  63.3 us
    all_to_all x8, starting transfers between devices, exchange(): return lax.all_to_all(value, axes, 0, 0, tiled=True)  51.5 us
    ppermute x17, starting transfers between devices, shift(): return lax.ppermute(value, axis, [(i, (i + by) % n) for i in range(n)])  35.7 us
    all_to_all x1, blocking collectives, exchange(): return lax.all_to_all(value, axes, 0, 0, tiled=True)  20.8 us
    dot_general x4, matrix products, dot_t(): lax.dot_general(a, b, (((1,), (1,)), ((), ())), preferred_element_type=F32)  20.4 us
    all_to_all x8, waiting for transfers between devices, exchange(): return lax.all_to_all(value, axes, 0, 0, tiled=True)  19.7 us
    pallas_call x1, Pallas kernels, score(): pl.pallas_call(score_kernel, grid_spec=spec, out_shape=jax.ShapeDtypeStru...  15.8 us
    ppermute x1, waiting for transfers between devices, to_owner(): return lax.ppermute(value, ('zh', 'zl'), pairs)  11.6 us
  transfers between devices with their start and end apart: 32, of which 15 were waited for; matrix products, arithmetic and copies ran while one was open for 17% of the time, Pallas kernels for 1%

profile of v1, /device:TPU:2, one launch (start us, length us, event | category | flops | bytes accessed | tf_op | source)
XLA Modules:
  0.0 301.4 jit_solution(12922250746527089290)
XLA Ops:
  7.3 7.3 %collective-permute-start.3 = (bf16[128,1792]{1,0:T(8,128)(2,1)}, bf16[128,1792]{1,0:T(8,128)(2,1)S(1)}, u32[]{:S(2)}, u32[]{:S(2)}) collective-permute-start(bf16[128,1792]{1,0:T(8,128)(2,1)} %bitcast.78), channel_id=1, source_target_pairs={{0,32},{16,48},{32,0},{48,16},{1,33},{17,49},{33,1},{49,17},{2,34}... | collective-permute-start | bytes 1376264 | tf_op jit(solution)/shard_map/ppermute | solution.py:17
  14.6 13.0 %collective-permute-done.3 = bf16[128,1792]{1,0:T(8,128)(2,1)S(1)} collective-permute-done((bf16[128,1792]{1,0:T(8,128)(2,1)}, bf16[128,1792]{1,0:T(8,128)(2,1)S(1)}, u32[]{:S(2)}, u32[]{:S(2)}) %collective-permute-start.3) | collective-permute-done | bytes 458784 | tf_op jit(solution)/shard_map/ppermute | solution.py:17
  28.4 9.6 %collective-permute-start.2 = (bf16[128,1792]{1,0:T(8,128)(2,1)}, bf16[128,1792]{1,0:T(8,128)(2,1)S(1)}, u32[]{:S(2)}, u32[]{:S(2)}) collective-permute-start(bf16[128,1792]{1,0:T(8,128)(2,1)} %bitcast.79), channel_id=1, source_target_pairs={{0,16},{16,32},{32,48},{48,0},{1,17},{17,33},{33,49},{49,1},{2,18}... | collective-permute-start | bytes 1376264 | tf_op jit(solution)/shard_map/ppermute | solution.py:17
  38.0 2.8 collective-permute-start.1
  40.8 19.5 %collective-permute-done.2 = bf16[128,1792]{1,0:T(8,128)(2,1)S(1)} collective-permute-done((bf16[128,1792]{1,0:T(8,128)(2,1)}, bf16[128,1792]{1,0:T(8,128)(2,1)S(1)}, u32[]{:S(2)}, u32[]{:S(2)}) %collective-permute-start.2) | collective-permute-done | bytes 458784 | tf_op jit(solution)/shard_map/ppermute | solution.py:17
  61.4 1.3 collective-permute-done.8
  63.1 1.7 pad_maximum_fusion
  64.8 1.8 copy-done.1
  68.3 6.7 %all-to-all-start.4 = ((bf16[8,8,1152]{2,1,0:T(8,128)(2,1)}), bf16[8,8,1152]{2,1,0:T(8,128)(2,1)S(1)}, u32[]{:S(2)}, u32[]{:S(2)}) async-start(bf16[8,8,1152]{2,1,0:T(8,128)(2,1)} %pad_maximum_fusion.6), calls=%async_computation.4 | async-start | bytes 294912 | tf_op jit(solution)/shard_map/all_to_all | solution.py:35
  75.0 3.0 collective-permute-start.5
  78.0 2.4 collective-permute-start.9
  80.4 4.9 %collective-permute-start.10 = (bf16[512,256]{1,0:T(8,128)(2,1)S(1)}, bf16[512,256]{1,0:T(8,128)(2,1)S(1)}, u32[]{:S(2)}, u32[]{:S(2)}) collective-permute-start(bf16[512,256]{1,0:T(8,128)(2,1)S(1)} %maximum_select_fusion.w0), channel_id=1, source_target_pairs={{0,32},{16,48},{32,0},{48,16},{1,33},{17,49},{33,1},{49,17},{2,34}... | collective-permute-start | bytes 786440 | tf_op jit(solution)/shard_map/ppermute | solution.py:17
  87.6 7.2 %all-to-all-start.5 = ((bf16[16,8,256]{2,1,0:T(8,128)(2,1)}), bf16[16,8,256]{2,1,0:T(8,128)(2,1)S(1)}, u32[]{:S(2)}, u32[]{:S(2)}) async-start(bf16[16,8,256]{2,1,0:T(8,128)(2,1)} %broadcast_in_dim.8), calls=%async_computation.5 | async-start | bytes 131072 | tf_op jit(solution)/shard_map/all_to_all | solution.py:35
  95.5 2.3 collective-permute-done.10.w2
  97.9 4.8 %collective-permute-done.11.w3 = bf16[512,256]{1,0:T(8,128)(2,1)S(1)} collective-permute-done((bf16[512,256]{1,0:T(8,128)(2,1)S(1)}, bf16[512,256]{1,0:T(8,128)(2,1)S(1)}, u32[]{:S(2)}, u32[]{:S(2)}) %collective-permute-start.11) | collective-permute-done | bytes 262176 | tf_op jit(solution)/shard_map/ppermute | solution.py:17
  103.4 3.2 %rotate_in.1 = bf16[512,1024]{1,0:T(8,128)(2,1)} custom-call(s32[2]{0:T(128)} %pad_add_fusion.at_ref, bf16[128,512]{1,0:T(8,128)(2,1)} %bitcast.82, bf16[128,512]{1,0:T(8,128)(2,1)} %copy-done.13, bf16[128,512]{1,0:T(8,128)(2,1)} %copy-done.14, bf16[128,512]{1,0:T(8,128)(2,1)} %copy-done.15, bf16[512,256]{1,0:T(8,128)(2,1)} %copy-done.3, ...), custom_call_target="tpu_custom_call" | custom-call | flops 536870912 | bytes 3145728 | tf_op jit(solution)/shard_map/rotate_in/pallas_call | solution.py:65
  107.4 4.8 %all-to-all-start.3 = ((bf16[4,128,1024]{2,1,0:T(8,128)(2,1)}), bf16[4,128,1024]{2,1,0:T(8,128)(2,1)S(1)}, u32[]{:S(2)}, u32[]{:S(2)}) async-start(bf16[4,128,1024]{2,1,0:T(8,128)(2,1)} %bitcast.71), calls=%async_computation.3 | async-start | bytes 2097152 | tf_op jit(solution)/shard_map/all_to_all | solution.py:35
  112.2 11.6 %all-to-all-done.3 = bf16[4,128,1024]{2,1,0:T(8,128)(2,1)S(1)} async-done(((bf16[4,128,1024]{2,1,0:T(8,128)(2,1)}), bf16[4,128,1024]{2,1,0:T(8,128)(2,1)S(1)}, u32[]{:S(2)}, u32[]{:S(2)}) %all-to-all-start.3) | async-done | bytes 1048608 | tf_op jit(solution)/shard_map/all_to_all | solution.py:35
  124.6 12.4 %all-to-all-start.6 = ((bf16[8,8,4992]{2,1,0:T(8,128)(2,1)}), bf16[8,8,4992]{2,1,0:T(8,128)(2,1)S(1)}, u32[]{:S(2)}, u32[]{:S(2)}) async-start(bf16[8,8,4992]{2,1,0:T(8,128)(2,1)} %broadcast_in_dim.9), calls=%async_computation.6 | async-start | bytes 1277952 | tf_op jit(solution)/shard_map/all_to_all | solution.py:35
  138.7 11.6 %collective-permute-done.12 = bf16[128,1024]{1,0:T(8,128)(2,1)S(1)} collective-permute-done((bf16[128,1024]{1,0:T(8,128)(2,1)S(1)}, bf16[128,1024]{1,0:T(8,128)(2,1)S(1)}, u32[]{:S(2)}, u32[]{:S(2)}) %collective-permute-start.12) | collective-permute-done | bytes 262176 | tf_op jit(solution)/shard_map/ppermute | solution.py:31
  150.4 3.5 %collective-permute-start.14 = (bf16[128,1024]{1,0:T(8,128)(2,1)S(1)}, bf16[128,1024]{1,0:T(8,128)(2,1)S(1)}, u32[]{:S(2)}, u32[]{:S(2)}) collective-permute-start(bf16[128,1024]{1,0:T(8,128)(2,1)S(1)} %add_convert_fusion.1), channel_id=1, source_target_pairs={{0,32},{20,52},{32,0},{52,20},{1,33},{21,53},{33,1},{53,21},{2,34}... | collective-permute-start | bytes 786440 | tf_op jit(solution)/shard_map/ppermute | solution.py:26
  153.9 2.0 collective-permute-start.15
  155.9 1.5 collective-permute-start.13
  157.4 5.5 %convolution_convert_fusion.2 = bf16[896,512]{0,1:T(8,128)(2,1)} fusion(bf16[896,1792]{1,0:T(8,128)(2,1)} %copy-done.1, bf16[512,1792]{1,0:T(8,128)(2,1)} %bitcast.90), kind=kOutput, calls=%fused_computation.7 | convolution fusion | flops 1644625920 | bytes 5963776 | tf_op jit(solution)/shard_map/dot_general | solution.py:47
  162.9 4.8 %all-to-all-start = ((bf16[4,128,896]{2,1,0:T(8,128)(2,1)}), bf16[4,128,896]{2,1,0:T(8,128)(2,1)S(1)}, u32[]{:S(2)}, u32[]{:S(2)}) async-start(bf16[4,128,896]{2,1,0:T(8,128)(2,1)} %bitcast.5), calls=%async_computation | async-start | bytes 1835008 | tf_op jit(solution)/shard_map/all_to_all | solution.py:35
  167.7 1.3 collective-permute-done.13
  169.7 5.5 %convolution_convert_fusion.1 = bf16[896,512]{0,1:T(8,128)(2,1)} fusion(bf16[896,1792]{1,0:T(8,128)(2,1)} %copy-done.1, bf16[512,1792]{1,0:T(8,128)(2,1)} %all-gather.9.cloned.1.call-done), kind=kOutput, calls=%fused_computation.6 | convolution fusion | flops 1644625920 | bytes 5963776 | tf_op jit(solution)/shard_map/dot_general | solution.py:47
  175.3 2.2 all-to-all-done
  177.4 4.9 %all-to-all-start.2 = ((bf16[4,128,896]{2,1,0:T(8,128)(2,1)}), bf16[4,128,896]{2,1,0:T(8,128)(2,1)S(1)}, u32[]{:S(2)}, u32[]{:S(2)}) async-start(bf16[4,128,896]{2,1,0:T(8,128)(2,1)} %bitcast.75), calls=%async_computation.2 | async-start | bytes 1835008 | tf_op jit(solution)/shard_map/all_to_all | solution.py:35
  182.4 8.3 %convolution_convert_fusion = bf16[1024,896]{1,0:T(8,128)(2,1)} fusion(bf16[1024,1792]{1,0:T(8,128)(2,1)} %bitcast.89, bf16[896,1792]{1,0:T(8,128)(2,1)} %copy-done.1), kind=kOutput, calls=%fused_computation.5 | convolution fusion | flops 3289251840 | bytes 8716288 | tf_op jit(solution)/shard_map/dot_general | solution.py:47
  191.1 5.8 %all-to-all-start.1 = ((bf16[8,128,896]{2,1,0:T(8,128)(2,1)}), bf16[8,128,896]{2,1,0:T(8,128)(2,1)}, u32[]{:S(2)}, u32[]{:S(2)}) async-start(bf16[8,128,896]{2,1,0:T(8,128)(2,1)} %bitcast.72), calls=%async_computation.1 | async-start | bytes 3670016 | tf_op jit(solution)/shard_map/all_to_all | solution.py:35
  197.0 1.8 fusion.11
  198.8 2.4 collective-permute-start.17
  201.2 1.4 collective-permute-start.16
  203.7 16.2 %collective-permute-done.18 = bf16[2,128,1024]{2,1,0:T(8,128)(2,1)} collective-permute-done((bf16[2,128,1024]{2,1,0:T(8,128)(2,1)}, bf16[2,128,1024]{2,1,0:T(8,128)(2,1)}, u32[]{:S(2)}, u32[]{:S(2)}) %collective-permute-start.18) | collective-permute-done | bytes 524320 | tf_op jit(solution)/shard_map/ppermute | solution.py:17
  220.5 3.0 pad_maximum_fusion.1.act
  225.5 2.0 copy.31
  227.5 2.1 convert_reduce_fusion.1
  229.6 1.8 convert_reduce_fusion
  231.4 1.7 fusion.5
  234.1 1.6 fusion.2
  235.7 2.4 copy.32.value
  239.0 5.5 %collective-permute-done.4 = bf16[2,128,896]{2,1,0:T(8,128)(2,1)} collective-permute-done((bf16[2,128,896]{2,1,0:T(8,128)(2,1)}, bf16[2,128,896]{2,1,0:T(8,128)(2,1)}, u32[]{:S(2)}, u32[]{:S(2)}) %collective-permute-start.4) | collective-permute-done | bytes 458784 | tf_op jit(solution)/shard_map/ppermute | solution.py:17
  244.5 1.9 add_convert_fusion.grad
  246.4 15.8 %score.1 = f32[8,128]{1,0:T(8,128)} custom-call(s32[2]{0:T(128)} %pad_add_fusion.at_ref, bf16[2,128,896]{2,1,0:T(8,128)(2,1)} %add_convert_fusion.grad, bf16[4,2,128,1024]{3,2,1,0:T(8,128)(2,1)} %pad_maximum_fusion.1.act, bf16[448,4096]{1,0:T(8,128)(2,1)} %eig0.1, bf16[448,4096]{1,0:T(8,128)(2,1)} %collective-permute-done.19.eig1, ...), custom_call_target="tpu_custom_call" | custom-call | flops 3758096384 | bytes 7340032 | tf_op jit(solution)/shard_map/score/pallas_call | solution.py:127
  263.2 20.8 %all_to_all.45 = f32[16,2,16]{2,1,0:T(2,128)S(1)} all-to-all(f32[16,2,16]{2,1,0:T(2,128)S(1)} %broadcast_in_dim.10), channel_id=1, replica_groups=mesh['y'=4,'zh'=4,'c'=2,'zl'=2,'x'=4] {'y','zh'}, dimensions={0} | all-to-all | bytes 4096 | tf_op jit(solution)/shard_map/all_to_all | solution.py:35
  284.7 4.8 %all-to-all-start.8 = ((f32[16,2,16]{2,1,0:T(2,128)}), f32[16,2,16]{2,1,0:T(2,128)S(1)}, u32[]{:S(2)}, u32[]{:S(2)}) async-start(f32[16,2,16]{2,1,0:T(2,128)} %broadcast_in_dim.11), calls=%async_computation.8 | async-start | bytes 32768 | tf_op jit(solution)/shard_map/all_to_all | solution.py:35
  289.5 4.7 %all-to-all-done.8 = f32[16,2,16]{2,1,0:T(2,128)S(1)} async-done(((f32[16,2,16]{2,1,0:T(2,128)}), f32[16,2,16]{2,1,0:T(2,128)S(1)}, u32[]{:S(2)}, u32[]{:S(2)}) %all-to-all-start.8) | async-done | bytes 2080 | tf_op jit(solution)/shard_map/all_to_all | solution.py:35
  (105 shorter events, 20.9 us)
Async XLA Ops:
  6.5 58.2 %copy-start = (bf16[16,8,1792]{2,1,0:T(8,128)(2,1)S(1)}, bf16[16,8,1792]{2,1,0:T(8,128)(2,1)}, u32[]{:S(2)}) copy-start(bf16[16,8,1792]{2,1,0:T(8,128)(2,1)} %param.12) | copy-start | bytes 1376260
  6.5 54.8 %copy-start.11 = (bf16[512,128]{1,0:T(8,128)(2,1)S(1)}, bf16[512,128]{1,0:T(8,128)(2,1)}, u32[]{:S(2)}) copy-start(bf16[512,128]{1,0:T(8,128)(2,1)} %param.10) | copy-start | bytes 393220
  6.5 56.3 %copy-start.16 = (bf16[16,8,512]{2,1,0:T(8,128)(2,1)S(1)}, bf16[16,8,512]{2,1,0:T(8,128)(2,1)}, u32[]{:S(2)}) copy-start(bf16[16,8,512]{2,1,0:T(8,128)(2,1)} %param.13) | copy-start | bytes 393220
  6.5 150.9 %all-gather.5.cloned.1.call-start = ((), (), s32[]{:S(2)}) async-start(), calls=%async_computation.9 | async-start | bytes 2293760 | tf_op jit(solution)/shard_map/all_gather | solution.py:192
  7.3 55.8 %copy-start.4 = (bf16[1792,448]{0,1:T(8,128)(2,1)S(1)}, bf16[1792,448]{0,1:T(8,128)(2,1)}, u32[]{:S(2)}) copy-start(bf16[1792,448]{0,1:T(8,128)(2,1)} %param.9) | copy-start | bytes 4816900
  7.3 162.5 %all-gather.9.cloned.1.call-start = ((), (), s32[]{:S(2)}) async-start(), calls=%async_computation.11 | async-start | bytes 2293760 | tf_op jit(solution)/shard_map/all_gather | solution.py:192
  7.3 20.3 %collective-permute-start.3 = (bf16[128,1792]{1,0:T(8,128)(2,1)}, bf16[128,1792]{1,0:T(8,128)(2,1)S(1)}, u32[]{:S(2)}, u32[]{:S(2)}) collective-permute-start(bf16[128,1792]{1,0:T(8,128)(2,1)} %bitcast.78), channel_id=1, source_target_pairs={{0,32},{16,48},{32,0},{48,16},{1,33},{17,49},{33,1},{49,17},{2,34}... | collective-permute-start | bytes 1376264 | tf_op jit(solution)/shard_map/ppermute | solution.py:17
  27.6 0.8 copy-start.7
  28.4 154.0 %all-gather.7.cloned.1.call-start = ((), (), s32[]{:S(2)}) async-start(), calls=%async_computation.10 | async-start | bytes 4587520 | tf_op jit(solution)/shard_map/all_gather | solution.py:192
  28.4 31.9 %collective-permute-start.2 = (bf16[128,1792]{1,0:T(8,128)(2,1)}, bf16[128,1792]{1,0:T(8,128)(2,1)S(1)}, u32[]{:S(2)}, u32[]{:S(2)}) collective-permute-start(bf16[128,1792]{1,0:T(8,128)(2,1)} %bitcast.79), channel_id=1, source_target_pairs={{0,16},{16,32},{32,48},{48,0},{1,17},{17,33},{33,49},{49,1},{2,18}... | collective-permute-start | bytes 1376264 | tf_op jit(solution)/shard_map/ppermute | solution.py:17
  38.0 22.3 %collective-permute-start.1 = (bf16[128,1792]{1,0:T(8,128)(2,1)}, bf16[128,1792]{1,0:T(8,128)(2,1)S(1)}, u32[]{:S(2)}, u32[]{:S(2)}) collective-permute-start(bf16[128,1792]{1,0:T(8,128)(2,1)} %bitcast.80), channel_id=1, source_target_pairs={{0,48},{16,0},{32,16},{48,32},{1,49},{17,1},{33,17},{49,33},{2,50}... | collective-permute-start | bytes 1376264 | tf_op jit(solution)/shard_map/ppermute | solution.py:17
  40.8 22.2 %collective-permute-start = (bf16[448,1792]{1,0:T(8,128)(2,1)}, bf16[448,1792]{1,0:T(8,128)(2,1)}, u32[]{:S(2)}, u32[]{:S(2)}) collective-permute-start(bf16[448,1792]{1,0:T(8,128)(2,1)} %bitcast.73), channel_id=1, source_target_pairs={{0,8},{8,0},{1,9},{9,1},{2,10},{10,2},{3,11},{11,3},{4,12},{12,4},... | collective-permute-start | bytes 4816904 | tf_op jit(solution)/shard_map/ppermute | solution.py:17
  61.3 1.4 collective-permute-start.8
  62.9 22.5 %copy-start.3 = (bf16[512,256]{1,0:T(8,128)(2,1)}, bf16[512,256]{1,0:T(8,128)(2,1)S(1)}, u32[]{:S(2)}) copy-start(bf16[512,256]{1,0:T(8,128)(2,1)S(1)} %maximum_select_fusion.w0) | copy-start | bytes 786436
  64.7 1.8 copy-start.1
  64.7 10.3 %copy-start.12 = (bf16[1,128,512]{2,1,0:T(8,128)(2,1)S(1)}, bf16[1,128,512]{2,1,0:T(8,128)(2,1)}, u32[]{:S(2)}) copy-start(bf16[1,128,512]{2,1,0:T(8,128)(2,1)} %param.8) | copy-start | bytes 393220
  68.3 18.7 %all-to-all-start.4 = ((bf16[8,8,1152]{2,1,0:T(8,128)(2,1)}), bf16[8,8,1152]{2,1,0:T(8,128)(2,1)S(1)}, u32[]{:S(2)}, u32[]{:S(2)}) async-start(bf16[8,8,1152]{2,1,0:T(8,128)(2,1)} %pad_maximum_fusion.6), calls=%async_computation.4 | async-start | bytes 294912 | tf_op jit(solution)/shard_map/all_to_all | solution.py:35
  75.0 11.0 %collective-permute-start.5 = (bf16[128,512]{1,0:T(8,128)(2,1)S(1)}, bf16[128,512]{1,0:T(8,128)(2,1)S(1)}, u32[]{:S(2)}, u32[]{:S(2)}) collective-permute-start(bf16[128,512]{1,0:T(8,128)(2,1)S(1)} %bitcast.83), channel_id=1, source_target_pairs={{0,192},{64,0},{128,64},{192,128},{1,193},{65,1},{129,65},{193,129... | collective-permute-start | bytes 393224 | tf_op jit(solution)/shard_map/ppermute | solution.py:17
  78.0 17.5 %collective-permute-start.9 = (bf16[512,256]{1,0:T(8,128)(2,1)S(1)}, bf16[512,256]{1,0:T(8,128)(2,1)S(1)}, u32[]{:S(2)}, u32[]{:S(2)}) collective-permute-start(bf16[512,256]{1,0:T(8,128)(2,1)S(1)} %maximum_select_fusion.w0), channel_id=1, source_target_pairs={{0,48},{16,0},{32,16},{48,32},{1,49},{17,1},{33,17},{49,33},{2,50}... | collective-permute-start | bytes 786440 | tf_op jit(solution)/shard_map/ppermute | solution.py:17
  80.4 17.4 %collective-permute-start.10 = (bf16[512,256]{1,0:T(8,128)(2,1)S(1)}, bf16[512,256]{1,0:T(8,128)(2,1)S(1)}, u32[]{:S(2)}, u32[]{:S(2)}) collective-permute-start(bf16[512,256]{1,0:T(8,128)(2,1)S(1)} %maximum_select_fusion.w0), channel_id=1, source_target_pairs={{0,32},{16,48},{32,0},{48,16},{1,33},{17,49},{33,1},{49,17},{2,34}... | collective-permute-start | bytes 786440 | tf_op jit(solution)/shard_map/ppermute | solution.py:17
  85.3 17.4 %collective-permute-start.11 = (bf16[512,256]{1,0:T(8,128)(2,1)S(1)}, bf16[512,256]{1,0:T(8,128)(2,1)S(1)}, u32[]{:S(2)}, u32[]{:S(2)}) collective-permute-start(bf16[512,256]{1,0:T(8,128)(2,1)S(1)} %maximum_select_fusion.w0), channel_id=1, source_target_pairs={{0,16},{16,32},{32,48},{48,0},{1,17},{17,33},{33,49},{49,1},{2,18}... | collective-permute-start | bytes 786440 | tf_op jit(solution)/shard_map/ppermute | solution.py:17
  85.3 10.1 %collective-permute-start.6 = (bf16[128,512]{1,0:T(8,128)(2,1)S(1)}, bf16[128,512]{1,0:T(8,128)(2,1)S(1)}, u32[]{:S(2)}, u32[]{:S(2)}) collective-permute-start(bf16[128,512]{1,0:T(8,128)(2,1)S(1)} %bitcast.84), channel_id=1, source_target_pairs={{0,128},{64,192},{128,0},{192,64},{1,129},{65,193},{129,1},{193,65... | collective-permute-start | bytes 393224 | tf_op jit(solution)/shard_map/ppermute | solution.py:17
  86.0 16.7 %copy-start.13 = (bf16[128,512]{1,0:T(8,128)(2,1)}, bf16[128,512]{1,0:T(8,128)(2,1)S(1)}, u32[]{:S(2)}) copy-start(bf16[128,512]{1,0:T(8,128)(2,1)S(1)} %collective-permute-done.5.a1) | copy-start | bytes 393220
  86.0 9.5 %collective-permute-start.7 = (bf16[128,512]{1,0:T(8,128)(2,1)S(1)}, bf16[128,512]{1,0:T(8,128)(2,1)S(1)}, u32[]{:S(2)}, u32[]{:S(2)}) collective-permute-start(bf16[128,512]{1,0:T(8,128)(2,1)S(1)} %bitcast.85), channel_id=1, source_target_pairs={{0,64},{64,128},{128,192},{192,0},{1,65},{65,129},{129,193},{193,1... | collective-permute-start | bytes 393224 | tf_op jit(solution)/shard_map/ppermute | solution.py:17
  87.6 19.8 %all-to-all-start.5 = ((bf16[16,8,256]{2,1,0:T(8,128)(2,1)}), bf16[16,8,256]{2,1,0:T(8,128)(2,1)S(1)}, u32[]{:S(2)}, u32[]{:S(2)}) async-start(bf16[16,8,256]{2,1,0:T(8,128)(2,1)} %broadcast_in_dim.8), calls=%async_computation.5 | async-start | bytes 131072 | tf_op jit(solution)/shard_map/all_to_all | solution.py:35
  95.5 7.2 %copy-start.14 = (bf16[128,512]{1,0:T(8,128)(2,1)}, bf16[128,512]{1,0:T(8,128)(2,1)S(1)}, u32[]{:S(2)}) copy-start(bf16[128,512]{1,0:T(8,128)(2,1)S(1)} %collective-permute-done.6.a2) | copy-start | bytes 393220
  95.5 7.2 %copy-start.15 = (bf16[128,512]{1,0:T(8,128)(2,1)}, bf16[128,512]{1,0:T(8,128)(2,1)S(1)}, u32[]{:S(2)}) copy-start(bf16[128,512]{1,0:T(8,128)(2,1)S(1)} %collective-permute-done.7.a3) | copy-start | bytes 393220
  95.5 7.2 %copy-start.8 = (bf16[512,256]{1,0:T(8,128)(2,1)}, bf16[512,256]{1,0:T(8,128)(2,1)S(1)}, u32[]{:S(2)}) copy-start(bf16[512,256]{1,0:T(8,128)(2,1)S(1)} %collective-permute-done.9.w1) | copy-start | bytes 786436
  97.9 4.9 %copy-start.9 = (bf16[512,256]{1,0:T(8,128)(2,1)}, bf16[512,256]{1,0:T(8,128)(2,1)S(1)}, u32[]{:S(2)}) copy-start(bf16[512,256]{1,0:T(8,128)(2,1)S(1)} %collective-permute-done.10.w2) | copy-start | bytes 786436
  107.4 16.4 %all-to-all-start.3 = ((bf16[4,128,1024]{2,1,0:T(8,128)(2,1)}), bf16[4,128,1024]{2,1,0:T(8,128)(2,1)S(1)}, u32[]{:S(2)}, u32[]{:S(2)}) async-start(bf16[4,128,1024]{2,1,0:T(8,128)(2,1)} %bitcast.71), calls=%async_computation.3 | async-start | bytes 2097152 | tf_op jit(solution)/shard_map/all_to_all | solution.py:35
  124.6 38.3 %all-to-all-start.6 = ((bf16[8,8,4992]{2,1,0:T(8,128)(2,1)}), bf16[8,8,4992]{2,1,0:T(8,128)(2,1)S(1)}, u32[]{:S(2)}, u32[]{:S(2)}) async-start(bf16[8,8,4992]{2,1,0:T(8,128)(2,1)} %broadcast_in_dim.9), calls=%async_computation.6 | async-start | bytes 1277952 | tf_op jit(solution)/shard_map/all_to_all | solution.py:35
  137.3 13.1 %collective-permute-start.12 = (bf16[128,1024]{1,0:T(8,128)(2,1)S(1)}, bf16[128,1024]{1,0:T(8,128)(2,1)S(1)}, u32[]{:S(2)}, u32[]{:S(2)}) collective-permute-start(bf16[128,1024]{1,0:T(8,128)(2,1)S(1)} %reduce_sum.78), channel_id=1, source_target_pairs={{4,0},{16,20},{36,32},{48,52},{5,1},{17,21},{37,33},{49,53},{6,2},... | collective-permute-start | bytes 786440 | tf_op jit(solution)/shard_map/ppermute | solution.py:31
  138.6 107.8 %collective-permute-start.19 = (bf16[448,4096]{1,0:T(8,128)(2,1)}, bf16[448,4096]{1,0:T(8,128)(2,1)}, u32[]{:S(2)}, u32[]{:S(2)}) collective-permute-start(bf16[448,4096]{1,0:T(8,128)(2,1)} %eig0.1), channel_id=1, source_target_pairs={{0,8},{8,0},{1,9},{9,1},{2,10},{10,2},{3,11},{11,3},{4,12},{12,4},... | collective-permute-start | bytes 11010056 | tf_op jit(solution)/shard_map/ppermute | solution.py:17
  150.4 46.5 %collective-permute-start.14 = (bf16[128,1024]{1,0:T(8,128)(2,1)S(1)}, bf16[128,1024]{1,0:T(8,128)(2,1)S(1)}, u32[]{:S(2)}, u32[]{:S(2)}) collective-permute-start(bf16[128,1024]{1,0:T(8,128)(2,1)S(1)} %add_convert_fusion.1), channel_id=1, source_target_pairs={{0,32},{20,52},{32,0},{52,20},{1,33},{21,53},{33,1},{53,21},{2,34}... | collective-permute-start | bytes 786440 | tf_op jit(solution)/shard_map/ppermute | solution.py:26
  153.9 43.0 %collective-permute-start.15 = (bf16[128,1024]{1,0:T(8,128)(2,1)S(1)}, bf16[128,1024]{1,0:T(8,128)(2,1)}, u32[]{:S(2)}, u32[]{:S(2)}) collective-permute-start(bf16[128,1024]{1,0:T(8,128)(2,1)S(1)} %add_convert_fusion.1), channel_id=1, source_target_pairs={{0,48},{20,4},{32,16},{52,36},{1,49},{21,5},{33,17},{53,37},{2,50}... | collective-permute-start | bytes 786440 | tf_op jit(solution)/shard_map/ppermute | solution.py:26
  155.9 13.1 %collective-permute-start.13 = (bf16[128,1024]{1,0:T(8,128)(2,1)S(1)}, bf16[128,1024]{1,0:T(8,128)(2,1)S(1)}, u32[]{:S(2)}, u32[]{:S(2)}) collective-permute-start(bf16[128,1024]{1,0:T(8,128)(2,1)S(1)} %add_convert_fusion.1), channel_id=1, source_target_pairs={{0,16},{20,36},{32,48},{52,4},{1,17},{21,37},{33,49},{53,5},{2,18}... | collective-permute-start | bytes 786440 | tf_op jit(solution)/shard_map/ppermute | solution.py:26
  162.9 14.5 %all-to-all-start = ((bf16[4,128,896]{2,1,0:T(8,128)(2,1)}), bf16[4,128,896]{2,1,0:T(8,128)(2,1)S(1)}, u32[]{:S(2)}, u32[]{:S(2)}) async-start(bf16[4,128,896]{2,1,0:T(8,128)(2,1)} %bitcast.5), calls=%async_computation | async-start | bytes 1835008 | tf_op jit(solution)/shard_map/all_to_all | solution.py:35
  177.4 13.7 %all-to-all-start.2 = ((bf16[4,128,896]{2,1,0:T(8,128)(2,1)}), bf16[4,128,896]{2,1,0:T(8,128)(2,1)S(1)}, u32[]{:S(2)}, u32[]{:S(2)}) async-start(bf16[4,128,896]{2,1,0:T(8,128)(2,1)} %bitcast.75), calls=%async_computation.2 | async-start | bytes 1835008 | tf_op jit(solution)/shard_map/all_to_all | solution.py:35
  191.1 5.9 %copy-start.2 = (bf16[4,128,896]{2,1,0:T(8,128)(2,1)}, bf16[4,128,896]{2,1,0:T(8,128)(2,1)S(1)}, u32[]{:S(2)}) copy-start(bf16[4,128,896]{2,1,0:T(8,128)(2,1)S(1)} %all-to-all-done.2) | copy-start | bytes 2752516
  191.1 38.5 %all-to-all-start.1 = ((bf16[8,128,896]{2,1,0:T(8,128)(2,1)}), bf16[8,128,896]{2,1,0:T(8,128)(2,1)}, u32[]{:S(2)}, u32[]{:S(2)}) async-start(bf16[8,128,896]{2,1,0:T(8,128)(2,1)} %bitcast.72), calls=%async_computation.1 | async-start | bytes 3670016 | tf_op jit(solution)/shard_map/all_to_all | solution.py:35
  198.8 21.1 %collective-permute-start.18 = (bf16[2,128,1024]{2,1,0:T(8,128)(2,1)}, bf16[2,128,1024]{2,1,0:T(8,128)(2,1)}, u32[]{:S(2)}, u32[]{:S(2)}) collective-permute-start(bf16[2,128,1024]{2,1,0:T(8,128)(2,1)} %get-tuple-element.12), channel_id=1, source_target_pairs={{0,64},{64,128},{128,192},{192,0},{1,65},{65,129},{129,193},{193,1... | collective-permute-start | bytes 1572872 | tf_op jit(solution)/shard_map/ppermute | solution.py:17
  198.8 21.1 %collective-permute-start.17 = (bf16[2,128,1024]{2,1,0:T(8,128)(2,1)}, bf16[2,128,1024]{2,1,0:T(8,128)(2,1)}, u32[]{:S(2)}, u32[]{:S(2)}) collective-permute-start(bf16[2,128,1024]{2,1,0:T(8,128)(2,1)} %get-tuple-element.12), channel_id=1, source_target_pairs={{0,128},{64,192},{128,0},{192,64},{1,129},{65,193},{129,1},{193,65... | collective-permute-start | bytes 1572872 | tf_op jit(solution)/shard_map/ppermute | solution.py:17
  201.2 19.3 %collective-permute-start.16 = (bf16[2,128,1024]{2,1,0:T(8,128)(2,1)}, bf16[2,128,1024]{2,1,0:T(8,128)(2,1)}, u32[]{:S(2)}, u32[]{:S(2)}) collective-permute-start(bf16[2,128,1024]{2,1,0:T(8,128)(2,1)} %get-tuple-element.12), channel_id=1, source_target_pairs={{0,192},{64,0},{128,64},{192,128},{1,193},{65,1},{129,65},{193,129... | collective-permute-start | bytes 1572872 | tf_op jit(solution)/shard_map/ppermute | solution.py:17
  203.7 21.8 %collective-permute-start.20 = (bf16[64,4992]{1,0:T(8,128)(2,1)}, bf16[64,4992]{1,0:T(8,128)(2,1)}, u32[]{:S(2)}, u32[]{:S(2)}) collective-permute-start(bf16[64,4992]{1,0:T(8,128)(2,1)} %concatenate.37), channel_id=1, source_target_pairs={{0,8},{8,0},{1,9},{9,1},{2,10},{10,2},{3,11},{11,3},{4,12},{12,4},... | collective-permute-start | bytes 1916936 | tf_op jit(solution)/shard_map/ppermute | solution.py:17
  229.6 1.8 copy-start.6
  234.0 10.5 %collective-permute-start.4 = (bf16[2,128,896]{2,1,0:T(8,128)(2,1)}, bf16[2,128,896]{2,1,0:T(8,128)(2,1)}, u32[]{:S(2)}, u32[]{:S(2)}) collective-permute-start(bf16[2,128,896]{2,1,0:T(8,128)(2,1)} %pad_maximum_fusion.4), channel_id=1, source_target_pairs={{0,4},{4,0},{1,5},{5,1},{2,6},{6,2},{3,7},{7,3},{8,12},{12,8},{9,1... | collective-permute-start | bytes 1376264 | tf_op jit(solution)/shard_map/ppermute | solution.py:17
  235.7 8.8 %copy-start.5 = (bf16[1,128,896]{2,1,0:T(8,128)(2,1)S(1)}, bf16[1,128,896]{2,1,0:T(8,128)(2,1)}, u32[]{:S(2)}) copy-start(bf16[1,128,896]{2,1,0:T(8,128)(2,1)} %get-tuple-element.14) | copy-start | bytes 688132
  284.7 9.6 %all-to-all-start.8 = ((f32[16,2,16]{2,1,0:T(2,128)}), f32[16,2,16]{2,1,0:T(2,128)S(1)}, u32[]{:S(2)}, u32[]{:S(2)}) async-start(f32[16,2,16]{2,1,0:T(2,128)} %broadcast_in_dim.11), calls=%async_computation.8 | async-start | bytes 32768 | tf_op jit(solution)/shard_map/all_to_all | solution.py:35
  (1 other events, 0.7 us)
Sparse Core Ops, SparseCore 0:
  9.1 34.1 all-gather.4
  45.1 31.1 all-gather.8
  78.1 47.1 all-gather.6

commit v2 on v1

--- a/solution.py
+++ b/solution.py
@@ -47,29 +47,32 @@
     return lax.dot_general(a, b, (((1,), (1,)), ((), ())), preferred_element_type=F32)
 
 
-def rotate_in_kernel(at_ref, a0, a1, a2, a3, w0, w1, w2, w3, out, act):
+def rotate_in_kernel(at_ref, a0, a1, a2, a3, w0, w1, out, act):
     tokens = a0.shape[0]
-    n = w0.shape[1]
+    n = w0.shape[2]
     for d, a in enumerate((a0, a1, a2, a3)):
         y = lax.rem(at_ref[0] + d, 4)
         act[pl.ds(pl.multiple_of(y * tokens, tokens), tokens), :] = a[...]
-    for d, w in enumerate((w0, w1, w2, w3)):
-        zh = lax.rem(at_ref[1] + d, 4)
-        out[:, pl.ds(pl.multiple_of(zh * n, n), n)] = dot(act[...], w[...]).astype(BF)
+    for k, w in enumerate((w0, w1)):
+        core = at_ref[2] if k == 0 else 1 - at_ref[2]
+        for d in range(4):
+            zh = lax.rem(at_ref[1] + d, 4)
+            here = pl.multiple_of((2 * zh + core) * n, n)
+            out[:, pl.ds(here, n)] = dot(act[...], w[d]).astype(BF)
 
 
 def rotate_in(at, acts, bases):
     tokens, unit = acts[0].shape
-    n = bases[0].shape[1]
+    n = bases[0].shape[2]
     vmem = pl.BlockSpec(memory_space=pltpu.VMEM)
     return pl.pallas_call(
         rotate_in_kernel,
-        in_specs=[pl.BlockSpec(memory_space=pltpu.SMEM)] + [vmem] * 8,
+        in_specs=[pl.BlockSpec(memory_space=pltpu.SMEM)] + [vmem] * 6,
         out_specs=vmem,
-        out_shape=jax.ShapeDtypeStruct((4 * tokens, 4 * n), BF),
+        out_shape=jax.ShapeDtypeStruct((4 * tokens, 8 * n), BF),
         scratch_shapes=[pltpu.VMEM((4 * tokens, unit), BF)],
         cost_estimate=pl.CostEstimate(
-            flops=2 * 16 * tokens * unit * n, bytes_accessed=2 * 16 * tokens * (unit + n), transcendentals=0
+            flops=2 * 32 * tokens * unit * n, bytes_accessed=2 * 16 * tokens * (unit + n), transcendentals=0
         ),
         name="rotate_in",
     )(at, *acts, *bases)
@@ -148,19 +151,17 @@
 
     same = li == zi % 2
     low = jnp.where(same, zi, (zi + 3) % 4) // 2
-    at = jnp.stack([yi, zi]).astype(jnp.int32)
+    at = jnp.stack([yi, zi, ci]).astype(jnp.int32)
 
     out_t = basis_out.T
     out_both = jnp.concatenate([out_t, shift(out_t, "c", 1)], 0)
     out_both = lax.optimization_barrier(out_both)
-    in_other = shift(basis_in, "c", 1)
-    in_both = jnp.where(
-        first, jnp.concatenate([basis_in, in_other], 1), jnp.concatenate([in_other, basis_in], 1)
-    )
-    both = in_both.shape[1]
     eigen_other = shift(eigen_vals, "c", 1)
 
-    part = rotate_in(at, gather(act_in[0], "y"), gather(in_both, "zh"))
+    in_own = jnp.stack(gather(basis_in, "zh"))
+    in_other = shift(in_own, "c", 1)
+    both = 2 * basis_in.shape[1]
+    part = rotate_in(at, gather(act_in[0], "y"), (in_own, in_other))
     part = exchange(part.reshape(4, tokens, 4 * both), "x").astype(F32).sum(0).astype(BF)
     part = (part.astype(F32) + to_owner(part).astype(F32)).astype(BF)
     plus, far, minus = (from_owner(part, by) for by in (1, 2, 3))
@@ -169,6 +170,9 @@
 
     mine = lax.dynamic_slice_in_dim(query_out.reshape(rows, unit), ci * half_rows, half_rows, 0)
     mine_in = lax.dynamic_slice_in_dim(query_in.reshape(rows, -1), ci * half_rows, half_rows, 0)
+    in_both = jnp.concatenate(
+        [jnp.where(first, basis_in, in_other[0]), jnp.where(first, in_other[0], basis_in)], 1
+    )
     query = jnp.concatenate([dot_t(mine, out_both), dot(mine_in, in_both)], 1).astype(BF)
     some = half_rows // 8
     query = exchange(query.reshape(8, some, -1), ("zl", "x")).reshape(8, some, -1)

time: 305 us -> 300 us (0.984)
  starting transfers between devices: 95.5 us -> 90.4 us
    all_to_all x8, starting transfers between devices: 51.5 us -> 41.3 us  [exchange(): return lax.all_to_all(value, axes, 0, 0, tiled=True)]
    ppermute x17, starting transfers between devices: 35.7 us -> 38.9 us  [shift(): return lax.ppermute(value, axis, [(i, (i + by) % n) for i in range(n)])]
    ppermute x17, waiting for transfers between devices: 63.3 us -> 66.5 us  [shift(): return lax.ppermute(value, axis, [(i, (i + by) % n) for i in range(n)])]
  transfers between devices with their start and end apart: 32 -> 32, of which waited for: 15 -> 19; matrix products, arithmetic and copies ran while one was open for 17% -> 17% of each run, Pallas kernels for 1% -> 1%
where the time goes in v2:
time: 300 us; the launch traced here: 297 us
  waiting for transfers between devices  98.1 us (33%)
  starting transfers between devices  90.4 us (30%)
  other arithmetic  21.8 us (7%)
  matrix products  20.6 us (7%)
  Pallas kernels  19.7 us (7%)
  blocking collectives  19.6 us (7%)
  local copies, waits for them, and re-layouts  13.4 us (4%)
  between operations  13.4 us (4%)
    ppermute x17, waiting for transfers between devices, shift(): return lax.ppermute(value, axis, [(i, (i + by) % n) for i in range(n)])  66.5 us
    all_to_all x8, starting transfers between devices, exchange(): return lax.all_to_all(value, axes, 0, 0, tiled=True)  41.3 us
    ppermute x17, starting transfers between devices, shift(): return lax.ppermute(value, axis, [(i, (i + by) % n) for i in range(n)])  38.9 us
    all_to_all x8, waiting for transfers between devices, exchange(): return lax.all_to_all(value, axes, 0, 0, tiled=True)  21.2 us
    dot_general x4, matrix products, dot_t(): lax.dot_general(a, b, (((1,), (1,)), ((), ())), preferred_element_type=F32)  20.4 us
    all_to_all x1, blocking collectives, exchange(): return lax.all_to_all(value, axes, 0, 0, tiled=True)  19.6 us
    pallas_call x1, Pallas kernels, score(): pl.pallas_call(score_kernel, grid_spec=spec, out_shape=jax.ShapeDtypeStru...  15.8 us
    ppermute x1, waiting for transfers between devices, to_owner(): return lax.ppermute(value, ('zh', 'zl'), pairs)  9.44 us
  transfers between devices with their start and end apart: 32, of which 19 were waited for; matrix products, arithmetic and copies ran while one was open for 17% of the time, Pallas kernels for 1%

profile of v2, /device:TPU:2, one launch (start us, length us, event | category | flops | bytes accessed | tf_op | source)
XLA Modules:
  0.0 297.0 jit_solution(2116192076700959789)
XLA Ops:
  7.3 7.3 %collective-permute-start.3 = (bf16[128,1792]{1,0:T(8,128)(2,1)}, bf16[128,1792]{1,0:T(8,128)(2,1)S(1)}, u32[]{:S(2)}, u32[]{:S(2)}) collective-permute-start(bf16[128,1792]{1,0:T(8,128)(2,1)} %bitcast.89), channel_id=1, source_target_pairs={{0,32},{16,48},{32,0},{48,16},{1,33},{17,49},{33,1},{49,17},{2,34}... | collective-permute-start | bytes 1376264 | tf_op jit(solution)/shard_map/ppermute | solution.py:17
  14.6 13.0 %collective-permute-done.3 = bf16[128,1792]{1,0:T(8,128)(2,1)S(1)} collective-permute-done((bf16[128,1792]{1,0:T(8,128)(2,1)}, bf16[128,1792]{1,0:T(8,128)(2,1)S(1)}, u32[]{:S(2)}, u32[]{:S(2)}) %collective-permute-start.3) | collective-permute-done | bytes 458784 | tf_op jit(solution)/shard_map/ppermute | solution.py:17
  28.4 9.6 %collective-permute-start.2 = (bf16[128,1792]{1,0:T(8,128)(2,1)}, bf16[128,1792]{1,0:T(8,128)(2,1)S(1)}, u32[]{:S(2)}, u32[]{:S(2)}) collective-permute-start(bf16[128,1792]{1,0:T(8,128)(2,1)} %bitcast.90), channel_id=1, source_target_pairs={{0,16},{16,32},{32,48},{48,0},{1,17},{17,33},{33,49},{49,1},{2,18}... | collective-permute-start | bytes 1376264 | tf_op jit(solution)/shard_map/ppermute | solution.py:17
  38.0 2.8 collective-permute-start.1
  40.8 19.5 %collective-permute-done.2 = bf16[128,1792]{1,0:T(8,128)(2,1)S(1)} collective-permute-done((bf16[128,1792]{1,0:T(8,128)(2,1)}, bf16[128,1792]{1,0:T(8,128)(2,1)S(1)}, u32[]{:S(2)}, u32[]{:S(2)}) %collective-permute-start.2) | collective-permute-done | bytes 458784 | tf_op jit(solution)/shard_map/ppermute | solution.py:17
  61.8 6.3 %collective-permute-start.9 = (bf16[512,128]{1,0:T(8,128)(2,1)S(1)}, bf16[512,128]{1,0:T(8,128)(2,1)S(1)}, u32[]{:S(2)}, u32[]{:S(2)}) collective-permute-start(bf16[512,128]{1,0:T(8,128)(2,1)S(1)} %copy-done.8), channel_id=1, source_target_pairs={{0,32},{16,48},{32,0},{48,16},{1,33},{17,49},{33,1},{49,17},{2,34}... | collective-permute-start | bytes 393224 | tf_op jit(solution)/shard_map/ppermute | solution.py:17
  68.1 2.1 collective-permute-start.8
  70.1 3.7 %collective-permute-done.10 = bf16[512,128]{1,0:T(8,128)(2,1)S(1)} collective-permute-done((bf16[512,128]{1,0:T(8,128)(2,1)S(1)}, bf16[512,128]{1,0:T(8,128)(2,1)S(1)}, u32[]{:S(2)}, u32[]{:S(2)}) %collective-permute-start.10) | collective-permute-done | bytes 131104 | tf_op jit(solution)/shard_map/ppermute | solution.py:17
  73.8 2.0 collective-permute-done.9
  75.9 4.9 %collective-permute-done.8 = bf16[512,128]{1,0:T(8,128)(2,1)S(1)} collective-permute-done((bf16[512,128]{1,0:T(8,128)(2,1)S(1)}, bf16[512,128]{1,0:T(8,128)(2,1)S(1)}, u32[]{:S(2)}, u32[]{:S(2)}) %collective-permute-start.8) | collective-permute-done | bytes 131104 | tf_op jit(solution)/shard_map/ppermute | solution.py:17
  80.9 1.9 collective-permute-done.11.w1
  83.1 1.6 pad_maximum_fusion
  84.7 1.7 copy-done.1
  88.3 4.8 %all-to-all-start.4 = ((bf16[8,8,1152]{2,1,0:T(8,128)(2,1)}), bf16[8,8,1152]{2,1,0:T(8,128)(2,1)S(1)}, u32[]{:S(2)}, u32[]{:S(2)}) async-start(bf16[8,8,1152]{2,1,0:T(8,128)(2,1)} %pad_maximum_fusion.7), calls=%async_computation.4 | async-start | bytes 294912 | tf_op jit(solution)/shard_map/all_to_all | solution.py:35
  93.1 3.1 %collective-permute-start.5 = (bf16[128,512]{1,0:T(8,128)(2,1)S(1)}, bf16[128,512]{1,0:T(8,128)(2,1)S(1)}, u32[]{:S(2)}, u32[]{:S(2)}) collective-permute-start(bf16[128,512]{1,0:T(8,128)(2,1)S(1)} %bitcast.94), channel_id=1, source_target_pairs={{0,192},{64,0},{128,64},{192,128},{1,193},{65,1},{129,65},{193,129... | collective-permute-start | bytes 393224 | tf_op jit(solution)/shard_map/ppermute | solution.py:17
  98.9 6.2 %all-to-all-start.5 = ((bf16[16,8,256]{2,1,0:T(8,128)(2,1)}), bf16[16,8,256]{2,1,0:T(8,128)(2,1)S(1)}, u32[]{:S(2)}, u32[]{:S(2)}) async-start(bf16[16,8,256]{2,1,0:T(8,128)(2,1)} %broadcast_in_dim.8), calls=%async_computation.5 | async-start | bytes 131072 | tf_op jit(solution)/shard_map/all_to_all | solution.py:35
  106.9 2.1 collective-permute-done.7.a3
  109.6 3.8 %rotate_in.1 = bf16[512,1024]{1,0:T(8,128)(2,1)} custom-call(s32[3]{0:T(128)} %pad_add_fusion.at_ref, bf16[128,512]{1,0:T(8,128)(2,1)} %bitcast.93, bf16[128,512]{1,0:T(8,128)(2,1)} %copy-done.11, bf16[128,512]{1,0:T(8,128)(2,1)} %copy-done.12, bf16[128,512]{1,0:T(8,128)(2,1)} %copy-done.13, bf16[4,512,128]{2,1,0:T(8,128)(2,1)} %copy-done.3, ...), custom_call_target="tpu_custom_call" | custom-call | flops 536870912 | bytes 2621440 | tf_op jit(solution)/shard_map/rotate_in/pallas_call | solution.py:68
  113.4 1.8 all-to-all-done.5
  115.3 5.0 %all-to-all-start.3 = ((bf16[4,128,1024]{2,1,0:T(8,128)(2,1)}), bf16[4,128,1024]{2,1,0:T(8,128)(2,1)S(1)}, u32[]{:S(2)}, u32[]{:S(2)}) async-start(bf16[4,128,1024]{2,1,0:T(8,128)(2,1)} %bitcast.81), calls=%async_computation.3 | async-start | bytes 2097152 | tf_op jit(solution)/shard_map/all_to_all | solution.py:35
  120.3 11.5 %all-to-all-done.3 = bf16[4,128,1024]{2,1,0:T(8,128)(2,1)S(1)} async-done(((bf16[4,128,1024]{2,1,0:T(8,128)(2,1)}), bf16[4,128,1024]{2,1,0:T(8,128)(2,1)S(1)}, u32[]{:S(2)}, u32[]{:S(2)}) %all-to-all-start.3) | async-done | bytes 1048608 | tf_op jit(solution)/shard_map/all_to_all | solution.py:35
  132.6 4.9 %all-to-all-start.6 = ((bf16[8,8,4992]{2,1,0:T(8,128)(2,1)}), bf16[8,8,4992]{2,1,0:T(8,128)(2,1)S(1)}, u32[]{:S(2)}, u32[]{:S(2)}) async-start(bf16[8,8,4992]{2,1,0:T(8,128)(2,1)} %broadcast_in_dim.9), calls=%async_computation.6 | async-start | bytes 1277952 | tf_op jit(solution)/shard_map/all_to_all | solution.py:35
  139.2 9.4 %collective-permute-done.12 = bf16[128,1024]{1,0:T(8,128)(2,1)S(1)} collective-permute-done((bf16[128,1024]{1,0:T(8,128)(2,1)S(1)}, bf16[128,1024]{1,0:T(8,128)(2,1)S(1)}, u32[]{:S(2)}, u32[]{:S(2)}) %collective-permute-start.12) | collective-permute-done | bytes 262176 | tf_op jit(solution)/shard_map/ppermute | solution.py:31
  148.7 5.4 %collective-permute-start.14 = (bf16[128,1024]{1,0:T(8,128)(2,1)S(1)}, bf16[128,1024]{1,0:T(8,128)(2,1)S(1)}, u32[]{:S(2)}, u32[]{:S(2)}) collective-permute-start(bf16[128,1024]{1,0:T(8,128)(2,1)S(1)} %add_convert_fusion.1), channel_id=1, source_target_pairs={{0,32},{20,52},{32,0},{52,20},{1,33},{21,53},{33,1},{53,21},{2,34}... | collective-permute-start | bytes 786440 | tf_op jit(solution)/shard_map/ppermute | solution.py:26
  154.0 2.0 collective-permute-start.15
  157.5 5.5 %convolution_convert_fusion.2 = bf16[896,512]{0,1:T(8,128)(2,1)} fusion(bf16[896,1792]{1,0:T(8,128)(2,1)} %copy-done.1, bf16[512,1792]{1,0:T(8,128)(2,1)} %bitcast.103), kind=kOutput, calls=%fused_computation.7 | convolution fusion | flops 1644625920 | bytes 5963776 | tf_op jit(solution)/shard_map/dot_general | solution.py:47
  163.1 4.8 %all-to-all-start = ((bf16[4,128,896]{2,1,0:T(8,128)(2,1)}), bf16[4,128,896]{2,1,0:T(8,128)(2,1)S(1)}, u32[]{:S(2)}, u32[]{:S(2)}) async-start(bf16[4,128,896]{2,1,0:T(8,128)(2,1)} %bitcast.6), calls=%async_computation | async-start | bytes 1835008 | tf_op jit(solution)/shard_map/all_to_all | solution.py:35
  168.8 5.5 %convolution_convert_fusion.1 = bf16[896,512]{0,1:T(8,128)(2,1)} fusion(bf16[896,1792]{1,0:T(8,128)(2,1)} %copy-done.1, bf16[512,1792]{1,0:T(8,128)(2,1)} %all-gather.9.cloned.1.call-done), kind=kOutput, calls=%fused_computation.6 | convolution fusion | flops 1644625920 | bytes 5963776 | tf_op jit(solution)/shard_map/dot_general | solution.py:47
  174.3 2.3 all-to-all-done
  176.5 4.9 %all-to-all-start.2 = ((bf16[4,128,896]{2,1,0:T(8,128)(2,1)}), bf16[4,128,896]{2,1,0:T(8,128)(2,1)S(1)}, u32[]{:S(2)}, u32[]{:S(2)}) async-start(bf16[4,128,896]{2,1,0:T(8,128)(2,1)} %bitcast.85), calls=%async_computation.2 | async-start | bytes 1835008 | tf_op jit(solution)/shard_map/all_to_all | solution.py:35
  181.5 8.3 %convolution_convert_fusion = bf16[1024,896]{1,0:T(8,128)(2,1)} fusion(bf16[1024,1792]{1,0:T(8,128)(2,1)} %bitcast.102, bf16[896,1792]{1,0:T(8,128)(2,1)} %copy-done.1), kind=kOutput, calls=%fused_computation.5 | convolution fusion | flops 3289251840 | bytes 8716288 | tf_op jit(solution)/shard_map/dot_general | solution.py:47
  190.2 5.8 %all-to-all-start.1 = ((bf16[8,128,896]{2,1,0:T(8,128)(2,1)}), bf16[8,128,896]{2,1,0:T(8,128)(2,1)}, u32[]{:S(2)}, u32[]{:S(2)}) async-start(bf16[8,128,896]{2,1,0:T(8,128)(2,1)} %bitcast.82), calls=%async_computation.1 | async-start | bytes 3670016 | tf_op jit(solution)/shard_map/all_to_all | solution.py:35
  196.1 1.8 fusion.15
  199.5 2.7 collective-permute-start.17
  204.7 8.6 %collective-permute-done.18 = bf16[2,128,1024]{2,1,0:T(8,128)(2,1)} collective-permute-done((bf16[2,128,1024]{2,1,0:T(8,128)(2,1)}, bf16[2,128,1024]{2,1,0:T(8,128)(2,1)}, u32[]{:S(2)}, u32[]{:S(2)}) %collective-permute-start.18) | collective-permute-done | bytes 524320 | tf_op jit(solution)/shard_map/ppermute | solution.py:17
  213.4 5.6 %collective-permute-done.17 = bf16[2,128,1024]{2,1,0:T(8,128)(2,1)} collective-permute-done((bf16[2,128,1024]{2,1,0:T(8,128)(2,1)}, bf16[2,128,1024]{2,1,0:T(8,128)(2,1)}, u32[]{:S(2)}, u32[]{:S(2)}) %collective-permute-start.17) | collective-permute-done | bytes 524320 | tf_op jit(solution)/shard_map/ppermute | solution.py:17
  219.0 3.0 pad_maximum_fusion.1.act
  223.9 2.0 copy.31
  225.9 2.1 convert_reduce_fusion.1
  228.0 1.8 convert_reduce_fusion
  229.8 1.7 fusion.5
  234.0 2.3 copy.32.value
  237.2 4.0 %collective-permute-done.4 = bf16[2,128,896]{2,1,0:T(8,128)(2,1)} collective-permute-done((bf16[2,128,896]{2,1,0:T(8,128)(2,1)}, bf16[2,128,896]{2,1,0:T(8,128)(2,1)}, u32[]{:S(2)}, u32[]{:S(2)}) %collective-permute-start.4) | collective-permute-done | bytes 458784 | tf_op jit(solution)/shard_map/ppermute | solution.py:17
  241.2 1.9 add_convert_fusion.grad
  243.1 15.8 %score.1 = f32[8,128]{1,0:T(8,128)} custom-call(s32[3]{0:T(128)} %pad_add_fusion.at_ref, bf16[2,128,896]{2,1,0:T(8,128)(2,1)} %add_convert_fusion.grad, bf16[4,2,128,1024]{3,2,1,0:T(8,128)(2,1)} %pad_maximum_fusion.1.act, bf16[448,4096]{1,0:T(8,128)(2,1)} %eig0.1, bf16[448,4096]{1,0:T(8,128)(2,1)} %collective-permute-done.19.eig1, ...), custom_call_target="tpu_custom_call" | custom-call | flops 3758096384 | bytes 7340032 | tf_op jit(solution)/shard_map/score/pallas_call | solution.py:130
  260.0 19.6 %all_to_all.45 = f32[16,2,16]{2,1,0:T(2,128)S(1)} all-to-all(f32[16,2,16]{2,1,0:T(2,128)S(1)} %broadcast_in_dim.10), channel_id=1, replica_groups=mesh['y'=4,'zh'=4,'c'=2,'zl'=2,'x'=4] {'y','zh'}, dimensions={0} | all-to-all | bytes 4096 | tf_op jit(solution)/shard_map/all_to_all | solution.py:35
  280.3 4.8 %all-to-all-start.8 = ((f32[16,2,16]{2,1,0:T(2,128)}), f32[16,2,16]{2,1,0:T(2,128)S(1)}, u32[]{:S(2)}, u32[]{:S(2)}) async-start(f32[16,2,16]{2,1,0:T(2,128)} %broadcast_in_dim.11), calls=%async_computation.8 | async-start | bytes 32768 | tf_op jit(solution)/shard_map/all_to_all | solution.py:35
  285.1 4.7 %all-to-all-done.8 = f32[16,2,16]{2,1,0:T(2,128)S(1)} async-done(((f32[16,2,16]{2,1,0:T(2,128)}), f32[16,2,16]{2,1,0:T(2,128)S(1)}, u32[]{:S(2)}, u32[]{:S(2)}) %all-to-all-start.8) | async-done | bytes 2080 | tf_op jit(solution)/shard_map/all_to_all | solution.py:35
  (102 shorter events, 27.5 us)
Async XLA Ops:
  6.5 78.2 %copy-start = (bf16[16,8,1792]{2,1,0:T(8,128)(2,1)S(1)}, bf16[16,8,1792]{2,1,0:T(8,128)(2,1)}, u32[]{:S(2)}) copy-start(bf16[16,8,1792]{2,1,0:T(8,128)(2,1)} %param.12) | copy-start | bytes 1376260
  6.5 54.8 %copy-start.8 = (bf16[512,128]{1,0:T(8,128)(2,1)S(1)}, bf16[512,128]{1,0:T(8,128)(2,1)}, u32[]{:S(2)}) copy-start(bf16[512,128]{1,0:T(8,128)(2,1)} %param.10) | copy-start | bytes 393220
  6.5 151.0 %all-gather.5.cloned.1.call-start = ((), (), s32[]{:S(2)}) async-start(), calls=%async_computation.9 | async-start | bytes 2293760 | tf_op jit(solution)/shard_map/all_gather | solution.py:196
  7.3 161.5 %all-gather.9.cloned.1.call-start = ((), (), s32[]{:S(2)}) async-start(), calls=%async_computation.11 | async-start | bytes 2293760 | tf_op jit(solution)/shard_map/all_gather | solution.py:196
  7.3 20.3 %collective-permute-start.3 = (bf16[128,1792]{1,0:T(8,128)(2,1)}, bf16[128,1792]{1,0:T(8,128)(2,1)S(1)}, u32[]{:S(2)}, u32[]{:S(2)}) collective-permute-start(bf16[128,1792]{1,0:T(8,128)(2,1)} %bitcast.89), channel_id=1, source_target_pairs={{0,32},{16,48},{32,0},{48,16},{1,33},{17,49},{33,1},{49,17},{2,34}... | collective-permute-start | bytes 1376264 | tf_op jit(solution)/shard_map/ppermute | solution.py:17
  27.6 0.8 copy-start.9
  28.4 153.1 %all-gather.7.cloned.1.call-start = ((), (), s32[]{:S(2)}) async-start(), calls=%async_computation.10 | async-start | bytes 4587520 | tf_op jit(solution)/shard_map/all_gather | solution.py:196
  28.4 31.9 %collective-permute-start.2 = (bf16[128,1792]{1,0:T(8,128)(2,1)}, bf16[128,1792]{1,0:T(8,128)(2,1)S(1)}, u32[]{:S(2)}, u32[]{:S(2)}) collective-permute-start(bf16[128,1792]{1,0:T(8,128)(2,1)} %bitcast.90), channel_id=1, source_target_pairs={{0,16},{16,32},{32,48},{48,0},{1,17},{17,33},{33,49},{49,1},{2,18}... | collective-permute-start | bytes 1376264 | tf_op jit(solution)/shard_map/ppermute | solution.py:17
  38.0 22.3 %collective-permute-start.1 = (bf16[128,1792]{1,0:T(8,128)(2,1)}, bf16[128,1792]{1,0:T(8,128)(2,1)S(1)}, u32[]{:S(2)}, u32[]{:S(2)}) collective-permute-start(bf16[128,1792]{1,0:T(8,128)(2,1)} %bitcast.91), channel_id=1, source_target_pairs={{0,48},{16,0},{32,16},{48,32},{1,49},{17,1},{33,17},{49,33},{2,50}... | collective-permute-start | bytes 1376264 | tf_op jit(solution)/shard_map/ppermute | solution.py:17
  40.8 42.2 %collective-permute-start = (bf16[448,1792]{1,0:T(8,128)(2,1)}, bf16[448,1792]{1,0:T(8,128)(2,1)}, u32[]{:S(2)}, u32[]{:S(2)}) collective-permute-start(bf16[448,1792]{1,0:T(8,128)(2,1)} %bitcast.83), channel_id=1, source_target_pairs={{0,8},{8,0},{1,9},{9,1},{2,10},{10,2},{3,11},{11,3},{4,12},{12,4},... | collective-permute-start | bytes 4816904 | tf_op jit(solution)/shard_map/ppermute | solution.py:17
  60.3 22.6 %copy-start.14 = (bf16[16,8,512]{2,1,0:T(8,128)(2,1)S(1)}, bf16[16,8,512]{2,1,0:T(8,128)(2,1)}, u32[]{:S(2)}) copy-start(bf16[16,8,512]{2,1,0:T(8,128)(2,1)} %param.13) | copy-start | bytes 393220
  60.3 22.8 %copy-start.4 = (bf16[1792,448]{0,1:T(8,128)(2,1)S(1)}, bf16[1792,448]{0,1:T(8,128)(2,1)}, u32[]{:S(2)}) copy-start(bf16[1792,448]{0,1:T(8,128)(2,1)} %param.9) | copy-start | bytes 4816900
  61.3 12.5 %collective-permute-start.10 = (bf16[512,128]{1,0:T(8,128)(2,1)S(1)}, bf16[512,128]{1,0:T(8,128)(2,1)S(1)}, u32[]{:S(2)}, u32[]{:S(2)}) collective-permute-start(bf16[512,128]{1,0:T(8,128)(2,1)S(1)} %copy-done.8), channel_id=1, source_target_pairs={{0,16},{16,32},{32,48},{48,0},{1,17},{17,33},{33,49},{49,1},{2,18}... | collective-permute-start | bytes 393224 | tf_op jit(solution)/shard_map/ppermute | solution.py:17
  61.8 14.1 %collective-permute-start.9 = (bf16[512,128]{1,0:T(8,128)(2,1)S(1)}, bf16[512,128]{1,0:T(8,128)(2,1)S(1)}, u32[]{:S(2)}, u32[]{:S(2)}) collective-permute-start(bf16[512,128]{1,0:T(8,128)(2,1)S(1)} %copy-done.8), channel_id=1, source_target_pairs={{0,32},{16,48},{32,0},{48,16},{1,33},{17,49},{33,1},{49,17},{2,34}... | collective-permute-start | bytes 393224 | tf_op jit(solution)/shard_map/ppermute | solution.py:17
  68.1 12.7 %collective-permute-start.8 = (bf16[512,128]{1,0:T(8,128)(2,1)S(1)}, bf16[512,128]{1,0:T(8,128)(2,1)S(1)}, u32[]{:S(2)}, u32[]{:S(2)}) collective-permute-start(bf16[512,128]{1,0:T(8,128)(2,1)S(1)} %copy-done.8), channel_id=1, source_target_pairs={{0,48},{16,0},{32,16},{48,32},{1,49},{17,1},{33,17},{49,33},{2,50}... | collective-permute-start | bytes 393224 | tf_op jit(solution)/shard_map/ppermute | solution.py:17
  80.8 3.9 %copy-start.3 = (bf16[4,512,128]{2,1,0:T(8,128)(2,1)}, bf16[4,512,128]{2,1,0:T(8,128)(2,1)S(1)}, u32[]{:S(2)}) copy-start(bf16[4,512,128]{2,1,0:T(8,128)(2,1)S(1)} %pad_maximum_fusion.3.w0) | copy-start | bytes 1572868
  80.8 2.0 collective-permute-start.11
  82.8 1.9 copy-start.7
  84.7 1.8 copy-start.1
  84.7 8.4 %copy-start.10 = (bf16[1,128,512]{2,1,0:T(8,128)(2,1)S(1)}, bf16[1,128,512]{2,1,0:T(8,128)(2,1)}, u32[]{:S(2)}) copy-start(bf16[1,128,512]{2,1,0:T(8,128)(2,1)} %param.8) | copy-start | bytes 393220
  88.3 9.9 %all-to-all-start.4 = ((bf16[8,8,1152]{2,1,0:T(8,128)(2,1)}), bf16[8,8,1152]{2,1,0:T(8,128)(2,1)S(1)}, u32[]{:S(2)}, u32[]{:S(2)}) async-start(bf16[8,8,1152]{2,1,0:T(8,128)(2,1)} %pad_maximum_fusion.7), calls=%async_computation.4 | async-start | bytes 294912 | tf_op jit(solution)/shard_map/all_to_all | solution.py:35
  93.1 12.6 %collective-permute-start.5 = (bf16[128,512]{1,0:T(8,128)(2,1)S(1)}, bf16[128,512]{1,0:T(8,128)(2,1)S(1)}, u32[]{:S(2)}, u32[]{:S(2)}) collective-permute-start(bf16[128,512]{1,0:T(8,128)(2,1)S(1)} %bitcast.94), channel_id=1, source_target_pairs={{0,192},{64,0},{128,64},{192,128},{1,193},{65,1},{129,65},{193,129... | collective-permute-start | bytes 393224 | tf_op jit(solution)/shard_map/ppermute | solution.py:17
  96.2 10.7 %collective-permute-start.6 = (bf16[128,512]{1,0:T(8,128)(2,1)S(1)}, bf16[128,512]{1,0:T(8,128)(2,1)S(1)}, u32[]{:S(2)}, u32[]{:S(2)}) collective-permute-start(bf16[128,512]{1,0:T(8,128)(2,1)S(1)} %bitcast.95), channel_id=1, source_target_pairs={{0,128},{64,192},{128,0},{192,64},{1,129},{65,193},{129,1},{193,65... | collective-permute-start | bytes 393224 | tf_op jit(solution)/shard_map/ppermute | solution.py:17
  96.7 12.2 %collective-permute-start.7 = (bf16[128,512]{1,0:T(8,128)(2,1)S(1)}, bf16[128,512]{1,0:T(8,128)(2,1)S(1)}, u32[]{:S(2)}, u32[]{:S(2)}) collective-permute-start(bf16[128,512]{1,0:T(8,128)(2,1)S(1)} %bitcast.96), channel_id=1, source_target_pairs={{0,64},{64,128},{128,192},{192,0},{1,65},{65,129},{129,193},{193,1... | collective-permute-start | bytes 393224 | tf_op jit(solution)/shard_map/ppermute | solution.py:17
  98.9 16.4 %all-to-all-start.5 = ((bf16[16,8,256]{2,1,0:T(8,128)(2,1)}), bf16[16,8,256]{2,1,0:T(8,128)(2,1)S(1)}, u32[]{:S(2)}, u32[]{:S(2)}) async-start(bf16[16,8,256]{2,1,0:T(8,128)(2,1)} %broadcast_in_dim.8), calls=%async_computation.5 | async-start | bytes 131072 | tf_op jit(solution)/shard_map/all_to_all | solution.py:35
  105.7 3.3 %copy-start.11 = (bf16[128,512]{1,0:T(8,128)(2,1)}, bf16[128,512]{1,0:T(8,128)(2,1)S(1)}, u32[]{:S(2)}) copy-start(bf16[128,512]{1,0:T(8,128)(2,1)S(1)} %collective-permute-done.5.a1) | copy-start | bytes 393220
  106.9 2.1 copy-start.12
  109.0 0.6 copy-start.13
  115.3 16.5 %all-to-all-start.3 = ((bf16[4,128,1024]{2,1,0:T(8,128)(2,1)}), bf16[4,128,1024]{2,1,0:T(8,128)(2,1)S(1)}, u32[]{:S(2)}, u32[]{:S(2)}) async-start(bf16[4,128,1024]{2,1,0:T(8,128)(2,1)} %bitcast.81), calls=%async_computation.3 | async-start | bytes 2097152 | tf_op jit(solution)/shard_map/all_to_all | solution.py:35
  132.6 30.4 %all-to-all-start.6 = ((bf16[8,8,4992]{2,1,0:T(8,128)(2,1)}), bf16[8,8,4992]{2,1,0:T(8,128)(2,1)S(1)}, u32[]{:S(2)}, u32[]{:S(2)}) async-start(bf16[8,8,4992]{2,1,0:T(8,128)(2,1)} %broadcast_in_dim.9), calls=%async_computation.6 | async-start | bytes 1277952 | tf_op jit(solution)/shard_map/all_to_all | solution.py:35
  137.7 10.9 %collective-permute-start.12 = (bf16[128,1024]{1,0:T(8,128)(2,1)S(1)}, bf16[128,1024]{1,0:T(8,128)(2,1)S(1)}, u32[]{:S(2)}, u32[]{:S(2)}) collective-permute-start(bf16[128,1024]{1,0:T(8,128)(2,1)S(1)} %reduce_sum.78), channel_id=1, source_target_pairs={{4,0},{16,20},{36,32},{48,52},{5,1},{17,21},{37,33},{49,53},{6,2},... | collective-permute-start | bytes 786440 | tf_op jit(solution)/shard_map/ppermute | solution.py:31
  139.0 104.1 %collective-permute-start.19 = (bf16[448,4096]{1,0:T(8,128)(2,1)}, bf16[448,4096]{1,0:T(8,128)(2,1)}, u32[]{:S(2)}, u32[]{:S(2)}) collective-permute-start(bf16[448,4096]{1,0:T(8,128)(2,1)} %eig0.1), channel_id=1, source_target_pairs={{0,8},{8,0},{1,9},{9,1},{2,10},{10,2},{3,11},{11,3},{4,12},{12,4},... | collective-permute-start | bytes 11010056 | tf_op jit(solution)/shard_map/ppermute | solution.py:17
  148.7 47.4 %collective-permute-start.14 = (bf16[128,1024]{1,0:T(8,128)(2,1)S(1)}, bf16[128,1024]{1,0:T(8,128)(2,1)S(1)}, u32[]{:S(2)}, u32[]{:S(2)}) collective-permute-start(bf16[128,1024]{1,0:T(8,128)(2,1)S(1)} %add_convert_fusion.1), channel_id=1, source_target_pairs={{0,32},{20,52},{32,0},{52,20},{1,33},{21,53},{33,1},{53,21},{2,34}... | collective-permute-start | bytes 786440 | tf_op jit(solution)/shard_map/ppermute | solution.py:26
  154.0 42.0 %collective-permute-start.15 = (bf16[128,1024]{1,0:T(8,128)(2,1)S(1)}, bf16[128,1024]{1,0:T(8,128)(2,1)}, u32[]{:S(2)}, u32[]{:S(2)}) collective-permute-start(bf16[128,1024]{1,0:T(8,128)(2,1)S(1)} %add_convert_fusion.1), channel_id=1, source_target_pairs={{0,48},{20,4},{32,16},{52,36},{1,49},{21,5},{33,17},{53,37},{2,50}... | collective-permute-start | bytes 786440 | tf_op jit(solution)/shard_map/ppermute | solution.py:26
  156.0 12.0 %collective-permute-start.13 = (bf16[128,1024]{1,0:T(8,128)(2,1)S(1)}, bf16[128,1024]{1,0:T(8,128)(2,1)S(1)}, u32[]{:S(2)}, u32[]{:S(2)}) collective-permute-start(bf16[128,1024]{1,0:T(8,128)(2,1)S(1)} %add_convert_fusion.1), channel_id=1, source_target_pairs={{0,16},{20,36},{32,48},{52,4},{1,17},{21,37},{33,49},{53,5},{2,18}... | collective-permute-start | bytes 786440 | tf_op jit(solution)/shard_map/ppermute | solution.py:26
  163.1 13.5 %all-to-all-start = ((bf16[4,128,896]{2,1,0:T(8,128)(2,1)}), bf16[4,128,896]{2,1,0:T(8,128)(2,1)S(1)}, u32[]{:S(2)}, u32[]{:S(2)}) async-start(bf16[4,128,896]{2,1,0:T(8,128)(2,1)} %bitcast.6), calls=%async_computation | async-start | bytes 1835008 | tf_op jit(solution)/shard_map/all_to_all | solution.py:35
  176.5 13.7 %all-to-all-start.2 = ((bf16[4,128,896]{2,1,0:T(8,128)(2,1)}), bf16[4,128,896]{2,1,0:T(8,128)(2,1)S(1)}, u32[]{:S(2)}, u32[]{:S(2)}) async-start(bf16[4,128,896]{2,1,0:T(8,128)(2,1)} %bitcast.85), calls=%async_computation.2 | async-start | bytes 1835008 | tf_op jit(solution)/shard_map/all_to_all | solution.py:35
  190.2 5.9 %copy-start.2 = (bf16[4,128,896]{2,1,0:T(8,128)(2,1)}, bf16[4,128,896]{2,1,0:T(8,128)(2,1)S(1)}, u32[]{:S(2)}) copy-start(bf16[4,128,896]{2,1,0:T(8,128)(2,1)S(1)} %all-to-all-done.2) | copy-start | bytes 2752516
  190.2 37.8 %all-to-all-start.1 = ((bf16[8,128,896]{2,1,0:T(8,128)(2,1)}), bf16[8,128,896]{2,1,0:T(8,128)(2,1)}, u32[]{:S(2)}, u32[]{:S(2)}) async-start(bf16[8,128,896]{2,1,0:T(8,128)(2,1)} %bitcast.82), calls=%async_computation.1 | async-start | bytes 3670016 | tf_op jit(solution)/shard_map/all_to_all | solution.py:35
  197.9 15.4 %collective-permute-start.18 = (bf16[2,128,1024]{2,1,0:T(8,128)(2,1)}, bf16[2,128,1024]{2,1,0:T(8,128)(2,1)}, u32[]{:S(2)}, u32[]{:S(2)}) collective-permute-start(bf16[2,128,1024]{2,1,0:T(8,128)(2,1)} %get-tuple-element.14), channel_id=1, source_target_pairs={{0,64},{64,128},{128,192},{192,0},{1,65},{65,129},{129,193},{193,1... | collective-permute-start | bytes 1572872 | tf_op jit(solution)/shard_map/ppermute | solution.py:17
  199.5 19.5 %collective-permute-start.17 = (bf16[2,128,1024]{2,1,0:T(8,128)(2,1)}, bf16[2,128,1024]{2,1,0:T(8,128)(2,1)}, u32[]{:S(2)}, u32[]{:S(2)}) collective-permute-start(bf16[2,128,1024]{2,1,0:T(8,128)(2,1)} %get-tuple-element.14), channel_id=1, source_target_pairs={{0,128},{64,192},{128,0},{192,64},{1,129},{65,193},{129,1},{193,65... | collective-permute-start | bytes 1572872 | tf_op jit(solution)/shard_map/ppermute | solution.py:17
  202.2 16.8 %collective-permute-start.16 = (bf16[2,128,1024]{2,1,0:T(8,128)(2,1)}, bf16[2,128,1024]{2,1,0:T(8,128)(2,1)}, u32[]{:S(2)}, u32[]{:S(2)}) collective-permute-start(bf16[2,128,1024]{2,1,0:T(8,128)(2,1)} %get-tuple-element.14), channel_id=1, source_target_pairs={{0,192},{64,0},{128,64},{192,128},{1,193},{65,1},{129,65},{193,129... | collective-permute-start | bytes 1572872 | tf_op jit(solution)/shard_map/ppermute | solution.py:17
  204.7 19.2 %collective-permute-start.20 = (bf16[64,4992]{1,0:T(8,128)(2,1)}, bf16[64,4992]{1,0:T(8,128)(2,1)}, u32[]{:S(2)}, u32[]{:S(2)}) collective-permute-start(bf16[64,4992]{1,0:T(8,128)(2,1)} %concatenate.33), channel_id=1, source_target_pairs={{0,8},{8,0},{1,9},{9,1},{2,10},{10,2},{3,11},{11,3},{4,12},{12,4},... | collective-permute-start | bytes 1916936 | tf_op jit(solution)/shard_map/ppermute | solution.py:17
  228.0 1.8 copy-start.6
  232.4 8.8 %collective-permute-start.4 = (bf16[2,128,896]{2,1,0:T(8,128)(2,1)}, bf16[2,128,896]{2,1,0:T(8,128)(2,1)}, u32[]{:S(2)}, u32[]{:S(2)}) collective-permute-start(bf16[2,128,896]{2,1,0:T(8,128)(2,1)} %pad_maximum_fusion.5), channel_id=1, source_target_pairs={{0,4},{4,0},{1,5},{5,1},{2,6},{6,2},{3,7},{7,3},{8,12},{12,8},{9,1... | collective-permute-start | bytes 1376264 | tf_op jit(solution)/shard_map/ppermute | solution.py:17
  234.0 7.2 %copy-start.5 = (bf16[1,128,896]{2,1,0:T(8,128)(2,1)S(1)}, bf16[1,128,896]{2,1,0:T(8,128)(2,1)}, u32[]{:S(2)}) copy-start(bf16[1,128,896]{2,1,0:T(8,128)(2,1)} %get-tuple-element.16) | copy-start | bytes 688132
  280.3 9.6 %all-to-all-start.8 = ((f32[16,2,16]{2,1,0:T(2,128)}), f32[16,2,16]{2,1,0:T(2,128)S(1)}, u32[]{:S(2)}, u32[]{:S(2)}) async-start(f32[16,2,16]{2,1,0:T(2,128)} %broadcast_in_dim.11), calls=%async_computation.8 | async-start | bytes 32768 | tf_op jit(solution)/shard_map/all_to_all | solution.py:35
Sparse Core Ops, SparseCore 0:
  9.1 34.1 all-gather.4
  45.1 31.1 all-gather.8
  78.1 52.6 all-gather.6

commit v3 on v2

v3 whole, which is shorter than its diff:
```python
import functools

import jax
import jax.numpy as jnp
from jax import lax
from jax.experimental import pallas as pl
from jax.experimental.pallas import tpu as pltpu
from jax.sharding import Mesh, PartitionSpec as P


AXES = ("y", "zh", "c", "zl", "x")
SIZES = (4, 4, 2, 2, 4)
BF = jnp.bfloat16
F32 = jnp.float32


def shift(value, axis, by):
    n = SIZES[AXES.index(axis)]
    return lax.ppermute(value, axis, [(i, (i + by) % n) for i in range(n)])


def gather(value, axis):
    return [value] + [shift(value, axis, -by) for by in (1, 2, 3)]


def from_owner(value, by):
    pairs = [(2 * h + h % 2, 2 * ((h - by) % 4) + h % 2) for h in range(4)]
    return lax.ppermute(value, ("zh", "zl"), pairs)


def to_owner(value):
    pairs = [(2 * h + 1 - h % 2, 2 * h + h % 2) for h in range(4)]
    return lax.ppermute(value, ("zh", "zl"), pairs)


def exchange(value, axes):
    return lax.all_to_all(value, axes, 0, 0, tiled=True)


def spread(value, axes, n):
    return exchange(jnp.broadcast_to(value[None], (n,) + value.shape), axes)


def dot(a, b):
    return jnp.dot(a, b, preferred_element_type=F32)


def dot_t(a, b):
    return lax.dot_general(a, b, (((1,), (1,)), ((), ())), preferred_element_type=F32)


def rotate_in_kernel(at_ref, a0, a1, a2, a3, q, w0, w1, out, value, act):
    tokens = a0.shape[0]
    n = w0.shape[2]
    for d, a in enumerate((a0, a1, a2, a3)):
        y = lax.rem(at_ref[0] + d, 4)
        act[pl.ds(pl.multiple_of(y * tokens, tokens), tokens), :] = a[...]
    act[4 * tokens :, :] = q[...]
    for k, w in enumerate((w0, w1)):
        core = at_ref[2] if k == 0 else 1 - at_ref[2]
        for d in range(4):
            zh = lax.rem(at_ref[1] + d, 4)
            here = pl.ds(pl.multiple_of((2 * zh + core) * n, n), n)
            product = dot(act[...], w[d]).astype(BF)
            out[:, here] = product[: 4 * tokens]
            value[:, here] = product[4 * tokens :]


def rotate_in(at, acts, query, bases):
    tokens, unit = acts[0].shape
    rows = query.shape[0]
    n = bases[0].shape[2]
    vmem = pl.BlockSpec(memory_space=pltpu.VMEM)
    return pl.pallas_call(
        rotate_in_kernel,
        in_specs=[pl.BlockSpec(memory_space=pltpu.SMEM)] + [vmem] * 7,
        out_specs=(vmem, vmem),
        out_shape=(
            jax.ShapeDtypeStruct((4 * tokens, 8 * n), BF),
            jax.ShapeDtypeStruct((rows, 8 * n), BF),
        ),
        scratch_shapes=[pltpu.VMEM((4 * tokens + rows, unit), BF)],
        cost_estimate=pl.CostEstimate(
            flops=2 * 32 * tokens * unit * n, bytes_accessed=2 * 16 * tokens * (unit + n), transcendentals=0
        ),
        name="rotate_in",
    )(at, *acts, query, *bases)


def split_kernel(flag, a, b, keep, give):
    def total(ref):
        return sum(ref[k, 0].astype(F32) for k in range(4)).astype(BF)

    @pl.when(flag[0] == 1)
    def _():
        keep[...] = total(a)
        give[...] = total(b)

    @pl.when(flag[0] == 0)
    def _():
        keep[...] = total(b)
        give[...] = total(a)


def split(flag, a, b):
    (left, at_left), (right, at_right) = a, b
    tokens, both = left.shape[2:]
    tile = tokens // 4
    block = (4, 1, tile, both)
    out = pl.BlockSpec((tile, both), lambda t, _: (t, 0))
    shape = jax.ShapeDtypeStruct((tokens, both), BF)
    spec = pltpu.PrefetchScalarGridSpec(
        num_scalar_prefetch=1,
        grid=(4,),
        in_specs=[
            pl.BlockSpec(block, lambda t, _: (0, at_left, t, 0)),
            pl.BlockSpec(block, lambda t, _: (0, at_right, t, 0)),
        ],
        out_specs=(out, out),
    )
    return pl.pallas_call(
        split_kernel,
        grid_spec=spec,
        out_shape=(shape, shape),
        cost_estimate=pl.CostEstimate(
            flops=8 * tokens * both, bytes_accessed=20 * tokens * both, transcendentals=0
        ),
        name="split",
    )(flag, left, right)


def score_kernel(slot, at_ref, keep, got, v0, v1, v2, v3, other, eig0, eig1, query, out, flipped, total, act, held):
    step = pl.program_id(0)
    n = eig0.shape[0]
    tokens = keep.shape[0]
    half = other.shape[1]
    width = act.shape[1] // 4

    @pl.when(step == 0)
    def _():
        grad = keep[...].astype(F32) + got[...].astype(F32)
        flipped[...] = grad.T.astype(BF)
        total[...] = jnp.zeros_like(total)

    for d, ref in enumerate((v0, v1, v2, v3)):

        @pl.when(step == d)
        def _(ref=ref):
            act[...] = ref[slot * tokens : (slot + 1) * tokens, :]
            held[:half, :] = ref[2 * tokens :, :]

    held[half:, :] = other[0]

    def body(e, _):
        cols = pl.ds(pl.multiple_of(e * width, width), width)
        for k, eig in enumerate((eig0, eig1)):
            here = slice(k * n, (k + 1) * n)
            contracted = dot(flipped[here, :], act[:, cols])
            scaled = (contracted * (1.0 / eig[:, cols].astype(F32))).astype(BF)
            total[here, :] += dot_t(scaled, held[:, cols])
        return 0

    lax.fori_loop(0, 4, body, 0)

    @pl.when(step == pl.num_programs(0) - 1)
    def _():
        out[0:1, :] = (total[...] * query[...]).sum(0, keepdims=True)


def score(slot, at, keep, got, acts, other, eig0, eig1, query):
    tokens, both = keep.shape
    n = eig0.shape[0]
    cols = acts[0].shape[1]
    half = other.shape[1]
    rows = 2 * half

    def whole(a):
        return pl.BlockSpec(a.shape, lambda j, at: (0,) * a.ndim)

    spec = pltpu.PrefetchScalarGridSpec(
        num_scalar_prefetch=1,
        grid=(4,),
        in_specs=[whole(keep), whole(got)]
        + [whole(a) for a in acts]
        + [
            pl.BlockSpec((1, half, cols), lambda j, at: (j, 0, 0)),
            pl.BlockSpec((n, cols), lambda j, at: (0, lax.rem(at[0] + j, 4))),
            pl.BlockSpec((n, cols), lambda j, at: (0, lax.rem(at[0] + j, 4))),
            whole(query),
        ],
        out_specs=pl.BlockSpec((8, rows), lambda j, at: (0, 0)),
        scratch_shapes=[
            pltpu.VMEM((both, tokens), BF),
            pltpu.VMEM((both, rows), F32),
            pltpu.VMEM((tokens, cols), BF),
            pltpu.VMEM((rows, cols), BF),
        ],
    )
    return pl.pallas_call(
        functools.partial(score_kernel, slot),
        grid_spec=spec,
        out_shape=jax.ShapeDtypeStruct((8, rows), F32),
        cost_estimate=pl.CostEstimate(
            flops=2 * both * 4 * cols * (tokens + rows),
            bytes_accessed=2 * both * 4 * cols,
            transcendentals=0,
        ),
    )(at, keep, got, *acts, other, eig0, eig1, query)[0]


def shards(grad_out, act_in, basis_out, basis_in, eigen_vals, query_out, query_in):
    yi, zi, ci, li = (lax.axis_index(a) for a in ("y", "zh", "c", "zl"))
    tokens, unit = grad_out.shape[1:]
    queries, rank = query_out.shape[:2]
    rows = queries * rank
    half_rows = rows // 2
    width = basis_out.shape[1]
    first = ci == 0

    same = li == zi % 2
    at = jnp.stack([yi, zi, ci]).astype(jnp.int32)

    out_t = basis_out.T
    out_both = jnp.concatenate([out_t, shift(out_t, "c", 1)], 0)
    out_both = lax.optimization_barrier(out_both)
    eigen_other = shift(eigen_vals, "c", 1)

    mine = lax.dynamic_slice_in_dim(query_out.reshape(rows, unit), ci * half_rows, half_rows, 0)
    mine_in = lax.dynamic_slice_in_dim(query_in.reshape(rows, -1), ci * half_rows, half_rows, 0)
    in_own = jnp.stack(gather(basis_in, "zh"))
    in_other = shift(in_own, "c", 1)
    part, value = rotate_in(at, gather(act_in[0], "y"), mine_in, (in_own, in_other))
    part = exchange(part.reshape(4, tokens, -1), "x").astype(F32).sum(0).astype(BF)
    part = (part.astype(F32) + to_owner(part).astype(F32)).astype(BF)
    plus, far, minus = (from_owner(part, by) for by in (1, 2, 3))

    query = jnp.concatenate([dot_t(mine, out_both).astype(BF), value], 1)
    some = half_rows // 8
    query = exchange(query.reshape(8, some, -1), ("zl", "x")).reshape(8, some, -1)
    query = query.astype(F32).sum(0).astype(BF)
    query = spread(query, ("zl", "x"), 8).reshape(half_rows, -1)
    value = query[:, 2 * width :]
    query = query[:, : 2 * width]
    swapped = jnp.concatenate([query[:, width:], query[:, :width]], 1)
    query = jnp.concatenate([query, shift(swapped, "c", 1)], 0)
    query_rot = query.astype(F32).T

    act_rot = jnp.concatenate(
        [jnp.where(same, part, minus), jnp.where(same, far, plus), value], 0
    )
    act_rot = gather(act_rot, "y")
    value_other = shift(jnp.stack([a[2 * tokens :] for a in act_rot]), "c", 1)

    grad = grad_out[0]
    plus, far, minus = (shift(grad, "zh", -by) for by in (1, 2, 3))
    blocks = []
    for some_blocks in ((grad,), (plus, minus), (far,)):
        some_blocks = jnp.stack(some_blocks)
        found = lax.all_gather(some_blocks, "y", axis=0, tiled=True)
        product = dot_t(found.reshape(-1, unit), out_both).astype(BF)
        product = exchange(product.reshape(-1, tokens, 2 * width), "x")
        blocks.append(product.reshape(4, -1, tokens, 2 * width))
    flag = same.astype(jnp.int32)[None]
    result = []
    for slot, (a, b, keeps) in enumerate(
        (((blocks[0], 0), (blocks[1], 1), flag), ((blocks[2], 0), (blocks[1], 0), flag))
    ):
        keep, give = split(keeps, a, b)
        got = shift(give, "zl", 1)
        result.append(
            score(slot, at, keep, got, act_rot, value_other, eigen_vals, eigen_other, query_rot)
        )
    result = jnp.stack(result)
    low = jnp.where(same, zi, (zi + 3) % 4) // 2

    result = result.reshape(2, queries, rank).sum(-1)
    result = jnp.where(low == 0, result, result[::-1])
    turned = jnp.concatenate([result[:, queries // 2 :], result[:, : queries // 2]], 1)
    result = jnp.where(first, result, turned)
    result = spread(result, ("y", "zh"), 16).reshape(16, 2, queries).sum(0)
    result = spread(result, ("c", "zl", "x"), 16).reshape(2, 2, 4, 2, queries)
    result = result.transpose(2, 3, 1, 0, 4).reshape(8, 4, queries)
    return lax.dynamic_index_in_dim(result, li * 4 + lax.axis_index("x"), 0, False)


def solution(mesh):
    fine = Mesh(mesh.devices.reshape(SIZES), AXES)
    dp, factor = ("y", "zh", "c"), ("zl", "x")
    in_specs = (
        P(dp, None, factor),
        P(dp, None, factor),
        P(factor, dp),
        P(factor, dp),
        P(dp, None),
        P(None, None, factor),
        P(None, None, factor),
    )

    return jax.shard_map(
        shards, mesh=fine, in_specs=in_specs, out_specs=P(factor, None), check_vma=False
    )
```

time: 300 us -> 269 us (0.90)
  waiting for transfers between devices: 98.1 us -> 73.1 us
  Pallas kernels: 19.7 us -> 36.5 us
  other arithmetic: 21.8 us -> 8.06 us
  starting transfers between devices: 90.4 us -> 84 us
    ppermute x17 -> x19, waiting for transfers between devices: 66.5 us -> 40.8 us  [shift(): return lax.ppermute(value, axis, [(i, (i + by) % n) for i in range(n)])]
    pallas_call x1 -> x4, Pallas kernels: 15.8 us -> 32.6 us  [the longest x2 25.4 us: score(): pl.pallas_call(functools.partial(score_kernel, slot), grid_spec=spec, out...]
    ppermute x3, waiting for transfers between devices: 0.21 us -> 8.94 us  [from_owner(): return lax.ppermute(value, ('zh', 'zl'), pairs)]
    ppermute x1, waiting for transfers between devices: 9.44 us -> 2.58 us  [to_owner(): return lax.ppermute(value, ('zh', 'zl'), pairs)]
    another operation x6 -> x2, other arithmetic: 8.12 us -> 1.78 us  [the longest x1 1.77 us: shards(): value_other = shift(jnp.stack([a[2 * tokens:] for a in act_rot]), 'c', 1)]
    ppermute x17 -> x19, starting transfers between devices: 38.9 us -> 33.2 us  [shift(): return lax.ppermute(value, axis, [(i, (i + by) % n) for i in range(n)])]
    reduce_sum x4 -> x1, other arithmetic: 4.9 us -> 0.19 us  [shards(): exchange(part.reshape(4, tokens, -1), 'x').astype(F32).sum(0).astype(BF)]
    another operation x0 -> x4, local copies, waits for them, and re-layouts: none -> 3.41 us  [shards(): value_other = shift(jnp.stack([a[2 * tokens:] for a in act_rot]), 'c', 1)]
  transfers between devices with their start and end apart: 32 -> 33, of which waited for: 19 -> 17; matrix products, arithmetic and copies ran while one was open for 17% -> 13% of each run, Pallas kernels for 1% -> 9%
where the time goes in v3:
time: 269 us; the launch traced here: 266 us
  starting transfers between devices  84 us (31%)
  waiting for transfers between devices  73.1 us (27%)
  Pallas kernels  36.5 us (14%)
  matrix products  20.4 us (8%)
  blocking collectives  18.1 us (7%)
  between operations  13.4 us (5%)
  local copies, waits for them, and re-layouts  12.4 us (5%)
  other arithmetic  8.06 us (3%)
    ppermute x19, waiting for transfers between devices, shift(): return lax.ppermute(value, axis, [(i, (i + by) % n) for i in range(n)])  40.8 us
    all_to_all x7, starting transfers between devices, exchange(): return lax.all_to_all(value, axes, 0, 0, tiled=True)  39.5 us
    ppermute x19, starting transfers between devices, shift(): return lax.ppermute(value, axis, [(i, (i + by) % n) for i in range(n)])  33.2 us
    pallas_call x2, Pallas kernels, score(): pl.pallas_call(functools.partial(score_kernel, slot), grid_spec=spec, out...  25.4 us
    dot_general x4, matrix products, dot_t(): lax.dot_general(a, b, (((1,), (1,)), ((), ())), preferred_element_type=F32)  20.4 us
    all_to_all x7, waiting for transfers between devices, exchange(): return lax.all_to_all(value, axes, 0, 0, tiled=True)  20 us
    all_to_all x1, blocking collectives, exchange(): return lax.all_to_all(value, axes, 0, 0, tiled=True)  18.1 us
    ppermute x3, starting transfers between devices, from_owner(): return lax.ppermute(value, ('zh', 'zl'), pairs)  9.9 us
  transfers between devices with their start and end apart: 33, of which 17 were waited for; matrix products, arithmetic and copies ran while one was open for 13% of the time, Pallas kernels for 9%

profile of v3, /device:TPU:2, one launch (start us, length us, event | category | flops | bytes accessed | tf_op | source)
XLA Modules:
  0.0 266.0 jit_solution(16666669216277186407)
XLA Ops:
  7.3 3.3 %collective-permute-start.2 = (bf16[128,1792]{1,0:T(8,128)(2,1)}, bf16[128,1792]{1,0:T(8,128)(2,1)S(1)}, u32[]{:S(2)}, u32[]{:S(2)}) collective-permute-start(bf16[128,1792]{1,0:T(8,128)(2,1)} %bitcast.67), channel_id=1, source_target_pairs={{0,16},{16,32},{32,48},{48,0},{1,17},{17,33},{33,49},{49,1},{2,18}... | collective-permute-start | bytes 1376264 | tf_op jit(solution)/shard_map/ppermute | solution.py:19
  10.7 3.1 %collective-permute-start.1 = (bf16[128,1792]{1,0:T(8,128)(2,1)}, bf16[128,1792]{1,0:T(8,128)(2,1)S(1)}, u32[]{:S(2)}, u32[]{:S(2)}) collective-permute-start(bf16[128,1792]{1,0:T(8,128)(2,1)} %bitcast.68), channel_id=1, source_target_pairs={{0,48},{16,0},{32,16},{48,32},{1,49},{17,1},{33,17},{49,33},{2,50}... | collective-permute-start | bytes 1376264 | tf_op jit(solution)/shard_map/ppermute | solution.py:19
  13.8 14.0 %collective-permute-done.2 = bf16[128,1792]{1,0:T(8,128)(2,1)S(1)} collective-permute-done((bf16[128,1792]{1,0:T(8,128)(2,1)}, bf16[128,1792]{1,0:T(8,128)(2,1)S(1)}, u32[]{:S(2)}, u32[]{:S(2)}) %collective-permute-start.2) | collective-permute-done | bytes 458784 | tf_op jit(solution)/shard_map/ppermute | solution.py:19
  27.8 7.6 %collective-permute-done.1 = bf16[128,1792]{1,0:T(8,128)(2,1)S(1)} collective-permute-done((bf16[128,1792]{1,0:T(8,128)(2,1)}, bf16[128,1792]{1,0:T(8,128)(2,1)S(1)}, u32[]{:S(2)}, u32[]{:S(2)}) %collective-permute-start.1) | collective-permute-done | bytes 458784 | tf_op jit(solution)/shard_map/ppermute | solution.py:19
  36.5 2.8 %collective-permute-start.7 = (bf16[512,128]{1,0:T(8,128)(2,1)S(1)}, bf16[512,128]{1,0:T(8,128)(2,1)S(1)}, u32[]{:S(2)}, u32[]{:S(2)}) collective-permute-start(bf16[512,128]{1,0:T(8,128)(2,1)S(1)} %copy-done.11), channel_id=1, source_target_pairs={{0,48},{16,0},{32,16},{48,32},{1,49},{17,1},{33,17},{49,33},{2,50}... | collective-permute-start | bytes 393224 | tf_op jit(solution)/shard_map/ppermute | solution.py:19
  40.4 3.5 %collective-permute-start.8 = (bf16[512,128]{1,0:T(8,128)(2,1)S(1)}, bf16[512,128]{1,0:T(8,128)(2,1)S(1)}, u32[]{:S(2)}, u32[]{:S(2)}) collective-permute-start(bf16[512,128]{1,0:T(8,128)(2,1)S(1)} %copy-done.11), channel_id=1, source_target_pairs={{0,32},{16,48},{32,0},{48,16},{1,33},{17,49},{33,1},{49,17},{2,34}... | collective-permute-start | bytes 393224 | tf_op jit(solution)/shard_map/ppermute | solution.py:19
  44.8 2.1 collective-permute-done.9
  47.0 2.9 %collective-permute-done.8 = bf16[512,128]{1,0:T(8,128)(2,1)S(1)} collective-permute-done((bf16[512,128]{1,0:T(8,128)(2,1)S(1)}, bf16[512,128]{1,0:T(8,128)(2,1)S(1)}, u32[]{:S(2)}, u32[]{:S(2)}) %collective-permute-start.8) | collective-permute-done | bytes 131104 | tf_op jit(solution)/shard_map/ppermute | solution.py:19
  50.0 1.6 collective-permute-start.6
  51.6 3.0 %collective-permute-start.5 = (bf16[128,512]{1,0:T(8,128)(2,1)S(1)}, bf16[128,512]{1,0:T(8,128)(2,1)}, u32[]{:S(2)}, u32[]{:S(2)}) collective-permute-start(bf16[128,512]{1,0:T(8,128)(2,1)S(1)} %bitcast.81), channel_id=1, source_target_pairs={{0,128},{64,192},{128,0},{192,64},{1,129},{65,193},{129,1},{193,65... | collective-permute-start | bytes 393224 | tf_op jit(solution)/shard_map/ppermute | solution.py:19
  54.6 1.3 collective-permute-start.4
  57.2 4.1 %collective-permute-done.5.a2 = bf16[128,512]{1,0:T(8,128)(2,1)} collective-permute-done((bf16[128,512]{1,0:T(8,128)(2,1)S(1)}, bf16[128,512]{1,0:T(8,128)(2,1)}, u32[]{:S(2)}, u32[]{:S(2)}) %collective-permute-start.5) | collective-permute-done | bytes 131104 | tf_op jit(solution)/shard_map/ppermute | solution.py:19
  62.1 4.0 %rotate_in.1 = (bf16[512,1024]{1,0:T(8,128)(2,1)}, bf16[64,1024]{1,0:T(8,128)(2,1)}) custom-call(s32[3]{0:T(128)} %pad_add_fusion.at_ref, bf16[128,512]{1,0:T(8,128)(2,1)} %bitcast.79, bf16[128,512]{1,0:T(8,128)(2,1)} %collective-permute-done.4.a1, bf16[128,512]{1,0:T(8,128)(2,1)} %collective-permute-done.5.a2, bf16[128,512]{1,0:T(8,128)(2,1)} %copy-done.15, ...), custom_call_target="tpu_custom_call" | custom-call | flops 536870912 | bytes 2621440 | tf_op jit(solution)/shard_map/rotate_in/pallas_call | solution.py:74
  66.1 4.8 %all-to-all-start.2 = ((bf16[4,128,1024]{2,1,0:T(8,128)(2,1)}), bf16[4,128,1024]{2,1,0:T(8,128)(2,1)S(1)}, u32[]{:S(2)}, u32[]{:S(2)}) async-start(bf16[4,128,1024]{2,1,0:T(8,128)(2,1)} %bitcast.63), calls=%async_computation.2 | async-start | bytes 2097152 | tf_op jit(solution)/shard_map/all_to_all | solution.py:37
  70.9 5.5 %collective-permute-start.21 = (bf16[128,1792]{1,0:T(8,128)(2,1)}, bf16[128,1792]{1,0:T(8,128)(2,1)}, u32[]{:S(2)}, u32[]{:S(2)}) collective-permute-start(bf16[128,1792]{1,0:T(8,128)(2,1)} %bitcast.69), channel_id=1, source_target_pairs={{0,32},{16,48},{32,0},{48,16},{1,33},{17,49},{33,1},{49,17},{2,34}... | collective-permute-start | bytes 1376264 | tf_op jit(solution)/shard_map/ppermute | solution.py:19
  76.4 7.9 %all-to-all-done.2 = bf16[4,128,1024]{2,1,0:T(8,128)(2,1)S(1)} async-done(((bf16[4,128,1024]{2,1,0:T(8,128)(2,1)}), bf16[4,128,1024]{2,1,0:T(8,128)(2,1)S(1)}, u32[]{:S(2)}, u32[]{:S(2)}) %all-to-all-start.2) | async-done | bytes 1048608 | tf_op jit(solution)/shard_map/all_to_all | solution.py:37
  84.5 1.3 collective-permute-start.11
  85.8 1.6 pad_maximum_fusion
  87.4 1.8 copy-done.2
  91.0 9.2 %all-to-all-start.3 = ((bf16[8,8,1920]{2,1,0:T(8,128)(2,1)}), bf16[8,8,1920]{2,1,0:T(8,128)(2,1)S(1)}, u32[]{:S(2)}, u32[]{:S(2)}) async-start(bf16[8,8,1920]{2,1,0:T(8,128)(2,1)} %maximum_bitcast_fusion), calls=%async_computation.3 | async-start | bytes 491520 | tf_op jit(solution)/shard_map/all_to_all | solution.py:37
  100.3 2.6 collective-permute-done.11
  102.9 3.1 %collective-permute-start.12 = (bf16[128,1024]{1,0:T(8,128)(2,1)S(1)}, bf16[128,1024]{1,0:T(8,128)(2,1)S(1)}, u32[]{:S(2)}, u32[]{:S(2)}) collective-permute-start(bf16[128,1024]{1,0:T(8,128)(2,1)S(1)} %add_convert_fusion), channel_id=1, source_target_pairs={{0,16},{20,36},{32,48},{52,4},{1,17},{21,37},{33,49},{53,5},{2,18}... | collective-permute-start | bytes 786440 | tf_op jit(solution)/shard_map/ppermute | solution.py:28
  106.0 2.0 collective-permute-start.14
  108.0 4.8 %collective-permute-start.13 = (bf16[128,1024]{1,0:T(8,128)(2,1)S(1)}, bf16[128,1024]{1,0:T(8,128)(2,1)S(1)}, u32[]{:S(2)}, u32[]{:S(2)}) collective-permute-start(bf16[128,1024]{1,0:T(8,128)(2,1)S(1)} %add_convert_fusion), channel_id=1, source_target_pairs={{0,32},{20,52},{32,0},{52,20},{1,33},{21,53},{33,1},{53,21},{2,34}... | collective-permute-start | bytes 786440 | tf_op jit(solution)/shard_map/ppermute | solution.py:28
  113.7 4.8 %all-to-all-start.4 = ((bf16[8,8,1920]{2,1,0:T(8,128)(2,1)}), bf16[8,8,1920]{2,1,0:T(8,128)(2,1)S(1)}, u32[]{:S(2)}, u32[]{:S(2)}) async-start(bf16[8,8,1920]{2,1,0:T(8,128)(2,1)} %broadcast_in_dim.12), calls=%async_computation.4 | async-start | bytes 491520 | tf_op jit(solution)/shard_map/all_to_all | solution.py:37
  118.6 8.9 %collective-permute-done.13 = bf16[128,1024]{1,0:T(8,128)(2,1)S(1)} collective-permute-done((bf16[128,1024]{1,0:T(8,128)(2,1)S(1)}, bf16[128,1024]{1,0:T(8,128)(2,1)S(1)}, u32[]{:S(2)}, u32[]{:S(2)}) %collective-permute-start.13) | collective-permute-done | bytes 262176 | tf_op jit(solution)/shard_map/ppermute | solution.py:28
  127.6 2.5 all-to-all-done.4
  130.9 4.1 %collective-permute-start.16 = (bf16[320,1024]{1,0:T(8,128)(2,1)S(1)}, bf16[320,1024]{1,0:T(8,128)(2,1)}, u32[]{:S(2)}, u32[]{:S(2)}) collective-permute-start(bf16[320,1024]{1,0:T(8,128)(2,1)S(1)} %pad_maximum_fusion.2.v0), channel_id=1, source_target_pairs={{0,128},{64,192},{128,0},{192,64},{1,129},{65,193},{129,1},{193,65... | collective-permute-start | bytes 1966088 | tf_op jit(solution)/shard_map/ppermute | solution.py:19
  135.0 5.5 %convolution_convert_fusion.2 = bf16[896,512]{0,1:T(8,128)(2,1)} fusion(bf16[896,1792]{1,0:T(8,128)(2,1)} %copy-done.2, bf16[512,1792]{1,0:T(8,128)(2,1)} %bitcast.78), kind=kOutput, calls=%fused_computation.3 | convolution fusion | flops 1644625920 | bytes 5963776 | tf_op jit(solution)/shard_map/dot_general | solution.py:49
  140.5 5.2 %all-to-all-start = ((bf16[4,128,896]{2,1,0:T(8,128)(2,1)}), bf16[4,128,896]{2,1,0:T(8,128)(2,1)S(1)}, u32[]{:S(2)}, u32[]{:S(2)}) async-start(bf16[4,128,896]{2,1,0:T(8,128)(2,1)} %bitcast.7), calls=%async_computation | async-start | bytes 1835008 | tf_op jit(solution)/shard_map/all_to_all | solution.py:37
  145.6 8.3 %convolution_convert_fusion = bf16[1024,896]{1,0:T(8,128)(2,1)} fusion(bf16[1024,1792]{1,0:T(8,128)(2,1)} %bitcast.77, bf16[896,1792]{1,0:T(8,128)(2,1)} %copy-done.2), kind=kOutput, calls=%fused_computation.1 | convolution fusion | flops 3289251840 | bytes 8716288 | tf_op jit(solution)/shard_map/dot_general | solution.py:49
  154.0 1.7 all-to-all-done
  156.7 5.0 %all-to-all-start.1 = ((bf16[8,128,896]{2,1,0:T(8,128)(2,1)}), bf16[8,128,896]{2,1,0:T(8,128)(2,1)S(1)}, u32[]{:S(2)}, u32[]{:S(2)}) async-start(bf16[8,128,896]{2,1,0:T(8,128)(2,1)} %bitcast.57), calls=%async_computation.1 | async-start | bytes 3670016 | tf_op jit(solution)/shard_map/all_to_all | solution.py:37
  163.5 8.3 %collective-permute-done.16.v2 = bf16[320,1024]{1,0:T(8,128)(2,1)} collective-permute-done((bf16[320,1024]{1,0:T(8,128)(2,1)S(1)}, bf16[320,1024]{1,0:T(8,128)(2,1)}, u32[]{:S(2)}, u32[]{:S(2)}) %collective-permute-start.16) | collective-permute-done | bytes 655392 | tf_op jit(solution)/shard_map/ppermute | solution.py:19
  171.7 1.6 slice_bitcast_fusion.1
  173.3 5.5 %convolution_convert_fusion.1 = bf16[896,512]{0,1:T(8,128)(2,1)} fusion(bf16[896,1792]{1,0:T(8,128)(2,1)} %copy-done.2, bf16[512,1792]{1,0:T(8,128)(2,1)} %all-gather.9.cloned.1.call-done), kind=kOutput, calls=%fused_computation.2 | convolution fusion | flops 1644625920 | bytes 5963776 | tf_op jit(solution)/shard_map/dot_general | solution.py:49
  178.8 1.7 all-to-all-done.1
  180.5 5.7 %all-to-all-start.5 = ((bf16[4,128,896]{2,1,0:T(8,128)(2,1)}), bf16[4,128,896]{2,1,0:T(8,128)(2,1)}, u32[]{:S(2)}, u32[]{:S(2)}) async-start(bf16[4,128,896]{2,1,0:T(8,128)(2,1)} %bitcast.64), calls=%async_computation.5 | async-start | bytes 1835008 | tf_op jit(solution)/shard_map/all_to_all | solution.py:37
  187.1 1.8 pad_maximum_fusion.4
  190.5 3.6 %split.2 = (bf16[128,896]{1,0:T(8,128)(2,1)}, bf16[128,896]{1,0:T(8,128)(2,1)}) custom-call(s32[1]{0:T(128)} %bitcast.3.flag, bf16[4,1,128,896]{3,2,1,0:T(8,128)(2,1)} %bitcast.56, bf16[4,2,128,896]{3,2,1,0:T(8,128)(2,1)} %bitcast.54), custom_call_target="tpu_custom_call" | custom-call | flops 917504 | bytes 2293760 | tf_op jit(solution)/shard_map/split/pallas_call | solution.py:121
  194.2 1.5 all-to-all-done.5
  195.7 3.6 %split.3 = (bf16[128,896]{1,0:T(8,128)(2,1)}, bf16[128,896]{1,0:T(8,128)(2,1)}) custom-call(s32[1]{0:T(128)} %bitcast.3.flag, bf16[4,1,128,896]{3,2,1,0:T(8,128)(2,1)} %bitcast.32.a, bf16[4,2,128,896]{3,2,1,0:T(8,128)(2,1)} %bitcast.55), custom_call_target="tpu_custom_call" | custom-call | flops 917504 | bytes 2293760 | tf_op jit(solution)/shard_map/split/pallas_call | solution.py:121
  199.3 1.7 collective-permute-start.22
  203.4 12.6 %shard_map.73 = f32[8,128]{1,0:T(8,128)} custom-call(s32[3]{0:T(128)} %pad_add_fusion.at_ref, bf16[128,896]{1,0:T(8,128)(2,1)} %get-tuple-element.11.keep, bf16[128,896]{1,0:T(8,128)(2,1)} %copy-done.8, bf16[320,1024]{1,0:T(8,128)(2,1)} %copy-done.3, bf16[320,1024]{1,0:T(8,128)(2,1)} %collective-permute-done.15.v1, ...), custom_call_target="tpu_custom_call" | custom-call | flops 1879048192 | bytes 7340032 | tf_op jit(solution)/shard_map/pallas_call | solution.py:199
  216.8 12.8 %shard_map.74 = f32[8,128]{1,0:T(8,128)} custom-call(s32[3]{0:T(128)} %pad_add_fusion.at_ref, bf16[128,896]{1,0:T(8,128)(2,1)} %get-tuple-element.15.keep, bf16[128,896]{1,0:T(8,128)(2,1)} %copy-done.9, bf16[320,1024]{1,0:T(8,128)(2,1)} %copy-done.3, bf16[320,1024]{1,0:T(8,128)(2,1)} %collective-permute-done.15.v1, ...), custom_call_target="tpu_custom_call" | custom-call | flops 1879048192 | bytes 7340032 | tf_op jit(solution)/shard_map/pallas_call | solution.py:199
  230.6 18.1 %all_to_all.40 = f32[16,2,16]{2,1,0:T(2,128)S(1)} all-to-all(f32[16,2,16]{2,1,0:T(2,128)S(1)} %broadcast_in_dim.26), channel_id=1, replica_groups=mesh['y'=4,'zh'=4,'c'=2,'zl'=2,'x'=4] {'y','zh'}, dimensions={0} | all-to-all | bytes 4096 | tf_op jit(solution)/shard_map/all_to_all | solution.py:37
  249.3 4.8 %all-to-all-start.7 = ((f32[16,2,16]{2,1,0:T(2,128)}), f32[16,2,16]{2,1,0:T(2,128)S(1)}, u32[]{:S(2)}, u32[]{:S(2)}) async-start(f32[16,2,16]{2,1,0:T(2,128)} %broadcast_in_dim.27), calls=%async_computation.7 | async-start | bytes 32768 | tf_op jit(solution)/shard_map/all_to_all | solution.py:37
  254.2 4.7 %all-to-all-done.7 = f32[16,2,16]{2,1,0:T(2,128)S(1)} async-done(((f32[16,2,16]{2,1,0:T(2,128)}), f32[16,2,16]{2,1,0:T(2,128)S(1)}, u32[]{:S(2)}, u32[]{:S(2)}) %all-to-all-start.7) | async-done | bytes 2080 | tf_op jit(solution)/shard_map/all_to_all | solution.py:37
  (104 shorter events, 20.8 us)
Async XLA Ops:
  6.5 80.9 %copy-start = (bf16[16,8,1792]{2,1,0:T(8,128)(2,1)S(1)}, bf16[16,8,1792]{2,1,0:T(8,128)(2,1)}, u32[]{:S(2)}) copy-start(bf16[16,8,1792]{2,1,0:T(8,128)(2,1)} %param.12) | copy-start | bytes 1376260
  6.5 30.0 %copy-start.11 = (bf16[512,128]{1,0:T(8,128)(2,1)S(1)}, bf16[512,128]{1,0:T(8,128)(2,1)}, u32[]{:S(2)}) copy-start(bf16[512,128]{1,0:T(8,128)(2,1)} %param.10) | copy-start | bytes 393220
  6.5 37.4 %copy-start.6 = (bf16[1792,448]{0,1:T(8,128)(2,1)S(1)}, bf16[1792,448]{0,1:T(8,128)(2,1)}, u32[]{:S(2)}) copy-start(bf16[1792,448]{0,1:T(8,128)(2,1)} %param.9) | copy-start | bytes 4816900
  6.5 43.5 %copy-start.14 = (bf16[1,128,512]{2,1,0:T(8,128)(2,1)S(1)}, bf16[1,128,512]{2,1,0:T(8,128)(2,1)}, u32[]{:S(2)}) copy-start(bf16[1,128,512]{2,1,0:T(8,128)(2,1)} %param.8) | copy-start | bytes 393220
  6.5 49.9 %copy-start.12 = (bf16[16,8,512]{2,1,0:T(8,128)(2,1)S(1)}, bf16[16,8,512]{2,1,0:T(8,128)(2,1)}, u32[]{:S(2)}) copy-start(bf16[16,8,512]{2,1,0:T(8,128)(2,1)} %param.13) | copy-start | bytes 393220
  6.5 128.4 %all-gather.5.cloned.1.call-start = ((), (), s32[]{:S(2)}) async-start(), calls=%async_computation.8 | async-start | bytes 2293760 | tf_op jit(solution)/shard_map/all_gather | solution.py:259
  7.3 138.4 %all-gather.7.cloned.1.call-start = ((), (), s32[]{:S(2)}) async-start(), calls=%async_computation.9 | async-start | bytes 4587520 | tf_op jit(solution)/shard_map/all_gather | solution.py:259
  7.3 20.5 %collective-permute-start.2 = (bf16[128,1792]{1,0:T(8,128)(2,1)}, bf16[128,1792]{1,0:T(8,128)(2,1)S(1)}, u32[]{:S(2)}, u32[]{:S(2)}) collective-permute-start(bf16[128,1792]{1,0:T(8,128)(2,1)} %bitcast.67), channel_id=1, source_target_pairs={{0,16},{16,32},{32,48},{48,0},{1,17},{17,33},{33,49},{49,1},{2,18}... | collective-permute-start | bytes 1376264 | tf_op jit(solution)/shard_map/ppermute | solution.py:19
  10.7 24.8 %collective-permute-start.1 = (bf16[128,1792]{1,0:T(8,128)(2,1)}, bf16[128,1792]{1,0:T(8,128)(2,1)S(1)}, u32[]{:S(2)}, u32[]{:S(2)}) collective-permute-start(bf16[128,1792]{1,0:T(8,128)(2,1)} %bitcast.68), channel_id=1, source_target_pairs={{0,48},{16,0},{32,16},{48,32},{1,49},{17,1},{33,17},{49,33},{2,50}... | collective-permute-start | bytes 1376264 | tf_op jit(solution)/shard_map/ppermute | solution.py:19
  36.5 8.3 %collective-permute-start.7 = (bf16[512,128]{1,0:T(8,128)(2,1)S(1)}, bf16[512,128]{1,0:T(8,128)(2,1)S(1)}, u32[]{:S(2)}, u32[]{:S(2)}) collective-permute-start(bf16[512,128]{1,0:T(8,128)(2,1)S(1)} %copy-done.11), channel_id=1, source_target_pairs={{0,48},{16,0},{32,16},{48,32},{1,49},{17,1},{33,17},{49,33},{2,50}... | collective-permute-start | bytes 393224 | tf_op jit(solution)/shard_map/ppermute | solution.py:19
  39.4 7.6 %collective-permute-start.9 = (bf16[512,128]{1,0:T(8,128)(2,1)S(1)}, bf16[512,128]{1,0:T(8,128)(2,1)S(1)}, u32[]{:S(2)}, u32[]{:S(2)}) collective-permute-start(bf16[512,128]{1,0:T(8,128)(2,1)S(1)} %copy-done.11), channel_id=1, source_target_pairs={{0,16},{16,32},{32,48},{48,0},{1,17},{17,33},{33,49},{49,1},{2,18}... | collective-permute-start | bytes 393224 | tf_op jit(solution)/shard_map/ppermute | solution.py:19
  40.4 9.4 %collective-permute-start.8 = (bf16[512,128]{1,0:T(8,128)(2,1)S(1)}, bf16[512,128]{1,0:T(8,128)(2,1)S(1)}, u32[]{:S(2)}, u32[]{:S(2)}) collective-permute-start(bf16[512,128]{1,0:T(8,128)(2,1)S(1)} %copy-done.11), channel_id=1, source_target_pairs={{0,32},{16,48},{32,0},{48,16},{1,33},{17,49},{33,1},{49,17},{2,34}... | collective-permute-start | bytes 393224 | tf_op jit(solution)/shard_map/ppermute | solution.py:19
  43.9 41.8 %collective-permute-start = (bf16[448,1792]{1,0:T(8,128)(2,1)S(1)}, bf16[448,1792]{1,0:T(8,128)(2,1)}, u32[]{:S(2)}, u32[]{:S(2)}) collective-permute-start(bf16[448,1792]{1,0:T(8,128)(2,1)S(1)} %bitcast.58), channel_id=1, source_target_pairs={{0,8},{8,0},{1,9},{9,1},{2,10},{10,2},{3,11},{11,3},{4,12},{12,4},... | collective-permute-start | bytes 4816904 | tf_op jit(solution)/shard_map/ppermute | solution.py:19
  49.9 11.4 %copy-start.7 = (bf16[4,512,128]{2,1,0:T(8,128)(2,1)}, bf16[4,512,128]{2,1,0:T(8,128)(2,1)S(1)}, u32[]{:S(2)}) copy-start(bf16[4,512,128]{2,1,0:T(8,128)(2,1)S(1)} %pad_maximum_fusion.3.w0) | copy-start | bytes 1572868
  49.9 11.4 %collective-permute-start.10 = (bf16[4,512,128]{2,1,0:T(8,128)(2,1)S(1)}, bf16[4,512,128]{2,1,0:T(8,128)(2,1)S(1)}, u32[]{:S(2)}, u32[]{:S(2)}) collective-permute-start(bf16[4,512,128]{2,1,0:T(8,128)(2,1)S(1)} %pad_maximum_fusion.3.w0), channel_id=1, source_target_pairs={{0,8},{8,0},{1,9},{9,1},{2,10},{10,2},{3,11},{11,3},{4,12},{12,4},... | collective-permute-start | bytes 1572872 | tf_op jit(solution)/shard_map/ppermute | solution.py:19
  50.0 7.1 %collective-permute-start.6 = (bf16[128,512]{1,0:T(8,128)(2,1)S(1)}, bf16[128,512]{1,0:T(8,128)(2,1)S(1)}, u32[]{:S(2)}, u32[]{:S(2)}) collective-permute-start(bf16[128,512]{1,0:T(8,128)(2,1)S(1)} %bitcast.80), channel_id=1, source_target_pairs={{0,64},{64,128},{128,192},{192,0},{1,65},{65,129},{129,193},{193,1... | collective-permute-start | bytes 393224 | tf_op jit(solution)/shard_map/ppermute | solution.py:19
  51.6 9.7 %collective-permute-start.5 = (bf16[128,512]{1,0:T(8,128)(2,1)S(1)}, bf16[128,512]{1,0:T(8,128)(2,1)}, u32[]{:S(2)}, u32[]{:S(2)}) collective-permute-start(bf16[128,512]{1,0:T(8,128)(2,1)S(1)} %bitcast.81), channel_id=1, source_target_pairs={{0,128},{64,192},{128,0},{192,64},{1,129},{65,193},{129,1},{193,65... | collective-permute-start | bytes 393224 | tf_op jit(solution)/shard_map/ppermute | solution.py:19
  54.6 6.7 %collective-permute-start.4 = (bf16[128,512]{1,0:T(8,128)(2,1)S(1)}, bf16[128,512]{1,0:T(8,128)(2,1)}, u32[]{:S(2)}, u32[]{:S(2)}) collective-permute-start(bf16[128,512]{1,0:T(8,128)(2,1)S(1)} %bitcast.82), channel_id=1, source_target_pairs={{0,192},{64,0},{128,64},{192,128},{1,193},{65,1},{129,65},{193,129... | collective-permute-start | bytes 393224 | tf_op jit(solution)/shard_map/ppermute | solution.py:19
  57.2 4.1 %copy-start.15 = (bf16[128,512]{1,0:T(8,128)(2,1)}, bf16[128,512]{1,0:T(8,128)(2,1)S(1)}, u32[]{:S(2)}) copy-start(bf16[128,512]{1,0:T(8,128)(2,1)S(1)} %collective-permute-done.6.a3) | copy-start | bytes 393220
  61.3 0.8 copy-start.13
  66.1 18.2 %all-to-all-start.2 = ((bf16[4,128,1024]{2,1,0:T(8,128)(2,1)}), bf16[4,128,1024]{2,1,0:T(8,128)(2,1)S(1)}, u32[]{:S(2)}, u32[]{:S(2)}) async-start(bf16[4,128,1024]{2,1,0:T(8,128)(2,1)} %bitcast.63), calls=%async_computation.2 | async-start | bytes 2097152 | tf_op jit(solution)/shard_map/all_to_all | solution.py:37
  70.9 42.1 %collective-permute-start.21 = (bf16[128,1792]{1,0:T(8,128)(2,1)}, bf16[128,1792]{1,0:T(8,128)(2,1)}, u32[]{:S(2)}, u32[]{:S(2)}) collective-permute-start(bf16[128,1792]{1,0:T(8,128)(2,1)} %bitcast.69), channel_id=1, source_target_pairs={{0,32},{16,48},{32,0},{48,16},{1,33},{17,49},{33,1},{49,17},{2,34}... | collective-permute-start | bytes 1376264 | tf_op jit(solution)/shard_map/ppermute | solution.py:19
  84.5 18.4 %collective-permute-start.11 = (bf16[128,1024]{1,0:T(8,128)(2,1)S(1)}, bf16[128,1024]{1,0:T(8,128)(2,1)S(1)}, u32[]{:S(2)}, u32[]{:S(2)}) collective-permute-start(bf16[128,1024]{1,0:T(8,128)(2,1)S(1)} %reduce_sum.42), channel_id=1, source_target_pairs={{4,0},{16,20},{36,32},{48,52},{5,1},{17,21},{37,33},{49,53},{6,2},... | collective-permute-start | bytes 786440 | tf_op jit(solution)/shard_map/ppermute | solution.py:33
  87.4 1.8 copy-start.2
  87.4 2.9 %copy-start.10 = (bf16[64,1024]{1,0:T(8,128)(2,1)S(1)}, bf16[64,1024]{1,0:T(8,128)(2,1)}, u32[]{:S(2)}) copy-start(bf16[64,1024]{1,0:T(8,128)(2,1)} %get-tuple-element.14) | copy-start | bytes 393220
  91.0 22.0 %all-to-all-start.3 = ((bf16[8,8,1920]{2,1,0:T(8,128)(2,1)}), bf16[8,8,1920]{2,1,0:T(8,128)(2,1)S(1)}, u32[]{:S(2)}, u32[]{:S(2)}) async-start(bf16[8,8,1920]{2,1,0:T(8,128)(2,1)} %maximum_bitcast_fusion), calls=%async_computation.3 | async-start | bytes 491520 | tf_op jit(solution)/shard_map/all_to_all | solution.py:37
  100.3 73.0 %all-gather.9.cloned.1.call-start = ((), (), s32[]{:S(2)}) async-start(), calls=%async_computation.10 | async-start | bytes 2293760 | tf_op jit(solution)/shard_map/all_gather | solution.py:259
  102.9 15.6 %collective-permute-start.12 = (bf16[128,1024]{1,0:T(8,128)(2,1)S(1)}, bf16[128,1024]{1,0:T(8,128)(2,1)S(1)}, u32[]{:S(2)}, u32[]{:S(2)}) collective-permute-start(bf16[128,1024]{1,0:T(8,128)(2,1)S(1)} %add_convert_fusion), channel_id=1, source_target_pairs={{0,16},{20,36},{32,48},{52,4},{1,17},{21,37},{33,49},{53,5},{2,18}... | collective-permute-start | bytes 786440 | tf_op jit(solution)/shard_map/ppermute | solution.py:28
  106.0 12.6 %collective-permute-start.14 = (bf16[128,1024]{1,0:T(8,128)(2,1)S(1)}, bf16[128,1024]{1,0:T(8,128)(2,1)S(1)}, u32[]{:S(2)}, u32[]{:S(2)}) collective-permute-start(bf16[128,1024]{1,0:T(8,128)(2,1)S(1)} %add_convert_fusion), channel_id=1, source_target_pairs={{0,48},{20,4},{32,16},{52,36},{1,49},{21,5},{33,17},{53,37},{2,50}... | collective-permute-start | bytes 786440 | tf_op jit(solution)/shard_map/ppermute | solution.py:28
  108.0 19.5 %collective-permute-start.13 = (bf16[128,1024]{1,0:T(8,128)(2,1)S(1)}, bf16[128,1024]{1,0:T(8,128)(2,1)S(1)}, u32[]{:S(2)}, u32[]{:S(2)}) collective-permute-start(bf16[128,1024]{1,0:T(8,128)(2,1)S(1)} %add_convert_fusion), channel_id=1, source_target_pairs={{0,32},{20,52},{32,0},{52,20},{1,33},{21,53},{33,1},{53,21},{2,34}... | collective-permute-start | bytes 786440 | tf_op jit(solution)/shard_map/ppermute | solution.py:28
  112.8 89.1 %collective-permute-start.19 = (bf16[448,4096]{1,0:T(8,128)(2,1)}, bf16[448,4096]{1,0:T(8,128)(2,1)}, u32[]{:S(2)}, u32[]{:S(2)}) collective-permute-start(bf16[448,4096]{1,0:T(8,128)(2,1)} %eig0.3), channel_id=1, source_target_pairs={{0,8},{8,0},{1,9},{9,1},{2,10},{10,2},{3,11},{11,3},{4,12},{12,4},... | collective-permute-start | bytes 11010056 | tf_op jit(solution)/shard_map/ppermute | solution.py:19
  113.7 16.3 %all-to-all-start.4 = ((bf16[8,8,1920]{2,1,0:T(8,128)(2,1)}), bf16[8,8,1920]{2,1,0:T(8,128)(2,1)S(1)}, u32[]{:S(2)}, u32[]{:S(2)}) async-start(bf16[8,8,1920]{2,1,0:T(8,128)(2,1)} %broadcast_in_dim.12), calls=%async_computation.4 | async-start | bytes 491520 | tf_op jit(solution)/shard_map/all_to_all | solution.py:37
  130.2 31.5 %copy-start.3 = (bf16[320,1024]{1,0:T(8,128)(2,1)}, bf16[320,1024]{1,0:T(8,128)(2,1)S(1)}, u32[]{:S(2)}) copy-start(bf16[320,1024]{1,0:T(8,128)(2,1)S(1)} %pad_maximum_fusion.2.v0) | copy-start | bytes 1966084
  130.2 32.4 %collective-permute-start.17 = (bf16[320,1024]{1,0:T(8,128)(2,1)S(1)}, bf16[320,1024]{1,0:T(8,128)(2,1)}, u32[]{:S(2)}, u32[]{:S(2)}) collective-permute-start(bf16[320,1024]{1,0:T(8,128)(2,1)S(1)} %pad_maximum_fusion.2.v0), channel_id=1, source_target_pairs={{0,64},{64,128},{128,192},{192,0},{1,65},{65,129},{129,193},{193,1... | collective-permute-start | bytes 1966088 | tf_op jit(solution)/shard_map/ppermute | solution.py:19
  130.9 40.8 %collective-permute-start.16 = (bf16[320,1024]{1,0:T(8,128)(2,1)S(1)}, bf16[320,1024]{1,0:T(8,128)(2,1)}, u32[]{:S(2)}, u32[]{:S(2)}) collective-permute-start(bf16[320,1024]{1,0:T(8,128)(2,1)S(1)} %pad_maximum_fusion.2.v0), channel_id=1, source_target_pairs={{0,128},{64,192},{128,0},{192,64},{1,129},{65,193},{129,1},{193,65... | collective-permute-start | bytes 1966088 | tf_op jit(solution)/shard_map/ppermute | solution.py:19
  140.5 15.2 %all-to-all-start = ((bf16[4,128,896]{2,1,0:T(8,128)(2,1)}), bf16[4,128,896]{2,1,0:T(8,128)(2,1)S(1)}, u32[]{:S(2)}, u32[]{:S(2)}) async-start(bf16[4,128,896]{2,1,0:T(8,128)(2,1)} %bitcast.7), calls=%async_computation | async-start | bytes 1835008 | tf_op jit(solution)/shard_map/all_to_all | solution.py:37
  155.7 1.0 copy-start.4
  156.7 23.8 %all-to-all-start.1 = ((bf16[8,128,896]{2,1,0:T(8,128)(2,1)}), bf16[8,128,896]{2,1,0:T(8,128)(2,1)S(1)}, u32[]{:S(2)}, u32[]{:S(2)}) async-start(bf16[8,128,896]{2,1,0:T(8,128)(2,1)} %bitcast.57), calls=%async_computation.1 | async-start | bytes 3670016 | tf_op jit(solution)/shard_map/all_to_all | solution.py:37
  161.7 24.5 %collective-permute-start.15 = (bf16[320,1024]{1,0:T(8,128)(2,1)S(1)}, bf16[320,1024]{1,0:T(8,128)(2,1)}, u32[]{:S(2)}, u32[]{:S(2)}) collective-permute-start(bf16[320,1024]{1,0:T(8,128)(2,1)S(1)} %pad_maximum_fusion.2.v0), channel_id=1, source_target_pairs={{0,192},{64,0},{128,64},{192,128},{1,193},{65,1},{129,65},{193,129... | collective-permute-start | bytes 1966088 | tf_op jit(solution)/shard_map/ppermute | solution.py:19
  180.5 10.0 %copy-start.1 = (bf16[8,128,896]{2,1,0:T(8,128)(2,1)}, bf16[8,128,896]{2,1,0:T(8,128)(2,1)S(1)}, u32[]{:S(2)}) copy-start(bf16[8,128,896]{2,1,0:T(8,128)(2,1)S(1)} %all-to-all-done.1) | copy-start | bytes 5505028
  180.5 15.3 %all-to-all-start.5 = ((bf16[4,128,896]{2,1,0:T(8,128)(2,1)}), bf16[4,128,896]{2,1,0:T(8,128)(2,1)}, u32[]{:S(2)}, u32[]{:S(2)}) async-start(bf16[4,128,896]{2,1,0:T(8,128)(2,1)} %bitcast.64), calls=%async_computation.5 | async-start | bytes 1835008 | tf_op jit(solution)/shard_map/all_to_all | solution.py:37
  188.8 13.1 %collective-permute-start.18 = (bf16[4,64,1024]{2,1,0:T(8,128)(2,1)}, bf16[4,64,1024]{2,1,0:T(8,128)(2,1)S(1)}, u32[]{:S(2)}, u32[]{:S(2)}) collective-permute-start(bf16[4,64,1024]{2,1,0:T(8,128)(2,1)} %pad_maximum_fusion.4), channel_id=1, source_target_pairs={{0,8},{8,0},{1,9},{9,1},{2,10},{10,2},{3,11},{11,3},{4,12},{12,4},... | collective-permute-start | bytes 1572872 | tf_op jit(solution)/shard_map/ppermute | solution.py:19
  189.9 11.1 %collective-permute-start.20 = (bf16[64,896]{0,1:T(8,128)(2,1)}, bf16[64,896]{0,1:T(8,128)(2,1)S(1)}, u32[]{:S(2)}, u32[]{:S(2)}) collective-permute-start(bf16[64,896]{0,1:T(8,128)(2,1)} %pad_maximum_fusion.5), channel_id=1, source_target_pairs={{0,8},{8,0},{1,9},{9,1},{2,10},{10,2},{3,11},{11,3},{4,12},{12,4},... | collective-permute-start | bytes 344072 | tf_op jit(solution)/shard_map/ppermute | solution.py:19
  194.0 8.7 %collective-permute-start.3 = (bf16[128,896]{1,0:T(8,128)(2,1)}, bf16[128,896]{1,0:T(8,128)(2,1)S(1)}, u32[]{:S(2)}, u32[]{:S(2)}) collective-permute-start(bf16[128,896]{1,0:T(8,128)(2,1)} %get-tuple-element.12), channel_id=1, source_target_pairs={{0,4},{4,0},{1,5},{5,1},{2,6},{6,2},{3,7},{7,3},{8,12},{12,8},{9,1... | collective-permute-start | bytes 688136 | tf_op jit(solution)/shard_map/ppermute | solution.py:19
  199.3 16.7 %collective-permute-start.22 = (bf16[128,896]{1,0:T(8,128)(2,1)}, bf16[128,896]{1,0:T(8,128)(2,1)S(1)}, u32[]{:S(2)}, u32[]{:S(2)}) collective-permute-start(bf16[128,896]{1,0:T(8,128)(2,1)} %get-tuple-element.16), channel_id=1, source_target_pairs={{0,4},{4,0},{1,5},{5,1},{2,6},{6,2},{3,7},{7,3},{8,12},{12,8},{9,1... | collective-permute-start | bytes 688136 | tf_op jit(solution)/shard_map/ppermute | solution.py:19
  202.0 0.8 copy-start.5
  216.8 13.5 %slice-start = ((f32[8,128]{1,0:T(8,128)}), f32[1,128]{1,0:T(1,128)S(1)}, s32[]{:S(2)}) async-start(f32[8,128]{1,0:T(8,128)} %shard_map.73), calls=%async_computation.11 | async-start | bytes 1024 | tf_op jit(solution)/shard_map/slice | solution.py:199
  249.3 9.6 %all-to-all-start.7 = ((f32[16,2,16]{2,1,0:T(2,128)}), f32[16,2,16]{2,1,0:T(2,128)S(1)}, u32[]{:S(2)}, u32[]{:S(2)}) async-start(f32[16,2,16]{2,1,0:T(2,128)} %broadcast_in_dim.27), calls=%async_computation.7 | async-start | bytes 32768 | tf_op jit(solution)/shard_map/all_to_all | solution.py:37
  (2 other events, 1.4 us)
Sparse Core Ops, SparseCore 0:
  9.2 34.1 all-gather.4
  45.1 46.3 all-gather.6
  113.1 40.2 all-gather.8

commit v4 on v3

--- a/solution.py
+++ b/solution.py
@@ -105,13 +105,13 @@
 def split(flag, a, b):
     (left, at_left), (right, at_right) = a, b
     tokens, both = left.shape[2:]
-    tile = tokens // 4
+    tile = tokens // 2
     block = (4, 1, tile, both)
     out = pl.BlockSpec((tile, both), lambda t, _: (t, 0))
     shape = jax.ShapeDtypeStruct((tokens, both), BF)
     spec = pltpu.PrefetchScalarGridSpec(
         num_scalar_prefetch=1,
-        grid=(4,),
+        grid=(2,),
         in_specs=[
             pl.BlockSpec(block, lambda t, _: (0, at_left, t, 0)),
             pl.BlockSpec(block, lambda t, _: (0, at_right, t, 0)),
@@ -129,9 +129,9 @@
     )(flag, left, right)
 
 
-def score_kernel(slot, at_ref, keep, got, v0, v1, v2, v3, other, eig0, eig1, query, out, flipped, total, act, held):
+def score_kernel(slot, at_ref, keep, got, v0, v1, v2, v3, other, inv0, inv1, query, out, flipped, total, act, held):
     step = pl.program_id(0)
-    n = eig0.shape[0]
+    n = inv0.shape[0]
     tokens = keep.shape[0]
     half = other.shape[1]
     width = act.shape[1] // 4
@@ -153,10 +153,10 @@
 
     def body(e, _):
         cols = pl.ds(pl.multiple_of(e * width, width), width)
-        for k, eig in enumerate((eig0, eig1)):
+        for k, inv in enumerate((inv0, inv1)):
             here = slice(k * n, (k + 1) * n)
             contracted = dot(flipped[here, :], act[:, cols])
-            scaled = (contracted * (1.0 / eig[:, cols].astype(F32))).astype(BF)
+            scaled = (contracted * inv[:, cols]).astype(BF)
             total[here, :] += dot_t(scaled, held[:, cols])
         return 0
 
@@ -167,9 +167,9 @@
         out[0:1, :] = (total[...] * query[...]).sum(0, keepdims=True)
 
 
-def score(slot, at, keep, got, acts, other, eig0, eig1, query):
+def score(slot, at, keep, got, acts, other, inv0, inv1, query):
     tokens, both = keep.shape
-    n = eig0.shape[0]
+    n = inv0.shape[0]
     cols = acts[0].shape[1]
     half = other.shape[1]
     rows = 2 * half
@@ -202,10 +202,10 @@
         out_shape=jax.ShapeDtypeStruct((8, rows), F32),
         cost_estimate=pl.CostEstimate(
             flops=2 * both * 4 * cols * (tokens + rows),
-            bytes_accessed=2 * both * 4 * cols,
+            bytes_accessed=4 * both * 4 * cols,
             transcendentals=0,
         ),
-    )(at, keep, got, *acts, other, eig0, eig1, query)[0]
+    )(at, keep, got, *acts, other, inv0, inv1, query)[0]
 
 
 def shards(grad_out, act_in, basis_out, basis_in, eigen_vals, query_out, query_in):
@@ -224,6 +224,8 @@
     out_both = jnp.concatenate([out_t, shift(out_t, "c", 1)], 0)
     out_both = lax.optimization_barrier(out_both)
     eigen_other = shift(eigen_vals, "c", 1)
+    inv0 = 1.0 / eigen_vals.astype(F32)
+    inv1 = 1.0 / eigen_other.astype(F32)
 
     mine = lax.dynamic_slice_in_dim(query_out.reshape(rows, unit), ci * half_rows, half_rows, 0)
     mine_in = lax.dynamic_slice_in_dim(query_in.reshape(rows, -1), ci * half_rows, half_rows, 0)
@@ -268,7 +270,7 @@
         keep, give = split(keeps, a, b)
         got = shift(give, "zl", 1)
         result.append(
-            score(slot, at, keep, got, act_rot, value_other, eigen_vals, eigen_other, query_rot)
+            score(slot, at, keep, got, act_rot, value_other, inv0, inv1, query_rot)
         )
     result = jnp.stack(result)
     low = jnp.where(same, zi, (zi + 3) % 4) // 2

time: 269 us -> 280 us (1.041)
  other arithmetic: 8.06 us -> 20.1 us
  waiting for transfers between devices: 73.1 us -> 76 us
    div x0 -> x2, other arithmetic: none -> 12 us  [the longest x1 6.01 us: shards(): inv0 = 1.0 / eigen_vals.astype(F32)]
    all_to_all x7, waiting for transfers between devices: 20 us -> 23.1 us  [exchange(): return lax.all_to_all(value, axes, 0, 0, tiled=True)]
  transfers between devices with their start and end apart: 33 -> 33, of which waited for: 17 -> 15; matrix products, arithmetic and copies ran while one was open for 13% -> 16% of each run, Pallas kernels for 9% -> 8%
where the time goes in v4:
time: 280 us; the launch traced here: 277 us
  starting transfers between devices  83.5 us (30%)
  waiting for transfers between devices  76 us (27%)
  Pallas kernels  35.5 us (13%)
  matrix products  20.4 us (7%)
  other arithmetic  20.1 us (7%)
  blocking collectives  16.6 us (6%)
  between operations  13.4 us (5%)
  local copies, waits for them, and re-layouts  11.7 us (4%)
    ppermute x19, waiting for transfers between devices, shift(): return lax.ppermute(value, axis, [(i, (i + by) % n) for i in range(n)])  40.4 us
    all_to_all x7, starting transfers between devices, exchange(): return lax.all_to_all(value, axes, 0, 0, tiled=True)  39.5 us
    ppermute x19, starting transfers between devices, shift(): return lax.ppermute(value, axis, [(i, (i + by) % n) for i in range(n)])  32.9 us
    pallas_call x2, Pallas kernels, score(): pl.pallas_call(functools.partial(score_kernel, slot), grid_spec=spec, out...  27 us
    all_to_all x7, waiting for transfers between devices, exchange(): return lax.all_to_all(value, axes, 0, 0, tiled=True)  23.1 us
    dot_general x4, matrix products, dot_t(): lax.dot_general(a, b, (((1,), (1,)), ((), ())), preferred_element_type=F32)  20.4 us
    all_to_all x1, blocking collectives, exchange(): return lax.all_to_all(value, axes, 0, 0, tiled=True)  16.6 us
    ppermute x3, starting transfers between devices, from_owner(): return lax.ppermute(value, ('zh', 'zl'), pairs)  9.75 us
  transfers between devices with their start and end apart: 33, of which 15 were waited for; matrix products, arithmetic and copies ran while one was open for 16% of the time, Pallas kernels for 8%

profile of v4, /device:TPU:2, one launch (start us, length us, event | category | flops | bytes accessed | tf_op | source)
XLA Modules:
  0.0 277.3 jit_solution(14071898582138240148)
XLA Ops:
  7.3 3.3 %collective-permute-start.2 = (bf16[128,1792]{1,0:T(8,128)(2,1)}, bf16[128,1792]{1,0:T(8,128)(2,1)S(1)}, u32[]{:S(2)}, u32[]{:S(2)}) collective-permute-start(bf16[128,1792]{1,0:T(8,128)(2,1)} %bitcast.67), channel_id=1, source_target_pairs={{0,16},{16,32},{32,48},{48,0},{1,17},{17,33},{33,49},{49,1},{2,18}... | collective-permute-start | bytes 1376264 | tf_op jit(solution)/shard_map/ppermute | solution.py:19
  10.7 3.1 %collective-permute-start.1 = (bf16[128,1792]{1,0:T(8,128)(2,1)}, bf16[128,1792]{1,0:T(8,128)(2,1)S(1)}, u32[]{:S(2)}, u32[]{:S(2)}) collective-permute-start(bf16[128,1792]{1,0:T(8,128)(2,1)} %bitcast.68), channel_id=1, source_target_pairs={{0,48},{16,0},{32,16},{48,32},{1,49},{17,1},{33,17},{49,33},{2,50}... | collective-permute-start | bytes 1376264 | tf_op jit(solution)/shard_map/ppermute | solution.py:19
  13.8 14.0 %collective-permute-done.2 = bf16[128,1792]{1,0:T(8,128)(2,1)S(1)} collective-permute-done((bf16[128,1792]{1,0:T(8,128)(2,1)}, bf16[128,1792]{1,0:T(8,128)(2,1)S(1)}, u32[]{:S(2)}, u32[]{:S(2)}) %collective-permute-start.2) | collective-permute-done | bytes 458784 | tf_op jit(solution)/shard_map/ppermute | solution.py:19
  27.8 7.6 %collective-permute-done.1 = bf16[128,1792]{1,0:T(8,128)(2,1)S(1)} collective-permute-done((bf16[128,1792]{1,0:T(8,128)(2,1)}, bf16[128,1792]{1,0:T(8,128)(2,1)S(1)}, u32[]{:S(2)}, u32[]{:S(2)}) %collective-permute-start.1) | collective-permute-done | bytes 458784 | tf_op jit(solution)/shard_map/ppermute | solution.py:19
  36.5 2.8 %collective-permute-start.7 = (bf16[512,128]{1,0:T(8,128)(2,1)S(1)}, bf16[512,128]{1,0:T(8,128)(2,1)S(1)}, u32[]{:S(2)}, u32[]{:S(2)}) collective-permute-start(bf16[512,128]{1,0:T(8,128)(2,1)S(1)} %copy-done.11), channel_id=1, source_target_pairs={{0,48},{16,0},{32,16},{48,32},{1,49},{17,1},{33,17},{49,33},{2,50}... | collective-permute-start | bytes 393224 | tf_op jit(solution)/shard_map/ppermute | solution.py:19
  40.4 3.5 %collective-permute-start.8 = (bf16[512,128]{1,0:T(8,128)(2,1)S(1)}, bf16[512,128]{1,0:T(8,128)(2,1)S(1)}, u32[]{:S(2)}, u32[]{:S(2)}) collective-permute-start(bf16[512,128]{1,0:T(8,128)(2,1)S(1)} %copy-done.11), channel_id=1, source_target_pairs={{0,32},{16,48},{32,0},{48,16},{1,33},{17,49},{33,1},{49,17},{2,34}... | collective-permute-start | bytes 393224 | tf_op jit(solution)/shard_map/ppermute | solution.py:19
  44.8 2.1 collective-permute-done.9
  47.0 2.9 %collective-permute-done.8 = bf16[512,128]{1,0:T(8,128)(2,1)S(1)} collective-permute-done((bf16[512,128]{1,0:T(8,128)(2,1)S(1)}, bf16[512,128]{1,0:T(8,128)(2,1)S(1)}, u32[]{:S(2)}, u32[]{:S(2)}) %collective-permute-start.8) | collective-permute-done | bytes 131104 | tf_op jit(solution)/shard_map/ppermute | solution.py:19
  50.0 1.6 collective-permute-start.6
  51.6 3.0 %collective-permute-start.5 = (bf16[128,512]{1,0:T(8,128)(2,1)S(1)}, bf16[128,512]{1,0:T(8,128)(2,1)}, u32[]{:S(2)}, u32[]{:S(2)}) collective-permute-start(bf16[128,512]{1,0:T(8,128)(2,1)S(1)} %bitcast.81), channel_id=1, source_target_pairs={{0,128},{64,192},{128,0},{192,64},{1,129},{65,193},{129,1},{193,65... | collective-permute-start | bytes 393224 | tf_op jit(solution)/shard_map/ppermute | solution.py:19
  54.6 1.3 collective-permute-start.4
  57.2 4.1 %collective-permute-done.5.a2 = bf16[128,512]{1,0:T(8,128)(2,1)} collective-permute-done((bf16[128,512]{1,0:T(8,128)(2,1)S(1)}, bf16[128,512]{1,0:T(8,128)(2,1)}, u32[]{:S(2)}, u32[]{:S(2)}) %collective-permute-start.5) | collective-permute-done | bytes 131104 | tf_op jit(solution)/shard_map/ppermute | solution.py:19
  62.1 4.0 %rotate_in.1 = (bf16[512,1024]{1,0:T(8,128)(2,1)}, bf16[64,1024]{1,0:T(8,128)(2,1)}) custom-call(s32[3]{0:T(128)} %pad_add_fusion.at_ref, bf16[128,512]{1,0:T(8,128)(2,1)} %bitcast.79, bf16[128,512]{1,0:T(8,128)(2,1)} %collective-permute-done.4.a1, bf16[128,512]{1,0:T(8,128)(2,1)} %collective-permute-done.5.a2, bf16[128,512]{1,0:T(8,128)(2,1)} %copy-done.15, ...), custom_call_target="tpu_custom_call" | custom-call | flops 536870912 | bytes 2621440 | tf_op jit(solution)/shard_map/rotate_in/pallas_call | solution.py:74
  66.0 4.8 %all-to-all-start.2 = ((bf16[4,128,1024]{2,1,0:T(8,128)(2,1)}), bf16[4,128,1024]{2,1,0:T(8,128)(2,1)S(1)}, u32[]{:S(2)}, u32[]{:S(2)}) async-start(bf16[4,128,1024]{2,1,0:T(8,128)(2,1)} %bitcast.63), calls=%async_computation.2 | async-start | bytes 2097152 | tf_op jit(solution)/shard_map/all_to_all | solution.py:37
  70.9 5.5 %collective-permute-start.21 = (bf16[128,1792]{1,0:T(8,128)(2,1)}, bf16[128,1792]{1,0:T(8,128)(2,1)}, u32[]{:S(2)}, u32[]{:S(2)}) collective-permute-start(bf16[128,1792]{1,0:T(8,128)(2,1)} %bitcast.69), channel_id=1, source_target_pairs={{0,32},{16,48},{32,0},{48,16},{1,33},{17,49},{33,1},{49,17},{2,34}... | collective-permute-start | bytes 1376264 | tf_op jit(solution)/shard_map/ppermute | solution.py:19
  76.3 7.9 %all-to-all-done.2 = bf16[4,128,1024]{2,1,0:T(8,128)(2,1)S(1)} async-done(((bf16[4,128,1024]{2,1,0:T(8,128)(2,1)}), bf16[4,128,1024]{2,1,0:T(8,128)(2,1)S(1)}, u32[]{:S(2)}, u32[]{:S(2)}) %all-to-all-start.2) | async-done | bytes 1048608 | tf_op jit(solution)/shard_map/all_to_all | solution.py:37
  84.4 1.3 collective-permute-start.11
  85.7 1.6 pad_maximum_fusion
  87.4 1.6 copy-done.2
  90.8 9.2 %all-to-all-start.3 = ((bf16[8,8,1920]{2,1,0:T(8,128)(2,1)}), bf16[8,8,1920]{2,1,0:T(8,128)(2,1)S(1)}, u32[]{:S(2)}, u32[]{:S(2)}) async-start(bf16[8,8,1920]{2,1,0:T(8,128)(2,1)} %maximum_bitcast_fusion), calls=%async_computation.3 | async-start | bytes 491520 | tf_op jit(solution)/shard_map/all_to_all | solution.py:37
  100.1 2.7 collective-permute-done.11
  102.9 3.0 %collective-permute-start.12 = (bf16[128,1024]{1,0:T(8,128)(2,1)S(1)}, bf16[128,1024]{1,0:T(8,128)(2,1)S(1)}, u32[]{:S(2)}, u32[]{:S(2)}) collective-permute-start(bf16[128,1024]{1,0:T(8,128)(2,1)S(1)} %add_convert_fusion), channel_id=1, source_target_pairs={{0,16},{20,36},{32,48},{52,4},{1,17},{21,37},{33,49},{53,5},{2,18}... | collective-permute-start | bytes 786440 | tf_op jit(solution)/shard_map/ppermute | solution.py:28
  105.8 1.9 collective-permute-start.14
  107.8 4.8 %collective-permute-start.13 = (bf16[128,1024]{1,0:T(8,128)(2,1)S(1)}, bf16[128,1024]{1,0:T(8,128)(2,1)S(1)}, u32[]{:S(2)}, u32[]{:S(2)}) collective-permute-start(bf16[128,1024]{1,0:T(8,128)(2,1)S(1)} %add_convert_fusion), channel_id=1, source_target_pairs={{0,32},{20,52},{32,0},{52,20},{1,33},{21,53},{33,1},{53,21},{2,34}... | collective-permute-start | bytes 786440 | tf_op jit(solution)/shard_map/ppermute | solution.py:28
  113.6 4.8 %all-to-all-start.4 = ((bf16[8,8,1920]{2,1,0:T(8,128)(2,1)}), bf16[8,8,1920]{2,1,0:T(8,128)(2,1)S(1)}, u32[]{:S(2)}, u32[]{:S(2)}) async-start(bf16[8,8,1920]{2,1,0:T(8,128)(2,1)} %broadcast_in_dim.12), calls=%async_computation.4 | async-start | bytes 491520 | tf_op jit(solution)/shard_map/all_to_all | solution.py:37
  118.4 9.0 %collective-permute-done.13 = bf16[128,1024]{1,0:T(8,128)(2,1)S(1)} collective-permute-done((bf16[128,1024]{1,0:T(8,128)(2,1)S(1)}, bf16[128,1024]{1,0:T(8,128)(2,1)S(1)}, u32[]{:S(2)}, u32[]{:S(2)}) %collective-permute-start.13) | collective-permute-done | bytes 262176 | tf_op jit(solution)/shard_map/ppermute | solution.py:28
  127.5 2.4 all-to-all-done.4
  131.8 5.6 %convolution_convert_fusion.2 = bf16[896,512]{0,1:T(8,128)(2,1)} fusion(bf16[896,1792]{1,0:T(8,128)(2,1)} %copy-done.2, bf16[512,1792]{1,0:T(8,128)(2,1)} %bitcast.78), kind=kOutput, calls=%fused_computation.5 | convolution fusion | flops 1644625920 | bytes 5963776 | tf_op jit(solution)/shard_map/dot_general | solution.py:49
  137.4 5.2 %all-to-all-start = ((bf16[4,128,896]{2,1,0:T(8,128)(2,1)}), bf16[4,128,896]{2,1,0:T(8,128)(2,1)S(1)}, u32[]{:S(2)}, u32[]{:S(2)}) async-start(bf16[4,128,896]{2,1,0:T(8,128)(2,1)} %bitcast.7), calls=%async_computation | async-start | bytes 1835008 | tf_op jit(solution)/shard_map/all_to_all | solution.py:37
  142.6 8.3 %convolution_convert_fusion = bf16[1024,896]{1,0:T(8,128)(2,1)} fusion(bf16[1024,1792]{1,0:T(8,128)(2,1)} %bitcast.77, bf16[896,1792]{1,0:T(8,128)(2,1)} %copy-done.2), kind=kOutput, calls=%fused_computation.3 | convolution fusion | flops 3289251840 | bytes 8716288 | tf_op jit(solution)/shard_map/dot_general | solution.py:49
  150.9 4.6 %all-to-all-done = bf16[4,128,896]{2,1,0:T(8,128)(2,1)S(1)} async-done(((bf16[4,128,896]{2,1,0:T(8,128)(2,1)}), bf16[4,128,896]{2,1,0:T(8,128)(2,1)S(1)}, u32[]{:S(2)}, u32[]{:S(2)}) %all-to-all-start) | async-done | bytes 917536 | tf_op jit(solution)/shard_map/all_to_all | solution.py:37
  156.4 5.0 %all-to-all-start.1 = ((bf16[8,128,896]{2,1,0:T(8,128)(2,1)}), bf16[8,128,896]{2,1,0:T(8,128)(2,1)S(1)}, u32[]{:S(2)}, u32[]{:S(2)}) async-start(bf16[8,128,896]{2,1,0:T(8,128)(2,1)} %bitcast.57), calls=%async_computation.1 | async-start | bytes 3670016 | tf_op jit(solution)/shard_map/all_to_all | solution.py:37
  161.4 6.0 %convert_divide_fusion.1.inv0 = f32[448,4096]{1,0:T(8,128)} fusion(bf16[448,4096]{1,0:T(8,128)(2,1)} %param.11), kind=kLoop, calls=%fused_computation.1 | loop fusion | flops 3670016 | bytes 11010048 | tf_op jit(solution)/shard_map/div | solution.py:227
  167.4 3.9 %collective-permute-start.16 = (bf16[320,1024]{1,0:T(8,128)(2,1)S(1)}, bf16[320,1024]{1,0:T(8,128)(2,1)}, u32[]{:S(2)}, u32[]{:S(2)}) collective-permute-start(bf16[320,1024]{1,0:T(8,128)(2,1)S(1)} %pad_maximum_fusion.2.v0), channel_id=1, source_target_pairs={{0,128},{64,192},{128,0},{192,64},{1,129},{65,193},{129,1},{193,65... | collective-permute-start | bytes 1966088 | tf_op jit(solution)/shard_map/ppermute | solution.py:19
  172.4 1.9 convert_bitcast_fusion.query
  174.3 5.5 %convolution_convert_fusion.1 = bf16[896,512]{0,1:T(8,128)(2,1)} fusion(bf16[896,1792]{1,0:T(8,128)(2,1)} %copy-done.2, bf16[512,1792]{1,0:T(8,128)(2,1)} %all-gather.9.cloned.1.call-done), kind=kOutput, calls=%fused_computation.4 | convolution fusion | flops 1644625920 | bytes 5963776 | tf_op jit(solution)/shard_map/dot_general | solution.py:49
  179.8 3.5 %all-to-all-done.1 = bf16[8,128,896]{2,1,0:T(8,128)(2,1)S(1)} async-done(((bf16[8,128,896]{2,1,0:T(8,128)(2,1)}), bf16[8,128,896]{2,1,0:T(8,128)(2,1)S(1)}, u32[]{:S(2)}, u32[]{:S(2)}) %all-to-all-start.1) | async-done | bytes 1835040 | tf_op jit(solution)/shard_map/all_to_all | solution.py:37
  183.3 5.6 %all-to-all-start.5 = ((bf16[4,128,896]{2,1,0:T(8,128)(2,1)}), bf16[4,128,896]{2,1,0:T(8,128)(2,1)}, u32[]{:S(2)}, u32[]{:S(2)}) async-start(bf16[4,128,896]{2,1,0:T(8,128)(2,1)} %bitcast.64), calls=%async_computation.5 | async-start | bytes 1835008 | tf_op jit(solution)/shard_map/all_to_all | solution.py:37
  190.8 8.6 %collective-permute-done.15.v1 = bf16[320,1024]{1,0:T(8,128)(2,1)} collective-permute-done((bf16[320,1024]{1,0:T(8,128)(2,1)S(1)}, bf16[320,1024]{1,0:T(8,128)(2,1)}, u32[]{:S(2)}, u32[]{:S(2)}) %collective-permute-start.15) | collective-permute-done | bytes 655392 | tf_op jit(solution)/shard_map/ppermute | solution.py:19
  201.2 2.3 split.2
  203.5 2.3 split.3
  205.7 2.0 collective-permute-start.22
  207.7 6.0 %convert_divide_fusion.inv1 = f32[448,4096]{1,0:T(8,128)} fusion(bf16[448,4096]{1,0:T(8,128)(2,1)} %collective-permute-done.19), kind=kLoop, calls=%fused_computation | loop fusion | flops 3670016 | bytes 11010048 | tf_op jit(solution)/shard_map/div | solution.py:228
  214.6 13.4 %shard_map.73 = f32[8,128]{1,0:T(8,128)} custom-call(s32[3]{0:T(128)} %pad_add_fusion.at_ref, bf16[128,896]{1,0:T(8,128)(2,1)} %get-tuple-element.11.keep, bf16[128,896]{1,0:T(8,128)(2,1)} %copy-done.9, bf16[320,1024]{1,0:T(8,128)(2,1)} %copy-done.3, bf16[320,1024]{1,0:T(8,128)(2,1)} %collective-permute-done.15.v1, ...), custom_call_target="tpu_custom_call" | custom-call | flops 1879048192 | bytes 14680064 | tf_op jit(solution)/shard_map/pallas_call | solution.py:199
  228.7 13.5 %shard_map.74 = f32[8,128]{1,0:T(8,128)} custom-call(s32[3]{0:T(128)} %pad_add_fusion.at_ref, bf16[128,896]{1,0:T(8,128)(2,1)} %get-tuple-element.15.keep, bf16[128,896]{1,0:T(8,128)(2,1)} %copy-done.8, bf16[320,1024]{1,0:T(8,128)(2,1)} %copy-done.3, bf16[320,1024]{1,0:T(8,128)(2,1)} %collective-permute-done.15.v1, ...), custom_call_target="tpu_custom_call" | custom-call | flops 1879048192 | bytes 14680064 | tf_op jit(solution)/shard_map/pallas_call | solution.py:199
  243.3 16.6 %all_to_all.40 = f32[16,2,16]{2,1,0:T(2,128)S(1)} all-to-all(f32[16,2,16]{2,1,0:T(2,128)S(1)} %broadcast_in_dim.26), channel_id=1, replica_groups=mesh['y'=4,'zh'=4,'c'=2,'zl'=2,'x'=4] {'y','zh'}, dimensions={0} | all-to-all | bytes 4096 | tf_op jit(solution)/shard_map/all_to_all | solution.py:37
  260.6 4.8 %all-to-all-start.7 = ((f32[16,2,16]{2,1,0:T(2,128)}), f32[16,2,16]{2,1,0:T(2,128)S(1)}, u32[]{:S(2)}, u32[]{:S(2)}) async-start(f32[16,2,16]{2,1,0:T(2,128)} %broadcast_in_dim.27), calls=%async_computation.7 | async-start | bytes 32768 | tf_op jit(solution)/shard_map/all_to_all | solution.py:37
  265.4 4.7 %all-to-all-done.7 = f32[16,2,16]{2,1,0:T(2,128)S(1)} async-done(((f32[16,2,16]{2,1,0:T(2,128)}), f32[16,2,16]{2,1,0:T(2,128)S(1)}, u32[]{:S(2)}, u32[]{:S(2)}) %all-to-all-start.7) | async-done | bytes 2080 | tf_op jit(solution)/shard_map/all_to_all | solution.py:37
  (106 shorter events, 20.4 us)
Async XLA Ops:
  6.5 80.8 %copy-start = (bf16[16,8,1792]{2,1,0:T(8,128)(2,1)S(1)}, bf16[16,8,1792]{2,1,0:T(8,128)(2,1)}, u32[]{:S(2)}) copy-start(bf16[16,8,1792]{2,1,0:T(8,128)(2,1)} %param.12) | copy-start | bytes 1376260
  6.5 30.0 %copy-start.11 = (bf16[512,128]{1,0:T(8,128)(2,1)S(1)}, bf16[512,128]{1,0:T(8,128)(2,1)}, u32[]{:S(2)}) copy-start(bf16[512,128]{1,0:T(8,128)(2,1)} %param.10) | copy-start | bytes 393220
  6.5 37.4 %copy-start.6 = (bf16[1792,448]{0,1:T(8,128)(2,1)S(1)}, bf16[1792,448]{0,1:T(8,128)(2,1)}, u32[]{:S(2)}) copy-start(bf16[1792,448]{0,1:T(8,128)(2,1)} %param.9) | copy-start | bytes 4816900
  6.5 43.5 %copy-start.14 = (bf16[1,128,512]{2,1,0:T(8,128)(2,1)S(1)}, bf16[1,128,512]{2,1,0:T(8,128)(2,1)}, u32[]{:S(2)}) copy-start(bf16[1,128,512]{2,1,0:T(8,128)(2,1)} %param.8) | copy-start | bytes 393220
  6.5 49.9 %copy-start.12 = (bf16[16,8,512]{2,1,0:T(8,128)(2,1)S(1)}, bf16[16,8,512]{2,1,0:T(8,128)(2,1)}, u32[]{:S(2)}) copy-start(bf16[16,8,512]{2,1,0:T(8,128)(2,1)} %param.13) | copy-start | bytes 393220
  6.5 125.3 %all-gather.5.cloned.1.call-start = ((), (), s32[]{:S(2)}) async-start(), calls=%async_computation.8 | async-start | bytes 2293760 | tf_op jit(solution)/shard_map/all_gather | solution.py:261
  7.3 135.3 %all-gather.7.cloned.1.call-start = ((), (), s32[]{:S(2)}) async-start(), calls=%async_computation.9 | async-start | bytes 4587520 | tf_op jit(solution)/shard_map/all_gather | solution.py:261
  7.3 20.5 %collective-permute-start.2 = (bf16[128,1792]{1,0:T(8,128)(2,1)}, bf16[128,1792]{1,0:T(8,128)(2,1)S(1)}, u32[]{:S(2)}, u32[]{:S(2)}) collective-permute-start(bf16[128,1792]{1,0:T(8,128)(2,1)} %bitcast.67), channel_id=1, source_target_pairs={{0,16},{16,32},{32,48},{48,0},{1,17},{17,33},{33,49},{49,1},{2,18}... | collective-permute-start | bytes 1376264 | tf_op jit(solution)/shard_map/ppermute | solution.py:19
  10.7 24.8 %collective-permute-start.1 = (bf16[128,1792]{1,0:T(8,128)(2,1)}, bf16[128,1792]{1,0:T(8,128)(2,1)S(1)}, u32[]{:S(2)}, u32[]{:S(2)}) collective-permute-start(bf16[128,1792]{1,0:T(8,128)(2,1)} %bitcast.68), channel_id=1, source_target_pairs={{0,48},{16,0},{32,16},{48,32},{1,49},{17,1},{33,17},{49,33},{2,50}... | collective-permute-start | bytes 1376264 | tf_op jit(solution)/shard_map/ppermute | solution.py:19
  36.5 8.3 %collective-permute-start.7 = (bf16[512,128]{1,0:T(8,128)(2,1)S(1)}, bf16[512,128]{1,0:T(8,128)(2,1)S(1)}, u32[]{:S(2)}, u32[]{:S(2)}) collective-permute-start(bf16[512,128]{1,0:T(8,128)(2,1)S(1)} %copy-done.11), channel_id=1, source_target_pairs={{0,48},{16,0},{32,16},{48,32},{1,49},{17,1},{33,17},{49,33},{2,50}... | collective-permute-start | bytes 393224 | tf_op jit(solution)/shard_map/ppermute | solution.py:19
  39.3 7.6 %collective-permute-start.9 = (bf16[512,128]{1,0:T(8,128)(2,1)S(1)}, bf16[512,128]{1,0:T(8,128)(2,1)S(1)}, u32[]{:S(2)}, u32[]{:S(2)}) collective-permute-start(bf16[512,128]{1,0:T(8,128)(2,1)S(1)} %copy-done.11), channel_id=1, source_target_pairs={{0,16},{16,32},{32,48},{48,0},{1,17},{17,33},{33,49},{49,1},{2,18}... | collective-permute-start | bytes 393224 | tf_op jit(solution)/shard_map/ppermute | solution.py:19
  40.4 9.4 %collective-permute-start.8 = (bf16[512,128]{1,0:T(8,128)(2,1)S(1)}, bf16[512,128]{1,0:T(8,128)(2,1)S(1)}, u32[]{:S(2)}, u32[]{:S(2)}) collective-permute-start(bf16[512,128]{1,0:T(8,128)(2,1)S(1)} %copy-done.11), channel_id=1, source_target_pairs={{0,32},{16,48},{32,0},{48,16},{1,33},{17,49},{33,1},{49,17},{2,34}... | collective-permute-start | bytes 393224 | tf_op jit(solution)/shard_map/ppermute | solution.py:19
  43.9 41.8 %collective-permute-start = (bf16[448,1792]{1,0:T(8,128)(2,1)S(1)}, bf16[448,1792]{1,0:T(8,128)(2,1)}, u32[]{:S(2)}, u32[]{:S(2)}) collective-permute-start(bf16[448,1792]{1,0:T(8,128)(2,1)S(1)} %bitcast.58), channel_id=1, source_target_pairs={{0,8},{8,0},{1,9},{9,1},{2,10},{10,2},{3,11},{11,3},{4,12},{12,4},... | collective-permute-start | bytes 4816904 | tf_op jit(solution)/shard_map/ppermute | solution.py:19
  49.9 11.4 %copy-start.7 = (bf16[4,512,128]{2,1,0:T(8,128)(2,1)}, bf16[4,512,128]{2,1,0:T(8,128)(2,1)S(1)}, u32[]{:S(2)}) copy-start(bf16[4,512,128]{2,1,0:T(8,128)(2,1)S(1)} %pad_maximum_fusion.3.w0) | copy-start | bytes 1572868
  49.9 11.4 %collective-permute-start.10 = (bf16[4,512,128]{2,1,0:T(8,128)(2,1)S(1)}, bf16[4,512,128]{2,1,0:T(8,128)(2,1)S(1)}, u32[]{:S(2)}, u32[]{:S(2)}) collective-permute-start(bf16[4,512,128]{2,1,0:T(8,128)(2,1)S(1)} %pad_maximum_fusion.3.w0), channel_id=1, source_target_pairs={{0,8},{8,0},{1,9},{9,1},{2,10},{10,2},{3,11},{11,3},{4,12},{12,4},... | collective-permute-start | bytes 1572872 | tf_op jit(solution)/shard_map/ppermute | solution.py:19
  50.0 7.1 %collective-permute-start.6 = (bf16[128,512]{1,0:T(8,128)(2,1)S(1)}, bf16[128,512]{1,0:T(8,128)(2,1)S(1)}, u32[]{:S(2)}, u32[]{:S(2)}) collective-permute-start(bf16[128,512]{1,0:T(8,128)(2,1)S(1)} %bitcast.80), channel_id=1, source_target_pairs={{0,64},{64,128},{128,192},{192,0},{1,65},{65,129},{129,193},{193,1... | collective-permute-start | bytes 393224 | tf_op jit(solution)/shard_map/ppermute | solution.py:19
  51.6 9.7 %collective-permute-start.5 = (bf16[128,512]{1,0:T(8,128)(2,1)S(1)}, bf16[128,512]{1,0:T(8,128)(2,1)}, u32[]{:S(2)}, u32[]{:S(2)}) collective-permute-start(bf16[128,512]{1,0:T(8,128)(2,1)S(1)} %bitcast.81), channel_id=1, source_target_pairs={{0,128},{64,192},{128,0},{192,64},{1,129},{65,193},{129,1},{193,65... | collective-permute-start | bytes 393224 | tf_op jit(solution)/shard_map/ppermute | solution.py:19
  54.6 6.7 %collective-permute-start.4 = (bf16[128,512]{1,0:T(8,128)(2,1)S(1)}, bf16[128,512]{1,0:T(8,128)(2,1)}, u32[]{:S(2)}, u32[]{:S(2)}) collective-permute-start(bf16[128,512]{1,0:T(8,128)(2,1)S(1)} %bitcast.82), channel_id=1, source_target_pairs={{0,192},{64,0},{128,64},{192,128},{1,193},{65,1},{129,65},{193,129... | collective-permute-start | bytes 393224 | tf_op jit(solution)/shard_map/ppermute | solution.py:19
  57.2 4.1 %copy-start.15 = (bf16[128,512]{1,0:T(8,128)(2,1)}, bf16[128,512]{1,0:T(8,128)(2,1)S(1)}, u32[]{:S(2)}) copy-start(bf16[128,512]{1,0:T(8,128)(2,1)S(1)} %collective-permute-done.6.a3) | copy-start | bytes 393220
  66.0 18.2 %all-to-all-start.2 = ((bf16[4,128,1024]{2,1,0:T(8,128)(2,1)}), bf16[4,128,1024]{2,1,0:T(8,128)(2,1)S(1)}, u32[]{:S(2)}, u32[]{:S(2)}) async-start(bf16[4,128,1024]{2,1,0:T(8,128)(2,1)} %bitcast.63), calls=%async_computation.2 | async-start | bytes 2097152 | tf_op jit(solution)/shard_map/all_to_all | solution.py:37
  70.9 41.9 %collective-permute-start.21 = (bf16[128,1792]{1,0:T(8,128)(2,1)}, bf16[128,1792]{1,0:T(8,128)(2,1)}, u32[]{:S(2)}, u32[]{:S(2)}) collective-permute-start(bf16[128,1792]{1,0:T(8,128)(2,1)} %bitcast.69), channel_id=1, source_target_pairs={{0,32},{16,48},{32,0},{48,16},{1,33},{17,49},{33,1},{49,17},{2,34}... | collective-permute-start | bytes 1376264 | tf_op jit(solution)/shard_map/ppermute | solution.py:19
  84.4 18.4 %collective-permute-start.11 = (bf16[128,1024]{1,0:T(8,128)(2,1)S(1)}, bf16[128,1024]{1,0:T(8,128)(2,1)S(1)}, u32[]{:S(2)}, u32[]{:S(2)}) collective-permute-start(bf16[128,1024]{1,0:T(8,128)(2,1)S(1)} %reduce_sum.42), channel_id=1, source_target_pairs={{4,0},{16,20},{36,32},{48,52},{5,1},{17,21},{37,33},{49,53},{6,2},... | collective-permute-start | bytes 786440 | tf_op jit(solution)/shard_map/ppermute | solution.py:33
  87.4 1.7 copy-start.2
  87.4 2.7 copy-start.10
  90.8 22.0 %all-to-all-start.3 = ((bf16[8,8,1920]{2,1,0:T(8,128)(2,1)}), bf16[8,8,1920]{2,1,0:T(8,128)(2,1)S(1)}, u32[]{:S(2)}, u32[]{:S(2)}) async-start(bf16[8,8,1920]{2,1,0:T(8,128)(2,1)} %maximum_bitcast_fusion), calls=%async_computation.3 | async-start | bytes 491520 | tf_op jit(solution)/shard_map/all_to_all | solution.py:37
  100.1 74.2 %all-gather.9.cloned.1.call-start = ((), (), s32[]{:S(2)}) async-start(), calls=%async_computation.10 | async-start | bytes 2293760 | tf_op jit(solution)/shard_map/all_gather | solution.py:261
  102.9 15.5 %collective-permute-start.12 = (bf16[128,1024]{1,0:T(8,128)(2,1)S(1)}, bf16[128,1024]{1,0:T(8,128)(2,1)S(1)}, u32[]{:S(2)}, u32[]{:S(2)}) collective-permute-start(bf16[128,1024]{1,0:T(8,128)(2,1)S(1)} %add_convert_fusion), channel_id=1, source_target_pairs={{0,16},{20,36},{32,48},{52,4},{1,17},{21,37},{33,49},{53,5},{2,18}... | collective-permute-start | bytes 786440 | tf_op jit(solution)/shard_map/ppermute | solution.py:28
  105.8 12.6 %collective-permute-start.14 = (bf16[128,1024]{1,0:T(8,128)(2,1)S(1)}, bf16[128,1024]{1,0:T(8,128)(2,1)S(1)}, u32[]{:S(2)}, u32[]{:S(2)}) collective-permute-start(bf16[128,1024]{1,0:T(8,128)(2,1)S(1)} %add_convert_fusion), channel_id=1, source_target_pairs={{0,48},{20,4},{32,16},{52,36},{1,49},{21,5},{33,17},{53,37},{2,50}... | collective-permute-start | bytes 786440 | tf_op jit(solution)/shard_map/ppermute | solution.py:28
  107.8 19.7 %collective-permute-start.13 = (bf16[128,1024]{1,0:T(8,128)(2,1)S(1)}, bf16[128,1024]{1,0:T(8,128)(2,1)S(1)}, u32[]{:S(2)}, u32[]{:S(2)}) collective-permute-start(bf16[128,1024]{1,0:T(8,128)(2,1)S(1)} %add_convert_fusion), channel_id=1, source_target_pairs={{0,32},{20,52},{32,0},{52,20},{1,33},{21,53},{33,1},{53,21},{2,34}... | collective-permute-start | bytes 786440 | tf_op jit(solution)/shard_map/ppermute | solution.py:28
  112.6 95.1 %collective-permute-start.19 = (bf16[448,4096]{1,0:T(8,128)(2,1)}, bf16[448,4096]{1,0:T(8,128)(2,1)}, u32[]{:S(2)}, u32[]{:S(2)}) collective-permute-start(bf16[448,4096]{1,0:T(8,128)(2,1)} %param.11), channel_id=1, source_target_pairs={{0,8},{8,0},{1,9},{9,1},{2,10},{10,2},{3,11},{11,3},{4,12},{12,4},... | collective-permute-start | bytes 11010056 | tf_op jit(solution)/shard_map/ppermute | solution.py:19
  113.6 16.3 %all-to-all-start.4 = ((bf16[8,8,1920]{2,1,0:T(8,128)(2,1)}), bf16[8,8,1920]{2,1,0:T(8,128)(2,1)S(1)}, u32[]{:S(2)}, u32[]{:S(2)}) async-start(bf16[8,8,1920]{2,1,0:T(8,128)(2,1)} %broadcast_in_dim.12), calls=%async_computation.4 | async-start | bytes 491520 | tf_op jit(solution)/shard_map/all_to_all | solution.py:37
  131.0 41.4 %collective-permute-start.20 = (bf16[64,896]{0,1:T(8,128)(2,1)}, bf16[64,896]{0,1:T(8,128)(2,1)}, u32[]{:S(2)}, u32[]{:S(2)}) collective-permute-start(bf16[64,896]{0,1:T(8,128)(2,1)} %pad_maximum_fusion.5), channel_id=1, source_target_pairs={{0,8},{8,0},{1,9},{9,1},{2,10},{10,2},{3,11},{11,3},{4,12},{12,4},... | collective-permute-start | bytes 344072 | tf_op jit(solution)/shard_map/ppermute | solution.py:19
  131.1 40.3 %copy-start.3 = (bf16[320,1024]{1,0:T(8,128)(2,1)}, bf16[320,1024]{1,0:T(8,128)(2,1)S(1)}, u32[]{:S(2)}) copy-start(bf16[320,1024]{1,0:T(8,128)(2,1)S(1)} %pad_maximum_fusion.2.v0) | copy-start | bytes 1966084
  131.1 57.8 %collective-permute-start.17 = (bf16[320,1024]{1,0:T(8,128)(2,1)S(1)}, bf16[320,1024]{1,0:T(8,128)(2,1)}, u32[]{:S(2)}, u32[]{:S(2)}) collective-permute-start(bf16[320,1024]{1,0:T(8,128)(2,1)S(1)} %pad_maximum_fusion.2.v0), channel_id=1, source_target_pairs={{0,64},{64,128},{128,192},{192,0},{1,65},{65,129},{129,193},{193,1... | collective-permute-start | bytes 1966088 | tf_op jit(solution)/shard_map/ppermute | solution.py:19
  137.4 18.1 %all-to-all-start = ((bf16[4,128,896]{2,1,0:T(8,128)(2,1)}), bf16[4,128,896]{2,1,0:T(8,128)(2,1)S(1)}, u32[]{:S(2)}, u32[]{:S(2)}) async-start(bf16[4,128,896]{2,1,0:T(8,128)(2,1)} %bitcast.7), calls=%async_computation | async-start | bytes 1835008 | tf_op jit(solution)/shard_map/all_to_all | solution.py:37
  155.5 0.9 copy-start.4
  156.4 26.9 %all-to-all-start.1 = ((bf16[8,128,896]{2,1,0:T(8,128)(2,1)}), bf16[8,128,896]{2,1,0:T(8,128)(2,1)S(1)}, u32[]{:S(2)}, u32[]{:S(2)}) async-start(bf16[8,128,896]{2,1,0:T(8,128)(2,1)} %bitcast.57), calls=%async_computation.1 | async-start | bytes 3670016 | tf_op jit(solution)/shard_map/all_to_all | solution.py:37
  167.4 22.4 %collective-permute-start.16 = (bf16[320,1024]{1,0:T(8,128)(2,1)S(1)}, bf16[320,1024]{1,0:T(8,128)(2,1)}, u32[]{:S(2)}, u32[]{:S(2)}) collective-permute-start(bf16[320,1024]{1,0:T(8,128)(2,1)S(1)} %pad_maximum_fusion.2.v0), channel_id=1, source_target_pairs={{0,128},{64,192},{128,0},{192,64},{1,129},{65,193},{129,1},{193,65... | collective-permute-start | bytes 1966088 | tf_op jit(solution)/shard_map/ppermute | solution.py:19
  171.4 28.0 %collective-permute-start.15 = (bf16[320,1024]{1,0:T(8,128)(2,1)S(1)}, bf16[320,1024]{1,0:T(8,128)(2,1)}, u32[]{:S(2)}, u32[]{:S(2)}) collective-permute-start(bf16[320,1024]{1,0:T(8,128)(2,1)S(1)} %pad_maximum_fusion.2.v0), channel_id=1, source_target_pairs={{0,192},{64,0},{128,64},{192,128},{1,193},{65,1},{129,65},{193,129... | collective-permute-start | bytes 1966088 | tf_op jit(solution)/shard_map/ppermute | solution.py:19
  183.3 17.9 %copy-start.1 = (bf16[8,128,896]{2,1,0:T(8,128)(2,1)}, bf16[8,128,896]{2,1,0:T(8,128)(2,1)S(1)}, u32[]{:S(2)}) copy-start(bf16[8,128,896]{2,1,0:T(8,128)(2,1)S(1)} %all-to-all-done.1) | copy-start | bytes 5505028
  183.3 20.2 %all-to-all-start.5 = ((bf16[4,128,896]{2,1,0:T(8,128)(2,1)}), bf16[4,128,896]{2,1,0:T(8,128)(2,1)}, u32[]{:S(2)}, u32[]{:S(2)}) async-start(bf16[4,128,896]{2,1,0:T(8,128)(2,1)} %bitcast.64), calls=%async_computation.5 | async-start | bytes 1835008 | tf_op jit(solution)/shard_map/all_to_all | solution.py:37
  201.1 12.6 %collective-permute-start.18 = (bf16[4,64,1024]{2,1,0:T(8,128)(2,1)}, bf16[4,64,1024]{2,1,0:T(8,128)(2,1)S(1)}, u32[]{:S(2)}, u32[]{:S(2)}) collective-permute-start(bf16[4,64,1024]{2,1,0:T(8,128)(2,1)} %pad_maximum_fusion.4), channel_id=1, source_target_pairs={{0,8},{8,0},{1,9},{9,1},{2,10},{10,2},{3,11},{11,3},{4,12},{12,4},... | collective-permute-start | bytes 1572872 | tf_op jit(solution)/shard_map/ppermute | solution.py:19
  203.5 10.3 %collective-permute-start.3 = (bf16[128,896]{1,0:T(8,128)(2,1)}, bf16[128,896]{1,0:T(8,128)(2,1)S(1)}, u32[]{:S(2)}, u32[]{:S(2)}) collective-permute-start(bf16[128,896]{1,0:T(8,128)(2,1)} %get-tuple-element.12), channel_id=1, source_target_pairs={{0,4},{4,0},{1,5},{5,1},{2,6},{6,2},{3,7},{7,3},{8,12},{12,8},{9,1... | collective-permute-start | bytes 688136 | tf_op jit(solution)/shard_map/ppermute | solution.py:19
  205.7 22.3 %collective-permute-start.22 = (bf16[128,896]{1,0:T(8,128)(2,1)}, bf16[128,896]{1,0:T(8,128)(2,1)S(1)}, u32[]{:S(2)}, u32[]{:S(2)}) collective-permute-start(bf16[128,896]{1,0:T(8,128)(2,1)} %get-tuple-element.16), channel_id=1, source_target_pairs={{0,4},{4,0},{1,5},{5,1},{2,6},{6,2},{3,7},{7,3},{8,12},{12,8},{9,1... | collective-permute-start | bytes 688136 | tf_op jit(solution)/shard_map/ppermute | solution.py:19
  213.7 0.8 copy-start.5
  213.8 0.9 copy-start.9
  228.7 14.2 %slice-start = ((f32[8,128]{1,0:T(8,128)}), f32[1,128]{1,0:T(1,128)S(1)}, s32[]{:S(2)}) async-start(f32[8,128]{1,0:T(8,128)} %shard_map.73), calls=%async_computation.11 | async-start | bytes 1024 | tf_op jit(solution)/shard_map/slice | solution.py:199
  260.6 9.6 %all-to-all-start.7 = ((f32[16,2,16]{2,1,0:T(2,128)}), f32[16,2,16]{2,1,0:T(2,128)S(1)}, u32[]{:S(2)}, u32[]{:S(2)}) async-start(f32[16,2,16]{2,1,0:T(2,128)} %broadcast_in_dim.27), calls=%async_computation.7 | async-start | bytes 32768 | tf_op jit(solution)/shard_map/all_to_all | solution.py:37
  (2 other events, 1.5 us)
Sparse Core Ops, SparseCore 0:
  9.2 34.1 all-gather.4
  45.1 46.3 all-gather.6
  112.9 38.0 all-gather.8

commit v5 on v4

--- a/solution.py
+++ b/solution.py
@@ -87,36 +87,35 @@
     )(at, *acts, query, *bases)
 
 
-def split_kernel(flag, a, b, keep, give):
-    def total(ref):
-        return sum(ref[k, 0].astype(F32) for k in range(4)).astype(BF)
-
-    @pl.when(flag[0] == 1)
+def split_kernel(at_ref, *refs):
+    keep, give = refs[8:]
+
+    def total(refs):
+        own = refs[0][0, 0].astype(F32)
+        return sum((r[0].astype(F32) for r in refs[1:]), own).astype(BF)
+
+    @pl.when(at_ref[3] == 1)
     def _():
-        keep[...] = total(a)
-        give[...] = total(b)
-
-    @pl.when(flag[0] == 0)
+        keep[...] = total(refs[:4])
+        give[...] = total(refs[4:8])
+
+    @pl.when(at_ref[3] == 0)
     def _():
-        keep[...] = total(b)
-        give[...] = total(a)
-
-
-def split(flag, a, b):
-    (left, at_left), (right, at_right) = a, b
-    tokens, both = left.shape[2:]
+        keep[...] = total(refs[4:8])
+        give[...] = total(refs[:4])
+
+
+def split(at, a, b):
+    tokens, both = a[0][0].shape[2:]
     tile = tokens // 2
-    block = (4, 1, tile, both)
-    out = pl.BlockSpec((tile, both), lambda t, _: (t, 0))
+    specs = []
+    for parts, which in (a, b):
+        specs.append(pl.BlockSpec((1, 1, tile, both), lambda t, at, w=which: (at[4], w, t, 0)))
+        specs += [pl.BlockSpec((1, tile, both), lambda t, at, w=which: (w, t, 0))] * 3
+    out = pl.BlockSpec((tile, both), lambda t, at: (t, 0))
     shape = jax.ShapeDtypeStruct((tokens, both), BF)
     spec = pltpu.PrefetchScalarGridSpec(
-        num_scalar_prefetch=1,
-        grid=(2,),
-        in_specs=[
-            pl.BlockSpec(block, lambda t, _: (0, at_left, t, 0)),
-            pl.BlockSpec(block, lambda t, _: (0, at_right, t, 0)),
-        ],
-        out_specs=(out, out),
+        num_scalar_prefetch=1, grid=(2,), in_specs=specs, out_specs=(out, out)
     )
     return pl.pallas_call(
         split_kernel,
@@ -125,8 +124,7 @@
         cost_estimate=pl.CostEstimate(
             flops=8 * tokens * both, bytes_accessed=20 * tokens * both, transcendentals=0
         ),
-        name="split",
-    )(flag, left, right)
+    )(at, *a[0], *b[0])
 
 
 def score_kernel(slot, at_ref, keep, got, v0, v1, v2, v3, other, inv0, inv1, query, out, flipped, total, act, held):
@@ -151,16 +149,16 @@
 
     held[half:, :] = other[0]
 
-    def body(e, _):
-        cols = pl.ds(pl.multiple_of(e * width, width), width)
+    def body(e):
+        cols = slice(e * width, (e + 1) * width)
         for k, inv in enumerate((inv0, inv1)):
             here = slice(k * n, (k + 1) * n)
             contracted = dot(flipped[here, :], act[:, cols])
             scaled = (contracted * inv[:, cols]).astype(BF)
             total[here, :] += dot_t(scaled, held[:, cols])
-        return 0
-
-    lax.fori_loop(0, 4, body, 0)
+
+    for e in range(4):
+        body(e)
 
     @pl.when(step == pl.num_programs(0) - 1)
     def _():
@@ -218,7 +216,8 @@
     first = ci == 0
 
     same = li == zi % 2
-    at = jnp.stack([yi, zi, ci]).astype(jnp.int32)
+    xi = lax.axis_index("x")
+    at = jnp.stack([yi, zi, ci, same, xi]).astype(jnp.int32)
 
     out_t = basis_out.T
     out_both = jnp.concatenate([out_t, shift(out_t, "c", 1)], 0)
@@ -260,14 +259,17 @@
         some_blocks = jnp.stack(some_blocks)
         found = lax.all_gather(some_blocks, "y", axis=0, tiled=True)
         product = dot_t(found.reshape(-1, unit), out_both).astype(BF)
-        product = exchange(product.reshape(-1, tokens, 2 * width), "x")
-        blocks.append(product.reshape(4, -1, tokens, 2 * width))
-    flag = same.astype(jnp.int32)[None]
+        product = product.reshape(4, -1, tokens, 2 * width)
+        parts = [product]
+        for by in (1, 2, 3):
+            part = lax.dynamic_index_in_dim(product, (xi + by) % 4, 0, False)
+            parts.append(shift(part, "x", by))
+        blocks.append(parts)
     result = []
-    for slot, (a, b, keeps) in enumerate(
-        (((blocks[0], 0), (blocks[1], 1), flag), ((blocks[2], 0), (blocks[1], 0), flag))
+    for slot, (a, b) in enumerate(
+        (((blocks[0], 0), (blocks[1], 1)), ((blocks[2], 0), (blocks[1], 0)))
     ):
-        keep, give = split(keeps, a, b)
+        keep, give = split(at, a, b)
         got = shift(give, "zl", 1)
         result.append(
             score(slot, at, keep, got, act_rot, value_other, inv0, inv1, query_rot)

time: 280 us -> 292 us (1.043)
  waiting for transfers between devices: 76 us -> 87.6 us
  local copies, waits for them, and re-layouts: 11.7 us -> 18.2 us
  matrix products: 20.4 us -> 17.2 us
  Pallas kernels: 35.5 us -> 32.5 us
    ppermute x19 -> x28, waiting for transfers between devices: 40.4 us -> 67.5 us  [shift(): return lax.ppermute(value, axis, [(i, (i + by) % n) for i in range(n)])]
    ppermute x19 -> x28, starting transfers between devices: 32.9 us -> 51.6 us  [shift(): return lax.ppermute(value, axis, [(i, (i + by) % n) for i in range(n)])]
    all_to_all x7 -> x4, starting transfers between devices: 39.5 us -> 22.2 us  [exchange(): return lax.all_to_all(value, axes, 0, 0, tiled=True)]
    ppermute x3, waiting for transfers between devices: 9.05 us -> 0.86 us  [from_owner(): return lax.ppermute(value, ('zh', 'zl'), pairs)]
    all_to_all x7 -> x4, waiting for transfers between devices: 23.1 us -> 18.5 us  [exchange(): return lax.all_to_all(value, axes, 0, 0, tiled=True)]
    pallas_call x2, Pallas kernels: 27 us -> 22.5 us  [score(): pl.pallas_call(functools.partial(score_kernel, slot), grid_spec=spec, out...]
    unnamed x35 -> x49, local copies, waits for them, and re-layouts: 5.39 us -> 8.61 us
    dot_general x4, matrix products: 20.4 us -> 17.2 us  [dot_t(): lax.dot_general(a, b, (((1,), (1,)), ((), ())), preferred_element_type=F32)]
  transfers between devices with their start and end apart: 33 -> 39, of which waited for: 15 -> 17; matrix products, arithmetic and copies ran while one was open for 16% -> 16% of each run, Pallas kernels for 8% -> 7%
where the time goes in v5:
time: 292 us; the launch traced here: 289 us
  waiting for transfers between devices  87.6 us (30%)
  starting transfers between devices  85.2 us (29%)
  Pallas kernels  32.5 us (11%)
  other arithmetic  20.2 us (7%)
  local copies, waits for them, and re-layouts  18.2 us (6%)
  matrix products  17.2 us (6%)
  blocking collectives  14.5 us (5%)
  between operations  13.5 us (5%)
    ppermute x28, waiting for transfers between devices, shift(): return lax.ppermute(value, axis, [(i, (i + by) % n) for i in range(n)])  67.5 us
    ppermute x28, starting transfers between devices, shift(): return lax.ppermute(value, axis, [(i, (i + by) % n) for i in range(n)])  51.6 us
    pallas_call x2, Pallas kernels, score(): pl.pallas_call(functools.partial(score_kernel, slot), grid_spec=spec, out...  22.5 us
    all_to_all x4, starting transfers between devices, exchange(): return lax.all_to_all(value, axes, 0, 0, tiled=True)  22.2 us
    all_to_all x4, waiting for transfers between devices, exchange(): return lax.all_to_all(value, axes, 0, 0, tiled=True)  18.5 us
    dot_general x4, matrix products, dot_t(): lax.dot_general(a, b, (((1,), (1,)), ((), ())), preferred_element_type=F32)  17.2 us
    all_to_all x1, blocking collectives, exchange(): return lax.all_to_all(value, axes, 0, 0, tiled=True)  14.5 us
    ppermute x3, starting transfers between devices, from_owner(): return lax.ppermute(value, ('zh', 'zl'), pairs)  10.1 us
  transfers between devices with their start and end apart: 39, of which 17 were waited for; matrix products, arithmetic and copies ran while one was open for 16% of the time, Pallas kernels for 7%

profile of v5, /device:TPU:2, one launch (start us, length us, event | category | flops | bytes accessed | tf_op | source)
XLA Modules:
  0.0 288.8 jit_solution(404725897525580106)
XLA Ops:
  7.3 7.3 %collective-permute-start.27 = (bf16[128,1792]{1,0:T(8,128)(2,1)}, bf16[128,1792]{1,0:T(8,128)(2,1)S(1)}, u32[]{:S(2)}, u32[]{:S(2)}) collective-permute-start(bf16[128,1792]{1,0:T(8,128)(2,1)} %bitcast.83), channel_id=1, source_target_pairs={{0,32},{16,48},{32,0},{48,16},{1,33},{17,49},{33,1},{49,17},{2,34}... | collective-permute-start | bytes 1376264 | tf_op jit(solution)/shard_map/ppermute | solution.py:19
  14.6 13.0 %collective-permute-done.27 = bf16[128,1792]{1,0:T(8,128)(2,1)S(1)} collective-permute-done((bf16[128,1792]{1,0:T(8,128)(2,1)}, bf16[128,1792]{1,0:T(8,128)(2,1)S(1)}, u32[]{:S(2)}, u32[]{:S(2)}) %collective-permute-start.27) | collective-permute-done | bytes 458784 | tf_op jit(solution)/shard_map/ppermute | solution.py:19
  28.4 12.3 %collective-permute-start.13 = (bf16[512,128]{1,0:T(8,128)(2,1)}, bf16[512,128]{1,0:T(8,128)(2,1)S(1)}, u32[]{:S(2)}, u32[]{:S(2)}) collective-permute-start(bf16[512,128]{1,0:T(8,128)(2,1)} %param.10), channel_id=1, source_target_pairs={{0,48},{16,0},{32,16},{48,32},{1,49},{17,1},{33,17},{49,33},{2,50}... | collective-permute-start | bytes 393224 | tf_op jit(solution)/shard_map/ppermute | solution.py:19
  40.7 3.3 %collective-permute-start.14 = (bf16[512,128]{1,0:T(8,128)(2,1)}, bf16[512,128]{1,0:T(8,128)(2,1)S(1)}, u32[]{:S(2)}, u32[]{:S(2)}) collective-permute-start(bf16[512,128]{1,0:T(8,128)(2,1)} %param.10), channel_id=1, source_target_pairs={{0,32},{16,48},{32,0},{48,16},{1,33},{17,49},{33,1},{49,17},{2,34}... | collective-permute-start | bytes 393224 | tf_op jit(solution)/shard_map/ppermute | solution.py:19
  44.0 5.3 %collective-permute-done.13 = bf16[512,128]{1,0:T(8,128)(2,1)S(1)} collective-permute-done((bf16[512,128]{1,0:T(8,128)(2,1)}, bf16[512,128]{1,0:T(8,128)(2,1)S(1)}, u32[]{:S(2)}, u32[]{:S(2)}) %collective-permute-start.13) | collective-permute-done | bytes 131104 | tf_op jit(solution)/shard_map/ppermute | solution.py:19
  49.4 3.3 %collective-permute-done.15 = bf16[512,128]{1,0:T(8,128)(2,1)S(1)} collective-permute-done((bf16[512,128]{1,0:T(8,128)(2,1)}, bf16[512,128]{1,0:T(8,128)(2,1)S(1)}, u32[]{:S(2)}, u32[]{:S(2)}) %collective-permute-start.15) | collective-permute-done | bytes 131104 | tf_op jit(solution)/shard_map/ppermute | solution.py:19
  54.8 4.4 %collective-permute-start.5 = (bf16[128,1792]{1,0:T(8,128)(2,1)}, bf16[128,1792]{1,0:T(8,128)(2,1)}, u32[]{:S(2)}, u32[]{:S(2)}) collective-permute-start(bf16[128,1792]{1,0:T(8,128)(2,1)} %bitcast.84), channel_id=1, source_target_pairs={{0,16},{16,32},{32,48},{48,0},{1,17},{17,33},{33,49},{49,1},{2,18}... | collective-permute-start | bytes 1376264 | tf_op jit(solution)/shard_map/ppermute | solution.py:19
  59.2 1.6 collective-permute-start.12
  60.7 8.8 %collective-permute-done.12.a3 = bf16[128,512]{1,0:T(8,128)(2,1)S(1)} collective-permute-done((bf16[128,512]{1,0:T(8,128)(2,1)}, bf16[128,512]{1,0:T(8,128)(2,1)S(1)}, u32[]{:S(2)}, u32[]{:S(2)}) %collective-permute-start.12) | collective-permute-done | bytes 131104 | tf_op jit(solution)/shard_map/ppermute | solution.py:19
  69.5 2.0 collective-permute-start.11
  71.5 8.5 %collective-permute-done.11.a2 = bf16[128,512]{1,0:T(8,128)(2,1)S(1)} collective-permute-done((bf16[128,512]{1,0:T(8,128)(2,1)}, bf16[128,512]{1,0:T(8,128)(2,1)S(1)}, u32[]{:S(2)}, u32[]{:S(2)}) %collective-permute-start.11) | collective-permute-done | bytes 131104 | tf_op jit(solution)/shard_map/ppermute | solution.py:19
  81.8 1.5 constant_dynamic-slice_fusion.1.q
  83.3 1.9 collective-permute-done.10.a1
  86.7 3.9 %rotate_in.1 = (bf16[512,1024]{1,0:T(8,128)(2,1)}, bf16[64,1024]{1,0:T(8,128)(2,1)}) custom-call(s32[5]{0:T(128)} %stack.72.at_ref, bf16[128,512]{1,0:T(8,128)(2,1)} %bitcast.98, bf16[128,512]{1,0:T(8,128)(2,1)} %copy-done.22, bf16[128,512]{1,0:T(8,128)(2,1)} %copy-done.21, bf16[128,512]{1,0:T(8,128)(2,1)} %copy-done.20, ...), custom_call_target="tpu_custom_call" | custom-call | flops 536870912 | bytes 2621440 | tf_op jit(solution)/shard_map/rotate_in/pallas_call | solution.py:74
  90.6 5.0 %all-to-all-start = ((bf16[4,128,1024]{2,1,0:T(8,128)(2,1)}), bf16[4,128,1024]{2,1,0:T(8,128)(2,1)S(1)}, u32[]{:S(2)}, u32[]{:S(2)}) async-start(bf16[4,128,1024]{2,1,0:T(8,128)(2,1)} %bitcast.82), calls=%async_computation | async-start | bytes 2097152 | tf_op jit(solution)/shard_map/all_to_all | solution.py:37
  95.6 2.2 pad_maximum_fusion.1
  97.9 9.3 %all-to-all-done = bf16[4,128,1024]{2,1,0:T(8,128)(2,1)S(1)} async-done(((bf16[4,128,1024]{2,1,0:T(8,128)(2,1)}), bf16[4,128,1024]{2,1,0:T(8,128)(2,1)S(1)}, u32[]{:S(2)}, u32[]{:S(2)}) %all-to-all-start) | async-done | bytes 1048608 | tf_op jit(solution)/shard_map/all_to_all | solution.py:37
  108.7 1.8 pad_maximum_fusion
  110.5 1.7 copy-done.2
  114.0 6.0 %all-to-all-start.1 = ((bf16[8,8,1920]{2,1,0:T(8,128)(2,1)}), bf16[8,8,1920]{2,1,0:T(8,128)(2,1)S(1)}, u32[]{:S(2)}, u32[]{:S(2)}) async-start(bf16[8,8,1920]{2,1,0:T(8,128)(2,1)} %maximum_bitcast_fusion), calls=%async_computation.1 | async-start | bytes 491520 | tf_op jit(solution)/shard_map/all_to_all | solution.py:37
  120.1 2.1 collective-permute-start.20
  122.2 6.5 %collective-permute-start.19 = (bf16[128,1024]{1,0:T(8,128)(2,1)S(1)}, bf16[128,1024]{1,0:T(8,128)(2,1)S(1)}, u32[]{:S(2)}, u32[]{:S(2)}) collective-permute-start(bf16[128,1024]{1,0:T(8,128)(2,1)S(1)} %add_convert_fusion), channel_id=1, source_target_pairs={{0,32},{20,52},{32,0},{52,20},{1,33},{21,53},{33,1},{53,21},{2,34}... | collective-permute-start | bytes 786440 | tf_op jit(solution)/shard_map/ppermute | solution.py:28
  128.7 1.5 collective-permute-start.18
  130.2 6.0 %convert_divide_fusion.1.inv0 = f32[448,4096]{1,0:T(8,128)} fusion(bf16[448,4096]{1,0:T(8,128)(2,1)} %param.11), kind=kLoop, calls=%fused_computation.1 | loop fusion | flops 3670016 | bytes 11010048 | tf_op jit(solution)/shard_map/div | solution.py:226
  136.9 4.8 %all-to-all-start.2 = ((bf16[8,8,1920]{2,1,0:T(8,128)(2,1)}), bf16[8,8,1920]{2,1,0:T(8,128)(2,1)S(1)}, u32[]{:S(2)}, u32[]{:S(2)}) async-start(bf16[8,8,1920]{2,1,0:T(8,128)(2,1)} %broadcast_in_dim.6), calls=%async_computation.2 | async-start | bytes 491520 | tf_op jit(solution)/shard_map/all_to_all | solution.py:37
  142.7 4.4 %all-to-all-done.2 = bf16[8,8,1920]{2,1,0:T(8,128)(2,1)S(1)} async-done(((bf16[8,8,1920]{2,1,0:T(8,128)(2,1)}), bf16[8,8,1920]{2,1,0:T(8,128)(2,1)S(1)}, u32[]{:S(2)}, u32[]{:S(2)}) %all-to-all-start.2) | async-done | bytes 245792 | tf_op jit(solution)/shard_map/all_to_all | solution.py:37
  147.8 1.4 collective-permute-start.23
  149.1 2.9 %collective-permute-start.22 = (bf16[320,1024]{1,0:T(8,128)(2,1)S(1)}, bf16[320,1024]{1,0:T(8,128)(2,1)}, u32[]{:S(2)}, u32[]{:S(2)}) collective-permute-start(bf16[320,1024]{1,0:T(8,128)(2,1)S(1)} %pad_maximum_fusion.2.v0), channel_id=1, source_target_pairs={{0,128},{64,192},{128,0},{192,64},{1,129},{65,193},{129,1},{193,65... | collective-permute-start | bytes 1966088 | tf_op jit(solution)/shard_map/ppermute | solution.py:19
  153.8 4.6 %convolution_convert_fusion.2 = bf16[896,512]{0,1:T(8,128)(2,1)S(1)} fusion(bf16[896,1792]{1,0:T(8,128)(2,1)} %copy-done.2, bf16[512,1792]{1,0:T(8,128)(2,1)} %bitcast.94), kind=kOutput, calls=%fused_computation.5 | convolution fusion | flops 1644625920 | bytes 5963776 | tf_op jit(solution)/shard_map/dot_general | solution.py:49
  160.1 4.6 %convolution_convert_fusion.1 = bf16[896,512]{0,1:T(8,128)(2,1)S(1)} fusion(bf16[896,1792]{1,0:T(8,128)(2,1)} %copy-done.2, bf16[512,1792]{1,0:T(8,128)(2,1)} %all-gather.9.cloned.1.call-done), kind=kOutput, calls=%fused_computation.4 | convolution fusion | flops 1644625920 | bytes 5963776 | tf_op jit(solution)/shard_map/dot_general | solution.py:49
  166.6 1.8 collective-permute-start.30
  168.4 7.0 %convolution_convert_fusion = bf16[1024,896]{1,0:T(8,128)(2,1)S(1)} fusion(bf16[1024,1792]{1,0:T(8,128)(2,1)} %bitcast.93, bf16[896,1792]{1,0:T(8,128)(2,1)} %copy-done.2), kind=kOutput, calls=%fused_computation.3 | convolution fusion | flops 3289251840 | bytes 8716288 | tf_op jit(solution)/shard_map/dot_general | solution.py:49
  175.9 5.4 %collective-permute-done.22.v2 = bf16[320,1024]{1,0:T(8,128)(2,1)} collective-permute-done((bf16[320,1024]{1,0:T(8,128)(2,1)S(1)}, bf16[320,1024]{1,0:T(8,128)(2,1)}, u32[]{:S(2)}, u32[]{:S(2)}) %collective-permute-start.22) | collective-permute-done | bytes 655392 | tf_op jit(solution)/shard_map/ppermute | solution.py:19
  181.3 1.8 collective-permute-start.8
  184.3 2.3 collective-permute-start.28
  186.6 1.8 collective-permute-start.6
  189.4 12.4 %collective-permute-done.28.refs_1_ = bf16[1,128,896]{2,1,0:T(8,128)(2,1)S(1)} collective-permute-done((bf16[1,128,896]{2,1,0:T(8,128)(2,1)S(1)}, bf16[1,128,896]{2,1,0:T(8,128)(2,1)S(1)}, u32[]{:S(2)}, u32[]{:S(2)}) %collective-permute-start.28) | collective-permute-done | bytes 229408 | tf_op jit(solution)/shard_map/ppermute | solution.py:19
  204.0 1.9 collective-permute-start.1
  207.7 3.8 %collective-permute-done.6.refs_5_ = bf16[2,128,896]{2,1,0:T(8,128)(2,1)S(1)} collective-permute-done((bf16[2,128,896]{2,1,0:T(8,128)(2,1)S(1)}, bf16[2,128,896]{2,1,0:T(8,128)(2,1)S(1)}, u32[]{:S(2)}, u32[]{:S(2)}) %collective-permute-start.6) | collective-permute-done | bytes 458784 | tf_op jit(solution)/shard_map/ppermute | solution.py:19
  212.4 3.0 %shard_map.75 = (bf16[128,896]{1,0:T(8,128)(2,1)}, bf16[128,896]{1,0:T(8,128)(2,1)}) custom-call(s32[5]{0:T(128)} %stack.72.at_ref, bf16[4,1,128,896]{3,2,1,0:T(8,128)(2,1)} %bitcast.76, bf16[1,128,896]{2,1,0:T(8,128)(2,1)} %copy-done.17, bf16[1,128,896]{2,1,0:T(8,128)(2,1)} %copy-done.15, bf16[1,128,896]{2,1,0:T(8,128)(2,1)} %collective-permute-done.30.refs_3_, ...), custom_call_target="tpu_custom_call" | custom-call | flops 917504 | bytes 2293760 | tf_op jit(solution)/shard_map/pallas_call | solution.py:120
  216.7 3.2 %collective-permute-done.1.refs_1_ = bf16[1,128,896]{2,1,0:T(8,128)(2,1)} collective-permute-done((bf16[1,128,896]{2,1,0:T(8,128)(2,1)}, bf16[1,128,896]{2,1,0:T(8,128)(2,1)}, u32[]{:S(2)}, u32[]{:S(2)}) %collective-permute-start.1) | collective-permute-done | bytes 229408 | tf_op jit(solution)/shard_map/ppermute | solution.py:19
  219.9 3.0 %shard_map.73 = (bf16[128,896]{1,0:T(8,128)(2,1)}, bf16[128,896]{1,0:T(8,128)(2,1)}) custom-call(s32[5]{0:T(128)} %stack.72.at_ref, bf16[4,1,128,896]{3,2,1,0:T(8,128)(2,1)} %bitcast.74, bf16[1,128,896]{2,1,0:T(8,128)(2,1)} %collective-permute-done.1.refs_1_, bf16[1,128,896]{2,1,0:T(8,128)(2,1)} %collective-permute-done.2.refs_2_, ...), custom_call_target="tpu_custom_call" | custom-call | flops 917504 | bytes 2293760 | tf_op jit(solution)/shard_map/pallas_call | solution.py:120
  224.2 6.0 %convert_divide_fusion.inv1 = f32[448,4096]{1,0:T(8,128)} fusion(bf16[448,4096]{1,0:T(8,128)(2,1)} %collective-permute-done.25), kind=kLoop, calls=%fused_computation | loop fusion | flops 3670016 | bytes 11010048 | tf_op jit(solution)/shard_map/div | solution.py:227
  231.2 11.2 %shard_map.74 = f32[8,128]{1,0:T(8,128)} custom-call(s32[5]{0:T(128)} %stack.72.at_ref, bf16[128,896]{1,0:T(8,128)(2,1)} %get-tuple-element.11.keep, bf16[128,896]{1,0:T(8,128)(2,1)} %copy-done.14, bf16[320,1024]{1,0:T(8,128)(2,1)} %copy-done.3, bf16[320,1024]{1,0:T(8,128)(2,1)} %collective-permute-done.21.v1, bf16[320,1024]{1,0:T(8,128)(2,1)} %collective-permute-done.22.v2, ...), custom_call_target="tpu_custom_call" | custom-call | flops 1879048192 | bytes 14680064 | tf_op jit(solution)/shard_map/pallas_call | solution.py:197
  243.0 11.3 %shard_map.76 = f32[8,128]{1,0:T(8,128)} custom-call(s32[5]{0:T(128)} %stack.72.at_ref, bf16[128,896]{1,0:T(8,128)(2,1)} %get-tuple-element.15.keep, bf16[128,896]{1,0:T(8,128)(2,1)} %copy-done.13, bf16[320,1024]{1,0:T(8,128)(2,1)} %copy-done.3, bf16[320,1024]{1,0:T(8,128)(2,1)} %collective-permute-done.21.v1, bf16[320,1024]{1,0:T(8,128)(2,1)} %collective-permute-done.22.v2, ...), custom_call_target="tpu_custom_call" | custom-call | flops 1879048192 | bytes 14680064 | tf_op jit(solution)/shard_map/pallas_call | solution.py:197
  255.4 14.5 %all_to_all.25 = f32[16,2,16]{2,1,0:T(2,128)S(1)} all-to-all(f32[16,2,16]{2,1,0:T(2,128)S(1)} %broadcast_in_dim.7), channel_id=1, replica_groups=mesh['y'=4,'zh'=4,'c'=2,'zl'=2,'x'=4] {'y','zh'}, dimensions={0} | all-to-all | bytes 4096 | tf_op jit(solution)/shard_map/all_to_all | solution.py:37
  270.5 6.5 %all-to-all-start.4 = ((f32[16,2,16]{2,1,0:T(2,128)}), f32[16,2,16]{2,1,0:T(2,128)S(1)}, u32[]{:S(2)}, u32[]{:S(2)}) async-start(f32[16,2,16]{2,1,0:T(2,128)} %broadcast_in_dim.8), calls=%async_computation.4 | async-start | bytes 32768 | tf_op jit(solution)/shard_map/all_to_all | solution.py:37
  276.9 4.8 %all-to-all-done.4 = f32[16,2,16]{2,1,0:T(2,128)S(1)} async-done(((f32[16,2,16]{2,1,0:T(2,128)}), f32[16,2,16]{2,1,0:T(2,128)S(1)}, u32[]{:S(2)}, u32[]{:S(2)}) %all-to-all-start.4) | async-done | bytes 2080 | tf_op jit(solution)/shard_map/all_to_all | solution.py:37
  (135 shorter events, 32.0 us)
Async XLA Ops:
  6.5 103.9 %copy-start = (bf16[16,8,1792]{2,1,0:T(8,128)(2,1)S(1)}, bf16[16,8,1792]{2,1,0:T(8,128)(2,1)}, u32[]{:S(2)}) copy-start(bf16[16,8,1792]{2,1,0:T(8,128)(2,1)} %param.12) | copy-start | bytes 1376260
  6.5 147.2 %all-gather.5.cloned.1.call-start = ((), (), s32[]{:S(2)}) async-start(), calls=%async_computation.5 | async-start | bytes 2293760 | tf_op jit(solution)/shard_map/all_gather | solution.py:260
  7.3 152.9 %all-gather.9.cloned.1.call-start = ((), (), s32[]{:S(2)}) async-start(), calls=%async_computation.7 | async-start | bytes 2293760 | tf_op jit(solution)/shard_map/all_gather | solution.py:260
  7.3 20.3 %collective-permute-start.27 = (bf16[128,1792]{1,0:T(8,128)(2,1)}, bf16[128,1792]{1,0:T(8,128)(2,1)S(1)}, u32[]{:S(2)}, u32[]{:S(2)}) collective-permute-start(bf16[128,1792]{1,0:T(8,128)(2,1)} %bitcast.83), channel_id=1, source_target_pairs={{0,32},{16,48},{32,0},{48,16},{1,33},{17,49},{33,1},{49,17},{2,34}... | collective-permute-start | bytes 1376264 | tf_op jit(solution)/shard_map/ppermute | solution.py:19
  28.4 21.0 %collective-permute-start.13 = (bf16[512,128]{1,0:T(8,128)(2,1)}, bf16[512,128]{1,0:T(8,128)(2,1)S(1)}, u32[]{:S(2)}, u32[]{:S(2)}) collective-permute-start(bf16[512,128]{1,0:T(8,128)(2,1)} %param.10), channel_id=1, source_target_pairs={{0,48},{16,0},{32,16},{48,32},{1,49},{17,1},{33,17},{49,33},{2,50}... | collective-permute-start | bytes 393224 | tf_op jit(solution)/shard_map/ppermute | solution.py:19
  40.7 12.0 %collective-permute-start.15 = (bf16[512,128]{1,0:T(8,128)(2,1)}, bf16[512,128]{1,0:T(8,128)(2,1)S(1)}, u32[]{:S(2)}, u32[]{:S(2)}) collective-permute-start(bf16[512,128]{1,0:T(8,128)(2,1)} %param.10), channel_id=1, source_target_pairs={{0,16},{16,32},{32,48},{48,0},{1,17},{17,33},{33,49},{49,1},{2,18}... | collective-permute-start | bytes 393224 | tf_op jit(solution)/shard_map/ppermute | solution.py:19
  40.7 13.0 %collective-permute-start.14 = (bf16[512,128]{1,0:T(8,128)(2,1)}, bf16[512,128]{1,0:T(8,128)(2,1)S(1)}, u32[]{:S(2)}, u32[]{:S(2)}) collective-permute-start(bf16[512,128]{1,0:T(8,128)(2,1)} %param.10), channel_id=1, source_target_pairs={{0,32},{16,48},{32,0},{48,16},{1,33},{17,49},{33,1},{49,17},{2,34}... | collective-permute-start | bytes 393224 | tf_op jit(solution)/shard_map/ppermute | solution.py:19
  44.0 64.6 %collective-permute-start = (bf16[448,1792]{1,0:T(8,128)(2,1)}, bf16[448,1792]{1,0:T(8,128)(2,1)}, u32[]{:S(2)}, u32[]{:S(2)}) collective-permute-start(bf16[448,1792]{1,0:T(8,128)(2,1)} %bitcast.77), channel_id=1, source_target_pairs={{0,8},{8,0},{1,9},{9,1},{2,10},{10,2},{3,11},{11,3},{4,12},{12,4},... | collective-permute-start | bytes 4816904 | tf_op jit(solution)/shard_map/ppermute | solution.py:19
  54.7 30.5 %copy-start.11 = (bf16[4,512,128]{2,1,0:T(8,128)(2,1)}, bf16[4,512,128]{2,1,0:T(8,128)(2,1)S(1)}, u32[]{:S(2)}) copy-start(bf16[4,512,128]{2,1,0:T(8,128)(2,1)S(1)} %pad_maximum_fusion.3.w0) | copy-start | bytes 1572868
  54.7 30.5 %collective-permute-start.16 = (bf16[4,512,128]{2,1,0:T(8,128)(2,1)S(1)}, bf16[4,512,128]{2,1,0:T(8,128)(2,1)S(1)}, u32[]{:S(2)}, u32[]{:S(2)}) collective-permute-start(bf16[4,512,128]{2,1,0:T(8,128)(2,1)S(1)} %pad_maximum_fusion.3.w0), channel_id=1, source_target_pairs={{0,8},{8,0},{1,9},{9,1},{2,10},{10,2},{3,11},{11,3},{4,12},{12,4},... | collective-permute-start | bytes 1572872 | tf_op jit(solution)/shard_map/ppermute | solution.py:19
  54.8 40.8 %collective-permute-start.5 = (bf16[128,1792]{1,0:T(8,128)(2,1)}, bf16[128,1792]{1,0:T(8,128)(2,1)}, u32[]{:S(2)}, u32[]{:S(2)}) collective-permute-start(bf16[128,1792]{1,0:T(8,128)(2,1)} %bitcast.84), channel_id=1, source_target_pairs={{0,16},{16,32},{32,48},{48,0},{1,17},{17,33},{33,49},{49,1},{2,18}... | collective-permute-start | bytes 1376264 | tf_op jit(solution)/shard_map/ppermute | solution.py:19
  59.2 36.4 %collective-permute-start.4 = (bf16[128,1792]{1,0:T(8,128)(2,1)}, bf16[128,1792]{1,0:T(8,128)(2,1)}, u32[]{:S(2)}, u32[]{:S(2)}) collective-permute-start(bf16[128,1792]{1,0:T(8,128)(2,1)} %bitcast.85), channel_id=1, source_target_pairs={{0,48},{16,0},{32,16},{48,32},{1,49},{17,1},{33,17},{49,33},{2,50}... | collective-permute-start | bytes 1376264 | tf_op jit(solution)/shard_map/ppermute | solution.py:19
  59.2 10.4 %collective-permute-start.12 = (bf16[128,512]{1,0:T(8,128)(2,1)}, bf16[128,512]{1,0:T(8,128)(2,1)S(1)}, u32[]{:S(2)}, u32[]{:S(2)}) collective-permute-start(bf16[128,512]{1,0:T(8,128)(2,1)} %bitcast.95), channel_id=1, source_target_pairs={{0,64},{64,128},{128,192},{192,0},{1,65},{65,129},{129,193},{193,1... | collective-permute-start | bytes 393224 | tf_op jit(solution)/shard_map/ppermute | solution.py:19
  69.5 15.7 %copy-start.20 = (bf16[128,512]{1,0:T(8,128)(2,1)}, bf16[128,512]{1,0:T(8,128)(2,1)S(1)}, u32[]{:S(2)}) copy-start(bf16[128,512]{1,0:T(8,128)(2,1)S(1)} %collective-permute-done.12.a3) | copy-start | bytes 393220
  69.5 10.5 %collective-permute-start.11 = (bf16[128,512]{1,0:T(8,128)(2,1)}, bf16[128,512]{1,0:T(8,128)(2,1)S(1)}, u32[]{:S(2)}, u32[]{:S(2)}) collective-permute-start(bf16[128,512]{1,0:T(8,128)(2,1)} %bitcast.96), channel_id=1, source_target_pairs={{0,128},{64,192},{128,0},{192,64},{1,129},{65,193},{129,1},{193,65... | collective-permute-start | bytes 393224 | tf_op jit(solution)/shard_map/ppermute | solution.py:19
  80.0 5.2 %collective-permute-start.10 = (bf16[128,512]{1,0:T(8,128)(2,1)}, bf16[128,512]{1,0:T(8,128)(2,1)S(1)}, u32[]{:S(2)}, u32[]{:S(2)}) collective-permute-start(bf16[128,512]{1,0:T(8,128)(2,1)} %bitcast.97), channel_id=1, source_target_pairs={{0,192},{64,0},{128,64},{192,128},{1,193},{65,1},{129,65},{193,129... | collective-permute-start | bytes 393224 | tf_op jit(solution)/shard_map/ppermute | solution.py:19
  90.6 18.1 %copy-start.10 = (bf16[1792,448]{0,1:T(8,128)(2,1)S(1)}, bf16[1792,448]{0,1:T(8,128)(2,1)}, u32[]{:S(2)}) copy-start(bf16[1792,448]{0,1:T(8,128)(2,1)} %param.9) | copy-start | bytes 4816900
  90.6 16.6 %all-to-all-start = ((bf16[4,128,1024]{2,1,0:T(8,128)(2,1)}), bf16[4,128,1024]{2,1,0:T(8,128)(2,1)S(1)}, u32[]{:S(2)}, u32[]{:S(2)}) async-start(bf16[4,128,1024]{2,1,0:T(8,128)(2,1)} %bitcast.82), calls=%async_computation | async-start | bytes 2097152 | tf_op jit(solution)/shard_map/all_to_all | solution.py:37
  95.5 72.8 %all-gather.7.cloned.1.call-start = ((), (), s32[]{:S(2)}) async-start(), calls=%async_computation.6 | async-start | bytes 4587520 | tf_op jit(solution)/shard_map/all_gather | solution.py:260
  97.8 126.5 %collective-permute-start.25 = (bf16[448,4096]{1,0:T(8,128)(2,1)}, bf16[448,4096]{1,0:T(8,128)(2,1)}, u32[]{:S(2)}, u32[]{:S(2)}) collective-permute-start(bf16[448,4096]{1,0:T(8,128)(2,1)} %param.11), channel_id=1, source_target_pairs={{0,8},{8,0},{1,9},{9,1},{2,10},{10,2},{3,11},{11,3},{4,12},{12,4},... | collective-permute-start | bytes 11010056 | tf_op jit(solution)/shard_map/ppermute | solution.py:19
  107.3 12.6 %collective-permute-start.17 = (bf16[128,1024]{1,0:T(8,128)(2,1)S(1)}, bf16[128,1024]{1,0:T(8,128)(2,1)S(1)}, u32[]{:S(2)}, u32[]{:S(2)}) collective-permute-start(bf16[128,1024]{1,0:T(8,128)(2,1)S(1)} %reduce_sum.42), channel_id=1, source_target_pairs={{4,0},{16,20},{36,32},{48,52},{5,1},{17,21},{37,33},{49,53},{6,2},... | collective-permute-start | bytes 786440 | tf_op jit(solution)/shard_map/ppermute | solution.py:33
  114.0 22.2 %all-to-all-start.1 = ((bf16[8,8,1920]{2,1,0:T(8,128)(2,1)}), bf16[8,8,1920]{2,1,0:T(8,128)(2,1)S(1)}, u32[]{:S(2)}, u32[]{:S(2)}) async-start(bf16[8,8,1920]{2,1,0:T(8,128)(2,1)} %maximum_bitcast_fusion), calls=%async_computation.1 | async-start | bytes 491520 | tf_op jit(solution)/shard_map/all_to_all | solution.py:37
  120.1 22.3 %collective-permute-start.20 = (bf16[128,1024]{1,0:T(8,128)(2,1)S(1)}, bf16[128,1024]{1,0:T(8,128)(2,1)S(1)}, u32[]{:S(2)}, u32[]{:S(2)}) collective-permute-start(bf16[128,1024]{1,0:T(8,128)(2,1)S(1)} %add_convert_fusion), channel_id=1, source_target_pairs={{0,48},{20,4},{32,16},{52,36},{1,49},{21,5},{33,17},{53,37},{2,50}... | collective-permute-start | bytes 786440 | tf_op jit(solution)/shard_map/ppermute | solution.py:28
  122.2 20.5 %collective-permute-start.19 = (bf16[128,1024]{1,0:T(8,128)(2,1)S(1)}, bf16[128,1024]{1,0:T(8,128)(2,1)S(1)}, u32[]{:S(2)}, u32[]{:S(2)}) collective-permute-start(bf16[128,1024]{1,0:T(8,128)(2,1)S(1)} %add_convert_fusion), channel_id=1, source_target_pairs={{0,32},{20,52},{32,0},{52,20},{1,33},{21,53},{33,1},{53,21},{2,34}... | collective-permute-start | bytes 786440 | tf_op jit(solution)/shard_map/ppermute | solution.py:28
  128.7 13.7 %collective-permute-start.18 = (bf16[128,1024]{1,0:T(8,128)(2,1)S(1)}, bf16[128,1024]{1,0:T(8,128)(2,1)S(1)}, u32[]{:S(2)}, u32[]{:S(2)}) collective-permute-start(bf16[128,1024]{1,0:T(8,128)(2,1)S(1)} %add_convert_fusion), channel_id=1, source_target_pairs={{0,16},{20,36},{32,48},{52,4},{1,17},{21,37},{33,49},{53,5},{2,18}... | collective-permute-start | bytes 786440 | tf_op jit(solution)/shard_map/ppermute | solution.py:28
  136.9 10.2 %all-to-all-start.2 = ((bf16[8,8,1920]{2,1,0:T(8,128)(2,1)}), bf16[8,8,1920]{2,1,0:T(8,128)(2,1)S(1)}, u32[]{:S(2)}, u32[]{:S(2)}) async-start(bf16[8,8,1920]{2,1,0:T(8,128)(2,1)} %broadcast_in_dim.6), calls=%async_computation.2 | async-start | bytes 491520 | tf_op jit(solution)/shard_map/all_to_all | solution.py:37
  147.6 5.3 %collective-permute-start.26 = (bf16[64,896]{0,1:T(8,128)(2,1)S(1)}, bf16[64,896]{0,1:T(8,128)(2,1)S(1)}, u32[]{:S(2)}, u32[]{:S(2)}) collective-permute-start(bf16[64,896]{0,1:T(8,128)(2,1)S(1)} %pad_maximum_fusion.5), channel_id=1, source_target_pairs={{0,8},{8,0},{1,9},{9,1},{2,10},{10,2},{3,11},{11,3},{4,12},{12,4},... | collective-permute-start | bytes 344072 | tf_op jit(solution)/shard_map/ppermute | solution.py:19
  147.7 10.6 %copy-start.3 = (bf16[320,1024]{1,0:T(8,128)(2,1)}, bf16[320,1024]{1,0:T(8,128)(2,1)S(1)}, u32[]{:S(2)}) copy-start(bf16[320,1024]{1,0:T(8,128)(2,1)S(1)} %pad_maximum_fusion.2.v0) | copy-start | bytes 1966084
  147.8 27.8 %collective-permute-start.23 = (bf16[320,1024]{1,0:T(8,128)(2,1)S(1)}, bf16[320,1024]{1,0:T(8,128)(2,1)}, u32[]{:S(2)}, u32[]{:S(2)}) collective-permute-start(bf16[320,1024]{1,0:T(8,128)(2,1)S(1)} %pad_maximum_fusion.2.v0), channel_id=1, source_target_pairs={{0,64},{64,128},{128,192},{192,0},{1,65},{65,129},{129,193},{193,1... | collective-permute-start | bytes 1966088 | tf_op jit(solution)/shard_map/ppermute | solution.py:19
  149.1 32.2 %collective-permute-start.22 = (bf16[320,1024]{1,0:T(8,128)(2,1)S(1)}, bf16[320,1024]{1,0:T(8,128)(2,1)}, u32[]{:S(2)}, u32[]{:S(2)}) collective-permute-start(bf16[320,1024]{1,0:T(8,128)(2,1)S(1)} %pad_maximum_fusion.2.v0), channel_id=1, source_target_pairs={{0,128},{64,192},{128,0},{192,64},{1,129},{65,193},{129,1},{193,65... | collective-permute-start | bytes 1966088 | tf_op jit(solution)/shard_map/ppermute | solution.py:19
  152.1 31.1 %collective-permute-start.21 = (bf16[320,1024]{1,0:T(8,128)(2,1)S(1)}, bf16[320,1024]{1,0:T(8,128)(2,1)}, u32[]{:S(2)}, u32[]{:S(2)}) collective-permute-start(bf16[320,1024]{1,0:T(8,128)(2,1)S(1)} %pad_maximum_fusion.2.v0), channel_id=1, source_target_pairs={{0,192},{64,0},{128,64},{192,128},{1,193},{65,1},{129,65},{193,129... | collective-permute-start | bytes 1966088 | tf_op jit(solution)/shard_map/ppermute | solution.py:19
  166.6 17.7 %collective-permute-start.30 = (bf16[1,128,896]{2,1,0:T(8,128)(2,1)}, bf16[1,128,896]{2,1,0:T(8,128)(2,1)}, u32[]{:S(2)}, u32[]{:S(2)}) collective-permute-start(bf16[1,128,896]{2,1,0:T(8,128)(2,1)} %get-tuple-element.23), channel_id=1, source_target_pairs={{0,3},{1,0},{2,1},{3,2},{4,7},{5,4},{6,5},{7,6},{8,11},{9,8},{10,9... | collective-permute-start | bytes 688136 | tf_op jit(solution)/shard_map/ppermute | solution.py:19
  168.4 16.0 %copy-start.16 = (bf16[1,128,896]{2,1,0:T(8,128)(2,1)S(1)}, bf16[1,128,896]{2,1,0:T(8,128)(2,1)}, u32[]{:S(2)}) copy-start(bf16[1,128,896]{2,1,0:T(8,128)(2,1)} %get-tuple-element.25) | copy-start | bytes 688132
  175.4 36.9 %copy-start.1 = (bf16[1024,896]{1,0:T(8,128)(2,1)}, bf16[1024,896]{1,0:T(8,128)(2,1)S(1)}, u32[]{:S(2)}) copy-start(bf16[1024,896]{1,0:T(8,128)(2,1)S(1)} %convolution_convert_fusion) | copy-start | bytes 5505028
  175.6 11.1 %collective-permute-start.29 = (bf16[1,128,896]{2,1,0:T(8,128)(2,1)}, bf16[1,128,896]{2,1,0:T(8,128)(2,1)S(1)}, u32[]{:S(2)}, u32[]{:S(2)}) collective-permute-start(bf16[1,128,896]{2,1,0:T(8,128)(2,1)} %get-tuple-element.24), channel_id=1, source_target_pairs={{0,2},{1,3},{2,0},{3,1},{4,6},{5,7},{6,4},{7,5},{8,10},{9,11},{10,... | collective-permute-start | bytes 688136 | tf_op jit(solution)/shard_map/ppermute | solution.py:19
  181.3 20.9 %collective-permute-start.8 = (bf16[2,128,896]{2,1,0:T(8,128)(2,1)S(1)}, bf16[2,128,896]{2,1,0:T(8,128)(2,1)S(1)}, u32[]{:S(2)}, u32[]{:S(2)}) collective-permute-start(bf16[2,128,896]{2,1,0:T(8,128)(2,1)S(1)} %get-tuple-element.17), channel_id=1, source_target_pairs={{0,3},{1,0},{2,1},{3,2},{4,7},{5,4},{6,5},{7,6},{8,11},{9,8},{10,9... | collective-permute-start | bytes 1376264 | tf_op jit(solution)/shard_map/ppermute | solution.py:19
  183.1 20.9 %collective-permute-start.7 = (bf16[2,128,896]{2,1,0:T(8,128)(2,1)S(1)}, bf16[2,128,896]{2,1,0:T(8,128)(2,1)S(1)}, u32[]{:S(2)}, u32[]{:S(2)}) collective-permute-start(bf16[2,128,896]{2,1,0:T(8,128)(2,1)S(1)} %get-tuple-element.18), channel_id=1, source_target_pairs={{0,2},{1,3},{2,0},{3,1},{4,6},{5,7},{6,4},{7,5},{8,10},{9,11},{10,... | collective-permute-start | bytes 1376264 | tf_op jit(solution)/shard_map/ppermute | solution.py:19
  184.3 17.4 %collective-permute-start.28 = (bf16[1,128,896]{2,1,0:T(8,128)(2,1)S(1)}, bf16[1,128,896]{2,1,0:T(8,128)(2,1)S(1)}, u32[]{:S(2)}, u32[]{:S(2)}) collective-permute-start(bf16[1,128,896]{2,1,0:T(8,128)(2,1)S(1)} %copy-done.16), channel_id=1, source_target_pairs={{0,1},{1,2},{2,3},{3,0},{4,5},{5,6},{6,7},{7,4},{8,9},{9,10},{10,1... | collective-permute-start | bytes 688136 | tf_op jit(solution)/shard_map/ppermute | solution.py:19
  186.6 17.4 %copy-start.15 = (bf16[1,128,896]{2,1,0:T(8,128)(2,1)}, bf16[1,128,896]{2,1,0:T(8,128)(2,1)S(1)}, u32[]{:S(2)}) copy-start(bf16[1,128,896]{2,1,0:T(8,128)(2,1)S(1)} %collective-permute-done.29.refs_2_) | copy-start | bytes 688132
  186.6 24.9 %collective-permute-start.6 = (bf16[2,128,896]{2,1,0:T(8,128)(2,1)S(1)}, bf16[2,128,896]{2,1,0:T(8,128)(2,1)S(1)}, u32[]{:S(2)}, u32[]{:S(2)}) collective-permute-start(bf16[2,128,896]{2,1,0:T(8,128)(2,1)S(1)} %get-tuple-element.19), channel_id=1, source_target_pairs={{0,1},{1,2},{2,3},{3,0},{4,5},{5,6},{6,7},{7,4},{8,9},{9,10},{10,1... | collective-permute-start | bytes 1376264 | tf_op jit(solution)/shard_map/ppermute | solution.py:19
  201.7 13.6 %collective-permute-start.3 = (bf16[1,128,896]{2,1,0:T(8,128)(2,1)}, bf16[1,128,896]{2,1,0:T(8,128)(2,1)}, u32[]{:S(2)}, u32[]{:S(2)}) collective-permute-start(bf16[1,128,896]{2,1,0:T(8,128)(2,1)} %get-tuple-element.20), channel_id=1, source_target_pairs={{0,3},{1,0},{2,1},{3,2},{4,7},{5,4},{6,5},{7,6},{8,11},{9,8},{10,9... | collective-permute-start | bytes 688136 | tf_op jit(solution)/shard_map/ppermute | solution.py:19
  202.2 14.4 %collective-permute-start.2 = (bf16[1,128,896]{2,1,0:T(8,128)(2,1)}, bf16[1,128,896]{2,1,0:T(8,128)(2,1)}, u32[]{:S(2)}, u32[]{:S(2)}) collective-permute-start(bf16[1,128,896]{2,1,0:T(8,128)(2,1)} %get-tuple-element.21), channel_id=1, source_target_pairs={{0,2},{1,3},{2,0},{3,1},{4,6},{5,7},{6,4},{7,5},{8,10},{9,11},{10,... | collective-permute-start | bytes 688136 | tf_op jit(solution)/shard_map/ppermute | solution.py:19
  204.0 15.9 %collective-permute-start.1 = (bf16[1,128,896]{2,1,0:T(8,128)(2,1)}, bf16[1,128,896]{2,1,0:T(8,128)(2,1)}, u32[]{:S(2)}, u32[]{:S(2)}) collective-permute-start(bf16[1,128,896]{2,1,0:T(8,128)(2,1)} %get-tuple-element.22), channel_id=1, source_target_pairs={{0,1},{1,2},{2,3},{3,0},{4,5},{5,6},{6,7},{7,4},{8,9},{9,10},{10,1... | collective-permute-start | bytes 688136 | tf_op jit(solution)/shard_map/ppermute | solution.py:19
  212.3 18.0 %collective-permute-start.24 = (bf16[4,64,1024]{2,1,0:T(8,128)(2,1)}, bf16[4,64,1024]{2,1,0:T(8,128)(2,1)S(1)}, u32[]{:S(2)}, u32[]{:S(2)}) collective-permute-start(bf16[4,64,1024]{2,1,0:T(8,128)(2,1)} %pad_maximum_fusion.4), channel_id=1, source_target_pairs={{0,8},{8,0},{1,9},{9,1},{2,10},{10,2},{3,11},{11,3},{4,12},{12,4},... | collective-permute-start | bytes 1572872 | tf_op jit(solution)/shard_map/ppermute | solution.py:19
  215.4 27.0 %collective-permute-start.31 = (bf16[128,896]{1,0:T(8,128)(2,1)}, bf16[128,896]{1,0:T(8,128)(2,1)S(1)}, u32[]{:S(2)}, u32[]{:S(2)}) collective-permute-start(bf16[128,896]{1,0:T(8,128)(2,1)} %get-tuple-element.16), channel_id=1, source_target_pairs={{0,4},{4,0},{1,5},{5,1},{2,6},{6,2},{3,7},{7,3},{8,12},{12,8},{9,1... | collective-permute-start | bytes 688136 | tf_op jit(solution)/shard_map/ppermute | solution.py:19
  223.0 7.3 %collective-permute-start.9 = (bf16[128,896]{1,0:T(8,128)(2,1)}, bf16[128,896]{1,0:T(8,128)(2,1)S(1)}, u32[]{:S(2)}, u32[]{:S(2)}) collective-permute-start(bf16[128,896]{1,0:T(8,128)(2,1)} %get-tuple-element.12), channel_id=1, source_target_pairs={{0,4},{4,0},{1,5},{5,1},{2,6},{6,2},{3,7},{7,3},{8,12},{12,8},{9,1... | collective-permute-start | bytes 688136 | tf_op jit(solution)/shard_map/ppermute | solution.py:19
  243.0 12.0 %slice-start = ((f32[8,128]{1,0:T(8,128)}), f32[1,128]{1,0:T(1,128)S(1)}, s32[]{:S(2)}) async-start(f32[8,128]{1,0:T(8,128)} %shard_map.74), calls=%async_computation.8 | async-start | bytes 1024 | tf_op jit(solution)/shard_map/slice | solution.py:197
  270.5 11.2 %all-to-all-start.4 = ((f32[16,2,16]{2,1,0:T(2,128)}), f32[16,2,16]{2,1,0:T(2,128)S(1)}, u32[]{:S(2)}, u32[]{:S(2)}) async-start(f32[16,2,16]{2,1,0:T(2,128)} %broadcast_in_dim.8), calls=%async_computation.4 | async-start | bytes 32768 | tf_op jit(solution)/shard_map/all_to_all | solution.py:37
  (15 other events, 35.0 us)
Sparse Core Ops, SparseCore 0:
  9.1 34.1 all-gather.4
  45.1 36.7 all-gather.8
  98.2 45.2 all-gather.6

commit v6 on v5

--- a/solution.py
+++ b/solution.py
@@ -1,5 +1,3 @@
-import functools
-
 import jax
 import jax.numpy as jnp
 from jax import lax
@@ -49,12 +47,12 @@
     return lax.dot_general(a, b, (((1,), (1,)), ((), ())), preferred_element_type=F32)
 
 
-def rotate_in_kernel(at_ref, a0, a1, a2, a3, q, w0, w1, out, value, act):
+def rotate_in_kernel(at_ref, a0, a1, a2, a3, q, w0, w1, p0, p1, p2, p3, value, act):
     tokens = a0.shape[0]
     n = w0.shape[2]
     for d, a in enumerate((a0, a1, a2, a3)):
-        y = lax.rem(at_ref[0] + d, 4)
-        act[pl.ds(pl.multiple_of(y * tokens, tokens), tokens), :] = a[...]
+        far = lax.rem(at_ref[0] + d + 4 - at_ref[4], 4)
+        act[pl.ds(pl.multiple_of(far * tokens, tokens), tokens), :] = a[...]
     act[4 * tokens :, :] = q[...]
     for k, w in enumerate((w0, w1)):
         core = at_ref[2] if k == 0 else 1 - at_ref[2]
@@ -62,7 +60,8 @@
             zh = lax.rem(at_ref[1] + d, 4)
             here = pl.ds(pl.multiple_of((2 * zh + core) * n, n), n)
             product = dot(act[...], w[d]).astype(BF)
-            out[:, here] = product[: 4 * tokens]
+            for e, out in enumerate((p0, p1, p2, p3)):
+                out[:, here] = product[e * tokens : (e + 1) * tokens]
             value[:, here] = product[4 * tokens :]
 
 
@@ -74,11 +73,9 @@
     return pl.pallas_call(
         rotate_in_kernel,
         in_specs=[pl.BlockSpec(memory_space=pltpu.SMEM)] + [vmem] * 7,
-        out_specs=(vmem, vmem),
-        out_shape=(
-            jax.ShapeDtypeStruct((4 * tokens, 8 * n), BF),
-            jax.ShapeDtypeStruct((rows, 8 * n), BF),
-        ),
+        out_specs=(vmem,) * 5,
+        out_shape=(jax.ShapeDtypeStruct((tokens, 8 * n), BF),) * 4
+        + (jax.ShapeDtypeStruct((rows, 8 * n), BF),),
         scratch_shapes=[pltpu.VMEM((4 * tokens + rows, unit), BF)],
         cost_estimate=pl.CostEstimate(
             flops=2 * 32 * tokens * unit * n, bytes_accessed=2 * 16 * tokens * (unit + n), transcendentals=0
@@ -127,83 +124,89 @@
     )(at, *a[0], *b[0])
 
 
-def score_kernel(slot, at_ref, keep, got, v0, v1, v2, v3, other, inv0, inv1, query, out, flipped, total, act, held):
+def score_kernel(
+    at_ref, k0, k1, g0, g1, v0, v1, v2, v3, other, inv0, inv1, query, out, flipped, total, act, held
+):
     step = pl.program_id(0)
     n = inv0.shape[0]
-    tokens = keep.shape[0]
+    tokens = k0.shape[0]
     half = other.shape[1]
-    width = act.shape[1] // 4
+    cols = inv0.shape[1]
+    width = cols // 2
 
     @pl.when(step == 0)
     def _():
-        grad = keep[...].astype(F32) + got[...].astype(F32)
-        flipped[...] = grad.T.astype(BF)
+        for s, (keep, got) in enumerate(((k0, g0), (k1, g1))):
+            grad = keep[...].astype(F32) + got[...].astype(F32)
+            flipped[s] = grad.T.astype(BF)
         total[...] = jnp.zeros_like(total)
 
     for d, ref in enumerate((v0, v1, v2, v3)):
 
-        @pl.when(step == d)
+        @pl.when(step // 2 == d)
         def _(ref=ref):
-            act[...] = ref[slot * tokens : (slot + 1) * tokens, :]
-            held[:half, :] = ref[2 * tokens :, :]
+            here = pl.ds(pl.multiple_of(lax.rem(step, 2) * cols, cols), cols)
+            act[...] = ref[: 2 * tokens, here]
+            held[:half, :] = ref[2 * tokens :, here]
 
     held[half:, :] = other[0]
-
-    def body(e):
-        cols = slice(e * width, (e + 1) * width)
+    for e in range(2):
+        here = slice(e * width, (e + 1) * width)
         for k, inv in enumerate((inv0, inv1)):
-            here = slice(k * n, (k + 1) * n)
-            contracted = dot(flipped[here, :], act[:, cols])
-            scaled = (contracted * inv[:, cols]).astype(BF)
-            total[here, :] += dot_t(scaled, held[:, cols])
-
-    for e in range(4):
-        body(e)
+            lines = slice(k * n, (k + 1) * n)
+            for s in range(2):
+                contracted = dot(flipped[s, lines, :], act[s * tokens : (s + 1) * tokens, here])
+                scaled = (contracted * inv[:, here]).astype(BF)
+                total[s, lines, :] += dot_t(scaled, held[:, here])
 
     @pl.when(step == pl.num_programs(0) - 1)
     def _():
-        out[0:1, :] = (total[...] * query[...]).sum(0, keepdims=True)
-
-
-def score(slot, at, keep, got, acts, other, inv0, inv1, query):
-    tokens, both = keep.shape
+        for s in range(2):
+            out[s : s + 1, :] = (total[s] * query[...]).sum(0, keepdims=True)
+
+
+def score(at, grads, acts, other, inv0, inv1, query):
+    tokens, both = grads[0].shape
     n = inv0.shape[0]
-    cols = acts[0].shape[1]
+    cols = acts[0].shape[1] // 2
     half = other.shape[1]
     rows = 2 * half
 
     def whole(a):
         return pl.BlockSpec(a.shape, lambda j, at: (0,) * a.ndim)
 
+    def strip(j, at):
+        return (0, 2 * lax.rem(at[0] + j // 2, 4) + lax.rem(j, 2))
+
     spec = pltpu.PrefetchScalarGridSpec(
         num_scalar_prefetch=1,
-        grid=(4,),
-        in_specs=[whole(keep), whole(got)]
-        + [whole(a) for a in acts]
+        grid=(8,),
+        in_specs=[whole(a) for a in (*grads, *acts)]
         + [
-            pl.BlockSpec((1, half, cols), lambda j, at: (j, 0, 0)),
-            pl.BlockSpec((n, cols), lambda j, at: (0, lax.rem(at[0] + j, 4))),
-            pl.BlockSpec((n, cols), lambda j, at: (0, lax.rem(at[0] + j, 4))),
+            pl.BlockSpec((1, half, cols), lambda j, at: (j // 2, 0, lax.rem(j, 2))),
+            pl.BlockSpec((n, cols), strip),
+            pl.BlockSpec((n, cols), strip),
             whole(query),
         ],
         out_specs=pl.BlockSpec((8, rows), lambda j, at: (0, 0)),
         scratch_shapes=[
-            pltpu.VMEM((both, tokens), BF),
-            pltpu.VMEM((both, rows), F32),
-            pltpu.VMEM((tokens, cols), BF),
+            pltpu.VMEM((2, both, tokens), BF),
+            pltpu.VMEM((2, both, rows), F32),
+            pltpu.VMEM((2 * tokens, cols), BF),
             pltpu.VMEM((rows, cols), BF),
         ],
     )
     return pl.pallas_call(
-        functools.partial(score_kernel, slot),
+        score_kernel,
         grid_spec=spec,
         out_shape=jax.ShapeDtypeStruct((8, rows), F32),
         cost_estimate=pl.CostEstimate(
-            flops=2 * both * 4 * cols * (tokens + rows),
-            bytes_accessed=4 * both * 4 * cols,
+            flops=2 * 2 * both * 8 * cols * (tokens + rows),
+            bytes_accessed=4 * both * 8 * cols,
             transcendentals=0,
         ),
-    )(at, keep, got, *acts, other, inv0, inv1, query)[0]
+        name="score",
+    )(at, *grads, *acts, other, inv0, inv1, query)[:2]
 
 
 def shards(grad_out, act_in, basis_out, basis_in, eigen_vals, query_out, query_in):
@@ -230,12 +233,16 @@
     mine_in = lax.dynamic_slice_in_dim(query_in.reshape(rows, -1), ci * half_rows, half_rows, 0)
     in_own = jnp.stack(gather(basis_in, "zh"))
     in_other = shift(in_own, "c", 1)
-    part, value = rotate_in(at, gather(act_in[0], "y"), mine_in, (in_own, in_other))
-    part = exchange(part.reshape(4, tokens, -1), "x").astype(F32).sum(0).astype(BF)
+    *parts, value = rotate_in(at, gather(act_in[0], "y"), mine_in, (in_own, in_other))
+    part = parts[0].astype(F32)
+    for by in (1, 2, 3):
+        part = part + shift(parts[by], "x", by).astype(F32)
+    part = part.astype(BF)
     part = (part.astype(F32) + to_owner(part).astype(F32)).astype(BF)
     plus, far, minus = (from_owner(part, by) for by in (1, 2, 3))
 
-    query = jnp.concatenate([dot_t(mine, out_both).astype(BF), value], 1)
+    query = dot_t(mine, out_both).astype(BF)
+    query = jnp.concatenate([query, value], 1)
     some = half_rows // 8
     query = exchange(query.reshape(8, some, -1), ("zl", "x")).reshape(8, some, -1)
     query = query.astype(F32).sum(0).astype(BF)
@@ -265,16 +272,12 @@
             part = lax.dynamic_index_in_dim(product, (xi + by) % 4, 0, False)
             parts.append(shift(part, "x", by))
         blocks.append(parts)
-    result = []
-    for slot, (a, b) in enumerate(
-        (((blocks[0], 0), (blocks[1], 1)), ((blocks[2], 0), (blocks[1], 0)))
-    ):
+    keeps, gots = [], []
+    for a, b in (((blocks[0], 0), (blocks[1], 1)), ((blocks[2], 0), (blocks[1], 0))):
         keep, give = split(at, a, b)
-        got = shift(give, "zl", 1)
-        result.append(
-            score(slot, at, keep, got, act_rot, value_other, inv0, inv1, query_rot)
-        )
-    result = jnp.stack(result)
+        keeps.append(keep)
+        gots.append(shift(give, "zl", 1))
+    result = score(at, (*keeps, *gots), act_rot, value_other, inv0, inv1, query_rot)
     low = jnp.where(same, zi, (zi + 3) % 4) // 2
 
     result = result.reshape(2, queries, rank).sum(-1)

time: 292 us -> 288 us (0.986)
  Pallas kernels: 32.5 us -> 25.3 us
  waiting for transfers between devices: 87.6 us -> 94.5 us
  local copies, waits for them, and re-layouts: 18.2 us -> 14.5 us
    ppermute x28 -> x31, waiting for transfers between devices: 67.5 us -> 76.8 us  [shift(): return lax.ppermute(value, axis, [(i, (i + by) % n) for i in range(n)])]
    all_to_all x4 -> x3, waiting for transfers between devices: 18.5 us -> 9.56 us  [exchange(): return lax.all_to_all(value, axes, 0, 0, tiled=True)]
    ppermute x1, waiting for transfers between devices: 0.01 us -> 7.34 us  [to_owner(): return lax.ppermute(value, ('zh', 'zl'), pairs)]
    pallas_call x2 -> x1, Pallas kernels: 22.5 us -> 15.5 us  [score(): pl.pallas_call(score_kernel, grid_spec=spec, out_shape=jax.ShapeDtypeStru...]
    ppermute x28 -> x31, starting transfers between devices: 51.6 us -> 57.6 us  [shift(): return lax.ppermute(value, axis, [(i, (i + by) % n) for i in range(n)])]
    all_to_all x4 -> x3, starting transfers between devices: 22.2 us -> 17.4 us  [exchange(): return lax.all_to_all(value, axes, 0, 0, tiled=True)]
    unnamed x49 -> x35, local copies, waits for them, and re-layouts: 8.61 us -> 4.71 us
  transfers between devices with their start and end apart: 39 -> 41, of which waited for: 17 -> 18; matrix products, arithmetic and copies ran while one was open for 16% -> 16% of each run, Pallas kernels for 7% -> 3%
where the time goes in v6:
time: 288 us; the launch traced here: 285 us
  waiting for transfers between devices  94.5 us (33%)
  starting transfers between devices  84.6 us (29%)
  Pallas kernels  25.3 us (9%)
  other arithmetic  21.6 us (8%)
  matrix products  17.2 us (6%)
  local copies, waits for them, and re-layouts  14.5 us (5%)
  blocking collectives  13.8 us (5%)
  between operations  13.5 us (5%)
    ppermute x31, waiting for transfers between devices, shift(): return lax.ppermute(value, axis, [(i, (i + by) % n) for i in range(n)])  76.8 us
    ppermute x31, starting transfers between devices, shift(): return lax.ppermute(value, axis, [(i, (i + by) % n) for i in range(n)])  57.6 us
    all_to_all x3, starting transfers between devices, exchange(): return lax.all_to_all(value, axes, 0, 0, tiled=True)  17.4 us
    dot_general x4, matrix products, dot_t(): lax.dot_general(a, b, (((1,), (1,)), ((), ())), preferred_element_type=F32)  17.2 us
    pallas_call x1, Pallas kernels, score(): pl.pallas_call(score_kernel, grid_spec=spec, out_shape=jax.ShapeDtypeStru...  15.5 us
    all_to_all x1, blocking collectives, exchange(): return lax.all_to_all(value, axes, 0, 0, tiled=True)  13.8 us
    all_to_all x3, waiting for transfers between devices, exchange(): return lax.all_to_all(value, axes, 0, 0, tiled=True)  9.56 us
    ppermute x3, starting transfers between devices, from_owner(): return lax.ppermute(value, ('zh', 'zl'), pairs)  8.25 us
  transfers between devices with their start and end apart: 41, of which 18 were waited for; matrix products, arithmetic and copies ran while one was open for 16% of the time, Pallas kernels for 3%

profile of v6, /device:TPU:2, one launch (start us, length us, event | category | flops | bytes accessed | tf_op | source)
XLA Modules:
  0.0 285.1 jit_solution(16368549681505610414)
XLA Ops:
  7.3 7.3 %collective-permute-start.9 = (bf16[128,1792]{1,0:T(8,128)(2,1)}, bf16[128,1792]{1,0:T(8,128)(2,1)S(1)}, u32[]{:S(2)}, u32[]{:S(2)}) collective-permute-start(bf16[128,1792]{1,0:T(8,128)(2,1)} %bitcast.83), channel_id=1, source_target_pairs={{0,32},{16,48},{32,0},{48,16},{1,33},{17,49},{33,1},{49,17},{2,34}... | collective-permute-start | bytes 1376264 | tf_op jit(solution)/shard_map/ppermute | solution.py:17
  14.6 13.0 %collective-permute-done.9 = bf16[128,1792]{1,0:T(8,128)(2,1)S(1)} collective-permute-done((bf16[128,1792]{1,0:T(8,128)(2,1)}, bf16[128,1792]{1,0:T(8,128)(2,1)S(1)}, u32[]{:S(2)}, u32[]{:S(2)}) %collective-permute-start.9) | collective-permute-done | bytes 458784 | tf_op jit(solution)/shard_map/ppermute | solution.py:17
  28.4 12.3 %collective-permute-start.18 = (bf16[512,128]{1,0:T(8,128)(2,1)}, bf16[512,128]{1,0:T(8,128)(2,1)S(1)}, u32[]{:S(2)}, u32[]{:S(2)}) collective-permute-start(bf16[512,128]{1,0:T(8,128)(2,1)} %param.10), channel_id=1, source_target_pairs={{0,48},{16,0},{32,16},{48,32},{1,49},{17,1},{33,17},{49,33},{2,50}... | collective-permute-start | bytes 393224 | tf_op jit(solution)/shard_map/ppermute | solution.py:17
  40.7 3.3 %collective-permute-start.19 = (bf16[512,128]{1,0:T(8,128)(2,1)}, bf16[512,128]{1,0:T(8,128)(2,1)S(1)}, u32[]{:S(2)}, u32[]{:S(2)}) collective-permute-start(bf16[512,128]{1,0:T(8,128)(2,1)} %param.10), channel_id=1, source_target_pairs={{0,32},{16,48},{32,0},{48,16},{1,33},{17,49},{33,1},{49,17},{2,34}... | collective-permute-start | bytes 393224 | tf_op jit(solution)/shard_map/ppermute | solution.py:17
  44.1 5.4 %collective-permute-done.18 = bf16[512,128]{1,0:T(8,128)(2,1)S(1)} collective-permute-done((bf16[512,128]{1,0:T(8,128)(2,1)}, bf16[512,128]{1,0:T(8,128)(2,1)S(1)}, u32[]{:S(2)}, u32[]{:S(2)}) %collective-permute-start.18) | collective-permute-done | bytes 131104 | tf_op jit(solution)/shard_map/ppermute | solution.py:17
  49.4 3.3 %collective-permute-done.20 = bf16[512,128]{1,0:T(8,128)(2,1)S(1)} collective-permute-done((bf16[512,128]{1,0:T(8,128)(2,1)}, bf16[512,128]{1,0:T(8,128)(2,1)S(1)}, u32[]{:S(2)}, u32[]{:S(2)}) %collective-permute-start.20) | collective-permute-done | bytes 131104 | tf_op jit(solution)/shard_map/ppermute | solution.py:17
  55.3 4.3 %collective-permute-start.5 = (bf16[128,1792]{1,0:T(8,128)(2,1)}, bf16[128,1792]{1,0:T(8,128)(2,1)S(1)}, u32[]{:S(2)}, u32[]{:S(2)}) collective-permute-start(bf16[128,1792]{1,0:T(8,128)(2,1)} %bitcast.84), channel_id=1, source_target_pairs={{0,16},{16,32},{32,48},{48,0},{1,17},{17,33},{33,49},{49,1},{2,18}... | collective-permute-start | bytes 1376264 | tf_op jit(solution)/shard_map/ppermute | solution.py:17
  59.6 1.6 collective-permute-start.17
  61.2 8.8 %collective-permute-done.17.a3 = bf16[128,512]{1,0:T(8,128)(2,1)} collective-permute-done((bf16[128,512]{1,0:T(8,128)(2,1)}, bf16[128,512]{1,0:T(8,128)(2,1)}, u32[]{:S(2)}, u32[]{:S(2)}) %collective-permute-start.17) | collective-permute-done | bytes 131104 | tf_op jit(solution)/shard_map/ppermute | solution.py:17
  70.0 2.0 collective-permute-start.16
  72.0 8.5 %collective-permute-done.16.a2 = bf16[128,512]{1,0:T(8,128)(2,1)} collective-permute-done((bf16[128,512]{1,0:T(8,128)(2,1)}, bf16[128,512]{1,0:T(8,128)(2,1)}, u32[]{:S(2)}, u32[]{:S(2)}) %collective-permute-start.16) | collective-permute-done | bytes 131104 | tf_op jit(solution)/shard_map/ppermute | solution.py:17
  83.4 2.3 collective-permute-done.15.a1
  85.7 3.8 %rotate_in.1 = (bf16[128,1024]{1,0:T(8,128)(2,1)}, bf16[128,1024]{1,0:T(8,128)(2,1)}, bf16[128,1024]{1,0:T(8,128)(2,1)}, bf16[128,1024]{1,0:T(8,128)(2,1)}, bf16[64,1024]{1,0:T(8,128)(2,1)}) custom-call(s32[5]{0:T(128)} %stack.69.at_ref, bf16[128,512]{1,0:T(8,128)(2,1)} %bitcast.98, bf16[128,512]{1,0:T(8,128)(2,1)} %collective-permute-done.15.a1, ...), custom_call_target="tpu_custom_call" | custom-call | flops 536870912 | bytes 2621440 | tf_op jit(solution)/shard_map/rotate_in/pallas_call | solution.py:73
  89.5 1.5 collective-permute-start.22
  92.1 2.2 collective-permute-start.24
  95.3 2.7 collective-permute-done.22
  98.0 2.9 %collective-permute-done.23 = bf16[128,1024]{1,0:T(8,128)(2,1)S(1)} collective-permute-done((bf16[128,1024]{1,0:T(8,128)(2,1)}, bf16[128,1024]{1,0:T(8,128)(2,1)S(1)}, u32[]{:S(2)}, u32[]{:S(2)}) %collective-permute-start.23) | collective-permute-done | bytes 262176 | tf_op jit(solution)/shard_map/ppermute | solution.py:17
  100.9 2.1 collective-permute-done.24
  105.6 7.3 %collective-permute-done.25 = bf16[128,1024]{1,0:T(8,128)(2,1)S(1)} collective-permute-done((bf16[128,1024]{1,0:T(8,128)(2,1)S(1)}, bf16[128,1024]{1,0:T(8,128)(2,1)S(1)}, u32[]{:S(2)}, u32[]{:S(2)}) %collective-permute-start.25) | collective-permute-done | bytes 262176 | tf_op jit(solution)/shard_map/ppermute | solution.py:31
  114.3 5.5 %collective-permute-start.27 = (bf16[128,1024]{1,0:T(8,128)(2,1)S(1)}, bf16[128,1024]{1,0:T(8,128)(2,1)}, u32[]{:S(2)}, u32[]{:S(2)}) collective-permute-start(bf16[128,1024]{1,0:T(8,128)(2,1)S(1)} %add_convert_fusion), channel_id=1, source_target_pairs={{0,32},{20,52},{32,0},{52,20},{1,33},{21,53},{33,1},{53,21},{2,34}... | collective-permute-start | bytes 786440 | tf_op jit(solution)/shard_map/ppermute | solution.py:26
  119.8 1.5 collective-permute-start.26
  121.3 1.6 pad_maximum_fusion
  123.0 1.7 copy-done.2
  126.5 4.2 %all-to-all-start = ((bf16[8,8,1920]{2,1,0:T(8,128)(2,1)}), bf16[8,8,1920]{2,1,0:T(8,128)(2,1)S(1)}, u32[]{:S(2)}, u32[]{:S(2)}) async-start(bf16[8,8,1920]{2,1,0:T(8,128)(2,1)} %maximum_bitcast_fusion), calls=%async_computation | async-start | bytes 491520 | tf_op jit(solution)/shard_map/all_to_all | solution.py:35
  130.7 6.0 %convert_divide_fusion.1.inv0 = f32[448,4096]{1,0:T(8,128)} fusion(bf16[448,4096]{1,0:T(8,128)(2,1)} %param.11), kind=kLoop, calls=%fused_computation.1 | loop fusion | flops 3670016 | bytes 11010048 | tf_op jit(solution)/shard_map/div | solution.py:229
  137.8 6.7 %all-to-all-start.1 = ((bf16[8,8,1920]{2,1,0:T(8,128)(2,1)}), bf16[8,8,1920]{2,1,0:T(8,128)(2,1)S(1)}, u32[]{:S(2)}, u32[]{:S(2)}) async-start(bf16[8,8,1920]{2,1,0:T(8,128)(2,1)} %broadcast_in_dim.6), calls=%async_computation.1 | async-start | bytes 491520 | tf_op jit(solution)/shard_map/all_to_all | solution.py:35
  145.5 4.3 %all-to-all-done.1 = bf16[8,8,1920]{2,1,0:T(8,128)(2,1)S(1)} async-done(((bf16[8,8,1920]{2,1,0:T(8,128)(2,1)}), bf16[8,8,1920]{2,1,0:T(8,128)(2,1)S(1)}, u32[]{:S(2)}, u32[]{:S(2)}) %all-to-all-start.1) | async-done | bytes 245792 | tf_op jit(solution)/shard_map/all_to_all | solution.py:35
  151.3 2.2 collective-permute-start.31
  153.5 2.8 collective-permute-start.30
  158.1 4.6 %convolution_convert_fusion.2 = bf16[896,512]{0,1:T(8,128)(2,1)S(1)} fusion(bf16[896,1792]{1,0:T(8,128)(2,1)} %copy-done.2, bf16[512,1792]{1,0:T(8,128)(2,1)} %bitcast.94), kind=kOutput, calls=%fused_computation.5 | convolution fusion | flops 1644625920 | bytes 5963776 | tf_op jit(solution)/shard_map/dot_general | solution.py:47
  163.6 4.6 %convolution_convert_fusion.1 = bf16[896,512]{0,1:T(8,128)(2,1)S(1)} fusion(bf16[896,1792]{1,0:T(8,128)(2,1)} %copy-done.2, bf16[512,1792]{1,0:T(8,128)(2,1)} %all-gather.9.cloned.1.call-done), kind=kOutput, calls=%fused_computation.4 | convolution fusion | flops 1644625920 | bytes 5963776 | tf_op jit(solution)/shard_map/dot_general | solution.py:47
  170.1 1.8 collective-permute-start.12
  171.9 7.0 %convolution_convert_fusion = bf16[1024,896]{1,0:T(8,128)(2,1)S(1)} fusion(bf16[1024,1792]{1,0:T(8,128)(2,1)} %bitcast.93, bf16[896,1792]{1,0:T(8,128)(2,1)} %copy-done.2), kind=kOutput, calls=%fused_computation.3 | convolution fusion | flops 3289251840 | bytes 8716288 | tf_op jit(solution)/shard_map/dot_general | solution.py:47
  179.4 6.4 %collective-permute-done.30.v2 = bf16[320,1024]{1,0:T(8,128)(2,1)} collective-permute-done((bf16[320,1024]{1,0:T(8,128)(2,1)}, bf16[320,1024]{1,0:T(8,128)(2,1)}, u32[]{:S(2)}, u32[]{:S(2)}) %collective-permute-start.30) | collective-permute-done | bytes 655392 | tf_op jit(solution)/shard_map/ppermute | solution.py:17
  185.8 1.8 collective-permute-start.8
  188.9 2.1 collective-permute-start.10
  191.0 1.8 collective-permute-start.6
  193.7 12.6 %collective-permute-done.10.refs_1_ = bf16[1,128,896]{2,1,0:T(8,128)(2,1)S(1)} collective-permute-done((bf16[1,128,896]{2,1,0:T(8,128)(2,1)S(1)}, bf16[1,128,896]{2,1,0:T(8,128)(2,1)S(1)}, u32[]{:S(2)}, u32[]{:S(2)}) %collective-permute-start.10) | collective-permute-done | bytes 229408 | tf_op jit(solution)/shard_map/ppermute | solution.py:17
  207.9 2.6 collective-permute-start.1
  212.2 4.0 %collective-permute-done.6.refs_5_ = bf16[2,128,896]{2,1,0:T(8,128)(2,1)} collective-permute-done((bf16[2,128,896]{2,1,0:T(8,128)(2,1)S(1)}, bf16[2,128,896]{2,1,0:T(8,128)(2,1)}, u32[]{:S(2)}, u32[]{:S(2)}) %collective-permute-start.6) | collective-permute-done | bytes 458784 | tf_op jit(solution)/shard_map/ppermute | solution.py:17
  216.2 3.0 %shard_map.74 = (bf16[128,896]{1,0:T(8,128)(2,1)}, bf16[128,896]{1,0:T(8,128)(2,1)}) custom-call(s32[5]{0:T(128)} %stack.69.at_ref, bf16[4,1,128,896]{3,2,1,0:T(8,128)(2,1)} %bitcast.75, bf16[1,128,896]{2,1,0:T(8,128)(2,1)} %copy-done.14, bf16[1,128,896]{2,1,0:T(8,128)(2,1)} %copy-done.12, bf16[1,128,896]{2,1,0:T(8,128)(2,1)} %collective-permute-done.12.refs_3_, ...), custom_call_target="tpu_custom_call" | custom-call | flops 917504 | bytes 2293760 | tf_op jit(solution)/shard_map/pallas_call | solution.py:117
  220.6 3.9 %collective-permute-done.1.refs_1_ = bf16[1,128,896]{2,1,0:T(8,128)(2,1)} collective-permute-done((bf16[1,128,896]{2,1,0:T(8,128)(2,1)}, bf16[1,128,896]{2,1,0:T(8,128)(2,1)}, u32[]{:S(2)}, u32[]{:S(2)}) %collective-permute-start.1) | collective-permute-done | bytes 229408 | tf_op jit(solution)/shard_map/ppermute | solution.py:17
  224.5 3.0 %shard_map.73 = (bf16[128,896]{1,0:T(8,128)(2,1)}, bf16[128,896]{1,0:T(8,128)(2,1)}) custom-call(s32[5]{0:T(128)} %stack.69.at_ref, bf16[4,1,128,896]{3,2,1,0:T(8,128)(2,1)} %bitcast.73, bf16[1,128,896]{2,1,0:T(8,128)(2,1)} %collective-permute-done.1.refs_1_, bf16[1,128,896]{2,1,0:T(8,128)(2,1)} %collective-permute-done.2.refs_2_, ...), custom_call_target="tpu_custom_call" | custom-call | flops 917504 | bytes 2293760 | tf_op jit(solution)/shard_map/pallas_call | solution.py:117
  228.8 6.1 %convert_divide_fusion.inv1 = f32[448,4096]{1,0:T(8,128)} fusion(bf16[448,4096]{1,0:T(8,128)(2,1)} %collective-permute-done.33), kind=kLoop, calls=%fused_computation | loop fusion | flops 3670016 | bytes 11010048 | tf_op jit(solution)/shard_map/div | solution.py:230
  235.6 15.5 %score.1 = f32[8,128]{1,0:T(8,128)} custom-call(s32[5]{0:T(128)} %stack.69.at_ref, bf16[128,896]{1,0:T(8,128)(2,1)} %get-tuple-element.14.k0, bf16[128,896]{1,0:T(8,128)(2,1)} %get-tuple-element.15.k1, bf16[128,896]{1,0:T(8,128)(2,1)} %copy-done.11, bf16[128,896]{1,0:T(8,128)(2,1)} %copy-done.10, bf16[320,1024]{1,0:T(8,128)(2,1)} %pad_maximum_fusion.2.v0, ...), custom_call_target="tpu_custom_call" | custom-call | flops 3758096384 | bytes 14680064 | tf_op jit(solution)/shard_map/score/pallas_call | solution.py:199
  252.2 13.8 %all_to_all.20 = f32[16,2,16]{2,1,0:T(2,128)S(1)} all-to-all(f32[16,2,16]{2,1,0:T(2,128)S(1)} %broadcast_in_dim.7), channel_id=1, replica_groups=mesh['y'=4,'zh'=4,'c'=2,'zl'=2,'x'=4] {'y','zh'}, dimensions={0} | all-to-all | bytes 4096 | tf_op jit(solution)/shard_map/all_to_all | solution.py:35
  266.6 6.6 %all-to-all-start.3 = ((f32[16,2,16]{2,1,0:T(2,128)}), f32[16,2,16]{2,1,0:T(2,128)S(1)}, u32[]{:S(2)}, u32[]{:S(2)}) async-start(f32[16,2,16]{2,1,0:T(2,128)} %broadcast_in_dim.8), calls=%async_computation.3 | async-start | bytes 32768 | tf_op jit(solution)/shard_map/all_to_all | solution.py:35
  273.2 4.8 %all-to-all-done.3 = f32[16,2,16]{2,1,0:T(2,128)S(1)} async-done(((f32[16,2,16]{2,1,0:T(2,128)}), f32[16,2,16]{2,1,0:T(2,128)S(1)}, u32[]{:S(2)}, u32[]{:S(2)}) %all-to-all-start.3) | async-done | bytes 2080 | tf_op jit(solution)/shard_map/all_to_all | solution.py:35
  (121 shorter events, 35.0 us)
Async XLA Ops:
  6.5 116.4 %copy-start = (bf16[16,8,1792]{2,1,0:T(8,128)(2,1)S(1)}, bf16[16,8,1792]{2,1,0:T(8,128)(2,1)}, u32[]{:S(2)}) copy-start(bf16[16,8,1792]{2,1,0:T(8,128)(2,1)} %param.12) | copy-start | bytes 1376260
  6.5 151.6 %all-gather.5.cloned.1.call-start = ((), (), s32[]{:S(2)}) async-start(), calls=%async_computation.4 | async-start | bytes 2293760 | tf_op jit(solution)/shard_map/all_gather | solution.py:267
  7.3 156.4 %all-gather.9.cloned.1.call-start = ((), (), s32[]{:S(2)}) async-start(), calls=%async_computation.6 | async-start | bytes 2293760 | tf_op jit(solution)/shard_map/all_gather | solution.py:267
  7.3 20.3 %collective-permute-start.9 = (bf16[128,1792]{1,0:T(8,128)(2,1)}, bf16[128,1792]{1,0:T(8,128)(2,1)S(1)}, u32[]{:S(2)}, u32[]{:S(2)}) collective-permute-start(bf16[128,1792]{1,0:T(8,128)(2,1)} %bitcast.83), channel_id=1, source_target_pairs={{0,32},{16,48},{32,0},{48,16},{1,33},{17,49},{33,1},{49,17},{2,34}... | collective-permute-start | bytes 1376264 | tf_op jit(solution)/shard_map/ppermute | solution.py:17
  28.4 143.5 %all-gather.7.cloned.1.call-start = ((), (), s32[]{:S(2)}) async-start(), calls=%async_computation.5 | async-start | bytes 4587520 | tf_op jit(solution)/shard_map/all_gather | solution.py:267
  28.4 21.0 %collective-permute-start.18 = (bf16[512,128]{1,0:T(8,128)(2,1)}, bf16[512,128]{1,0:T(8,128)(2,1)S(1)}, u32[]{:S(2)}, u32[]{:S(2)}) collective-permute-start(bf16[512,128]{1,0:T(8,128)(2,1)} %param.10), channel_id=1, source_target_pairs={{0,48},{16,0},{32,16},{48,32},{1,49},{17,1},{33,17},{49,33},{2,50}... | collective-permute-start | bytes 393224 | tf_op jit(solution)/shard_map/ppermute | solution.py:17
  40.7 12.0 %collective-permute-start.20 = (bf16[512,128]{1,0:T(8,128)(2,1)}, bf16[512,128]{1,0:T(8,128)(2,1)S(1)}, u32[]{:S(2)}, u32[]{:S(2)}) collective-permute-start(bf16[512,128]{1,0:T(8,128)(2,1)} %param.10), channel_id=1, source_target_pairs={{0,16},{16,32},{32,48},{48,0},{1,17},{17,33},{33,49},{49,1},{2,18}... | collective-permute-start | bytes 393224 | tf_op jit(solution)/shard_map/ppermute | solution.py:17
  40.7 13.0 %collective-permute-start.19 = (bf16[512,128]{1,0:T(8,128)(2,1)}, bf16[512,128]{1,0:T(8,128)(2,1)S(1)}, u32[]{:S(2)}, u32[]{:S(2)}) collective-permute-start(bf16[512,128]{1,0:T(8,128)(2,1)} %param.10), channel_id=1, source_target_pairs={{0,32},{16,48},{32,0},{48,16},{1,33},{17,49},{33,1},{49,17},{2,34}... | collective-permute-start | bytes 393224 | tf_op jit(solution)/shard_map/ppermute | solution.py:17
  54.7 31.0 %copy-start.8 = (bf16[4,512,128]{2,1,0:T(8,128)(2,1)}, bf16[4,512,128]{2,1,0:T(8,128)(2,1)S(1)}, u32[]{:S(2)}) copy-start(bf16[4,512,128]{2,1,0:T(8,128)(2,1)S(1)} %pad_maximum_fusion.3.w0) | copy-start | bytes 1572868
  54.7 31.0 %collective-permute-start.21 = (bf16[4,512,128]{2,1,0:T(8,128)(2,1)S(1)}, bf16[4,512,128]{2,1,0:T(8,128)(2,1)}, u32[]{:S(2)}, u32[]{:S(2)}) collective-permute-start(bf16[4,512,128]{2,1,0:T(8,128)(2,1)S(1)} %pad_maximum_fusion.3.w0), channel_id=1, source_target_pairs={{0,8},{8,0},{1,9},{9,1},{2,10},{10,2},{3,11},{11,3},{4,12},{12,4},... | collective-permute-start | bytes 1572872 | tf_op jit(solution)/shard_map/ppermute | solution.py:17
  54.8 66.5 %collective-permute-start = (bf16[448,1792]{1,0:T(8,128)(2,1)}, bf16[448,1792]{1,0:T(8,128)(2,1)}, u32[]{:S(2)}, u32[]{:S(2)}) collective-permute-start(bf16[448,1792]{1,0:T(8,128)(2,1)} %bitcast.76), channel_id=1, source_target_pairs={{0,8},{8,0},{1,9},{9,1},{2,10},{10,2},{3,11},{11,3},{4,12},{12,4},... | collective-permute-start | bytes 4816904 | tf_op jit(solution)/shard_map/ppermute | solution.py:17
  55.3 36.8 %collective-permute-start.5 = (bf16[128,1792]{1,0:T(8,128)(2,1)}, bf16[128,1792]{1,0:T(8,128)(2,1)S(1)}, u32[]{:S(2)}, u32[]{:S(2)}) collective-permute-start(bf16[128,1792]{1,0:T(8,128)(2,1)} %bitcast.84), channel_id=1, source_target_pairs={{0,16},{16,32},{32,48},{48,0},{1,17},{17,33},{33,49},{49,1},{2,18}... | collective-permute-start | bytes 1376264 | tf_op jit(solution)/shard_map/ppermute | solution.py:17
  59.6 34.6 %collective-permute-start.4 = (bf16[128,1792]{1,0:T(8,128)(2,1)}, bf16[128,1792]{1,0:T(8,128)(2,1)S(1)}, u32[]{:S(2)}, u32[]{:S(2)}) collective-permute-start(bf16[128,1792]{1,0:T(8,128)(2,1)} %bitcast.85), channel_id=1, source_target_pairs={{0,48},{16,0},{32,16},{48,32},{1,49},{17,1},{33,17},{49,33},{2,50}... | collective-permute-start | bytes 1376264 | tf_op jit(solution)/shard_map/ppermute | solution.py:17
  59.6 10.4 %collective-permute-start.17 = (bf16[128,512]{1,0:T(8,128)(2,1)}, bf16[128,512]{1,0:T(8,128)(2,1)}, u32[]{:S(2)}, u32[]{:S(2)}) collective-permute-start(bf16[128,512]{1,0:T(8,128)(2,1)} %bitcast.95), channel_id=1, source_target_pairs={{0,64},{64,128},{128,192},{192,0},{1,65},{65,129},{129,193},{193,1... | collective-permute-start | bytes 393224 | tf_op jit(solution)/shard_map/ppermute | solution.py:17
  70.0 10.4 %collective-permute-start.16 = (bf16[128,512]{1,0:T(8,128)(2,1)}, bf16[128,512]{1,0:T(8,128)(2,1)}, u32[]{:S(2)}, u32[]{:S(2)}) collective-permute-start(bf16[128,512]{1,0:T(8,128)(2,1)} %bitcast.96), channel_id=1, source_target_pairs={{0,128},{64,192},{128,0},{192,64},{1,129},{65,193},{129,1},{193,65... | collective-permute-start | bytes 393224 | tf_op jit(solution)/shard_map/ppermute | solution.py:17
  80.4 5.3 %collective-permute-start.15 = (bf16[128,512]{1,0:T(8,128)(2,1)}, bf16[128,512]{1,0:T(8,128)(2,1)}, u32[]{:S(2)}, u32[]{:S(2)}) collective-permute-start(bf16[128,512]{1,0:T(8,128)(2,1)} %bitcast.97), channel_id=1, source_target_pairs={{0,192},{64,0},{128,64},{192,128},{1,193},{65,1},{129,65},{193,129... | collective-permute-start | bytes 393224 | tf_op jit(solution)/shard_map/ppermute | solution.py:17
  83.4 37.9 %copy-start.7 = (bf16[1792,448]{0,1:T(8,128)(2,1)S(1)}, bf16[1792,448]{0,1:T(8,128)(2,1)}, u32[]{:S(2)}) copy-start(bf16[1792,448]{0,1:T(8,128)(2,1)} %param.9) | copy-start | bytes 4816900
  89.5 8.5 %collective-permute-start.22 = (bf16[128,1024]{1,0:T(8,128)(2,1)}, bf16[128,1024]{1,0:T(8,128)(2,1)S(1)}, u32[]{:S(2)}, u32[]{:S(2)}) collective-permute-start(bf16[128,1024]{1,0:T(8,128)(2,1)} %get-tuple-element.19), channel_id=1, source_target_pairs={{0,1},{1,2},{2,3},{3,0},{4,5},{5,6},{6,7},{7,4},{8,9},{9,10},{10,1... | collective-permute-start | bytes 786440 | tf_op jit(solution)/shard_map/ppermute | solution.py:17
  91.0 9.9 %collective-permute-start.23 = (bf16[128,1024]{1,0:T(8,128)(2,1)}, bf16[128,1024]{1,0:T(8,128)(2,1)S(1)}, u32[]{:S(2)}, u32[]{:S(2)}) collective-permute-start(bf16[128,1024]{1,0:T(8,128)(2,1)} %get-tuple-element.20), channel_id=1, source_target_pairs={{0,2},{1,3},{2,0},{3,1},{4,6},{5,7},{6,4},{7,5},{8,10},{9,11},{10,... | collective-permute-start | bytes 786440 | tf_op jit(solution)/shard_map/ppermute | solution.py:17
  92.1 10.9 %collective-permute-start.24 = (bf16[128,1024]{1,0:T(8,128)(2,1)}, bf16[128,1024]{1,0:T(8,128)(2,1)}, u32[]{:S(2)}, u32[]{:S(2)}) collective-permute-start(bf16[128,1024]{1,0:T(8,128)(2,1)} %get-tuple-element.21), channel_id=1, source_target_pairs={{0,3},{1,0},{2,1},{3,2},{4,7},{5,4},{6,5},{7,6},{8,11},{9,8},{10,9... | collective-permute-start | bytes 786440 | tf_op jit(solution)/shard_map/ppermute | solution.py:17
  104.2 8.7 %collective-permute-start.25 = (bf16[128,1024]{1,0:T(8,128)(2,1)S(1)}, bf16[128,1024]{1,0:T(8,128)(2,1)S(1)}, u32[]{:S(2)}, u32[]{:S(2)}) collective-permute-start(bf16[128,1024]{1,0:T(8,128)(2,1)S(1)} %add_convert_fusion.1), channel_id=1, source_target_pairs={{4,0},{16,20},{36,32},{48,52},{5,1},{17,21},{37,33},{49,53},{6,2},... | collective-permute-start | bytes 786440 | tf_op jit(solution)/shard_map/ppermute | solution.py:31
  105.5 123.3 %collective-permute-start.33 = (bf16[448,4096]{1,0:T(8,128)(2,1)}, bf16[448,4096]{1,0:T(8,128)(2,1)}, u32[]{:S(2)}, u32[]{:S(2)}) collective-permute-start(bf16[448,4096]{1,0:T(8,128)(2,1)} %param.11), channel_id=1, source_target_pairs={{0,8},{8,0},{1,9},{9,1},{2,10},{10,2},{3,11},{11,3},{4,12},{12,4},... | collective-permute-start | bytes 11010056 | tf_op jit(solution)/shard_map/ppermute | solution.py:17
  113.0 31.5 %collective-permute-start.28 = (bf16[128,1024]{1,0:T(8,128)(2,1)S(1)}, bf16[128,1024]{1,0:T(8,128)(2,1)S(1)}, u32[]{:S(2)}, u32[]{:S(2)}) collective-permute-start(bf16[128,1024]{1,0:T(8,128)(2,1)S(1)} %add_convert_fusion), channel_id=1, source_target_pairs={{0,48},{20,4},{32,16},{52,36},{1,49},{21,5},{33,17},{53,37},{2,50}... | collective-permute-start | bytes 786440 | tf_op jit(solution)/shard_map/ppermute | solution.py:26
  114.3 30.2 %collective-permute-start.27 = (bf16[128,1024]{1,0:T(8,128)(2,1)S(1)}, bf16[128,1024]{1,0:T(8,128)(2,1)}, u32[]{:S(2)}, u32[]{:S(2)}) collective-permute-start(bf16[128,1024]{1,0:T(8,128)(2,1)S(1)} %add_convert_fusion), channel_id=1, source_target_pairs={{0,32},{20,52},{32,0},{52,20},{1,33},{21,53},{33,1},{53,21},{2,34}... | collective-permute-start | bytes 786440 | tf_op jit(solution)/shard_map/ppermute | solution.py:26
  119.8 24.7 %collective-permute-start.26 = (bf16[128,1024]{1,0:T(8,128)(2,1)S(1)}, bf16[128,1024]{1,0:T(8,128)(2,1)S(1)}, u32[]{:S(2)}, u32[]{:S(2)}) collective-permute-start(bf16[128,1024]{1,0:T(8,128)(2,1)S(1)} %add_convert_fusion), channel_id=1, source_target_pairs={{0,16},{20,36},{32,48},{52,4},{1,17},{21,37},{33,49},{53,5},{2,18}... | collective-permute-start | bytes 786440 | tf_op jit(solution)/shard_map/ppermute | solution.py:26
  126.5 10.6 %all-to-all-start = ((bf16[8,8,1920]{2,1,0:T(8,128)(2,1)}), bf16[8,8,1920]{2,1,0:T(8,128)(2,1)S(1)}, u32[]{:S(2)}, u32[]{:S(2)}) async-start(bf16[8,8,1920]{2,1,0:T(8,128)(2,1)} %maximum_bitcast_fusion), calls=%async_computation | async-start | bytes 491520 | tf_op jit(solution)/shard_map/all_to_all | solution.py:35
  137.8 12.0 %all-to-all-start.1 = ((bf16[8,8,1920]{2,1,0:T(8,128)(2,1)}), bf16[8,8,1920]{2,1,0:T(8,128)(2,1)S(1)}, u32[]{:S(2)}, u32[]{:S(2)}) async-start(bf16[8,8,1920]{2,1,0:T(8,128)(2,1)} %broadcast_in_dim.6), calls=%async_computation.1 | async-start | bytes 491520 | tf_op jit(solution)/shard_map/all_to_all | solution.py:35
  150.3 6.8 %collective-permute-start.34 = (bf16[64,896]{0,1:T(8,128)(2,1)S(1)}, bf16[64,896]{0,1:T(8,128)(2,1)S(1)}, u32[]{:S(2)}, u32[]{:S(2)}) collective-permute-start(bf16[64,896]{0,1:T(8,128)(2,1)S(1)} %pad_maximum_fusion.5), channel_id=1, source_target_pairs={{0,8},{8,0},{1,9},{9,1},{2,10},{10,2},{3,11},{11,3},{4,12},{12,4},... | collective-permute-start | bytes 344072 | tf_op jit(solution)/shard_map/ppermute | solution.py:17
  151.3 27.7 %collective-permute-start.31 = (bf16[320,1024]{1,0:T(8,128)(2,1)}, bf16[320,1024]{1,0:T(8,128)(2,1)}, u32[]{:S(2)}, u32[]{:S(2)}) collective-permute-start(bf16[320,1024]{1,0:T(8,128)(2,1)} %pad_maximum_fusion.2.v0), channel_id=1, source_target_pairs={{0,64},{64,128},{128,192},{192,0},{1,65},{65,129},{129,193},{193,1... | collective-permute-start | bytes 1966088 | tf_op jit(solution)/shard_map/ppermute | solution.py:17
  153.5 32.3 %collective-permute-start.30 = (bf16[320,1024]{1,0:T(8,128)(2,1)}, bf16[320,1024]{1,0:T(8,128)(2,1)}, u32[]{:S(2)}, u32[]{:S(2)}) collective-permute-start(bf16[320,1024]{1,0:T(8,128)(2,1)} %pad_maximum_fusion.2.v0), channel_id=1, source_target_pairs={{0,128},{64,192},{128,0},{192,64},{1,129},{65,193},{129,1},{193,65... | collective-permute-start | bytes 1966088 | tf_op jit(solution)/shard_map/ppermute | solution.py:17
  156.4 31.3 %collective-permute-start.29 = (bf16[320,1024]{1,0:T(8,128)(2,1)}, bf16[320,1024]{1,0:T(8,128)(2,1)}, u32[]{:S(2)}, u32[]{:S(2)}) collective-permute-start(bf16[320,1024]{1,0:T(8,128)(2,1)} %pad_maximum_fusion.2.v0), channel_id=1, source_target_pairs={{0,192},{64,0},{128,64},{192,128},{1,193},{65,1},{129,65},{193,129... | collective-permute-start | bytes 1966088 | tf_op jit(solution)/shard_map/ppermute | solution.py:17
  170.1 18.8 %collective-permute-start.12 = (bf16[1,128,896]{2,1,0:T(8,128)(2,1)}, bf16[1,128,896]{2,1,0:T(8,128)(2,1)}, u32[]{:S(2)}, u32[]{:S(2)}) collective-permute-start(bf16[1,128,896]{2,1,0:T(8,128)(2,1)} %get-tuple-element.26), channel_id=1, source_target_pairs={{0,3},{1,0},{2,1},{3,2},{4,7},{5,4},{6,5},{7,6},{8,11},{9,8},{10,9... | collective-permute-start | bytes 688136 | tf_op jit(solution)/shard_map/ppermute | solution.py:17
  171.9 17.0 %copy-start.13 = (bf16[1,128,896]{2,1,0:T(8,128)(2,1)S(1)}, bf16[1,128,896]{2,1,0:T(8,128)(2,1)}, u32[]{:S(2)}) copy-start(bf16[1,128,896]{2,1,0:T(8,128)(2,1)} %get-tuple-element.28) | copy-start | bytes 688132
  178.9 37.3 %copy-start.1 = (bf16[1024,896]{1,0:T(8,128)(2,1)}, bf16[1024,896]{1,0:T(8,128)(2,1)S(1)}, u32[]{:S(2)}) copy-start(bf16[1024,896]{1,0:T(8,128)(2,1)S(1)} %convolution_convert_fusion) | copy-start | bytes 5505028
  179.1 11.9 %collective-permute-start.11 = (bf16[1,128,896]{2,1,0:T(8,128)(2,1)}, bf16[1,128,896]{2,1,0:T(8,128)(2,1)S(1)}, u32[]{:S(2)}, u32[]{:S(2)}) collective-permute-start(bf16[1,128,896]{2,1,0:T(8,128)(2,1)} %get-tuple-element.27), channel_id=1, source_target_pairs={{0,2},{1,3},{2,0},{3,1},{4,6},{5,7},{6,4},{7,5},{8,10},{9,11},{10,... | collective-permute-start | bytes 688136 | tf_op jit(solution)/shard_map/ppermute | solution.py:17
  185.8 20.9 %collective-permute-start.8 = (bf16[2,128,896]{2,1,0:T(8,128)(2,1)S(1)}, bf16[2,128,896]{2,1,0:T(8,128)(2,1)S(1)}, u32[]{:S(2)}, u32[]{:S(2)}) collective-permute-start(bf16[2,128,896]{2,1,0:T(8,128)(2,1)S(1)} %get-tuple-element.23), channel_id=1, source_target_pairs={{0,3},{1,0},{2,1},{3,2},{4,7},{5,4},{6,5},{7,6},{8,11},{9,8},{10,9... | collective-permute-start | bytes 1376264 | tf_op jit(solution)/shard_map/ppermute | solution.py:17
  187.6 20.2 %collective-permute-start.7 = (bf16[2,128,896]{2,1,0:T(8,128)(2,1)S(1)}, bf16[2,128,896]{2,1,0:T(8,128)(2,1)S(1)}, u32[]{:S(2)}, u32[]{:S(2)}) collective-permute-start(bf16[2,128,896]{2,1,0:T(8,128)(2,1)S(1)} %get-tuple-element.24), channel_id=1, source_target_pairs={{0,2},{1,3},{2,0},{3,1},{4,6},{5,7},{6,4},{7,5},{8,10},{9,11},{10,... | collective-permute-start | bytes 1376264 | tf_op jit(solution)/shard_map/ppermute | solution.py:17
  188.9 17.4 %collective-permute-start.10 = (bf16[1,128,896]{2,1,0:T(8,128)(2,1)S(1)}, bf16[1,128,896]{2,1,0:T(8,128)(2,1)S(1)}, u32[]{:S(2)}, u32[]{:S(2)}) collective-permute-start(bf16[1,128,896]{2,1,0:T(8,128)(2,1)S(1)} %copy-done.13), channel_id=1, source_target_pairs={{0,1},{1,2},{2,3},{3,0},{4,5},{5,6},{6,7},{7,4},{8,9},{9,10},{10,1... | collective-permute-start | bytes 688136 | tf_op jit(solution)/shard_map/ppermute | solution.py:17
  190.9 16.9 %copy-start.12 = (bf16[1,128,896]{2,1,0:T(8,128)(2,1)}, bf16[1,128,896]{2,1,0:T(8,128)(2,1)S(1)}, u32[]{:S(2)}) copy-start(bf16[1,128,896]{2,1,0:T(8,128)(2,1)S(1)} %collective-permute-done.11.refs_2_) | copy-start | bytes 688132
  191.0 25.2 %collective-permute-start.6 = (bf16[2,128,896]{2,1,0:T(8,128)(2,1)S(1)}, bf16[2,128,896]{2,1,0:T(8,128)(2,1)}, u32[]{:S(2)}, u32[]{:S(2)}) collective-permute-start(bf16[2,128,896]{2,1,0:T(8,128)(2,1)S(1)} %get-tuple-element.25), channel_id=1, source_target_pairs={{0,1},{1,2},{2,3},{3,0},{4,5},{5,6},{6,7},{7,4},{8,9},{9,10},{10,1... | collective-permute-start | bytes 1376264 | tf_op jit(solution)/shard_map/ppermute | solution.py:17
  206.3 13.0 %collective-permute-start.3 = (bf16[1,128,896]{2,1,0:T(8,128)(2,1)}, bf16[1,128,896]{2,1,0:T(8,128)(2,1)}, u32[]{:S(2)}, u32[]{:S(2)}) collective-permute-start(bf16[1,128,896]{2,1,0:T(8,128)(2,1)} %get-tuple-element.29), channel_id=1, source_target_pairs={{0,3},{1,0},{2,1},{3,2},{4,7},{5,4},{6,5},{7,6},{8,11},{9,8},{10,9... | collective-permute-start | bytes 688136 | tf_op jit(solution)/shard_map/ppermute | solution.py:17
  206.8 9.4 %copy-start.5 = (bf16[2,128,896]{2,1,0:T(8,128)(2,1)}, bf16[2,128,896]{2,1,0:T(8,128)(2,1)S(1)}, u32[]{:S(2)}) copy-start(bf16[2,128,896]{2,1,0:T(8,128)(2,1)S(1)} %collective-permute-done.8.refs_7_) | copy-start | bytes 1376260
  206.8 13.8 %collective-permute-start.2 = (bf16[1,128,896]{2,1,0:T(8,128)(2,1)}, bf16[1,128,896]{2,1,0:T(8,128)(2,1)}, u32[]{:S(2)}, u32[]{:S(2)}) collective-permute-start(bf16[1,128,896]{2,1,0:T(8,128)(2,1)} %get-tuple-element.30), channel_id=1, source_target_pairs={{0,2},{1,3},{2,0},{3,1},{4,6},{5,7},{6,4},{7,5},{8,10},{9,11},{10,... | collective-permute-start | bytes 688136 | tf_op jit(solution)/shard_map/ppermute | solution.py:17
  207.9 16.6 %collective-permute-start.1 = (bf16[1,128,896]{2,1,0:T(8,128)(2,1)}, bf16[1,128,896]{2,1,0:T(8,128)(2,1)}, u32[]{:S(2)}, u32[]{:S(2)}) collective-permute-start(bf16[1,128,896]{2,1,0:T(8,128)(2,1)} %get-tuple-element.31), channel_id=1, source_target_pairs={{0,1},{1,2},{2,3},{3,0},{4,5},{5,6},{6,7},{7,4},{8,9},{9,10},{10,1... | collective-permute-start | bytes 688136 | tf_op jit(solution)/shard_map/ppermute | solution.py:17
  216.2 18.6 %collective-permute-start.32 = (bf16[4,64,1024]{2,1,0:T(8,128)(2,1)}, bf16[4,64,1024]{2,1,0:T(8,128)(2,1)}, u32[]{:S(2)}, u32[]{:S(2)}) collective-permute-start(bf16[4,64,1024]{2,1,0:T(8,128)(2,1)} %pad_maximum_fusion.4), channel_id=1, source_target_pairs={{0,8},{8,0},{1,9},{9,1},{2,10},{10,2},{3,11},{11,3},{4,12},{12,4},... | collective-permute-start | bytes 1572872 | tf_op jit(solution)/shard_map/ppermute | solution.py:17
  219.3 15.6 %collective-permute-start.14 = (bf16[128,896]{1,0:T(8,128)(2,1)}, bf16[128,896]{1,0:T(8,128)(2,1)S(1)}, u32[]{:S(2)}, u32[]{:S(2)}) collective-permute-start(bf16[128,896]{1,0:T(8,128)(2,1)} %get-tuple-element.17), channel_id=1, source_target_pairs={{0,4},{4,0},{1,5},{5,1},{2,6},{6,2},{3,7},{7,3},{8,12},{12,8},{9,1... | collective-permute-start | bytes 688136 | tf_op jit(solution)/shard_map/ppermute | solution.py:17
  227.5 7.3 %collective-permute-start.13 = (bf16[128,896]{1,0:T(8,128)(2,1)}, bf16[128,896]{1,0:T(8,128)(2,1)S(1)}, u32[]{:S(2)}, u32[]{:S(2)}) collective-permute-start(bf16[128,896]{1,0:T(8,128)(2,1)} %get-tuple-element.16), channel_id=1, source_target_pairs={{0,4},{4,0},{1,5},{5,1},{2,6},{6,2},{3,7},{7,3},{8,12},{12,8},{9,1... | collective-permute-start | bytes 688136 | tf_op jit(solution)/shard_map/ppermute | solution.py:17
  266.6 11.4 %all-to-all-start.3 = ((f32[16,2,16]{2,1,0:T(2,128)}), f32[16,2,16]{2,1,0:T(2,128)S(1)}, u32[]{:S(2)}, u32[]{:S(2)}) async-start(f32[16,2,16]{2,1,0:T(2,128)} %broadcast_in_dim.8), calls=%async_computation.3 | async-start | bytes 32768 | tf_op jit(solution)/shard_map/all_to_all | solution.py:35
  (9 other events, 25.8 us)
Sparse Core Ops, SparseCore 0:
  9.1 34.1 all-gather.4
  45.1 36.7 all-gather.8
  95.4 43.5 all-gather.6

commit v7 on v6

--- a/solution.py
+++ b/solution.py
@@ -125,7 +125,7 @@
 
 
 def score_kernel(
-    at_ref, k0, k1, g0, g1, v0, v1, v2, v3, other, inv0, inv1, query, out, flipped, total, act, held
+    at_ref, k0, k1, g0, g1, v0, v1, va, vb, v3, other, inv0, inv1, query, out, flipped, total, act, held
 ):
     step = pl.program_id(0)
     n = inv0.shape[0]
@@ -141,13 +141,20 @@
             flipped[s] = grad.T.astype(BF)
         total[...] = jnp.zeros_like(total)
 
-    for d, ref in enumerate((v0, v1, v2, v3)):
+    strip = pl.ds(pl.multiple_of(lax.rem(step, 2) * cols, cols), cols)
+    for d, ref in ((0, v0), (1, v1), (3, v3)):
 
         @pl.when(step // 2 == d)
         def _(ref=ref):
-            here = pl.ds(pl.multiple_of(lax.rem(step, 2) * cols, cols), cols)
-            act[...] = ref[: 2 * tokens, here]
-            held[:half, :] = ref[2 * tokens :, here]
+            act[...] = ref[: 2 * tokens, strip]
+            held[:half, :] = ref[2 * tokens :, strip]
+
+    @pl.when(step // 2 == 2)
+    def _():
+        mid = va.shape[0]
+        act[:mid, :] = va[:, strip]
+        act[mid:, :] = vb[: 2 * tokens - mid, strip]
+        held[:half, :] = vb[2 * tokens - mid :, strip]
 
     held[half:, :] = other[0]
     for e in range(2):
@@ -256,8 +263,14 @@
     act_rot = jnp.concatenate(
         [jnp.where(same, part, minus), jnp.where(same, far, plus), value], 0
     )
-    act_rot = gather(act_rot, "y")
-    value_other = shift(jnp.stack([a[2 * tokens :] for a in act_rot]), "c", 1)
+    mid = act_rot.shape[0] // 2
+    plus, minus = shift(act_rot, "y", -1), shift(act_rot, "y", 1)
+    far_a = shift(plus[:mid], "y", -1)
+    far_b = shift(minus[mid:], "y", 1)
+    value_other = [a[2 * tokens :] for a in (act_rot, plus)]
+    value_other += [far_b[2 * tokens - mid :], minus[2 * tokens :]]
+    value_other = shift(jnp.stack(value_other), "c", 1)
+    act_rot = (act_rot, plus, far_a, far_b, minus)
 
     grad = grad_out[0]
     plus, far, minus = (shift(grad, "zh", -by) for by in (1, 2, 3))

time: 288 us -> 293 us (1.017)
  starting transfers between devices: 84.6 us -> 96.7 us
  waiting for transfers between devices: 94.5 us -> 84.9 us
  local copies, waits for them, and re-layouts: 14.5 us -> 17.8 us
    ppermute x31 -> x32, starting transfers between devices: 57.6 us -> 69.5 us  [shift(): return lax.ppermute(value, axis, [(i, (i + by) % n) for i in range(n)])]
    ppermute x31 -> x32, waiting for transfers between devices: 76.8 us -> 66.7 us  [shift(): return lax.ppermute(value, axis, [(i, (i + by) % n) for i in range(n)])]
    unnamed x35 -> x43, local copies, waits for them, and re-layouts: 4.71 us -> 5.98 us
  transfers between devices with their start and end apart: 41 -> 42, of which waited for: 18 -> 17; matrix products, arithmetic and copies ran while one was open for 16% -> 17% of each run, Pallas kernels for 3% -> 3%
where the time goes in v7:
time: 293 us; the launch traced here: 290 us
  starting transfers between devices  96.7 us (33%)
  waiting for transfers between devices  84.9 us (29%)
  Pallas kernels  25.4 us (9%)
  other arithmetic  20.7 us (7%)
  local copies, waits for them, and re-layouts  17.8 us (6%)
  matrix products  17.2 us (6%)
  between operations  13.5 us (5%)
  blocking collectives  13.4 us (5%)
    ppermute x32, starting transfers between devices, shift(): return lax.ppermute(value, axis, [(i, (i + by) % n) for i in range(n)])  69.5 us
    ppermute x32, waiting for transfers between devices, shift(): return lax.ppermute(value, axis, [(i, (i + by) % n) for i in range(n)])  66.7 us
    dot_general x4, matrix products, dot_t(): lax.dot_general(a, b, (((1,), (1,)), ((), ())), preferred_element_type=F32)  17.2 us
    all_to_all x3, starting transfers between devices, exchange(): return lax.all_to_all(value, axes, 0, 0, tiled=True)  17.1 us
    pallas_call x1, Pallas kernels, score(): pl.pallas_call(score_kernel, grid_spec=spec, out_shape=jax.ShapeDtypeStru...  15.5 us
    all_to_all x1, blocking collectives, exchange(): return lax.all_to_all(value, axes, 0, 0, tiled=True)  13.4 us
    all_to_all x3, waiting for transfers between devices, exchange(): return lax.all_to_all(value, axes, 0, 0, tiled=True)  10 us
    ppermute x3, starting transfers between devices, from_owner(): return lax.ppermute(value, ('zh', 'zl'), pairs)  8.74 us
  transfers between devices with their start and end apart: 42, of which 17 were waited for; matrix products, arithmetic and copies ran while one was open for 17% of the time, Pallas kernels for 3%

profile of v7, /device:TPU:2, one launch (start us, length us, event | category | flops | bytes accessed | tf_op | source)
XLA Modules:
  0.0 289.6 jit_solution(12740433798105106251)
XLA Ops:
  7.3 7.3 %collective-permute-start.9 = (bf16[128,1792]{1,0:T(8,128)(2,1)}, bf16[128,1792]{1,0:T(8,128)(2,1)S(1)}, u32[]{:S(2)}, u32[]{:S(2)}) collective-permute-start(bf16[128,1792]{1,0:T(8,128)(2,1)} %bitcast.83), channel_id=1, source_target_pairs={{0,32},{16,48},{32,0},{48,16},{1,33},{17,49},{33,1},{49,17},{2,34}... | collective-permute-start | bytes 1376264 | tf_op jit(solution)/shard_map/ppermute | solution.py:17
  14.6 13.0 %collective-permute-done.9 = bf16[128,1792]{1,0:T(8,128)(2,1)S(1)} collective-permute-done((bf16[128,1792]{1,0:T(8,128)(2,1)}, bf16[128,1792]{1,0:T(8,128)(2,1)S(1)}, u32[]{:S(2)}, u32[]{:S(2)}) %collective-permute-start.9) | collective-permute-done | bytes 458784 | tf_op jit(solution)/shard_map/ppermute | solution.py:17
  28.4 12.3 %collective-permute-start.18 = (bf16[512,128]{1,0:T(8,128)(2,1)}, bf16[512,128]{1,0:T(8,128)(2,1)S(1)}, u32[]{:S(2)}, u32[]{:S(2)}) collective-permute-start(bf16[512,128]{1,0:T(8,128)(2,1)} %param.10), channel_id=1, source_target_pairs={{0,48},{16,0},{32,16},{48,32},{1,49},{17,1},{33,17},{49,33},{2,50}... | collective-permute-start | bytes 393224 | tf_op jit(solution)/shard_map/ppermute | solution.py:17
  40.7 3.3 %collective-permute-start.19 = (bf16[512,128]{1,0:T(8,128)(2,1)}, bf16[512,128]{1,0:T(8,128)(2,1)S(1)}, u32[]{:S(2)}, u32[]{:S(2)}) collective-permute-start(bf16[512,128]{1,0:T(8,128)(2,1)} %param.10), channel_id=1, source_target_pairs={{0,32},{16,48},{32,0},{48,16},{1,33},{17,49},{33,1},{49,17},{2,34}... | collective-permute-start | bytes 393224 | tf_op jit(solution)/shard_map/ppermute | solution.py:17
  44.0 5.4 %collective-permute-done.18 = bf16[512,128]{1,0:T(8,128)(2,1)S(1)} collective-permute-done((bf16[512,128]{1,0:T(8,128)(2,1)}, bf16[512,128]{1,0:T(8,128)(2,1)S(1)}, u32[]{:S(2)}, u32[]{:S(2)}) %collective-permute-start.18) | collective-permute-done | bytes 131104 | tf_op jit(solution)/shard_map/ppermute | solution.py:17
  49.4 3.3 %collective-permute-done.20 = bf16[512,128]{1,0:T(8,128)(2,1)S(1)} collective-permute-done((bf16[512,128]{1,0:T(8,128)(2,1)}, bf16[512,128]{1,0:T(8,128)(2,1)S(1)}, u32[]{:S(2)}, u32[]{:S(2)}) %collective-permute-start.20) | collective-permute-done | bytes 131104 | tf_op jit(solution)/shard_map/ppermute | solution.py:17
  55.3 4.3 %collective-permute-start.5 = (bf16[128,1792]{1,0:T(8,128)(2,1)}, bf16[128,1792]{1,0:T(8,128)(2,1)S(1)}, u32[]{:S(2)}, u32[]{:S(2)}) collective-permute-start(bf16[128,1792]{1,0:T(8,128)(2,1)} %bitcast.84), channel_id=1, source_target_pairs={{0,16},{16,32},{32,48},{48,0},{1,17},{17,33},{33,49},{49,1},{2,18}... | collective-permute-start | bytes 1376264 | tf_op jit(solution)/shard_map/ppermute | solution.py:17
  61.2 8.8 %collective-permute-done.17.a3 = bf16[128,512]{1,0:T(8,128)(2,1)} collective-permute-done((bf16[128,512]{1,0:T(8,128)(2,1)}, bf16[128,512]{1,0:T(8,128)(2,1)}, u32[]{:S(2)}, u32[]{:S(2)}) %collective-permute-start.17) | collective-permute-done | bytes 131104 | tf_op jit(solution)/shard_map/ppermute | solution.py:17
  70.0 2.0 collective-permute-start.16
  71.9 8.5 %collective-permute-done.16.a2 = bf16[128,512]{1,0:T(8,128)(2,1)} collective-permute-done((bf16[128,512]{1,0:T(8,128)(2,1)}, bf16[128,512]{1,0:T(8,128)(2,1)}, u32[]{:S(2)}, u32[]{:S(2)}) %collective-permute-start.16) | collective-permute-done | bytes 131104 | tf_op jit(solution)/shard_map/ppermute | solution.py:17
  83.4 2.3 collective-permute-done.15.a1
  85.7 3.8 %rotate_in.1 = (bf16[128,1024]{1,0:T(8,128)(2,1)}, bf16[128,1024]{1,0:T(8,128)(2,1)}, bf16[128,1024]{1,0:T(8,128)(2,1)}, bf16[128,1024]{1,0:T(8,128)(2,1)}, bf16[64,1024]{1,0:T(8,128)(2,1)}) custom-call(s32[5]{0:T(128)} %stack.69.at_ref, bf16[128,512]{1,0:T(8,128)(2,1)} %bitcast.98, bf16[128,512]{1,0:T(8,128)(2,1)} %collective-permute-done.15.a1, ...), custom_call_target="tpu_custom_call" | custom-call | flops 536870912 | bytes 2621440 | tf_op jit(solution)/shard_map/rotate_in/pallas_call | solution.py:73
  92.1 2.2 collective-permute-start.24
  95.3 2.7 collective-permute-done.22
  98.0 2.9 collective-permute-done.23
  100.9 2.1 collective-permute-done.24
  105.6 7.3 %collective-permute-done.25 = bf16[128,1024]{1,0:T(8,128)(2,1)S(1)} collective-permute-done((bf16[128,1024]{1,0:T(8,128)(2,1)S(1)}, bf16[128,1024]{1,0:T(8,128)(2,1)S(1)}, u32[]{:S(2)}, u32[]{:S(2)}) %collective-permute-start.25) | collective-permute-done | bytes 262176 | tf_op jit(solution)/shard_map/ppermute | solution.py:31
  114.3 5.4 %collective-permute-start.27 = (bf16[128,1024]{1,0:T(8,128)(2,1)S(1)}, bf16[128,1024]{1,0:T(8,128)(2,1)S(1)}, u32[]{:S(2)}, u32[]{:S(2)}) collective-permute-start(bf16[128,1024]{1,0:T(8,128)(2,1)S(1)} %add_convert_fusion), channel_id=1, source_target_pairs={{0,32},{20,52},{32,0},{52,20},{1,33},{21,53},{33,1},{53,21},{2,34}... | collective-permute-start | bytes 786440 | tf_op jit(solution)/shard_map/ppermute | solution.py:26
  119.8 2.0 collective-permute-start.26
  121.8 1.6 pad_maximum_fusion
  123.4 1.7 copy-done.2
  126.9 4.2 %all-to-all-start = ((bf16[8,8,1920]{2,1,0:T(8,128)(2,1)}), bf16[8,8,1920]{2,1,0:T(8,128)(2,1)S(1)}, u32[]{:S(2)}, u32[]{:S(2)}) async-start(bf16[8,8,1920]{2,1,0:T(8,128)(2,1)} %maximum_bitcast_fusion), calls=%async_computation | async-start | bytes 491520 | tf_op jit(solution)/shard_map/all_to_all | solution.py:35
  131.1 6.0 %convert_divide_fusion.1.inv0 = f32[448,4096]{1,0:T(8,128)} fusion(bf16[448,4096]{1,0:T(8,128)(2,1)} %param.11), kind=kLoop, calls=%fused_computation.1 | loop fusion | flops 3670016 | bytes 11010048 | tf_op jit(solution)/shard_map/div | solution.py:236
  137.9 6.7 %all-to-all-start.1 = ((bf16[8,8,1920]{2,1,0:T(8,128)(2,1)}), bf16[8,8,1920]{2,1,0:T(8,128)(2,1)S(1)}, u32[]{:S(2)}, u32[]{:S(2)}) async-start(bf16[8,8,1920]{2,1,0:T(8,128)(2,1)} %broadcast_in_dim.6), calls=%async_computation.1 | async-start | bytes 491520 | tf_op jit(solution)/shard_map/all_to_all | solution.py:35
  144.6 5.3 %all-to-all-done.1 = bf16[8,8,1920]{2,1,0:T(8,128)(2,1)S(1)} async-done(((bf16[8,8,1920]{2,1,0:T(8,128)(2,1)}), bf16[8,8,1920]{2,1,0:T(8,128)(2,1)S(1)}, u32[]{:S(2)}, u32[]{:S(2)}) %all-to-all-start.1) | async-done | bytes 245792 | tf_op jit(solution)/shard_map/all_to_all | solution.py:35
  152.0 2.2 collective-permute-start.31
  156.6 4.6 %convolution_convert_fusion.2 = bf16[896,512]{0,1:T(8,128)(2,1)S(1)} fusion(bf16[896,1792]{1,0:T(8,128)(2,1)} %copy-done.2, bf16[512,1792]{1,0:T(8,128)(2,1)} %bitcast.94), kind=kOutput, calls=%fused_computation.5 | convolution fusion | flops 1644625920 | bytes 5963776 | tf_op jit(solution)/shard_map/dot_general | solution.py:47
  162.1 9.0 %collective-permute-done.31.v3 = bf16[320,1024]{1,0:T(8,128)(2,1)S(1)} collective-permute-done((bf16[320,1024]{1,0:T(8,128)(2,1)}, bf16[320,1024]{1,0:T(8,128)(2,1)S(1)}, u32[]{:S(2)}, u32[]{:S(2)}) %collective-permute-start.31) | collective-permute-done | bytes 655392 | tf_op jit(solution)/shard_map/ppermute | solution.py:17
  172.3 4.6 %convolution_convert_fusion.1 = bf16[896,512]{0,1:T(8,128)(2,1)S(1)} fusion(bf16[896,1792]{1,0:T(8,128)(2,1)} %copy-done.2, bf16[512,1792]{1,0:T(8,128)(2,1)} %all-gather.9.cloned.1.call-done), kind=kOutput, calls=%fused_computation.4 | convolution fusion | flops 1644625920 | bytes 5963776 | tf_op jit(solution)/shard_map/dot_general | solution.py:47
  178.6 1.8 collective-permute-start.12
  180.7 7.0 %convolution_convert_fusion = bf16[1024,896]{1,0:T(8,128)(2,1)S(1)} fusion(bf16[1024,1792]{1,0:T(8,128)(2,1)} %bitcast.93, bf16[896,1792]{1,0:T(8,128)(2,1)} %copy-done.2), kind=kOutput, calls=%fused_computation.3 | convolution fusion | flops 3289251840 | bytes 8716288 | tf_op jit(solution)/shard_map/dot_general | solution.py:47
  187.8 2.3 collective-permute-start.10
  191.8 3.0 %collective-permute-start.7 = (bf16[2,128,896]{2,1,0:T(8,128)(2,1)S(1)}, bf16[2,128,896]{2,1,0:T(8,128)(2,1)S(1)}, u32[]{:S(2)}, u32[]{:S(2)}) collective-permute-start(bf16[2,128,896]{2,1,0:T(8,128)(2,1)S(1)} %get-tuple-element.24), channel_id=1, source_target_pairs={{0,2},{1,3},{2,0},{3,1},{4,6},{5,7},{6,4},{7,5},{8,10},{9,11},{10,... | collective-permute-start | bytes 1376264 | tf_op jit(solution)/shard_map/ppermute | solution.py:17
  195.7 9.5 %collective-permute-start.6 = (bf16[2,128,896]{2,1,0:T(8,128)(2,1)S(1)}, bf16[2,128,896]{2,1,0:T(8,128)(2,1)}, u32[]{:S(2)}, u32[]{:S(2)}) collective-permute-start(bf16[2,128,896]{2,1,0:T(8,128)(2,1)S(1)} %get-tuple-element.25), channel_id=1, source_target_pairs={{0,1},{1,2},{2,3},{3,0},{4,5},{5,6},{6,7},{7,4},{8,9},{9,10},{10,1... | collective-permute-start | bytes 1376264 | tf_op jit(solution)/shard_map/ppermute | solution.py:17
  206.2 1.7 slice.51
  207.9 3.4 %collective-permute-done.8.refs_7_ = bf16[2,128,896]{2,1,0:T(8,128)(2,1)S(1)} collective-permute-done((bf16[2,128,896]{2,1,0:T(8,128)(2,1)S(1)}, bf16[2,128,896]{2,1,0:T(8,128)(2,1)S(1)}, u32[]{:S(2)}, u32[]{:S(2)}) %collective-permute-start.8) | collective-permute-done | bytes 458784 | tf_op jit(solution)/shard_map/ppermute | solution.py:17
  211.3 6.0 %collective-permute-start.2 = (bf16[1,128,896]{2,1,0:T(8,128)(2,1)}, bf16[1,128,896]{2,1,0:T(8,128)(2,1)}, u32[]{:S(2)}, u32[]{:S(2)}) collective-permute-start(bf16[1,128,896]{2,1,0:T(8,128)(2,1)} %get-tuple-element.30), channel_id=1, source_target_pairs={{0,2},{1,3},{2,0},{3,1},{4,6},{5,7},{6,4},{7,5},{8,10},{9,11},{10,... | collective-permute-start | bytes 688136 | tf_op jit(solution)/shard_map/ppermute | solution.py:17
  218.2 2.7 collective-permute-done.6.refs_5_
  220.9 3.1 %collective-permute-start.30 = (bf16[160,1024]{1,0:T(8,128)(2,1)}, bf16[160,1024]{1,0:T(8,128)(2,1)}, u32[]{:S(2)}, u32[]{:S(2)}) collective-permute-start(bf16[160,1024]{1,0:T(8,128)(2,1)} %slice.51), channel_id=1, source_target_pairs={{0,192},{64,0},{128,64},{192,128},{1,193},{65,1},{129,65},{193,129... | collective-permute-start | bytes 983048 | tf_op jit(solution)/shard_map/ppermute | solution.py:17
  224.0 3.0 %shard_map.74 = (bf16[128,896]{1,0:T(8,128)(2,1)}, bf16[128,896]{1,0:T(8,128)(2,1)}) custom-call(s32[5]{0:T(128)} %stack.69.at_ref, bf16[4,1,128,896]{3,2,1,0:T(8,128)(2,1)} %bitcast.75, bf16[1,128,896]{2,1,0:T(8,128)(2,1)} %copy-done.18, bf16[1,128,896]{2,1,0:T(8,128)(2,1)} %copy-done.17, bf16[1,128,896]{2,1,0:T(8,128)(2,1)} %copy-done.16, ...), custom_call_target="tpu_custom_call" | custom-call | flops 917504 | bytes 2293760 | tf_op jit(solution)/shard_map/pallas_call | solution.py:117
  227.6 3.1 %shard_map.73 = (bf16[128,896]{1,0:T(8,128)(2,1)}, bf16[128,896]{1,0:T(8,128)(2,1)}) custom-call(s32[5]{0:T(128)} %stack.69.at_ref, bf16[4,1,128,896]{3,2,1,0:T(8,128)(2,1)} %bitcast.73, bf16[1,128,896]{2,1,0:T(8,128)(2,1)} %collective-permute-done.1.refs_1_, bf16[1,128,896]{2,1,0:T(8,128)(2,1)} %collective-permute-done.2.refs_2_, ...), custom_call_target="tpu_custom_call" | custom-call | flops 917504 | bytes 2293760 | tf_op jit(solution)/shard_map/pallas_call | solution.py:117
  230.7 1.8 collective-permute-start.13
  232.4 6.0 %convert_divide_fusion.inv1 = f32[448,4096]{1,0:T(8,128)} fusion(bf16[448,4096]{1,0:T(8,128)(2,1)} %collective-permute-done.34), kind=kLoop, calls=%fused_computation | loop fusion | flops 3670016 | bytes 11010048 | tf_op jit(solution)/shard_map/div | solution.py:237
  238.5 1.8 collective-permute-done.13.g0
  241.0 15.5 %score.1 = f32[8,128]{1,0:T(8,128)} custom-call(s32[5]{0:T(128)} %stack.69.at_ref, bf16[128,896]{1,0:T(8,128)(2,1)} %get-tuple-element.14.k0, bf16[128,896]{1,0:T(8,128)(2,1)} %get-tuple-element.15.k1, bf16[128,896]{1,0:T(8,128)(2,1)} %copy-done.15, bf16[128,896]{1,0:T(8,128)(2,1)} %copy-done.14, bf16[320,1024]{1,0:T(8,128)(2,1)} %pad_maximum_fusion.2.v0, ...), custom_call_target="tpu_custom_call" | custom-call | flops 3758096384 | bytes 14680064 | tf_op jit(solution)/shard_map/score/pallas_call | solution.py:206
  257.5 13.4 %all_to_all.20 = f32[16,2,16]{2,1,0:T(2,128)S(1)} all-to-all(f32[16,2,16]{2,1,0:T(2,128)S(1)} %broadcast_in_dim.7), channel_id=1, replica_groups=mesh['y'=4,'zh'=4,'c'=2,'zl'=2,'x'=4] {'y','zh'}, dimensions={0} | all-to-all | bytes 4096 | tf_op jit(solution)/shard_map/all_to_all | solution.py:35
  271.5 6.2 %all-to-all-start.3 = ((f32[16,2,16]{2,1,0:T(2,128)}), f32[16,2,16]{2,1,0:T(2,128)S(1)}, u32[]{:S(2)}, u32[]{:S(2)}) async-start(f32[16,2,16]{2,1,0:T(2,128)} %broadcast_in_dim.8), calls=%async_computation.3 | async-start | bytes 32768 | tf_op jit(solution)/shard_map/all_to_all | solution.py:35
  277.8 4.7 %all-to-all-done.3 = f32[16,2,16]{2,1,0:T(2,128)S(1)} async-done(((f32[16,2,16]{2,1,0:T(2,128)}), f32[16,2,16]{2,1,0:T(2,128)S(1)}, u32[]{:S(2)}, u32[]{:S(2)}) %all-to-all-start.3) | async-done | bytes 2080 | tf_op jit(solution)/shard_map/all_to_all | solution.py:35
  (133 shorter events, 35.7 us)
Async XLA Ops:
  6.5 116.9 %copy-start = (bf16[16,8,1792]{2,1,0:T(8,128)(2,1)S(1)}, bf16[16,8,1792]{2,1,0:T(8,128)(2,1)}, u32[]{:S(2)}) copy-start(bf16[16,8,1792]{2,1,0:T(8,128)(2,1)} %param.12) | copy-start | bytes 1376260
  6.5 150.1 %all-gather.5.cloned.1.call-start = ((), (), s32[]{:S(2)}) async-start(), calls=%async_computation.4 | async-start | bytes 2293760 | tf_op jit(solution)/shard_map/all_gather | solution.py:280
  7.3 165.0 %all-gather.9.cloned.1.call-start = ((), (), s32[]{:S(2)}) async-start(), calls=%async_computation.6 | async-start | bytes 2293760 | tf_op jit(solution)/shard_map/all_gather | solution.py:280
  7.3 20.3 %collective-permute-start.9 = (bf16[128,1792]{1,0:T(8,128)(2,1)}, bf16[128,1792]{1,0:T(8,128)(2,1)S(1)}, u32[]{:S(2)}, u32[]{:S(2)}) collective-permute-start(bf16[128,1792]{1,0:T(8,128)(2,1)} %bitcast.83), channel_id=1, source_target_pairs={{0,32},{16,48},{32,0},{48,16},{1,33},{17,49},{33,1},{49,17},{2,34}... | collective-permute-start | bytes 1376264 | tf_op jit(solution)/shard_map/ppermute | solution.py:17
  28.4 152.3 %all-gather.7.cloned.1.call-start = ((), (), s32[]{:S(2)}) async-start(), calls=%async_computation.5 | async-start | bytes 4587520 | tf_op jit(solution)/shard_map/all_gather | solution.py:280
  28.4 21.0 %collective-permute-start.18 = (bf16[512,128]{1,0:T(8,128)(2,1)}, bf16[512,128]{1,0:T(8,128)(2,1)S(1)}, u32[]{:S(2)}, u32[]{:S(2)}) collective-permute-start(bf16[512,128]{1,0:T(8,128)(2,1)} %param.10), channel_id=1, source_target_pairs={{0,48},{16,0},{32,16},{48,32},{1,49},{17,1},{33,17},{49,33},{2,50}... | collective-permute-start | bytes 393224 | tf_op jit(solution)/shard_map/ppermute | solution.py:17
  40.7 12.0 %collective-permute-start.20 = (bf16[512,128]{1,0:T(8,128)(2,1)}, bf16[512,128]{1,0:T(8,128)(2,1)S(1)}, u32[]{:S(2)}, u32[]{:S(2)}) collective-permute-start(bf16[512,128]{1,0:T(8,128)(2,1)} %param.10), channel_id=1, source_target_pairs={{0,16},{16,32},{32,48},{48,0},{1,17},{17,33},{33,49},{49,1},{2,18}... | collective-permute-start | bytes 393224 | tf_op jit(solution)/shard_map/ppermute | solution.py:17
  40.7 13.0 %collective-permute-start.19 = (bf16[512,128]{1,0:T(8,128)(2,1)}, bf16[512,128]{1,0:T(8,128)(2,1)S(1)}, u32[]{:S(2)}, u32[]{:S(2)}) collective-permute-start(bf16[512,128]{1,0:T(8,128)(2,1)} %param.10), channel_id=1, source_target_pairs={{0,32},{16,48},{32,0},{48,16},{1,33},{17,49},{33,1},{49,17},{2,34}... | collective-permute-start | bytes 393224 | tf_op jit(solution)/shard_map/ppermute | solution.py:17
  54.7 31.0 %copy-start.11 = (bf16[4,512,128]{2,1,0:T(8,128)(2,1)}, bf16[4,512,128]{2,1,0:T(8,128)(2,1)S(1)}, u32[]{:S(2)}) copy-start(bf16[4,512,128]{2,1,0:T(8,128)(2,1)S(1)} %pad_maximum_fusion.3.w0) | copy-start | bytes 1572868
  54.7 31.0 %collective-permute-start.21 = (bf16[4,512,128]{2,1,0:T(8,128)(2,1)S(1)}, bf16[4,512,128]{2,1,0:T(8,128)(2,1)}, u32[]{:S(2)}, u32[]{:S(2)}) collective-permute-start(bf16[4,512,128]{2,1,0:T(8,128)(2,1)S(1)} %pad_maximum_fusion.3.w0), channel_id=1, source_target_pairs={{0,8},{8,0},{1,9},{9,1},{2,10},{10,2},{3,11},{11,3},{4,12},{12,4},... | collective-permute-start | bytes 1572872 | tf_op jit(solution)/shard_map/ppermute | solution.py:17
  54.8 67.0 %collective-permute-start = (bf16[448,1792]{1,0:T(8,128)(2,1)}, bf16[448,1792]{1,0:T(8,128)(2,1)}, u32[]{:S(2)}, u32[]{:S(2)}) collective-permute-start(bf16[448,1792]{1,0:T(8,128)(2,1)} %bitcast.76), channel_id=1, source_target_pairs={{0,8},{8,0},{1,9},{9,1},{2,10},{10,2},{3,11},{11,3},{4,12},{12,4},... | collective-permute-start | bytes 4816904 | tf_op jit(solution)/shard_map/ppermute | solution.py:17
  55.3 36.8 %collective-permute-start.5 = (bf16[128,1792]{1,0:T(8,128)(2,1)}, bf16[128,1792]{1,0:T(8,128)(2,1)S(1)}, u32[]{:S(2)}, u32[]{:S(2)}) collective-permute-start(bf16[128,1792]{1,0:T(8,128)(2,1)} %bitcast.84), channel_id=1, source_target_pairs={{0,16},{16,32},{32,48},{48,0},{1,17},{17,33},{33,49},{49,1},{2,18}... | collective-permute-start | bytes 1376264 | tf_op jit(solution)/shard_map/ppermute | solution.py:17
  59.6 34.6 %collective-permute-start.4 = (bf16[128,1792]{1,0:T(8,128)(2,1)}, bf16[128,1792]{1,0:T(8,128)(2,1)S(1)}, u32[]{:S(2)}, u32[]{:S(2)}) collective-permute-start(bf16[128,1792]{1,0:T(8,128)(2,1)} %bitcast.85), channel_id=1, source_target_pairs={{0,48},{16,0},{32,16},{48,32},{1,49},{17,1},{33,17},{49,33},{2,50}... | collective-permute-start | bytes 1376264 | tf_op jit(solution)/shard_map/ppermute | solution.py:17
  59.6 10.4 %collective-permute-start.17 = (bf16[128,512]{1,0:T(8,128)(2,1)}, bf16[128,512]{1,0:T(8,128)(2,1)}, u32[]{:S(2)}, u32[]{:S(2)}) collective-permute-start(bf16[128,512]{1,0:T(8,128)(2,1)} %bitcast.95), channel_id=1, source_target_pairs={{0,64},{64,128},{128,192},{192,0},{1,65},{65,129},{129,193},{193,1... | collective-permute-start | bytes 393224 | tf_op jit(solution)/shard_map/ppermute | solution.py:17
  70.0 10.4 %collective-permute-start.16 = (bf16[128,512]{1,0:T(8,128)(2,1)}, bf16[128,512]{1,0:T(8,128)(2,1)}, u32[]{:S(2)}, u32[]{:S(2)}) collective-permute-start(bf16[128,512]{1,0:T(8,128)(2,1)} %bitcast.96), channel_id=1, source_target_pairs={{0,128},{64,192},{128,0},{192,64},{1,129},{65,193},{129,1},{193,65... | collective-permute-start | bytes 393224 | tf_op jit(solution)/shard_map/ppermute | solution.py:17
  80.4 5.3 %collective-permute-start.15 = (bf16[128,512]{1,0:T(8,128)(2,1)}, bf16[128,512]{1,0:T(8,128)(2,1)}, u32[]{:S(2)}, u32[]{:S(2)}) collective-permute-start(bf16[128,512]{1,0:T(8,128)(2,1)} %bitcast.97), channel_id=1, source_target_pairs={{0,192},{64,0},{128,64},{192,128},{1,193},{65,1},{129,65},{193,129... | collective-permute-start | bytes 393224 | tf_op jit(solution)/shard_map/ppermute | solution.py:17
  83.4 38.4 %copy-start.8 = (bf16[1792,448]{0,1:T(8,128)(2,1)S(1)}, bf16[1792,448]{0,1:T(8,128)(2,1)}, u32[]{:S(2)}) copy-start(bf16[1792,448]{0,1:T(8,128)(2,1)} %param.9) | copy-start | bytes 4816900
  89.5 8.5 %collective-permute-start.22 = (bf16[128,1024]{1,0:T(8,128)(2,1)}, bf16[128,1024]{1,0:T(8,128)(2,1)S(1)}, u32[]{:S(2)}, u32[]{:S(2)}) collective-permute-start(bf16[128,1024]{1,0:T(8,128)(2,1)} %get-tuple-element.19), channel_id=1, source_target_pairs={{0,1},{1,2},{2,3},{3,0},{4,5},{5,6},{6,7},{7,4},{8,9},{9,10},{10,1... | collective-permute-start | bytes 786440 | tf_op jit(solution)/shard_map/ppermute | solution.py:17
  91.0 9.9 %collective-permute-start.23 = (bf16[128,1024]{1,0:T(8,128)(2,1)}, bf16[128,1024]{1,0:T(8,128)(2,1)S(1)}, u32[]{:S(2)}, u32[]{:S(2)}) collective-permute-start(bf16[128,1024]{1,0:T(8,128)(2,1)} %get-tuple-element.20), channel_id=1, source_target_pairs={{0,2},{1,3},{2,0},{3,1},{4,6},{5,7},{6,4},{7,5},{8,10},{9,11},{10,... | collective-permute-start | bytes 786440 | tf_op jit(solution)/shard_map/ppermute | solution.py:17
  92.1 10.9 %collective-permute-start.24 = (bf16[128,1024]{1,0:T(8,128)(2,1)}, bf16[128,1024]{1,0:T(8,128)(2,1)}, u32[]{:S(2)}, u32[]{:S(2)}) collective-permute-start(bf16[128,1024]{1,0:T(8,128)(2,1)} %get-tuple-element.21), channel_id=1, source_target_pairs={{0,3},{1,0},{2,1},{3,2},{4,7},{5,4},{6,5},{7,6},{8,11},{9,8},{10,9... | collective-permute-start | bytes 786440 | tf_op jit(solution)/shard_map/ppermute | solution.py:17
  104.2 8.7 %collective-permute-start.25 = (bf16[128,1024]{1,0:T(8,128)(2,1)S(1)}, bf16[128,1024]{1,0:T(8,128)(2,1)S(1)}, u32[]{:S(2)}, u32[]{:S(2)}) collective-permute-start(bf16[128,1024]{1,0:T(8,128)(2,1)S(1)} %add_convert_fusion.1), channel_id=1, source_target_pairs={{4,0},{16,20},{36,32},{48,52},{5,1},{17,21},{37,33},{49,53},{6,2},... | collective-permute-start | bytes 786440 | tf_op jit(solution)/shard_map/ppermute | solution.py:31
  105.5 126.9 %collective-permute-start.34 = (bf16[448,4096]{1,0:T(8,128)(2,1)}, bf16[448,4096]{1,0:T(8,128)(2,1)}, u32[]{:S(2)}, u32[]{:S(2)}) collective-permute-start(bf16[448,4096]{1,0:T(8,128)(2,1)} %param.11), channel_id=1, source_target_pairs={{0,8},{8,0},{1,9},{9,1},{2,10},{10,2},{3,11},{11,3},{4,12},{12,4},... | collective-permute-start | bytes 11010056 | tf_op jit(solution)/shard_map/ppermute | solution.py:17
  113.0 31.6 %collective-permute-start.28 = (bf16[128,1024]{1,0:T(8,128)(2,1)S(1)}, bf16[128,1024]{1,0:T(8,128)(2,1)S(1)}, u32[]{:S(2)}, u32[]{:S(2)}) collective-permute-start(bf16[128,1024]{1,0:T(8,128)(2,1)S(1)} %add_convert_fusion), channel_id=1, source_target_pairs={{0,48},{20,4},{32,16},{52,36},{1,49},{21,5},{33,17},{53,37},{2,50}... | collective-permute-start | bytes 786440 | tf_op jit(solution)/shard_map/ppermute | solution.py:26
  114.3 30.3 %collective-permute-start.27 = (bf16[128,1024]{1,0:T(8,128)(2,1)S(1)}, bf16[128,1024]{1,0:T(8,128)(2,1)S(1)}, u32[]{:S(2)}, u32[]{:S(2)}) collective-permute-start(bf16[128,1024]{1,0:T(8,128)(2,1)S(1)} %add_convert_fusion), channel_id=1, source_target_pairs={{0,32},{20,52},{32,0},{52,20},{1,33},{21,53},{33,1},{53,21},{2,34}... | collective-permute-start | bytes 786440 | tf_op jit(solution)/shard_map/ppermute | solution.py:26
  119.8 24.8 %collective-permute-start.26 = (bf16[128,1024]{1,0:T(8,128)(2,1)S(1)}, bf16[128,1024]{1,0:T(8,128)(2,1)}, u32[]{:S(2)}, u32[]{:S(2)}) collective-permute-start(bf16[128,1024]{1,0:T(8,128)(2,1)S(1)} %add_convert_fusion), channel_id=1, source_target_pairs={{0,16},{20,36},{32,48},{52,4},{1,17},{21,37},{33,49},{53,5},{2,18}... | collective-permute-start | bytes 786440 | tf_op jit(solution)/shard_map/ppermute | solution.py:26
  126.9 10.2 %all-to-all-start = ((bf16[8,8,1920]{2,1,0:T(8,128)(2,1)}), bf16[8,8,1920]{2,1,0:T(8,128)(2,1)S(1)}, u32[]{:S(2)}, u32[]{:S(2)}) async-start(bf16[8,8,1920]{2,1,0:T(8,128)(2,1)} %maximum_bitcast_fusion), calls=%async_computation | async-start | bytes 491520 | tf_op jit(solution)/shard_map/all_to_all | solution.py:35
  137.9 12.0 %all-to-all-start.1 = ((bf16[8,8,1920]{2,1,0:T(8,128)(2,1)}), bf16[8,8,1920]{2,1,0:T(8,128)(2,1)S(1)}, u32[]{:S(2)}, u32[]{:S(2)}) async-start(bf16[8,8,1920]{2,1,0:T(8,128)(2,1)} %broadcast_in_dim.6), calls=%async_computation.1 | async-start | bytes 491520 | tf_op jit(solution)/shard_map/all_to_all | solution.py:35
  150.4 5.3 %collective-permute-start.35 = (bf16[64,896]{0,1:T(8,128)(2,1)S(1)}, bf16[64,896]{0,1:T(8,128)(2,1)S(1)}, u32[]{:S(2)}, u32[]{:S(2)}) collective-permute-start(bf16[64,896]{0,1:T(8,128)(2,1)S(1)} %pad_maximum_fusion.5), channel_id=1, source_target_pairs={{0,8},{8,0},{1,9},{9,1},{2,10},{10,2},{3,11},{11,3},{4,12},{12,4},... | collective-permute-start | bytes 344072 | tf_op jit(solution)/shard_map/ppermute | solution.py:17
  152.0 19.1 %collective-permute-start.31 = (bf16[320,1024]{1,0:T(8,128)(2,1)}, bf16[320,1024]{1,0:T(8,128)(2,1)S(1)}, u32[]{:S(2)}, u32[]{:S(2)}) collective-permute-start(bf16[320,1024]{1,0:T(8,128)(2,1)} %pad_maximum_fusion.2.v0), channel_id=1, source_target_pairs={{0,64},{64,128},{128,192},{192,0},{1,65},{65,129},{129,193},{193,1... | collective-permute-start | bytes 1966088 | tf_op jit(solution)/shard_map/ppermute | solution.py:17
  154.1 33.7 %collective-permute-start.29 = (bf16[320,1024]{1,0:T(8,128)(2,1)}, bf16[320,1024]{1,0:T(8,128)(2,1)}, u32[]{:S(2)}, u32[]{:S(2)}) collective-permute-start(bf16[320,1024]{1,0:T(8,128)(2,1)} %pad_maximum_fusion.2.v0), channel_id=1, source_target_pairs={{0,192},{64,0},{128,64},{192,128},{1,193},{65,1},{129,65},{193,129... | collective-permute-start | bytes 1966088 | tf_op jit(solution)/shard_map/ppermute | solution.py:17
  171.9 36.0 %collective-permute-start.32 = (bf16[160,1024]{1,0:T(8,128)(2,1)}, bf16[160,1024]{1,0:T(8,128)(2,1)S(1)}, u32[]{:S(2)}, u32[]{:S(2)}) collective-permute-start(bf16[160,1024]{1,0:T(8,128)(2,1)} %slice.52), channel_id=1, source_target_pairs={{0,64},{64,128},{128,192},{192,0},{1,65},{65,129},{129,193},{193,1... | collective-permute-start | bytes 983048 | tf_op jit(solution)/shard_map/ppermute | solution.py:17
  178.6 11.6 %collective-permute-start.12 = (bf16[1,128,896]{2,1,0:T(8,128)(2,1)S(1)}, bf16[1,128,896]{2,1,0:T(8,128)(2,1)S(1)}, u32[]{:S(2)}, u32[]{:S(2)}) collective-permute-start(bf16[1,128,896]{2,1,0:T(8,128)(2,1)S(1)} %get-tuple-element.26), channel_id=1, source_target_pairs={{0,3},{1,0},{2,1},{3,2},{4,7},{5,4},{6,5},{7,6},{8,11},{9,8},{10,9... | collective-permute-start | bytes 688136 | tf_op jit(solution)/shard_map/ppermute | solution.py:17
  180.4 10.7 %collective-permute-start.11 = (bf16[1,128,896]{2,1,0:T(8,128)(2,1)S(1)}, bf16[1,128,896]{2,1,0:T(8,128)(2,1)S(1)}, u32[]{:S(2)}, u32[]{:S(2)}) collective-permute-start(bf16[1,128,896]{2,1,0:T(8,128)(2,1)S(1)} %get-tuple-element.27), channel_id=1, source_target_pairs={{0,2},{1,3},{2,0},{3,1},{4,6},{5,7},{6,4},{7,5},{8,10},{9,11},{10,... | collective-permute-start | bytes 688136 | tf_op jit(solution)/shard_map/ppermute | solution.py:17
  187.7 36.3 %copy-start.1 = (bf16[1024,896]{1,0:T(8,128)(2,1)}, bf16[1024,896]{1,0:T(8,128)(2,1)S(1)}, u32[]{:S(2)}) copy-start(bf16[1024,896]{1,0:T(8,128)(2,1)S(1)} %convolution_convert_fusion) | copy-start | bytes 5505028
  187.7 29.6 %copy-start.12 = (bf16[1,64,1024]{2,1,0:T(8,128)(2,1)S(1)}, bf16[1,64,1024]{2,1,0:T(8,128)(2,1)}, u32[]{:S(2)}) copy-start(bf16[1,64,1024]{2,1,0:T(8,128)(2,1)} %get-tuple-element.34) | copy-start | bytes 393220
  187.8 7.9 %collective-permute-start.10 = (bf16[1,128,896]{2,1,0:T(8,128)(2,1)}, bf16[1,128,896]{2,1,0:T(8,128)(2,1)S(1)}, u32[]{:S(2)}, u32[]{:S(2)}) collective-permute-start(bf16[1,128,896]{2,1,0:T(8,128)(2,1)} %get-tuple-element.28), channel_id=1, source_target_pairs={{0,1},{1,2},{2,3},{3,0},{4,5},{5,6},{6,7},{7,4},{8,9},{9,10},{10,1... | collective-permute-start | bytes 688136 | tf_op jit(solution)/shard_map/ppermute | solution.py:17
  190.8 20.4 %collective-permute-start.8 = (bf16[2,128,896]{2,1,0:T(8,128)(2,1)S(1)}, bf16[2,128,896]{2,1,0:T(8,128)(2,1)S(1)}, u32[]{:S(2)}, u32[]{:S(2)}) collective-permute-start(bf16[2,128,896]{2,1,0:T(8,128)(2,1)S(1)} %get-tuple-element.23), channel_id=1, source_target_pairs={{0,3},{1,0},{2,1},{3,2},{4,7},{5,4},{6,5},{7,6},{8,11},{9,8},{10,9... | collective-permute-start | bytes 1376264 | tf_op jit(solution)/shard_map/ppermute | solution.py:17
  191.8 25.5 %collective-permute-start.7 = (bf16[2,128,896]{2,1,0:T(8,128)(2,1)S(1)}, bf16[2,128,896]{2,1,0:T(8,128)(2,1)S(1)}, u32[]{:S(2)}, u32[]{:S(2)}) collective-permute-start(bf16[2,128,896]{2,1,0:T(8,128)(2,1)S(1)} %get-tuple-element.24), channel_id=1, source_target_pairs={{0,2},{1,3},{2,0},{3,1},{4,6},{5,7},{6,4},{7,5},{8,10},{9,11},{10,... | collective-permute-start | bytes 1376264 | tf_op jit(solution)/shard_map/ppermute | solution.py:17
  195.7 25.1 %collective-permute-start.6 = (bf16[2,128,896]{2,1,0:T(8,128)(2,1)S(1)}, bf16[2,128,896]{2,1,0:T(8,128)(2,1)}, u32[]{:S(2)}, u32[]{:S(2)}) collective-permute-start(bf16[2,128,896]{2,1,0:T(8,128)(2,1)S(1)} %get-tuple-element.25), channel_id=1, source_target_pairs={{0,1},{1,2},{2,3},{3,0},{4,5},{5,6},{6,7},{7,4},{8,9},{9,10},{10,1... | collective-permute-start | bytes 1376264 | tf_op jit(solution)/shard_map/ppermute | solution.py:17
  207.9 22.8 %copy-start.9 = (bf16[160,1024]{1,0:T(8,128)(2,1)}, bf16[160,1024]{1,0:T(8,128)(2,1)S(1)}, u32[]{:S(2)}) copy-start(bf16[160,1024]{1,0:T(8,128)(2,1)S(1)} %collective-permute-done.32.vb) | copy-start | bytes 983044
  207.9 19.2 %collective-permute-start.3 = (bf16[1,128,896]{2,1,0:T(8,128)(2,1)}, bf16[1,128,896]{2,1,0:T(8,128)(2,1)}, u32[]{:S(2)}, u32[]{:S(2)}) collective-permute-start(bf16[1,128,896]{2,1,0:T(8,128)(2,1)} %get-tuple-element.29), channel_id=1, source_target_pairs={{0,3},{1,0},{2,1},{3,2},{4,7},{5,4},{6,5},{7,6},{8,11},{9,8},{10,9... | collective-permute-start | bytes 688136 | tf_op jit(solution)/shard_map/ppermute | solution.py:17
  211.3 15.9 %collective-permute-start.2 = (bf16[1,128,896]{2,1,0:T(8,128)(2,1)}, bf16[1,128,896]{2,1,0:T(8,128)(2,1)}, u32[]{:S(2)}, u32[]{:S(2)}) collective-permute-start(bf16[1,128,896]{2,1,0:T(8,128)(2,1)} %get-tuple-element.30), channel_id=1, source_target_pairs={{0,2},{1,3},{2,0},{3,1},{4,6},{5,7},{6,4},{7,5},{8,10},{9,11},{10,... | collective-permute-start | bytes 688136 | tf_op jit(solution)/shard_map/ppermute | solution.py:17
  217.3 10.3 %collective-permute-start.1 = (bf16[1,128,896]{2,1,0:T(8,128)(2,1)}, bf16[1,128,896]{2,1,0:T(8,128)(2,1)}, u32[]{:S(2)}, u32[]{:S(2)}) collective-permute-start(bf16[1,128,896]{2,1,0:T(8,128)(2,1)} %get-tuple-element.31), channel_id=1, source_target_pairs={{0,1},{1,2},{2,3},{3,0},{4,5},{5,6},{6,7},{7,4},{8,9},{9,10},{10,1... | collective-permute-start | bytes 688136 | tf_op jit(solution)/shard_map/ppermute | solution.py:17
  220.9 17.6 %collective-permute-start.30 = (bf16[160,1024]{1,0:T(8,128)(2,1)}, bf16[160,1024]{1,0:T(8,128)(2,1)}, u32[]{:S(2)}, u32[]{:S(2)}) collective-permute-start(bf16[160,1024]{1,0:T(8,128)(2,1)} %slice.51), channel_id=1, source_target_pairs={{0,192},{64,0},{128,64},{192,128},{1,193},{65,1},{129,65},{193,129... | collective-permute-start | bytes 983048 | tf_op jit(solution)/shard_map/ppermute | solution.py:17
  227.0 11.4 %collective-permute-start.33 = (bf16[4,64,1024]{2,1,0:T(8,128)(2,1)}, bf16[4,64,1024]{2,1,0:T(8,128)(2,1)S(1)}, u32[]{:S(2)}, u32[]{:S(2)}) collective-permute-start(bf16[4,64,1024]{2,1,0:T(8,128)(2,1)} %pad_maximum_fusion.4), channel_id=1, source_target_pairs={{0,8},{8,0},{1,9},{9,1},{2,10},{10,2},{3,11},{11,3},{4,12},{12,4},... | collective-permute-start | bytes 1572872 | tf_op jit(solution)/shard_map/ppermute | solution.py:17
  227.2 11.3 %collective-permute-start.14 = (bf16[128,896]{1,0:T(8,128)(2,1)}, bf16[128,896]{1,0:T(8,128)(2,1)S(1)}, u32[]{:S(2)}, u32[]{:S(2)}) collective-permute-start(bf16[128,896]{1,0:T(8,128)(2,1)} %get-tuple-element.17), channel_id=1, source_target_pairs={{0,4},{4,0},{1,5},{5,1},{2,6},{6,2},{3,7},{7,3},{8,12},{12,8},{9,1... | collective-permute-start | bytes 688136 | tf_op jit(solution)/shard_map/ppermute | solution.py:17
  230.7 9.6 %collective-permute-start.13 = (bf16[128,896]{1,0:T(8,128)(2,1)}, bf16[128,896]{1,0:T(8,128)(2,1)S(1)}, u32[]{:S(2)}, u32[]{:S(2)}) collective-permute-start(bf16[128,896]{1,0:T(8,128)(2,1)} %get-tuple-element.16), channel_id=1, source_target_pairs={{0,4},{4,0},{1,5},{5,1},{2,6},{6,2},{3,7},{7,3},{8,12},{12,8},{9,1... | collective-permute-start | bytes 688136 | tf_op jit(solution)/shard_map/ppermute | solution.py:17
  271.5 11.0 %all-to-all-start.3 = ((f32[16,2,16]{2,1,0:T(2,128)}), f32[16,2,16]{2,1,0:T(2,128)S(1)}, u32[]{:S(2)}, u32[]{:S(2)}) async-start(f32[16,2,16]{2,1,0:T(2,128)} %broadcast_in_dim.8), calls=%async_computation.3 | async-start | bytes 32768 | tf_op jit(solution)/shard_map/all_to_all | solution.py:35
  (14 other events, 62.3 us)
Sparse Core Ops, SparseCore 0:
  9.1 34.1 all-gather.4
  45.1 36.7 all-gather.8
  95.4 43.5 all-gather.6

commit v8 on v6

--- a/solution.py
+++ b/solution.py
@@ -124,6 +124,26 @@
     )(at, *a[0], *b[0])
 
 
+def pick_kernel(a0, a1, a2, a3, out):
+    for d, a in enumerate((a0, a1, a2, a3)):
+        out[d] = a[...]
+
+
+def pick(arrays, rows):
+    total, cols = arrays[0].shape
+    return pl.pallas_call(
+        pick_kernel,
+        grid=(1,),
+        out_shape=jax.ShapeDtypeStruct((4, rows, cols), BF),
+        in_specs=[pl.BlockSpec((rows, cols), lambda j: (total // rows - 1, 0))] * 4,
+        out_specs=pl.BlockSpec((4, rows, cols), lambda j: (0, 0, 0)),
+        cost_estimate=pl.CostEstimate(
+            flops=0, bytes_accessed=16 * rows * cols, transcendentals=0
+        ),
+        name="pick",
+    )(*arrays)
+
+
 def score_kernel(
     at_ref, k0, k1, g0, g1, v0, v1, v2, v3, other, inv0, inv1, query, out, flipped, total, act, held
 ):
@@ -257,7 +277,7 @@
         [jnp.where(same, part, minus), jnp.where(same, far, plus), value], 0
     )
     act_rot = gather(act_rot, "y")
-    value_other = shift(jnp.stack([a[2 * tokens :] for a in act_rot]), "c", 1)
+    value_other = shift(pick(act_rot, half_rows), "c", 1)
 
     grad = grad_out[0]
     plus, far, minus = (shift(grad, "zh", -by) for by in (1, 2, 3))

time: 288 us -> 302 us (1.049)
  starting transfers between devices: 84.6 us -> 92.1 us
  other arithmetic: 21.6 us -> 15.9 us
  waiting for transfers between devices: 94.5 us -> 99.6 us
  blocking collectives: 13.8 us -> 17.3 us
    ppermute x31, waiting for transfers between devices: 76.8 us -> 84.7 us  [shift(): return lax.ppermute(value, axis, [(i, (i + by) % n) for i in range(n)])]
    ppermute x1, waiting for transfers between devices: 7.34 us -> 0.01 us  [to_owner(): return lax.ppermute(value, ('zh', 'zl'), pairs)]
    ppermute x3, waiting for transfers between devices: 0.01 us -> 4.89 us  [from_owner(): return lax.ppermute(value, ('zh', 'zl'), pairs)]
    ppermute x31, starting transfers between devices: 57.6 us -> 62.4 us  [shift(): return lax.ppermute(value, axis, [(i, (i + by) % n) for i in range(n)])]
    unnamed x35 -> x57, local copies, waits for them, and re-layouts: 4.71 us -> 8.48 us
    all_to_all x1, blocking collectives: 13.8 us -> 17.3 us  [exchange(): return lax.all_to_all(value, axes, 0, 0, tiled=True)]
  transfers between devices with their start and end apart: 41 -> 41, of which waited for: 18 -> 17; matrix products, arithmetic and copies ran while one was open for 16% -> 13% of each run, Pallas kernels for 3% -> 4%
where the time goes in v8:
time: 302 us; the launch traced here: 299 us
  waiting for transfers between devices  99.6 us (33%)
  starting transfers between devices  92.1 us (30%)
  Pallas kernels  27.3 us (9%)
  matrix products  17.3 us (6%)
  blocking collectives  17.3 us (6%)
  local copies, waits for them, and re-layouts  16.4 us (5%)
  other arithmetic  15.9 us (5%)
  between operations  13.6 us (5%)
    ppermute x31, waiting for transfers between devices, shift(): return lax.ppermute(value, axis, [(i, (i + by) % n) for i in range(n)])  84.7 us
    ppermute x31, starting transfers between devices, shift(): return lax.ppermute(value, axis, [(i, (i + by) % n) for i in range(n)])  62.4 us
    all_to_all x3, starting transfers between devices, exchange(): return lax.all_to_all(value, axes, 0, 0, tiled=True)  18.1 us
    dot_general x4, matrix products, dot_t(): lax.dot_general(a, b, (((1,), (1,)), ((), ())), preferred_element_type=F32)  17.3 us
    all_to_all x1, blocking collectives, exchange(): return lax.all_to_all(value, axes, 0, 0, tiled=True)  17.3 us
    pallas_call x1, Pallas kernels, score(): pl.pallas_call(score_kernel, grid_spec=spec, out_shape=jax.ShapeDtypeStru...  15.5 us
    ppermute x3, starting transfers between devices, from_owner(): return lax.ppermute(value, ('zh', 'zl'), pairs)  10.3 us
    all_to_all x3, waiting for transfers between devices, exchange(): return lax.all_to_all(value, axes, 0, 0, tiled=True)  9.91 us
  transfers between devices with their start and end apart: 41, of which 17 were waited for; matrix products, arithmetic and copies ran while one was open for 13% of the time, Pallas kernels for 4%

profile of v8, /device:TPU:2, one launch (start us, length us, event | category | flops | bytes accessed | tf_op | source)
XLA Modules:
  0.0 299.5 jit_solution(16803885031116631959)
XLA Ops:
  6.6 7.3 %collective-permute-start.9 = (bf16[128,1792]{1,0:T(8,128)(2,1)}, bf16[128,1792]{1,0:T(8,128)(2,1)S(1)}, u32[]{:S(2)}, u32[]{:S(2)}) collective-permute-start(bf16[128,1792]{1,0:T(8,128)(2,1)} %bitcast.75), channel_id=1, source_target_pairs={{0,32},{16,48},{32,0},{48,16},{1,33},{17,49},{33,1},{49,17},{2,34}... | collective-permute-start | bytes 1376264 | tf_op jit(solution)/shard_map/ppermute | solution.py:17
  13.9 13.0 %collective-permute-done.9 = bf16[128,1792]{1,0:T(8,128)(2,1)S(1)} collective-permute-done((bf16[128,1792]{1,0:T(8,128)(2,1)}, bf16[128,1792]{1,0:T(8,128)(2,1)S(1)}, u32[]{:S(2)}, u32[]{:S(2)}) %collective-permute-start.9) | collective-permute-done | bytes 458784 | tf_op jit(solution)/shard_map/ppermute | solution.py:17
  27.7 9.6 %collective-permute-start.5 = (bf16[128,1792]{1,0:T(8,128)(2,1)}, bf16[128,1792]{1,0:T(8,128)(2,1)S(1)}, u32[]{:S(2)}, u32[]{:S(2)}) collective-permute-start(bf16[128,1792]{1,0:T(8,128)(2,1)} %bitcast.76), channel_id=1, source_target_pairs={{0,16},{16,32},{32,48},{48,0},{1,17},{17,33},{33,49},{49,1},{2,18}... | collective-permute-start | bytes 1376264 | tf_op jit(solution)/shard_map/ppermute | solution.py:17
  37.3 2.8 collective-permute-start.4
  40.1 19.5 %collective-permute-done.5 = bf16[128,1792]{1,0:T(8,128)(2,1)S(1)} collective-permute-done((bf16[128,1792]{1,0:T(8,128)(2,1)}, bf16[128,1792]{1,0:T(8,128)(2,1)S(1)}, u32[]{:S(2)}, u32[]{:S(2)}) %collective-permute-start.5) | collective-permute-done | bytes 458784 | tf_op jit(solution)/shard_map/ppermute | solution.py:17
  60.7 4.4 %collective-permute-start.18 = (bf16[512,128]{1,0:T(8,128)(2,1)S(1)}, bf16[512,128]{1,0:T(8,128)(2,1)S(1)}, u32[]{:S(2)}, u32[]{:S(2)}) collective-permute-start(bf16[512,128]{1,0:T(8,128)(2,1)S(1)} %copy-done.23), channel_id=1, source_target_pairs={{0,48},{16,0},{32,16},{48,32},{1,49},{17,1},{33,17},{49,33},{2,50}... | collective-permute-start | bytes 393224 | tf_op jit(solution)/shard_map/ppermute | solution.py:17
  65.1 3.2 %collective-permute-start.19 = (bf16[512,128]{1,0:T(8,128)(2,1)S(1)}, bf16[512,128]{1,0:T(8,128)(2,1)S(1)}, u32[]{:S(2)}, u32[]{:S(2)}) collective-permute-start(bf16[512,128]{1,0:T(8,128)(2,1)S(1)} %copy-done.23), channel_id=1, source_target_pairs={{0,32},{16,48},{32,0},{48,16},{1,33},{17,49},{33,1},{49,17},{2,34}... | collective-permute-start | bytes 393224 | tf_op jit(solution)/shard_map/ppermute | solution.py:17
  68.3 8.5 %collective-permute-done.18 = bf16[512,128]{1,0:T(8,128)(2,1)S(1)} collective-permute-done((bf16[512,128]{1,0:T(8,128)(2,1)S(1)}, bf16[512,128]{1,0:T(8,128)(2,1)S(1)}, u32[]{:S(2)}, u32[]{:S(2)}) %collective-permute-start.18) | collective-permute-done | bytes 131104 | tf_op jit(solution)/shard_map/ppermute | solution.py:17
  76.9 2.3 collective-permute-done.20
  79.4 1.7 collective-permute-start.17
  81.0 2.9 collective-permute-start.16
  87.6 7.8 %collective-permute-done.16.a2 = bf16[128,512]{1,0:T(8,128)(2,1)} collective-permute-done((bf16[128,512]{1,0:T(8,128)(2,1)S(1)}, bf16[128,512]{1,0:T(8,128)(2,1)}, u32[]{:S(2)}, u32[]{:S(2)}) %collective-permute-start.16) | collective-permute-done | bytes 131104 | tf_op jit(solution)/shard_map/ppermute | solution.py:17
  96.3 3.7 %rotate_in.1 = (bf16[128,1024]{1,0:T(8,128)(2,1)}, bf16[128,1024]{1,0:T(8,128)(2,1)}, bf16[128,1024]{1,0:T(8,128)(2,1)}, bf16[128,1024]{1,0:T(8,128)(2,1)}, bf16[64,1024]{1,0:T(8,128)(2,1)}) custom-call(s32[5]{0:T(128)} %stack.54.at_ref, bf16[128,512]{1,0:T(8,128)(2,1)} %bitcast.87, bf16[128,512]{1,0:T(8,128)(2,1)} %collective-permute-done.15.a1, ...), custom_call_target="tpu_custom_call" | custom-call | flops 536870912 | bytes 2621440 | tf_op jit(solution)/shard_map/rotate_in/pallas_call | solution.py:73
  102.6 2.2 collective-permute-start.24
  104.8 4.6 %collective-permute-done.22 = bf16[128,1024]{1,0:T(8,128)(2,1)S(1)} collective-permute-done((bf16[128,1024]{1,0:T(8,128)(2,1)}, bf16[128,1024]{1,0:T(8,128)(2,1)S(1)}, u32[]{:S(2)}, u32[]{:S(2)}) %collective-permute-start.22) | collective-permute-done | bytes 262176 | tf_op jit(solution)/shard_map/ppermute | solution.py:17
  109.4 3.0 %collective-permute-done.23 = bf16[128,1024]{1,0:T(8,128)(2,1)S(1)} collective-permute-done((bf16[128,1024]{1,0:T(8,128)(2,1)}, bf16[128,1024]{1,0:T(8,128)(2,1)S(1)}, u32[]{:S(2)}, u32[]{:S(2)}) %collective-permute-start.23) | collective-permute-done | bytes 262176 | tf_op jit(solution)/shard_map/ppermute | solution.py:17
  112.4 2.1 collective-permute-done.24
  116.9 1.6 pad_maximum_fusion
  118.6 1.6 copy-done.2
  122.0 9.5 %all-to-all-start = ((bf16[8,8,1920]{2,1,0:T(8,128)(2,1)}), bf16[8,8,1920]{2,1,0:T(8,128)(2,1)S(1)}, u32[]{:S(2)}, u32[]{:S(2)}) async-start(bf16[8,8,1920]{2,1,0:T(8,128)(2,1)} %maximum_bitcast_fusion), calls=%async_computation | async-start | bytes 491520 | tf_op jit(solution)/shard_map/all_to_all | solution.py:35
  131.6 3.5 %collective-permute-start.26 = (bf16[128,1024]{1,0:T(8,128)(2,1)S(1)}, bf16[128,1024]{1,0:T(8,128)(2,1)S(1)}, u32[]{:S(2)}, u32[]{:S(2)}) collective-permute-start(bf16[128,1024]{1,0:T(8,128)(2,1)S(1)} %add_convert_fusion), channel_id=1, source_target_pairs={{0,16},{20,36},{32,48},{52,4},{1,17},{21,37},{33,49},{53,5},{2,18}... | collective-permute-start | bytes 786440 | tf_op jit(solution)/shard_map/ppermute | solution.py:26
  136.5 5.5 %collective-permute-start.27 = (bf16[128,1024]{1,0:T(8,128)(2,1)S(1)}, bf16[128,1024]{1,0:T(8,128)(2,1)S(1)}, u32[]{:S(2)}, u32[]{:S(2)}) collective-permute-start(bf16[128,1024]{1,0:T(8,128)(2,1)S(1)} %add_convert_fusion), channel_id=1, source_target_pairs={{0,32},{20,52},{32,0},{52,20},{1,33},{21,53},{33,1},{53,21},{2,34}... | collective-permute-start | bytes 786440 | tf_op jit(solution)/shard_map/ppermute | solution.py:26
  142.9 4.8 %all-to-all-start.1 = ((bf16[8,8,1920]{2,1,0:T(8,128)(2,1)}), bf16[8,8,1920]{2,1,0:T(8,128)(2,1)S(1)}, u32[]{:S(2)}, u32[]{:S(2)}) async-start(bf16[8,8,1920]{2,1,0:T(8,128)(2,1)} %broadcast_in_dim.6), calls=%async_computation.1 | async-start | bytes 491520 | tf_op jit(solution)/shard_map/all_to_all | solution.py:35
  147.7 4.9 %collective-permute-done.27 = bf16[128,1024]{1,0:T(8,128)(2,1)S(1)} collective-permute-done((bf16[128,1024]{1,0:T(8,128)(2,1)S(1)}, bf16[128,1024]{1,0:T(8,128)(2,1)S(1)}, u32[]{:S(2)}, u32[]{:S(2)}) %collective-permute-start.27) | collective-permute-done | bytes 262176 | tf_op jit(solution)/shard_map/ppermute | solution.py:26
  152.6 5.2 %all-to-all-done.1 = bf16[8,8,1920]{2,1,0:T(8,128)(2,1)S(1)} async-done(((bf16[8,8,1920]{2,1,0:T(8,128)(2,1)}), bf16[8,8,1920]{2,1,0:T(8,128)(2,1)S(1)}, u32[]{:S(2)}, u32[]{:S(2)}) %all-to-all-start.1) | async-done | bytes 245792 | tf_op jit(solution)/shard_map/all_to_all | solution.py:35
  158.0 2.9 collective-permute-start.30
  160.9 2.5 collective-permute-start.29
  163.9 4.6 %convolution_convert_fusion.1 = bf16[896,512]{0,1:T(8,128)(2,1)S(1)} fusion(bf16[896,1792]{1,0:T(8,128)(2,1)} %copy-done.2, bf16[512,1792]{1,0:T(8,128)(2,1)} %all-gather.9.cloned.1.call-done), kind=kOutput, calls=%fused_computation.4 | convolution fusion | flops 1644625920 | bytes 5963776 | tf_op jit(solution)/shard_map/dot_general | solution.py:47
  170.3 1.7 collective-permute-start.12
  172.0 7.0 %convolution_convert_fusion = bf16[1024,896]{1,0:T(8,128)(2,1)S(1)} fusion(bf16[1024,1792]{1,0:T(8,128)(2,1)} %bitcast.85, bf16[896,1792]{1,0:T(8,128)(2,1)} %copy-done.2), kind=kOutput, calls=%fused_computation.3 | convolution fusion | flops 3289251840 | bytes 8716288 | tf_op jit(solution)/shard_map/dot_general | solution.py:47
  180.9 11.5 %collective-permute-done.30.a2.v2 = bf16[320,1024]{1,0:T(8,128)(2,1)} collective-permute-done((bf16[320,1024]{1,0:T(8,128)(2,1)S(1)}, bf16[320,1024]{1,0:T(8,128)(2,1)}, u32[]{:S(2)}, u32[]{:S(2)}) %collective-permute-start.30) | collective-permute-done | bytes 655392 | tf_op jit(solution)/shard_map/ppermute | solution.py:17
  195.2 2.1 collective-permute-start.7
  197.2 4.7 %convolution_convert_fusion.2 = bf16[896,512]{0,1:T(8,128)(2,1)S(1)} fusion(bf16[896,1792]{1,0:T(8,128)(2,1)} %copy-done.2, bf16[512,1792]{1,0:T(8,128)(2,1)} %bitcast.86), kind=kOutput, calls=%fused_computation.5 | convolution fusion | flops 1644625920 | bytes 5963776 | tf_op jit(solution)/shard_map/dot_general | solution.py:47
  206.3 1.9 collective-permute-done.8.refs_7_
  208.2 5.8 %collective-permute-start.1 = (bf16[1,128,896]{2,1,0:T(8,128)(2,1)S(1)}, bf16[1,128,896]{2,1,0:T(8,128)(2,1)}, u32[]{:S(2)}, u32[]{:S(2)}) collective-permute-start(bf16[1,128,896]{2,1,0:T(8,128)(2,1)S(1)} %get-tuple-element.31), channel_id=1, source_target_pairs={{0,1},{1,2},{2,3},{3,0},{4,5},{5,6},{6,7},{7,4},{8,9},{9,10},{10,1... | collective-permute-start | bytes 688136 | tf_op jit(solution)/shard_map/ppermute | solution.py:17
  214.0 3.9 %collective-permute-done.7.refs_6_ = bf16[2,128,896]{2,1,0:T(8,128)(2,1)S(1)} collective-permute-done((bf16[2,128,896]{2,1,0:T(8,128)(2,1)}, bf16[2,128,896]{2,1,0:T(8,128)(2,1)S(1)}, u32[]{:S(2)}, u32[]{:S(2)}) %collective-permute-start.7) | collective-permute-done | bytes 458784 | tf_op jit(solution)/shard_map/ppermute | solution.py:17
  218.0 1.5 collective-permute-start.6
  219.5 3.9 %convert_divide_fusion.1.inv0 = f32[448,4096]{1,0:T(8,128)} fusion(bf16[448,4096]{1,0:T(8,128)(2,1)S(1)} %copy-done.4), kind=kLoop, calls=%fused_computation.1 | loop fusion | flops 3670016 | bytes 11010048 | tf_op jit(solution)/shard_map/div | solution.py:249
  225.4 2.0 pick.1
  227.4 4.9 %collective-permute-done.6.refs_5_ = bf16[2,128,896]{2,1,0:T(8,128)(2,1)S(1)} collective-permute-done((bf16[2,128,896]{2,1,0:T(8,128)(2,1)}, bf16[2,128,896]{2,1,0:T(8,128)(2,1)S(1)}, u32[]{:S(2)}, u32[]{:S(2)}) %collective-permute-start.6) | collective-permute-done | bytes 458784 | tf_op jit(solution)/shard_map/ppermute | solution.py:17
  233.1 3.0 %shard_map.74 = (bf16[128,896]{1,0:T(8,128)(2,1)}, bf16[128,896]{1,0:T(8,128)(2,1)}) custom-call(s32[5]{0:T(128)} %stack.54.at_ref, bf16[4,1,128,896]{3,2,1,0:T(8,128)(2,1)} %bitcast.65, bf16[1,128,896]{2,1,0:T(8,128)(2,1)} %collective-permute-done.10.refs_1_, bf16[1,128,896]{2,1,0:T(8,128)(2,1)} %collective-permute-done.11.refs_2_, ...), custom_call_target="tpu_custom_call" | custom-call | flops 917504 | bytes 2293760 | tf_op jit(solution)/shard_map/pallas_call | solution.py:117
  237.0 3.0 %shard_map.73 = (bf16[128,896]{1,0:T(8,128)(2,1)}, bf16[128,896]{1,0:T(8,128)(2,1)}) custom-call(s32[5]{0:T(128)} %stack.54.at_ref, bf16[4,1,128,896]{3,2,1,0:T(8,128)(2,1)} %bitcast.67, bf16[1,128,896]{2,1,0:T(8,128)(2,1)} %collective-permute-done.1.refs_1_, bf16[1,128,896]{2,1,0:T(8,128)(2,1)} %copy-done.21, bf16[1,128,896]{2,1,0:T(8,128)(2,1)} %copy-done.20, ...), custom_call_target="tpu_custom_call" | custom-call | flops 917504 | bytes 2293760 | tf_op jit(solution)/shard_map/pallas_call | solution.py:117
  240.0 2.1 collective-permute-start.13
  242.1 6.0 %convert_divide_fusion.inv1 = f32[448,4096]{1,0:T(8,128)} fusion(bf16[448,4096]{1,0:T(8,128)(2,1)} %collective-permute-done.33), kind=kLoop, calls=%fused_computation | loop fusion | flops 3670016 | bytes 11010048 | tf_op jit(solution)/shard_map/div | solution.py:250
  249.3 15.5 %score.1 = f32[8,128]{1,0:T(8,128)} custom-call(s32[5]{0:T(128)} %stack.54.at_ref, bf16[128,896]{1,0:T(8,128)(2,1)} %get-tuple-element.14.k0, bf16[128,896]{1,0:T(8,128)(2,1)} %get-tuple-element.15.k1, bf16[128,896]{1,0:T(8,128)(2,1)} %copy-done.16, bf16[128,896]{1,0:T(8,128)(2,1)} %copy-done.15, bf16[320,1024]{1,0:T(8,128)(2,1)} %copy-done.3, ...), custom_call_target="tpu_custom_call" | custom-call | flops 3758096384 | bytes 14680064 | tf_op jit(solution)/shard_map/score/pallas_call | solution.py:219
  265.8 17.3 %all_to_all.20 = f32[16,2,16]{2,1,0:T(2,128)S(1)} all-to-all(f32[16,2,16]{2,1,0:T(2,128)S(1)} %broadcast_in_dim.7), channel_id=1, replica_groups=mesh['y'=4,'zh'=4,'c'=2,'zl'=2,'x'=4] {'y','zh'}, dimensions={0} | all-to-all | bytes 4096 | tf_op jit(solution)/shard_map/all_to_all | solution.py:35
  283.8 3.8 %all-to-all-start.3 = ((f32[16,2,16]{2,1,0:T(2,128)}), f32[16,2,16]{2,1,0:T(2,128)S(1)}, u32[]{:S(2)}, u32[]{:S(2)}) async-start(f32[16,2,16]{2,1,0:T(2,128)} %broadcast_in_dim.8), calls=%async_computation.3 | async-start | bytes 32768 | tf_op jit(solution)/shard_map/all_to_all | solution.py:35
  287.6 4.7 %all-to-all-done.3 = f32[16,2,16]{2,1,0:T(2,128)S(1)} async-done(((f32[16,2,16]{2,1,0:T(2,128)}), f32[16,2,16]{2,1,0:T(2,128)S(1)}, u32[]{:S(2)}, u32[]{:S(2)}) %all-to-all-start.3) | async-done | bytes 2080 | tf_op jit(solution)/shard_map/all_to_all | solution.py:35
  (140 shorter events, 34.3 us)
Async XLA Ops:
  6.5 112.0 %copy-start = (bf16[16,8,1792]{2,1,0:T(8,128)(2,1)S(1)}, bf16[16,8,1792]{2,1,0:T(8,128)(2,1)}, u32[]{:S(2)}) copy-start(bf16[16,8,1792]{2,1,0:T(8,128)(2,1)} %param.12) | copy-start | bytes 1376260
  6.5 54.1 %copy-start.10 = (bf16[1792,448]{0,1:T(8,128)(2,1)S(1)}, bf16[1792,448]{0,1:T(8,128)(2,1)}, u32[]{:S(2)}) copy-start(bf16[1792,448]{0,1:T(8,128)(2,1)} %param.9) | copy-start | bytes 4816900
  6.5 54.2 %copy-start.23 = (bf16[512,128]{1,0:T(8,128)(2,1)S(1)}, bf16[512,128]{1,0:T(8,128)(2,1)}, u32[]{:S(2)}) copy-start(bf16[512,128]{1,0:T(8,128)(2,1)} %param.10) | copy-start | bytes 393220
  6.5 72.8 %copy-start.26 = (bf16[1,128,512]{2,1,0:T(8,128)(2,1)S(1)}, bf16[1,128,512]{2,1,0:T(8,128)(2,1)}, u32[]{:S(2)}) copy-start(bf16[1,128,512]{2,1,0:T(8,128)(2,1)} %param.8) | copy-start | bytes 393220
  6.5 79.3 %copy-start.24 = (bf16[16,8,512]{2,1,0:T(8,128)(2,1)S(1)}, bf16[16,8,512]{2,1,0:T(8,128)(2,1)}, u32[]{:S(2)}) copy-start(bf16[16,8,512]{2,1,0:T(8,128)(2,1)} %param.13) | copy-start | bytes 393220
  6.5 157.4 %all-gather.9.cloned.1.call-start = ((), (), s32[]{:S(2)}) async-start(), calls=%async_computation.6 | async-start | bytes 2293760 | tf_op jit(solution)/shard_map/all_gather | solution.py:287
  6.6 20.3 %collective-permute-start.9 = (bf16[128,1792]{1,0:T(8,128)(2,1)}, bf16[128,1792]{1,0:T(8,128)(2,1)S(1)}, u32[]{:S(2)}, u32[]{:S(2)}) collective-permute-start(bf16[128,1792]{1,0:T(8,128)(2,1)} %bitcast.75), channel_id=1, source_target_pairs={{0,32},{16,48},{32,0},{48,16},{1,33},{17,49},{33,1},{49,17},{2,34}... | collective-permute-start | bytes 1376264 | tf_op jit(solution)/shard_map/ppermute | solution.py:17
  27.6 144.4 %all-gather.7.cloned.1.call-start = ((), (), s32[]{:S(2)}) async-start(), calls=%async_computation.5 | async-start | bytes 4587520 | tf_op jit(solution)/shard_map/all_gather | solution.py:287
  27.7 31.9 %collective-permute-start.5 = (bf16[128,1792]{1,0:T(8,128)(2,1)}, bf16[128,1792]{1,0:T(8,128)(2,1)S(1)}, u32[]{:S(2)}, u32[]{:S(2)}) collective-permute-start(bf16[128,1792]{1,0:T(8,128)(2,1)} %bitcast.76), channel_id=1, source_target_pairs={{0,16},{16,32},{32,48},{48,0},{1,17},{17,33},{33,49},{49,1},{2,18}... | collective-permute-start | bytes 1376264 | tf_op jit(solution)/shard_map/ppermute | solution.py:17
  37.3 22.3 %collective-permute-start.4 = (bf16[128,1792]{1,0:T(8,128)(2,1)}, bf16[128,1792]{1,0:T(8,128)(2,1)S(1)}, u32[]{:S(2)}, u32[]{:S(2)}) collective-permute-start(bf16[128,1792]{1,0:T(8,128)(2,1)} %bitcast.77), channel_id=1, source_target_pairs={{0,48},{16,0},{32,16},{48,32},{1,49},{17,1},{33,17},{49,33},{2,50}... | collective-permute-start | bytes 1376264 | tf_op jit(solution)/shard_map/ppermute | solution.py:17
  60.6 56.3 %collective-permute-start = (bf16[448,1792]{1,0:T(8,128)(2,1)S(1)}, bf16[448,1792]{1,0:T(8,128)(2,1)}, u32[]{:S(2)}, u32[]{:S(2)}) collective-permute-start(bf16[448,1792]{1,0:T(8,128)(2,1)S(1)} %bitcast.68), channel_id=1, source_target_pairs={{0,8},{8,0},{1,9},{9,1},{2,10},{10,2},{3,11},{11,3},{4,12},{12,4},... | collective-permute-start | bytes 4816904 | tf_op jit(solution)/shard_map/ppermute | solution.py:17
  60.7 16.1 %collective-permute-start.18 = (bf16[512,128]{1,0:T(8,128)(2,1)S(1)}, bf16[512,128]{1,0:T(8,128)(2,1)S(1)}, u32[]{:S(2)}, u32[]{:S(2)}) collective-permute-start(bf16[512,128]{1,0:T(8,128)(2,1)S(1)} %copy-done.23), channel_id=1, source_target_pairs={{0,48},{16,0},{32,16},{48,32},{1,49},{17,1},{33,17},{49,33},{2,50}... | collective-permute-start | bytes 393224 | tf_op jit(solution)/shard_map/ppermute | solution.py:17
  65.1 14.0 %collective-permute-start.20 = (bf16[512,128]{1,0:T(8,128)(2,1)S(1)}, bf16[512,128]{1,0:T(8,128)(2,1)S(1)}, u32[]{:S(2)}, u32[]{:S(2)}) collective-permute-start(bf16[512,128]{1,0:T(8,128)(2,1)S(1)} %copy-done.23), channel_id=1, source_target_pairs={{0,16},{16,32},{32,48},{48,0},{1,17},{17,33},{33,49},{49,1},{2,18}... | collective-permute-start | bytes 393224 | tf_op jit(solution)/shard_map/ppermute | solution.py:17
  65.1 14.0 %collective-permute-start.19 = (bf16[512,128]{1,0:T(8,128)(2,1)S(1)}, bf16[512,128]{1,0:T(8,128)(2,1)S(1)}, u32[]{:S(2)}, u32[]{:S(2)}) collective-permute-start(bf16[512,128]{1,0:T(8,128)(2,1)S(1)} %copy-done.23), channel_id=1, source_target_pairs={{0,32},{16,48},{32,0},{48,16},{1,33},{17,49},{33,1},{49,17},{2,34}... | collective-permute-start | bytes 393224 | tf_op jit(solution)/shard_map/ppermute | solution.py:17
  79.2 16.2 %collective-permute-start.21 = (bf16[4,512,128]{2,1,0:T(8,128)(2,1)S(1)}, bf16[4,512,128]{2,1,0:T(8,128)(2,1)S(1)}, u32[]{:S(2)}, u32[]{:S(2)}) collective-permute-start(bf16[4,512,128]{2,1,0:T(8,128)(2,1)S(1)} %pad_maximum_fusion.3.w0), channel_id=1, source_target_pairs={{0,8},{8,0},{1,9},{9,1},{2,10},{10,2},{3,11},{11,3},{4,12},{12,4},... | collective-permute-start | bytes 1572872 | tf_op jit(solution)/shard_map/ppermute | solution.py:17
  79.4 8.2 %collective-permute-start.17 = (bf16[128,512]{1,0:T(8,128)(2,1)S(1)}, bf16[128,512]{1,0:T(8,128)(2,1)}, u32[]{:S(2)}, u32[]{:S(2)}) collective-permute-start(bf16[128,512]{1,0:T(8,128)(2,1)S(1)} %bitcast.88), channel_id=1, source_target_pairs={{0,64},{64,128},{128,192},{192,0},{1,65},{65,129},{129,193},{193,1... | collective-permute-start | bytes 393224 | tf_op jit(solution)/shard_map/ppermute | solution.py:17
  81.0 14.4 %collective-permute-start.16 = (bf16[128,512]{1,0:T(8,128)(2,1)S(1)}, bf16[128,512]{1,0:T(8,128)(2,1)}, u32[]{:S(2)}, u32[]{:S(2)}) collective-permute-start(bf16[128,512]{1,0:T(8,128)(2,1)S(1)} %bitcast.89), channel_id=1, source_target_pairs={{0,128},{64,192},{128,0},{192,64},{1,129},{65,193},{129,1},{193,65... | collective-permute-start | bytes 393224 | tf_op jit(solution)/shard_map/ppermute | solution.py:17
  83.9 11.5 %collective-permute-start.15 = (bf16[128,512]{1,0:T(8,128)(2,1)S(1)}, bf16[128,512]{1,0:T(8,128)(2,1)}, u32[]{:S(2)}, u32[]{:S(2)}) collective-permute-start(bf16[128,512]{1,0:T(8,128)(2,1)S(1)} %bitcast.90), channel_id=1, source_target_pairs={{0,192},{64,0},{128,64},{192,128},{1,193},{65,1},{129,65},{193,129... | collective-permute-start | bytes 393224 | tf_op jit(solution)/shard_map/ppermute | solution.py:17
  100.0 9.4 %collective-permute-start.22 = (bf16[128,1024]{1,0:T(8,128)(2,1)}, bf16[128,1024]{1,0:T(8,128)(2,1)S(1)}, u32[]{:S(2)}, u32[]{:S(2)}) collective-permute-start(bf16[128,1024]{1,0:T(8,128)(2,1)} %get-tuple-element.19), channel_id=1, source_target_pairs={{0,1},{1,2},{2,3},{3,0},{4,5},{5,6},{6,7},{7,4},{8,9},{9,10},{10,1... | collective-permute-start | bytes 786440 | tf_op jit(solution)/shard_map/ppermute | solution.py:17
  101.5 10.9 %collective-permute-start.23 = (bf16[128,1024]{1,0:T(8,128)(2,1)}, bf16[128,1024]{1,0:T(8,128)(2,1)S(1)}, u32[]{:S(2)}, u32[]{:S(2)}) collective-permute-start(bf16[128,1024]{1,0:T(8,128)(2,1)} %get-tuple-element.20), channel_id=1, source_target_pairs={{0,2},{1,3},{2,0},{3,1},{4,6},{5,7},{6,4},{7,5},{8,10},{9,11},{10,... | collective-permute-start | bytes 786440 | tf_op jit(solution)/shard_map/ppermute | solution.py:17
  102.6 11.9 %collective-permute-start.24 = (bf16[128,1024]{1,0:T(8,128)(2,1)}, bf16[128,1024]{1,0:T(8,128)(2,1)S(1)}, u32[]{:S(2)}, u32[]{:S(2)}) collective-permute-start(bf16[128,1024]{1,0:T(8,128)(2,1)} %get-tuple-element.21), channel_id=1, source_target_pairs={{0,3},{1,0},{2,1},{3,2},{4,7},{5,4},{6,5},{7,6},{8,11},{9,8},{10,9... | collective-permute-start | bytes 786440 | tf_op jit(solution)/shard_map/ppermute | solution.py:17
  115.6 15.9 %collective-permute-start.25 = (bf16[128,1024]{1,0:T(8,128)(2,1)S(1)}, bf16[128,1024]{1,0:T(8,128)(2,1)S(1)}, u32[]{:S(2)}, u32[]{:S(2)}) collective-permute-start(bf16[128,1024]{1,0:T(8,128)(2,1)S(1)} %add_convert_fusion.1), channel_id=1, source_target_pairs={{4,0},{16,20},{36,32},{48,52},{5,1},{17,21},{37,33},{49,53},{6,2},... | collective-permute-start | bytes 786440 | tf_op jit(solution)/shard_map/ppermute | solution.py:31
  122.0 20.0 %all-to-all-start = ((bf16[8,8,1920]{2,1,0:T(8,128)(2,1)}), bf16[8,8,1920]{2,1,0:T(8,128)(2,1)S(1)}, u32[]{:S(2)}, u32[]{:S(2)}) async-start(bf16[8,8,1920]{2,1,0:T(8,128)(2,1)} %maximum_bitcast_fusion), calls=%async_computation | async-start | bytes 491520 | tf_op jit(solution)/shard_map/all_to_all | solution.py:35
  131.6 65.7 %all-gather.5.cloned.1.call-start = ((), (), s32[]{:S(2)}) async-start(), calls=%async_computation.4 | async-start | bytes 2293760 | tf_op jit(solution)/shard_map/all_gather | solution.py:287
  131.6 16.1 %collective-permute-start.26 = (bf16[128,1024]{1,0:T(8,128)(2,1)S(1)}, bf16[128,1024]{1,0:T(8,128)(2,1)S(1)}, u32[]{:S(2)}, u32[]{:S(2)}) collective-permute-start(bf16[128,1024]{1,0:T(8,128)(2,1)S(1)} %add_convert_fusion), channel_id=1, source_target_pairs={{0,16},{20,36},{32,48},{52,4},{1,17},{21,37},{33,49},{53,5},{2,18}... | collective-permute-start | bytes 786440 | tf_op jit(solution)/shard_map/ppermute | solution.py:26
  135.2 12.6 %collective-permute-start.28 = (bf16[128,1024]{1,0:T(8,128)(2,1)S(1)}, bf16[128,1024]{1,0:T(8,128)(2,1)S(1)}, u32[]{:S(2)}, u32[]{:S(2)}) collective-permute-start(bf16[128,1024]{1,0:T(8,128)(2,1)S(1)} %add_convert_fusion), channel_id=1, source_target_pairs={{0,48},{20,4},{32,16},{52,36},{1,49},{21,5},{33,17},{53,37},{2,50}... | collective-permute-start | bytes 786440 | tf_op jit(solution)/shard_map/ppermute | solution.py:26
  136.5 16.2 %collective-permute-start.27 = (bf16[128,1024]{1,0:T(8,128)(2,1)S(1)}, bf16[128,1024]{1,0:T(8,128)(2,1)S(1)}, u32[]{:S(2)}, u32[]{:S(2)}) collective-permute-start(bf16[128,1024]{1,0:T(8,128)(2,1)S(1)} %add_convert_fusion), channel_id=1, source_target_pairs={{0,32},{20,52},{32,0},{52,20},{1,33},{21,53},{33,1},{53,21},{2,34}... | collective-permute-start | bytes 786440 | tf_op jit(solution)/shard_map/ppermute | solution.py:26
  141.9 100.1 %collective-permute-start.33 = (bf16[448,4096]{1,0:T(8,128)(2,1)}, bf16[448,4096]{1,0:T(8,128)(2,1)}, u32[]{:S(2)}, u32[]{:S(2)}) collective-permute-start(bf16[448,4096]{1,0:T(8,128)(2,1)} %param.11), channel_id=1, source_target_pairs={{0,8},{8,0},{1,9},{9,1},{2,10},{10,2},{3,11},{11,3},{4,12},{12,4},... | collective-permute-start | bytes 11010056 | tf_op jit(solution)/shard_map/ppermute | solution.py:17
  142.9 14.9 %all-to-all-start.1 = ((bf16[8,8,1920]{2,1,0:T(8,128)(2,1)}), bf16[8,8,1920]{2,1,0:T(8,128)(2,1)S(1)}, u32[]{:S(2)}, u32[]{:S(2)}) async-start(bf16[8,8,1920]{2,1,0:T(8,128)(2,1)} %broadcast_in_dim.6), calls=%async_computation.1 | async-start | bytes 491520 | tf_op jit(solution)/shard_map/all_to_all | solution.py:35
  157.9 22.4 %collective-permute-start.31 = (bf16[320,1024]{1,0:T(8,128)(2,1)S(1)}, bf16[320,1024]{1,0:T(8,128)(2,1)}, u32[]{:S(2)}, u32[]{:S(2)}) collective-permute-start(bf16[320,1024]{1,0:T(8,128)(2,1)S(1)} %pad_maximum_fusion.2.a0.v0), channel_id=1, source_target_pairs={{0,64},{64,128},{128,192},{192,0},{1,65},{65,129},{129,193},{193,1... | collective-permute-start | bytes 1966088 | tf_op jit(solution)/shard_map/ppermute | solution.py:17
  158.0 34.4 %collective-permute-start.30 = (bf16[320,1024]{1,0:T(8,128)(2,1)S(1)}, bf16[320,1024]{1,0:T(8,128)(2,1)}, u32[]{:S(2)}, u32[]{:S(2)}) collective-permute-start(bf16[320,1024]{1,0:T(8,128)(2,1)S(1)} %pad_maximum_fusion.2.a0.v0), channel_id=1, source_target_pairs={{0,128},{64,192},{128,0},{192,64},{1,129},{65,193},{129,1},{193,65... | collective-permute-start | bytes 1966088 | tf_op jit(solution)/shard_map/ppermute | solution.py:17
  160.9 33.0 %collective-permute-start.29 = (bf16[320,1024]{1,0:T(8,128)(2,1)S(1)}, bf16[320,1024]{1,0:T(8,128)(2,1)}, u32[]{:S(2)}, u32[]{:S(2)}) collective-permute-start(bf16[320,1024]{1,0:T(8,128)(2,1)S(1)} %pad_maximum_fusion.2.a0.v0), channel_id=1, source_target_pairs={{0,192},{64,0},{128,64},{192,128},{1,193},{65,1},{129,65},{193,129... | collective-permute-start | bytes 1966088 | tf_op jit(solution)/shard_map/ppermute | solution.py:17
  163.8 6.5 %collective-permute-start.34 = (bf16[64,896]{0,1:T(8,128)(2,1)S(1)}, bf16[64,896]{0,1:T(8,128)(2,1)S(1)}, u32[]{:S(2)}, u32[]{:S(2)}) collective-permute-start(bf16[64,896]{0,1:T(8,128)(2,1)S(1)} %pad_maximum_fusion.4), channel_id=1, source_target_pairs={{0,8},{8,0},{1,9},{9,1},{2,10},{10,2},{3,11},{11,3},{4,12},{12,4},... | collective-permute-start | bytes 344072 | tf_op jit(solution)/shard_map/ppermute | solution.py:17
  170.3 24.1 %collective-permute-start.12 = (bf16[1,128,896]{2,1,0:T(8,128)(2,1)S(1)}, bf16[1,128,896]{2,1,0:T(8,128)(2,1)S(1)}, u32[]{:S(2)}, u32[]{:S(2)}) collective-permute-start(bf16[1,128,896]{2,1,0:T(8,128)(2,1)S(1)} %get-tuple-element.26), channel_id=1, source_target_pairs={{0,3},{1,0},{2,1},{3,2},{4,7},{5,4},{6,5},{7,6},{8,11},{9,8},{10,9... | collective-permute-start | bytes 688136 | tf_op jit(solution)/shard_map/ppermute | solution.py:17
  179.0 22.9 %copy-start.1 = (bf16[1024,896]{1,0:T(8,128)(2,1)}, bf16[1024,896]{1,0:T(8,128)(2,1)S(1)}, u32[]{:S(2)}) copy-start(bf16[1024,896]{1,0:T(8,128)(2,1)S(1)} %convolution_convert_fusion) | copy-start | bytes 5505028
  180.3 23.4 %collective-permute-start.11 = (bf16[1,128,896]{2,1,0:T(8,128)(2,1)}, bf16[1,128,896]{2,1,0:T(8,128)(2,1)}, u32[]{:S(2)}, u32[]{:S(2)}) collective-permute-start(bf16[1,128,896]{2,1,0:T(8,128)(2,1)} %get-tuple-element.27), channel_id=1, source_target_pairs={{0,2},{1,3},{2,0},{3,1},{4,6},{5,7},{6,4},{7,5},{8,10},{9,11},{10,... | collective-permute-start | bytes 688136 | tf_op jit(solution)/shard_map/ppermute | solution.py:17
  192.4 12.7 %collective-permute-start.10 = (bf16[1,128,896]{2,1,0:T(8,128)(2,1)}, bf16[1,128,896]{2,1,0:T(8,128)(2,1)}, u32[]{:S(2)}, u32[]{:S(2)}) collective-permute-start(bf16[1,128,896]{2,1,0:T(8,128)(2,1)} %get-tuple-element.28), channel_id=1, source_target_pairs={{0,1},{1,2},{2,3},{3,0},{4,5},{5,6},{6,7},{7,4},{8,9},{9,10},{10,1... | collective-permute-start | bytes 688136 | tf_op jit(solution)/shard_map/ppermute | solution.py:17
  193.9 14.3 %collective-permute-start.8 = (bf16[2,128,896]{2,1,0:T(8,128)(2,1)}, bf16[2,128,896]{2,1,0:T(8,128)(2,1)S(1)}, u32[]{:S(2)}, u32[]{:S(2)}) collective-permute-start(bf16[2,128,896]{2,1,0:T(8,128)(2,1)} %get-tuple-element.23), channel_id=1, source_target_pairs={{0,3},{1,0},{2,1},{3,2},{4,7},{5,4},{6,5},{7,6},{8,11},{9,8},{10,9... | collective-permute-start | bytes 1376264 | tf_op jit(solution)/shard_map/ppermute | solution.py:17
  195.2 22.8 %collective-permute-start.7 = (bf16[2,128,896]{2,1,0:T(8,128)(2,1)}, bf16[2,128,896]{2,1,0:T(8,128)(2,1)S(1)}, u32[]{:S(2)}, u32[]{:S(2)}) collective-permute-start(bf16[2,128,896]{2,1,0:T(8,128)(2,1)} %get-tuple-element.24), channel_id=1, source_target_pairs={{0,2},{1,3},{2,0},{3,1},{4,6},{5,7},{6,4},{7,5},{8,10},{9,11},{10,... | collective-permute-start | bytes 1376264 | tf_op jit(solution)/shard_map/ppermute | solution.py:17
  197.2 22.3 %copy-start.4 = (bf16[448,4096]{1,0:T(8,128)(2,1)S(1)}, bf16[448,4096]{1,0:T(8,128)(2,1)}, u32[]{:S(2)}) copy-start(bf16[448,4096]{1,0:T(8,128)(2,1)} %param.11) | copy-start | bytes 11010052
  203.7 32.5 %collective-permute-start.3 = (bf16[1,128,896]{2,1,0:T(8,128)(2,1)}, bf16[1,128,896]{2,1,0:T(8,128)(2,1)S(1)}, u32[]{:S(2)}, u32[]{:S(2)}) collective-permute-start(bf16[1,128,896]{2,1,0:T(8,128)(2,1)} %get-tuple-element.29), channel_id=1, source_target_pairs={{0,3},{1,0},{2,1},{3,2},{4,7},{5,4},{6,5},{7,6},{8,11},{9,8},{10,9... | collective-permute-start | bytes 688136 | tf_op jit(solution)/shard_map/ppermute | solution.py:17
  205.1 31.1 %collective-permute-start.2 = (bf16[1,128,896]{2,1,0:T(8,128)(2,1)S(1)}, bf16[1,128,896]{2,1,0:T(8,128)(2,1)S(1)}, u32[]{:S(2)}, u32[]{:S(2)}) collective-permute-start(bf16[1,128,896]{2,1,0:T(8,128)(2,1)S(1)} %get-tuple-element.30), channel_id=1, source_target_pairs={{0,2},{1,3},{2,0},{3,1},{4,6},{5,7},{6,4},{7,5},{8,10},{9,11},{10,... | collective-permute-start | bytes 688136 | tf_op jit(solution)/shard_map/ppermute | solution.py:17
  208.2 28.1 %collective-permute-start.1 = (bf16[1,128,896]{2,1,0:T(8,128)(2,1)S(1)}, bf16[1,128,896]{2,1,0:T(8,128)(2,1)}, u32[]{:S(2)}, u32[]{:S(2)}) collective-permute-start(bf16[1,128,896]{2,1,0:T(8,128)(2,1)S(1)} %get-tuple-element.31), channel_id=1, source_target_pairs={{0,1},{1,2},{2,3},{3,0},{4,5},{5,6},{6,7},{7,4},{8,9},{9,10},{10,1... | collective-permute-start | bytes 688136 | tf_op jit(solution)/shard_map/ppermute | solution.py:17
  218.0 14.3 %collective-permute-start.6 = (bf16[2,128,896]{2,1,0:T(8,128)(2,1)}, bf16[2,128,896]{2,1,0:T(8,128)(2,1)S(1)}, u32[]{:S(2)}, u32[]{:S(2)}) collective-permute-start(bf16[2,128,896]{2,1,0:T(8,128)(2,1)} %get-tuple-element.25), channel_id=1, source_target_pairs={{0,1},{1,2},{2,3},{3,0},{4,5},{5,6},{6,7},{7,4},{8,9},{9,10},{10,1... | collective-permute-start | bytes 1376264 | tf_op jit(solution)/shard_map/ppermute | solution.py:17
  232.3 15.8 %collective-permute-start.32 = (bf16[4,64,1024]{2,1,0:T(8,128)(2,1)}, bf16[4,64,1024]{2,1,0:T(8,128)(2,1)S(1)}, u32[]{:S(2)}, u32[]{:S(2)}) collective-permute-start(bf16[4,64,1024]{2,1,0:T(8,128)(2,1)} %pick.1), channel_id=1, source_target_pairs={{0,8},{8,0},{1,9},{9,1},{2,10},{10,2},{3,11},{11,3},{4,12},{12,4},... | collective-permute-start | bytes 1572872 | tf_op jit(solution)/shard_map/ppermute | solution.py:17
  236.2 12.0 %collective-permute-start.14 = (bf16[128,896]{1,0:T(8,128)(2,1)}, bf16[128,896]{1,0:T(8,128)(2,1)S(1)}, u32[]{:S(2)}, u32[]{:S(2)}) collective-permute-start(bf16[128,896]{1,0:T(8,128)(2,1)} %get-tuple-element.17), channel_id=1, source_target_pairs={{0,4},{4,0},{1,5},{5,1},{2,6},{6,2},{3,7},{7,3},{8,12},{12,8},{9,1... | collective-permute-start | bytes 688136 | tf_op jit(solution)/shard_map/ppermute | solution.py:17
  240.0 8.6 %collective-permute-start.13 = (bf16[128,896]{1,0:T(8,128)(2,1)}, bf16[128,896]{1,0:T(8,128)(2,1)S(1)}, u32[]{:S(2)}, u32[]{:S(2)}) collective-permute-start(bf16[128,896]{1,0:T(8,128)(2,1)} %get-tuple-element.16), channel_id=1, source_target_pairs={{0,4},{4,0},{1,5},{5,1},{2,6},{6,2},{3,7},{7,3},{8,12},{12,8},{9,1... | collective-permute-start | bytes 688136 | tf_op jit(solution)/shard_map/ppermute | solution.py:17
  283.8 8.5 %all-to-all-start.3 = ((f32[16,2,16]{2,1,0:T(2,128)}), f32[16,2,16]{2,1,0:T(2,128)S(1)}, u32[]{:S(2)}, u32[]{:S(2)}) async-start(f32[16,2,16]{2,1,0:T(2,128)} %broadcast_in_dim.8), calls=%async_computation.3 | async-start | bytes 32768 | tf_op jit(solution)/shard_map/all_to_all | solution.py:35
  (20 other events, 79.7 us)
Sparse Core Ops, SparseCore 0:
  27.8 39.7 all-gather.8
  69.3 50.3 all-gather.6
  135.3 31.4 all-gather.4
